TPU v7x, 32 devices: a whole 2x2x4 slice. The times are simulated.
32 devices in a mesh: ctx: 8 (over z, y), fsdp: 4 (over x, core).
Axes of the slice: x: 2, y: 2, z: 4, core: 2. Of those that a mesh axis runs over, the one named last changes fastest.
Arguments:
- tokens: bfloat16 [4, 8, 2, 128, 1024], P('fsdp', 'ctx'), may hold values from -6 to 6
- doc_starts: int32 [4, 8, 2, 128], P('fsdp', 'ctx'), may hold values from 0 to 2047, as said below
- expert_ids: int32 [4, 8, 2, 128, 1], P('fsdp', 'ctx'), may hold values from 0 to 63; in each aligned block of 256 rows (0 to 255, 256 to 511, ..., all dimensions but the last counted through in order) at most 8 rows name the same one
- query_key_value_weight: float32 [1024, 3072], P('fsdp'), may hold values from -0.1875 to 0.1875
- output_weight_matrix: float32 [1024, 1024], P('fsdp'), may hold values from -1.5 to 1.5
- expert_in: float32 [64, 1024, 4096], P('ctx', None, 'fsdp'), may hold values from -0.1875 to 0.1875
- expert_out: float32 [64, 4096, 1024], P('ctx', 'fsdp'), may hold values from -0.09375 to 0.09375
- gain_one: float32 [1024], replicated, may hold values from 0.5 to 1.5
- gain_two: float32 [1024], replicated, may hold values from 0.5 to 1.5
- grad_output: bfloat16 [4, 8, 2, 128, 1024], P('fsdp', 'ctx'), may hold values from -6 to 6
Outputs:
- block_out: bfloat16 [4, 8, 2, 128, 1024], P('fsdp', 'ctx')
- grad_tokens: float32 [4, 8, 2, 128, 1024], P('fsdp', 'ctx')
- grad_qkv_weight: float32 [1024, 3072], P('fsdp')
- grad_out_weight: float32 [1024, 1024], P('fsdp')
- grad_expert_in: float32 [64, 1024, 4096], P('ctx', None, 'fsdp')
- grad_expert_out: float32 [64, 4096, 1024], P('ctx', 'fsdp')
- grad_gain_one: float32 [1024], P('fsdp')
- grad_gain_two: float32 [1024], P('fsdp')
Inputs may be any that keep to these rules, and one draw needn't show every extreme that they name: `doc_starts`: each entry is the stream position at which the token's document begins, never after the token's own position; documents are contiguous runs of at most 1024 tokens, every stream holds one document of exactly 1024 tokens, and the last token of every stream begins a document of its own. `expert_ids`: among the 256 rows of one stream on one device, no expert is named more than 8 times, and in some of these blocks one expert is named exactly 8 times.
All inputs are finite; a program needn't handle non-finite values.
Results may differ from a plain program's by a relative error of at most 0.018.
Values may be sent and summed in bfloat16 or wider, within the bound.
A program may use at most 320 MiB of HBM per device.

v0:
```python
import math

import jax
import jax.numpy as jnp
from jax import lax
from jax.sharding import PartitionSpec as P

HEADS = 16
EXPERTS = 64
CAP = 8


EPS = 1e-05
NEGATIVE = -1e30


def position_of(row_ids, ctx_count, half_rows):
    device = row_ids // (2 * half_rows)
    upper_half = row_ids // half_rows % 2
    offset = row_ids % half_rows
    return jnp.where(
        upper_half == 0,
        device * half_rows + offset,
        (2 * ctx_count - 1 - device) * half_rows + offset,
    )


def norm_forward(value, gain):
    row_mean = jnp.mean(value, axis=-1, keepdims=True)
    centred = value - row_mean
    inverse = lax.rsqrt(jnp.mean(centred * centred, axis=-1, keepdims=True) + EPS)
    normed = centred * inverse
    return (normed * gain, normed, inverse)


def norm_backward(gradient, normed, inverse, gain):
    scaled = gradient * gain
    mean_grad = jnp.mean(scaled, axis=-1, keepdims=True)
    mean_proj = jnp.mean(scaled * normed, axis=-1, keepdims=True)
    return (
        inverse * (scaled - mean_grad - normed * mean_proj),
        jnp.sum(gradient * normed, axis=(0, 1)),
    )


def scores(query, keys, query_pos, key_pos, query_start, score_scale):
    raw_scores = (
        jnp.einsum("qshe,kshe->shqk", query, keys, preferred_element_type=jnp.float32) * score_scale
    )
    visible = (key_pos[None, None, None, :] <= query_pos[None, None, :, None]) & (
        key_pos[None, None, None, :] >= query_start.T[:, None, :, None]
    )
    return jnp.where(visible, raw_scores, NEGATIVE)


def log_totals(query, keys, query_pos, query_start, score_scale, ctx_count, half_rows, key_block):
    block_count = keys.shape[0] // key_block
    carry_shape = (query.shape[1], query.shape[2], query.shape[0])

    def log_one_block(block_index, carried):
        running_max, running = carried
        first_row = block_index * key_block
        key_piece = lax.dynamic_slice_in_dim(keys, first_row, key_block, 0)
        key_pos = position_of(
            first_row + jnp.arange(key_block, dtype=jnp.int32), ctx_count, half_rows
        )
        score_rows = scores(query, key_piece, query_pos, key_pos, query_start, score_scale)
        new_max = jnp.maximum(running_max, jnp.max(score_rows, axis=-1))
        running = running * jnp.exp(running_max - new_max) + jnp.sum(
            jnp.exp(score_rows - new_max[..., None]), axis=-1
        )
        return (new_max, running)

    running_max, running = lax.fori_loop(
        0,
        block_count,
        log_one_block,
        (jnp.full(carry_shape, NEGATIVE, jnp.float32), jnp.zeros(carry_shape, jnp.float32)),
    )
    return running_max + jnp.log(running)


def attend(
    query,
    keys,
    values,
    query_pos,
    query_start,
    log_total,
    score_scale,
    ctx_count,
    half_rows,
    key_block,
):
    block_count = keys.shape[0] // key_block
    zeros_init = jnp.zeros(query.shape, jnp.float32)

    def attend_one_block(block_index, carried):
        output, remainder = carried
        first_row = block_index * key_block
        key_piece = lax.dynamic_slice_in_dim(keys, first_row, key_block, 0)
        value_piece = lax.dynamic_slice_in_dim(values, first_row, key_block, 0)
        key_pos = position_of(
            first_row + jnp.arange(key_block, dtype=jnp.int32), ctx_count, half_rows
        )
        weights = jnp.exp(
            scores(query, key_piece, query_pos, key_pos, query_start, score_scale)
            - log_total[..., None]
        )
        rounded = weights.astype(jnp.bfloat16)
        leftover = (weights - rounded.astype(jnp.float32)).astype(jnp.bfloat16)
        output = output + jnp.einsum(
            "shqk,kshe->qshe", rounded, value_piece, preferred_element_type=jnp.float32
        )
        remainder = remainder + jnp.einsum(
            "shqk,kshe->qshe", leftover, value_piece, preferred_element_type=jnp.float32
        )
        return (output, remainder)

    return lax.fori_loop(0, block_count, attend_one_block, (zeros_init, zeros_init))


def query_grads(
    query,
    keys,
    values,
    grad_heads,
    query_pos,
    query_start,
    log_total,
    row_delta,
    score_scale,
    ctx_count,
    half_rows,
    key_block,
):
    block_count = keys.shape[0] // key_block

    def query_one_block(block_index, running):
        first_row = block_index * key_block
        key_piece = lax.dynamic_slice_in_dim(keys, first_row, key_block, 0)
        value_piece = lax.dynamic_slice_in_dim(values, first_row, key_block, 0)
        key_pos = position_of(
            first_row + jnp.arange(key_block, dtype=jnp.int32), ctx_count, half_rows
        )
        weights = jnp.exp(
            scores(query, key_piece, query_pos, key_pos, query_start, score_scale)
            - log_total[..., None]
        )
        grad_weight = jnp.einsum(
            "qshe,kshe->shqk", grad_heads, value_piece, preferred_element_type=jnp.float32
        )
        grad_score = (weights * (grad_weight - row_delta[..., None])).astype(jnp.bfloat16)
        return running + jnp.einsum(
            "shqk,kshe->qshe", grad_score, key_piece, preferred_element_type=jnp.float32
        )

    return (
        lax.fori_loop(0, block_count, query_one_block, jnp.zeros(query.shape, jnp.float32))
        * score_scale
    )


def key_grads(
    query,
    grad_heads,
    query_pos,
    query_start,
    log_total,
    row_delta,
    key_piece,
    value_piece,
    key_pos,
    score_scale,
):
    weights = jnp.exp(
        scores(query, key_piece, query_pos, key_pos, query_start, score_scale)
        - log_total[..., None]
    )
    grad_weight = jnp.einsum(
        "qshe,kshe->shqk", grad_heads, value_piece, preferred_element_type=jnp.float32
    )
    grad_score = (weights * (grad_weight - row_delta[..., None])).astype(jnp.bfloat16)
    key_part = (
        jnp.einsum("shqk,qshe->kshe", grad_score, query, preferred_element_type=jnp.float32)
        * score_scale
    )
    value_part = jnp.einsum(
        "shqk,qshe->kshe",
        weights.astype(jnp.bfloat16),
        grad_heads,
        preferred_element_type=jnp.float32,
    )
    return (key_part, value_part)


def shards(
    tokens,
    doc_starts,
    expert_ids,
    query_key_value_weight,
    output_weight_matrix,
    expert_in,
    expert_out,
    gain_one,
    gain_two,
    grad_output,
):
    seq_dev = tokens.shape[0]
    half_rows = tokens.shape[3]
    model_width = tokens.shape[4]
    local_rows = 2 * half_rows
    ctx_count = lax.axis_size("ctx")
    head_count = HEADS
    head_size = model_width // head_count
    score_scale = head_size ** (-0.5)
    keys_total = ctx_count * local_rows
    key_block = min(512, keys_total)
    own_rows = lax.axis_index("ctx") * local_rows + jnp.arange(local_rows, dtype=jnp.int32)
    query_pos = position_of(own_rows, ctx_count, half_rows)
    query_start = doc_starts.reshape(seq_dev, local_rows).T
    routes_local = expert_ids.reshape(seq_dev, local_rows).T
    start_x = (
        tokens.reshape(seq_dev, local_rows, model_width).transpose(1, 0, 2).astype(jnp.float32)
    )
    cotangent = grad_output.reshape(seq_dev, local_rows, model_width).transpose(1, 0, 2)
    projection, out_proj = (
        lax.all_gather(query_key_value_weight.astype(jnp.bfloat16), "fsdp", axis=0, tiled=True),
        lax.all_gather(output_weight_matrix.astype(jnp.bfloat16), "fsdp", axis=0, tiled=True),
    )
    first_normed_rows, hat_one, inverse_one = norm_forward(start_x, gain_one)
    normed_low = first_normed_rows.astype(jnp.bfloat16)
    projected_rows = jnp.einsum(
        "tsd,de->tse", normed_low, projection, preferred_element_type=jnp.float32
    ).astype(jnp.bfloat16)
    query = projected_rows[..., :model_width]
    keys = projected_rows[..., model_width : 2 * model_width]
    values = projected_rows[..., 2 * model_width :]
    key_all, value_all = (
        lax.all_gather(keys, "ctx", axis=0, tiled=True),
        lax.all_gather(values, "ctx", axis=0, tiled=True),
    )
    query_heads = query.reshape(local_rows, seq_dev, head_count, head_size)
    key_heads = key_all.reshape(keys_total, seq_dev, head_count, head_size)
    value_heads = value_all.reshape(keys_total, seq_dev, head_count, head_size)
    log_total = log_totals(
        query_heads, key_heads, query_pos, query_start, score_scale, ctx_count, half_rows, key_block
    )
    mixed_heads_out, remainder = attend(
        query_heads,
        key_heads,
        value_heads,
        query_pos,
        query_start,
        log_total,
        score_scale,
        ctx_count,
        half_rows,
        key_block,
    )
    mixed_low = mixed_heads_out.astype(jnp.bfloat16).reshape(local_rows, seq_dev, model_width)
    attention_rows_out = jnp.einsum(
        "tsd,de->tse", mixed_low, out_proj, preferred_element_type=jnp.float32
    )
    middle = start_x + attention_rows_out
    normed_two, hat_two, inverse_two = norm_forward(middle, gain_two)
    routed = normed_two.astype(jnp.bfloat16)
    slot_count = EXPERTS * CAP
    per_owner = EXPERTS // ctx_count
    chosen = (routes_local[..., None] == jnp.arange(EXPERTS, dtype=jnp.int32)).astype(jnp.int32)
    rank_within = jnp.sum(chosen * jnp.cumsum(chosen, axis=0), axis=-1) - 1
    slot_index = routes_local * CAP + rank_within
    dispatch = (
        slot_index.T[:, None, :] == jnp.arange(slot_count, dtype=jnp.int32)[None, :, None]
    ).astype(jnp.bfloat16)
    dispatch = dispatch.reshape(seq_dev, ctx_count, per_owner, CAP, local_rows)
    send_rows = jnp.einsum(
        "snect,tsd->nescd", dispatch, routed, preferred_element_type=jnp.float32
    ).astype(jnp.bfloat16)
    send_grads = jnp.einsum(
        "snect,tsd->nescd", dispatch, cotangent, preferred_element_type=jnp.float32
    ).astype(jnp.bfloat16)
    got_rows, got_grads = (
        lax.all_to_all(send_rows, "ctx", split_axis=0, concat_axis=0, tiled=True),
        lax.all_to_all(send_grads, "ctx", split_axis=0, concat_axis=0, tiled=True),
    )
    in_low = expert_in.astype(jnp.bfloat16)
    out_low = expert_out.astype(jnp.bfloat16)
    all_rows, all_grads = (
        lax.all_gather(got_rows, "fsdp", axis=2, tiled=True),
        lax.all_gather(got_grads, "fsdp", axis=2, tiled=True),
    )
    hidden = jnp.einsum("nercd,edf->nercf", all_rows, in_low, preferred_element_type=jnp.float32)
    active = jax.nn.gelu(hidden).astype(jnp.bfloat16)
    partial_rows = jnp.einsum(
        "nercf,efd->nercd", active, out_low, preferred_element_type=jnp.float32
    )
    result = lax.psum_scatter(
        partial_rows.astype(jnp.bfloat16), "fsdp", scatter_dimension=2, tiled=True
    )
    upstream = jnp.einsum(
        "nercd,efd->nercf", all_grads, out_low, preferred_element_type=jnp.float32
    )
    unused, gelu_back = jax.vjp(jax.nn.gelu, hidden)
    grad_hidden = gelu_back(upstream)[0].astype(jnp.bfloat16)
    grad_in = jnp.einsum(
        "nercd,nercf->edf", all_rows, grad_hidden, preferred_element_type=jnp.float32
    )
    grad_outw = jnp.einsum(
        "nercf,nercd->efd", active, all_grads, preferred_element_type=jnp.float32
    )
    row_part = jnp.einsum(
        "nercf,edf->nercd", grad_hidden, in_low, preferred_element_type=jnp.float32
    )
    row_grad = lax.psum_scatter(row_part, "fsdp", scatter_dimension=2, tiled=True).astype(
        jnp.bfloat16
    )
    back_rows = lax.all_to_all(result, "ctx", split_axis=0, concat_axis=0, tiled=True)
    expert_sum = jnp.einsum(
        "snect,nescd->tsd", dispatch, back_rows, preferred_element_type=jnp.float32
    )
    output_rows = middle + expert_sum
    returned = lax.all_to_all(row_grad, "ctx", split_axis=0, concat_axis=0, tiled=True)
    grad_routed = jnp.einsum(
        "snect,nescd->tsd", dispatch, returned, preferred_element_type=jnp.float32
    )
    grad_mid_norm, grad_gain_two = norm_backward(grad_routed, hat_two, inverse_two, gain_two)
    grad_middle = cotangent.astype(jnp.float32) + grad_mid_norm
    grad_attn = grad_middle.astype(jnp.bfloat16)
    grad_outproj = jnp.einsum(
        "tsd,tse->de", mixed_low, grad_attn, preferred_element_type=jnp.float32
    )
    grad_mixed = jnp.einsum(
        "tse,de->tsd", grad_attn, out_proj, preferred_element_type=jnp.float32
    ).astype(jnp.bfloat16)
    grad_heads = grad_mixed.reshape(local_rows, seq_dev, head_count, head_size)
    full_mixed = mixed_heads_out + remainder
    row_delta = jnp.sum(grad_heads.astype(jnp.float32) * full_mixed, axis=-1).transpose(1, 2, 0)
    grad_query = query_grads(
        query_heads,
        key_heads,
        value_heads,
        grad_heads,
        query_pos,
        query_start,
        log_total,
        row_delta,
        score_scale,
        ctx_count,
        half_rows,
        key_block,
    ).astype(jnp.bfloat16)
    sub_rows = math.gcd(local_rows * lax.axis_size("ctx"), key_block)

    def one_piece(piece_index):
        piece_start = piece_index * sub_rows
        key_piece = lax.dynamic_slice_in_dim(key_heads, piece_start, sub_rows, 0)
        value_piece = lax.dynamic_slice_in_dim(value_heads, piece_start, sub_rows, 0)
        key_pos = position_of(
            piece_start + jnp.arange(sub_rows, dtype=jnp.int32), ctx_count, half_rows
        )
        key_part, value_part = key_grads(
            query_heads,
            grad_heads,
            query_pos,
            query_start,
            log_total,
            row_delta,
            key_piece,
            value_piece,
            key_pos,
            score_scale,
        )
        return jnp.concatenate(
            [
                key_part.reshape(sub_rows, seq_dev, model_width),
                value_part.reshape(sub_rows, seq_dev, model_width),
            ],
            axis=-1,
        )

    summed = lax.psum_scatter(
        lax.map(
            one_piece, jnp.arange(local_rows * lax.axis_size("ctx") // sub_rows, dtype=jnp.int32)
        ).reshape(local_rows * lax.axis_size("ctx"), seq_dev, 2 * model_width),
        "ctx",
        scatter_dimension=0,
        tiled=True,
    )
    grad_key = summed[..., :model_width].astype(jnp.bfloat16)
    grad_value = summed[..., model_width:].astype(jnp.bfloat16)
    grad_projected = jnp.concatenate(
        [grad_query.reshape(local_rows, seq_dev, model_width), grad_key, grad_value], axis=-1
    )
    grad_projection = jnp.einsum(
        "tsd,tse->de", normed_low, grad_projected, preferred_element_type=jnp.float32
    )
    grad_normed = jnp.einsum(
        "tse,de->tsd", grad_projected, projection, preferred_element_type=jnp.float32
    )
    grad_in_norm, grad_gain_one = norm_backward(grad_normed, hat_one, inverse_one, gain_one)
    grad_start = grad_middle + grad_in_norm
    shard_proj, shard_outproj, shard_gain_one, shard_gain_two = (
        lax.psum_scatter(
            grad_projection.astype(jnp.bfloat16), "fsdp", scatter_dimension=0, tiled=True
        ).astype(jnp.float32),
        lax.psum_scatter(
            grad_outproj.astype(jnp.bfloat16), "fsdp", scatter_dimension=0, tiled=True
        ).astype(jnp.float32),
        lax.psum_scatter(
            grad_gain_one.astype(jnp.bfloat16), "fsdp", scatter_dimension=0, tiled=True
        ).astype(jnp.float32),
        lax.psum_scatter(
            grad_gain_two.astype(jnp.bfloat16), "fsdp", scatter_dimension=0, tiled=True
        ).astype(jnp.float32),
    )
    shard_proj, shard_outproj, shard_gain_one, shard_gain_two = (
        lax.psum(shard_proj.astype(jnp.bfloat16), "ctx").astype(jnp.float32),
        lax.psum(shard_outproj.astype(jnp.bfloat16), "ctx").astype(jnp.float32),
        lax.psum(shard_gain_one.astype(jnp.bfloat16), "ctx").astype(jnp.float32),
        lax.psum(shard_gain_two.astype(jnp.bfloat16), "ctx").astype(jnp.float32),
    )
    block_out = output_rows.transpose(1, 0, 2).reshape(tokens.shape).astype(jnp.bfloat16)
    grad_tokens = grad_start.transpose(1, 0, 2).reshape(tokens.shape)
    return (
        block_out,
        grad_tokens,
        shard_proj,
        shard_outproj,
        grad_in,
        grad_outw,
        shard_gain_one,
        shard_gain_two,
    )


def solution(mesh):
    return jax.shard_map(
        shards,
        mesh=mesh,
        in_specs=(
            P("fsdp", "ctx", None, None, None),
            P("fsdp", "ctx", None, None),
            P("fsdp", "ctx", None, None, None),
            P("fsdp", None),
            P("fsdp", None),
            P("ctx", None, "fsdp"),
            P("ctx", "fsdp", None),
            P(),
            P(),
            P("fsdp", "ctx", None, None, None),
        ),
        out_specs=(
            P("fsdp", "ctx", None, None, None),
            P("fsdp", "ctx", None, None, None),
            P("fsdp", None),
            P("fsdp", None),
            P("ctx", None, "fsdp"),
            P("ctx", "fsdp", None),
            P("fsdp"),
            P("fsdp"),
        ),
        check_vma=False,
    )
```

profile of v0, /device:TPU:1, one launch (start us, length us, event | category | flops | bytes accessed | tf_op | source)
XLA Modules:
  0.0 1290.8 jit_solution(1480258991457605327)
XLA Ops:
  15.0 44.5 %all-gather.7.cloned.1.call-done = bf16[1024,3072]{1,0:T(8,128)(2,1)} async-done(((bf16[256,3072]{1,0:T(8,128)(2,1)}), bf16[1024,3072]{1,0:T(8,128)(2,1)}) %all-gather.7.cloned.1.call-update) | async-done | bytes 6291472 | tf_op jit(solution)/shard_map/all_gather | solution.py:228
  69.3 67.9 %all-gather.11.cloned.1.call-done = bf16[2048,1,1024]{2,0,1:T(8,128)(2,1)} async-done(((bf16[256,1,1024]{2,0,1:T(8,128)(2,1)}), bf16[2048,1,1024]{2,0,1:T(8,128)(2,1)}) %all-gather.11.cloned.1.call-update) | async-done | bytes 4194320 | tf_op jit(solution)/shard_map/all_gather | solution.py:240
  143.7 18.8 %while.70 = (s32[]{:T(128)}, f32[1,16,256]{2,1,0:T(8,128)S(1)}, f32[1,16,256]{2,1,0:T(8,128)S(1)}, s32[1,1,2,128]{3,2,1,0:T(2,128)S(1)}, bf16[2048,1,16,64]{0,3,...) while((s32[]{:T(128)}, f32[1,16,256]{2,1,0:T(8,128)S(1)}, ...), condition=%wide.region_5.6_spmd.clone, body=%wide.region_2.5_spmd.clone.sunk | while | flops 283566080 | bytes 18963640 | solution.py:74
  162.5 49.1 %all-gather.9.cloned.1.call-done = bf16[2048,1,1024]{2,0,1:T(8,128)(2,1)} async-done(((bf16[256,1,1024]{2,0,1:T(8,128)(2,1)}), bf16[2048,1,1024]{2,0,1:T(8,128)(2,1)}) %all-gather.9.cloned.1.call-update) | async-done | bytes 4194320 | tf_op jit(solution)/shard_map/all_gather | solution.py:241
  218.1 30.2 %while.71 = (s32[]{:T(128)}, f32[256,1,16,64]{0,3,2,1:T(8,128)S(1)}, f32[256,1,16,64]{0,3,2,1:T(8,128)}, bf16[2048,1,16,64]{0,3,2,1:T(8,128)(2,1)}, s32[1,1,2,12...) while((s32[]{:T(128)}, ...), condition=%wide.region_7.8_spmd.clone, body=%wide.region_6.7_spmd.clone.sunk | while | flops 829853696 | bytes 58629412 | solution.py:120
  252.6 28.5 %all_to_all.20 = bf16[8,8,1,8,1024]{4,3,1,2,0:T(8,128)(2,1)} all-to-all(bf16[8,8,1,8,1024]{4,3,1,2,0:T(8,128)(2,1)S(1)} %fusion.177), channel_id=1, replica_groups=mesh['ctx'=8,'fsdp'=4] {'ctx'}, dimensions={0} | all-to-all | bytes 2097152 | tf_op jit(solution)/shard_map/all_to_all | solution.py:284
  281.6 28.8 %all_to_all.21 = bf16[8,8,1,8,1024]{4,3,1,2,0:T(8,128)(2,1)} all-to-all(bf16[8,8,1,8,1024]{4,3,1,2,0:T(8,128)(2,1)S(1)} %fusion.178), channel_id=1, replica_groups=mesh['ctx'=8,'fsdp'=4] {'ctx'}, dimensions={0} | all-to-all | bytes 2097152 | tf_op jit(solution)/shard_map/all_to_all | solution.py:285
  316.3 20.7 %fusion.158 = (bf16[8,8,4,8,1024]{4,3,2,0,1:T(8,128)(2,1)}, f32[8,8,4,8,1024]{4,3,2,1,0:T(8,128)}) fusion(f32[8,1024,1024]{2,1,0:T(8,128)} %param.23, bf16[8,8,4,8,1024]{4,3,1,0,2:T(8,128)(2,1)} %all-gather.15.cloned.1.call-done), kind=kOutput, calls=%fused_computation.258 | convolution fusion | flops 4322230272 | bytes 50331648 | tf_op jit(solution)/shard_map/nercd,edf->nercf/dot_general | solution.py:293
  337.0 15.2 %all-gather.17.cloned.1.call-done = bf16[8,8,4,8,1024]{4,3,1,0,2:T(8,128)(2,1)} async-done(((bf16[8,8,1,8,1024]{4,3,1,0,2:T(8,128)(2,1)}), bf16[8,8,4,8,1024]{4,3,1,0,2:T(8,128)(2,1)}) %all-gather.17.cloned.1.call-update) | async-done | bytes 4194320 | tf_op jit(solution)/shard_map/all_gather | solution.py:291
  352.3 19.1 %fusion.154 = bf16[8,8,4,8,1024]{4,3,2,0,1:T(8,128)(2,1)} fusion(f32[8,8,4,8,1024]{4,3,2,1,0:T(8,128)} %get-tuple-element.1234, f32[8,1024,1024]{2,1,0:T(8,128)} %param.24, bf16[8,8,4,8,1024]{4,3,1,0,2:T(8,128)(2,1)} %all-gather.17.cloned.1.call-done), kind=kOutput, calls=%fused_computation.251 | convolution fusion | flops 4345298944 | bytes 50331648 | tf_op jit(solution)/shard_map/nercd,efd->nercf/dot_general | solution.py:301
  371.4 16.1 %fusion.172 = f32[8,8,4,8,1024]{4,3,2,0,1:T(8,128)} fusion(bf16[8,8,4,8,1024]{4,3,2,0,1:T(8,128)(2,1)} %fusion.154, f32[8,1024,1024]{2,1,0:T(8,128)} %param.23), kind=kOutput, calls=%fused_computation.273 | convolution fusion | flops 4303355904 | bytes 46137344 | tf_op jit(solution)/shard_map/nercf,edf->nercd/dot_general | solution.py:312
  387.5 146.5 %all-reduce.14 = bf16[8,8,4,8,1024]{4,3,2,0,1:T(8,128)(2,1)} all-reduce(f32[8,8,4,8,1024]{4,3,2,0,1:T(8,128)} %fusion.172), channel_id=3, replica_groups=mesh['ctx'=8,'fsdp'=4] {'fsdp'}, use_global_device_ids=true, to_apply=%region_14.15.clone | all-reduce | flops 2097152 | bytes 12582912
  542.7 25.2 %all-to-all-done.3 = bf16[8,8,1,8,1024]{4,3,2,1,0:T(8,128)(2,1)} async-done(((bf16[8,8,1,8,1024]{4,3,2,1,0:T(8,128)(2,1)}), bf16[8,8,1,8,1024]{4,3,2,1,0:T(8,128)(2,1)}, u32[]{:S(2)}, u32[]{:S(2)}) %all-to-all-start.3) | async-done | bytes 1048608 | tf_op jit(solution)/shard_map/all_to_all | solution.py:323
  576.1 130.5 %while.69 = (s32[]{:T(128)}, f32[4,512,1,2048]{3,1,0,2:T(8,128)}, s32[4]{0:T(128)S(1)}, s32[1,1,2,128]{3,2,1,0:T(2,128)S(1)}, bf16[2048,1,16,64]{0,3,2,1:T(8,128...) while((s32[]{:T(128)}, f32[4,512,1,2048]{3,1,0,2:T(8,128)}, ...), condition=%wide.region_21.22_spmd.clone, body=%wide.region_20.21_spmd.clone.sunk | while | flops 1096716288 | bytes 59170020 | solution.py:383
  583.5 7.3 fusion.267
  616.2 7.3 fusion.267
  648.8 7.3 fusion.267
  681.4 7.3 fusion.267
  706.7 17.0 %convert_bitcast_fusion = bf16[8,8,4,8,1024]{4,3,2,0,1:T(8,128)(2,1)} fusion(bf16[8,8,4,8,1024]{4,3,2,0,1:T(8,128)(2,1)} %get-tuple-element.1233, f32[8,1024,1024]{2,1,0:T(8,128)} %param.24), kind=kOutput, calls=%fused_computation.270 | convolution fusion | flops 4305453056 | bytes 41943040 | tf_op jit(solution)/shard_map/nercf,efd->nercd/dot_general | solution.py:295
  727.1 59.2 %while.72 = (s32[]{:T(128)}, f32[256,1,16,64]{0,3,2,1:T(8,128)}, bf16[2048,1,16,64]{0,3,2,1:T(8,128)(2,1)}, s32[1,1,2,128]{3,2,1,0:T(2,128)S(1)}, bf16[256,1,16,...) while((s32[]{:T(128)}, f32[256,1,16,64]{0,3,2,1:T(8,128)}, ...), condition=%wide.region_19.20_spmd.clone, body=%wide.region_18.19_spmd.clone.sunk | while | flops 818843648 | bytes 31761160 | solution.py:159
  733.4 7.5 fusion.284
  748.1 7.6 fusion.284
  763.0 7.5 fusion.284
  777.7 7.6 fusion.284
  787.9 201.4 %reduce-scatter.6.cloned.1.call-done = f32[256,1,2048]{2,0,1:T(8,128)} async-done(((f32[2048,1,2048]{2,0,1:T(8,128)}), f32[256,1,2048]{2,0,1:T(8,128)}) %reduce-scatter.6.cloned.1.call-update) | async-done | bytes 2097168 | tf_op jit(solution)/shard_map/reduce_scatter | solution.py:382
  996.7 19.9 %convolution_bitcast_fusion.1 = f32[8,1024,1024]{2,1,0:T(8,128)} fusion(bf16[8,8,4,8,1024]{4,3,2,0,1:T(8,128)(2,1)} %fusion.154, bf16[8,8,4,8,1024]{4,3,1,0,2:T(8,128)(2,1)} %all-gather.15.cloned.1.call-done), kind=kOutput, calls=%fused_computation.242 | convolution fusion | flops 4294967296 | bytes 41943040 | tf_op jit(solution)/shard_map/nercd,nercf->edf/dot_general | solution.py:306
  1016.6 59.5 %all-reduce.11.cloned.1.call-done = bf16[8,8,4,8,1024]{4,3,2,0,1:T(8,128)(2,1)} async-done(((bf16[8,8,4,8,1024]{4,3,2,0,1:T(8,128)(2,1)}), bf16[8,8,4,8,1024]{4,3,2,0,1:T(8,128)(2,1)}) %all-reduce.11.cloned.1.call-update) | async-done | bytes 4194320
  1084.6 26.3 %reduce-scatter.10.cloned.1.call-done = bf16[256,1024]{1,0:T(8,128)(2,1)} async-done(((bf16[1024,1024]{1,0:T(8,128)(2,1)}), bf16[256,1024]{1,0:T(8,128)(2,1)}) %reduce-scatter.10.cloned.1.call-update) | async-done | bytes 524304 | tf_op jit(solution)/shard_map/reduce_scatter | solution.py:407
  1110.9 61.5 %reduce-scatter.8.cloned.1.call-done = bf16[256,3072]{1,0:T(8,128)(2,1)} async-done(((bf16[1024,3072]{1,0:T(8,128)(2,1)}), bf16[256,3072]{1,0:T(8,128)(2,1)}) %reduce-scatter.8.cloned.1.call-update) | async-done | bytes 1572880 | tf_op jit(solution)/shard_map/reduce_scatter | solution.py:404
  1172.6 19.8 %convolution_bitcast_fusion = f32[8,1024,1024]{2,1,0:T(8,128)} fusion(bf16[8,8,4,8,1024]{4,3,1,0,2:T(8,128)(2,1)} %all-gather.17.cloned.1.call-done, bf16[8,8,4,8,1024]{4,3,2,0,1:T(8,128)(2,1)} %get-tuple-element.1233), kind=kOutput, calls=%fused_computation.241 | convolution fusion | flops 4294967296 | bytes 41943040 | tf_op jit(solution)/shard_map/nercf,nercd->efd/dot_general | solution.py:309
  1206.3 17.8 %all-reduce.4 = (bf16[256]{0:T(256)(128)(2,1)S(1)}, bf16[256]{0:T(256)(128)(2,1)S(1)}) all-reduce(bf16[256]{0:T(256)(128)(2,1)S(1)} %dynamic-slice.5, bf16[256]{0:T(256)(128)(2,1)S(1)} %dynamic-slice.7), channel_id=1, replica_groups=mesh['ctx'=8,'fsdp'=4] {'ctx'}, use_global_device_ids=true, to_apply=%region_31.32 | all-reduce | flops 512 | bytes 2048 | tf_op jit(solution)/shard_map/psum | solution.py:420
  1226.7 51.8 %all-reduce.13.cloned.1.call-done = (bf16[256,3072]{1,0:T(8,128)(2,1)}, bf16[256,1024]{1,0:T(8,128)(2,1)}) async-done(((bf16[256,3072]{1,0:T(8,128)(2,1)}, bf16[256,1024]{1,0:T(8,128)(2,1)}), (bf16[256,3072]{1,0:T(8,128)(2,1)}, bf16[256,1024]{1,0:T(8,128)(2,1)})) %all-reduce.13.cloned.1.call-update) | async-done | bytes 2097168 | tf_op jit(solution)/shard_map/psum | solution.py:418
  (315 shorter events, 275.6 us)
Async XLA Ops:
  7.2 52.4 %all-gather.7.cloned.1.call-start = ((), (), s32[]{:S(2)}) async-start(), calls=%async_computation.7 | async-start | bytes 7864320 | tf_op jit(solution)/shard_map/all_gather | solution.py:228
  10.5 126.7 %all-gather.11.cloned.1.call-start = ((), (), s32[]{:S(2)}) async-start(), calls=%async_computation.9 | async-start | bytes 4718592 | tf_op jit(solution)/shard_map/all_gather | solution.py:240
  15.0 51.0 %copy-start.19 = (f32[256,1024]{1,0:T(8,128)S(1)}, f32[256,1024]{1,0:T(8,128)}, u32[]{:S(2)}) copy-start(f32[256,1024]{1,0:T(8,128)} %param.22) | copy-start | bytes 3145732
  15.0 52.6 %copy-start.37 = (s32[1,1,2,128,1]{3,4,2,1,0:T(1,128)S(1)}, s32[1,1,2,128,1]{3,4,2,1,0:T(1,128)}, u32[]{:S(2)}) copy-start(s32[1,1,2,128,1]{3,4,2,1,0:T(1,128)} %param.20) | copy-start | bytes 3076
  15.0 53.5 %copy-start.7 = (bf16[1,1,2,128,1024]{4,3,2,1,0:T(8,128)(2,1)S(1)}, bf16[1,1,2,128,1024]{4,3,2,1,0:T(8,128)(2,1)}, u32[]{:S(2)}) copy-start(bf16[1,1,2,128,1024]{4,3,2,1,0:T(8,128)(2,1)} %param.18) | copy-start | bytes 1572868
  64.1 79.6 %copy-start.24 = (s32[1,1,2,128]{3,2,1,0:T(2,128)S(1)}, s32[1,1,2,128]{3,2,1,0:T(2,128)}, u32[]{:S(2)}) copy-start(s32[1,1,2,128]{3,2,1,0:T(2,128)} %param.19) | copy-start | bytes 3076
  65.2 146.4 %all-gather.9.cloned.1.call-start = ((), (), s32[]{:S(2)}) async-start(), calls=%async_computation.8 | async-start | bytes 4718592 | tf_op jit(solution)/shard_map/all_gather | solution.py:241
  66.0 182.4 %all-gather.13.cloned.1.call-start = ((), (), s32[]{:S(2)}) async-start(), calls=%async_computation.10 | async-start | bytes 2621440 | tf_op jit(solution)/shard_map/all_gather | solution.py:229
  66.9 249.4 %all-gather.15.cloned.1.call-start = ((), (), s32[]{:S(2)}) async-start(), calls=%async_computation.11 | async-start | bytes 5242880 | tf_op jit(solution)/shard_map/all_gather | solution.py:290
  67.5 500.4 %copy-start.25 = (s32[8,8,8]{2,0,1:T(8,128)}, s32[8,8,8]{2,0,1:T(8,128)S(1)}, u32[]{:S(2)}) copy-start(s32[8,8,8]{2,0,1:T(8,128)S(1)} %multiply_add_fusion) | copy-start | bytes 6148
  68.6 180.7 %copy-start.5 = (f32[1,1,2,128,1024]{4,3,2,1,0:T(8,128)}, f32[1,1,2,128,1024]{4,3,2,1,0:T(8,128)S(1)}, u32[]{:S(2)}) copy-start(f32[1,1,2,128,1024]{4,3,2,1,0:T(8,128)S(1)} %convert_element_type.332) | copy-start | bytes 3145732
  69.1 498.9 %copy-start.35 = (s32[256]{0:T(256)}, s32[256]{0:T(256)S(1)}, u32[]{:S(2)}) copy-start(s32[256]{0:T(256)S(1)} %add_add_fusion) | copy-start | bytes 3076
  218.1 33.9 %copy-start.38 = (f32[1024]{0:T(1024)S(1)}, f32[1024]{0:T(1024)}, u32[]{:S(2)}) copy-start(f32[1024]{0:T(1024)} %param.26) | copy-start | bytes 12292
  251.7 318.9 %copy-start.3 = (f32[256,1024]{1,0:T(8,128)}, f32[256,1024]{1,0:T(8,128)S(1)}, u32[]{:S(2)}) copy-start(f32[256,1024]{1,0:T(8,128)S(1)} %get-tuple-element.1232) | copy-start | bytes 3145732
  252.0 29.2 %copy-start.17 = (bf16[1,1,2,128,1024]{4,3,2,1,0:T(8,128)(2,1)S(1)}, bf16[1,1,2,128,1024]{4,3,2,1,0:T(8,128)(2,1)}, u32[]{:S(2)}) copy-start(bf16[1,1,2,128,1024]{4,3,2,1,0:T(8,128)(2,1)} %param.27) | copy-start | bytes 1572868
  252.0 58.4 %copy-start.40 = (u32[32]{0:T(128)S(1)}, u32[32]{0:T(128)}, u32[]{:S(2)}) copy-start(u32[32]{0:T(128)} %constant.816) | copy-start | bytes 388
  281.1 71.2 %all-gather.17.cloned.1.call-start = ((), (), s32[]{:S(2)}) async-start(), calls=%async_computation.12 | async-start | bytes 5242880 | tf_op jit(solution)/shard_map/all_gather | solution.py:291
  387.5 183.1 %copy-start.18 = (bf16[1,1,2,128,1024]{4,3,2,1,0:T(8,128)(2,1)S(1)}, bf16[1,1,2,128,1024]{4,3,2,1,0:T(8,128)(2,1)}, u32[]{:S(2)}) copy-start(bf16[1,1,2,128,1024]{4,3,2,1,0:T(8,128)(2,1)} %param.27) | copy-start | bytes 1572868
  536.0 38.7 %copy-start.14 = (f32[256,1,16,64]{0,3,2,1:T(8,128)S(1)}, f32[256,1,16,64]{0,3,2,1:T(8,128)}, u32[]{:S(2)}) copy-start(f32[256,1,16,64]{0,3,2,1:T(8,128)} %copy-done.13) | copy-start | bytes 3145732
  537.0 30.9 %all-to-all-start.3 = ((bf16[8,8,1,8,1024]{4,3,2,1,0:T(8,128)(2,1)}), bf16[8,8,1,8,1024]{4,3,2,1,0:T(8,128)(2,1)}, u32[]{:S(2)}, u32[]{:S(2)}) async-start(bf16[8,8,1,8,1024]{4,3,2,1,0:T(8,128)(2,1)} %copy.117), calls=%async_computation.3 | async-start | bytes 2097152 | tf_op jit(solution)/shard_map/all_to_all | solution.py:323
  542.4 446.8 %reduce-scatter.6.cloned.1.call-start = ((), (), s32[]{:S(2)}) async-start(), calls=%async_computation.13 | async-start | bytes 18874368 | tf_op jit(solution)/shard_map/reduce_scatter | solution.py:382
  706.6 369.5 %all-reduce.11.cloned.1.call-start = ((), (), s32[]{:S(2)}) async-start(), calls=%async_computation.16 | async-start | bytes 8388608
  723.8 387.2 %reduce-scatter.10.cloned.1.call-start = ((), (), s32[]{:S(2)}) async-start(), calls=%async_computation.15 | async-start | bytes 2621440 | tf_op jit(solution)/shard_map/reduce_scatter | solution.py:407
  726.6 445.9 %reduce-scatter.8.cloned.1.call-start = ((), (), s32[]{:S(2)}) async-start(), calls=%async_computation.14 | async-start | bytes 7864320 | tf_op jit(solution)/shard_map/reduce_scatter | solution.py:404
  727.0 264.9 %copy-start.6 = (f32[1,1,2,128,1024]{4,3,2,1,0:T(8,128)S(1)}, f32[1,1,2,128,1024]{4,3,2,1,0:T(8,128)}, u32[]{:S(2)}) copy-start(f32[1,1,2,128,1024]{4,3,2,1,0:T(8,128)} %copy-done.5) | copy-start | bytes 3145732
  727.0 264.9 %copy-start.27 = (f32[1024]{0:T(1024)S(1)}, f32[1024]{0:T(1024)}, u32[]{:S(2)}) copy-start(f32[1024]{0:T(1024)} %param.25) | copy-start | bytes 12292
  727.1 264.9 %copy-start.30 = (f32[256]{0:T(256)S(1)}, f32[256]{0:T(256)}, u32[]{:S(2)}) copy-start(f32[256]{0:T(256)} %copy-done.29) | copy-start | bytes 3076
  727.1 264.9 %copy-start.33 = (f32[256]{0:T(256)S(1)}, f32[256]{0:T(256)}, u32[]{:S(2)}) copy-start(f32[256]{0:T(256)} %copy-done.32) | copy-start | bytes 3076
  787.9 208.8 %copy-start.15 = (bf16[256,1,1024]{2,0,1:T(8,128)(2,1)}, bf16[256,1,1024]{2,0,1:T(8,128)(2,1)S(1)}, u32[]{:S(2)}) copy-start(bf16[256,1,1024]{2,0,1:T(8,128)(2,1)S(1)} %copy.121) | copy-start | bytes 1572868
  1079.2 113.3 %all-to-all-start.1 = ((bf16[8,8,1,8,1024]{4,3,2,1,0:T(8,128)(2,1)}), bf16[8,8,1,8,1024]{4,3,2,1,0:T(8,128)(2,1)}, u32[]{:S(2)}, u32[]{:S(2)}) async-start(bf16[8,8,1,8,1024]{4,3,2,1,0:T(8,128)(2,1)} %copy.111), calls=%async_computation.1 | async-start | bytes 2097152 | tf_op jit(solution)/shard_map/all_to_all | solution.py:318
  1084.4 194.1 %all-reduce.13.cloned.1.call-start = ((), (), s32[]{:S(2)}) async-start(), calls=%async_computation.17 | async-start | bytes 4194304 | tf_op jit(solution)/shard_map/psum | solution.py:418
  1192.4 32.9 %copy-start.2 = (f32[256,1,1024]{2,0,1:T(8,128)S(1)}, f32[256,1,1024]{2,0,1:T(8,128)}, u32[]{:S(2)}) copy-start(f32[256,1,1024]{2,0,1:T(8,128)} %copy-done) | copy-start | bytes 3145732
  (37 other events, 287.1 us)
Sparse Core Ops, SparseCore 0:
  10.6 48.8 all-gather.6
  65.4 71.7 all-gather.10
  139.9 71.6 all-gather.8
  213.6 22.4 all-gather.12
  281.2 35.0 all-gather.14
  317.8 34.4 all-gather.16
  706.8 282.4 reduce-scatter.5
  991.7 84.3 all-reduce.10
  1079.2 31.6 reduce-scatter.9
  1114.1 58.3 reduce-scatter.7
  1176.1 102.2 all-reduce.12
where the time goes:
time: 1300 us; the launch traced here: 1290 us
  waiting for transfers between devices  609 us (47%)
  matrix products  309 us (24%)
  blocking collectives  227 us (17%)
  local copies, waits for them, and re-layouts  72.5 us (6%)
  other arithmetic  42.3 us (3%)
  between operations  15.4 us (1%)
    reduce_scatter x1, waiting for transfers between devices, shards(): lax.psum_scatter(lax.map(one_piece, jnp.arange(local_rows * lax.axis_size...  201 us
    unnamed x2, blocking collectives  152 us
    dot_general x16, matrix products, scores(): jnp.einsum('qshe,kshe->shqk', query, keys, preferred_element_type=jnp.flo...  69.5 us
    all_gather x1, waiting for transfers between devices, shards(): lax.all_gather(keys, 'ctx', axis=0, tiled=True)  67.9 us
    reduce_scatter x1, waiting for transfers between devices, shards(): lax.psum_scatter(grad_projection.astype(jnp.bfloat16), 'fsdp', scatter_di...  61.5 us
    unnamed x12, waiting for transfers between devices  60.4 us
    psum x1, waiting for transfers between devices, shards(): lax.psum(shard_proj.astype(jnp.bfloat16), 'ctx').astype(jnp.float32)  51.8 us
    all_gather x1, waiting for transfers between devices, shards(): lax.all_gather(values, 'ctx', axis=0, tiled=True)  49.1 us
  transfers between devices with their start and end apart: 13, of which 11 were waited for; matrix products, arithmetic and copies ran while one was open for 17% of the time, Pallas kernels for 0%

commit v1 on v0

--- a/solution.py
+++ b/solution.py
@@ -3,6 +3,8 @@
 import jax
 import jax.numpy as jnp
 from jax import lax
+from jax.experimental import pallas as pl
+from jax.experimental.pallas import tpu as pltpu
 from jax.sharding import PartitionSpec as P
 
 HEADS = 16
@@ -268,7 +270,13 @@
     slot_count = EXPERTS * CAP
     per_owner = EXPERTS // ctx_count
     chosen = (routes_local[..., None] == jnp.arange(EXPERTS, dtype=jnp.int32)).astype(jnp.int32)
-    rank_within = jnp.sum(chosen * jnp.cumsum(chosen, axis=0), axis=-1) - 1
+    earlier = (
+        jnp.arange(local_rows)[:, None] >= jnp.arange(local_rows)[None, :]
+    ).astype(jnp.bfloat16)
+    running = jnp.einsum(
+        "tu,use->tse", earlier, chosen.astype(jnp.bfloat16), preferred_element_type=jnp.float32
+    )
+    rank_within = jnp.sum(chosen * running.astype(jnp.int32), axis=-1) - 1
     slot_index = routes_local * CAP + rank_within
     dispatch = (
         slot_index.T[:, None, :] == jnp.arange(slot_count, dtype=jnp.int32)[None, :, None]
@@ -434,9 +442,945 @@
     )
 
 
+BF = jnp.bfloat16
+F32 = jnp.float32
+MESH_ID = pl.DeviceIdType.MESH
+ANY = pl.BlockSpec(memory_space=pl.ANY)
+DMA = pltpu.SemaphoreType.DMA
+VMEM_CAP = 56 << 20
+
+
+def place():
+    c = lax.axis_index("ctx")
+    f = lax.axis_index("fsdp")
+    return c, f, c // 2, c % 2, f // 2, f % 2
+
+
+def remote(src, dst, send, recv, device):
+    return pltpu.make_async_remote_copy(
+        src_ref=src, dst_ref=dst, send_sem=send, recv_sem=recv, device_id=device, device_id_type=MESH_ID
+    )
+
+
+def block_at(c, half, count):
+    return c if half == 0 else 2 * count - 1 - c
+
+
+def params(side=True):
+    return pltpu.CompilerParams(has_side_effects=side, vmem_limit_bytes=VMEM_CAP)
+
+
+def gather_stream(normed, starts, weight):
+    count = lax.axis_size("ctx")
+    depth = count // 2
+    rows, width = weight.shape
+    pieces = 4
+    piece = rows // pieces
+
+    def kernel(n_ref, s_ref, w_ref, tok, st, wall, rs_t, ss_p, ss_up, ss_dn, ss_sib, rs_s, ss_s, rs_wx, ss_wx, rs_ws, ss_ws, rs_wf, ss_wf, loc):
+        c, f, z, y, x, k = place()
+        sib = (c, f + 1 - 2 * k)
+        xn = (c, (f + 2) % 4)
+        partner = (c + 1 - 2 * y, f + 1 - 2 * k)
+        up = (c + 2, f)
+        down = (c - 2, f)
+        holder = k == y
+
+        def wpart(ref, shard, i):
+            return ref.at[shard, pl.ds(i * piece, piece)]
+
+        for i in range(pieces):
+            remote(w_ref.at[pl.ds(i * piece, piece)], wpart(wall, f, i), ss_wx.at[i], rs_wx.at[i], xn).start()
+
+        def send_in(h):
+            return remote(
+                n_ref.at[h], tok.at[block_at(c, h, count)], ss_p.at[h], rs_t.at[block_at(c, h, count)], partner
+            )
+
+        def local_in(h):
+            return pltpu.make_async_copy(
+                n_ref.at[h], tok.at[block_at(c, h, count)], rs_t.at[block_at(c, h, count)]
+            )
+
+        @pl.when(holder)
+        def _():
+            for h in range(2):
+                local_in(h).start()
+
+        @pl.when(jnp.logical_not(holder))
+        def _():
+            for h in range(2):
+                send_in(h).start()
+
+        for zt in range(depth):
+            for kt in range(2):
+                dev = (2 * zt + k, 2 * x + kt)
+                slot = 2 * zt + kt
+                mine = holder & (z == zt) & (k == kt)
+
+                @pl.when(mine)
+                def _(dev=dev, slot=slot):
+                    pltpu.make_async_copy(s_ref, st.at[c], rs_s.at[c]).start()
+
+                @pl.when(jnp.logical_not(mine))
+                def _(dev=dev, slot=slot):
+                    remote(s_ref, st.at[c], ss_s.at[slot], rs_s.at[c], dev).start()
+
+        remote(w_ref, wall.at[f], ss_ws, rs_ws, sib).start()
+        pltpu.make_async_copy(w_ref, wall.at[f], loc).start()
+
+        def copy_block(zb, h, ss, dev):
+            b = block_at(2 * zb + k, h, count)
+            return remote(tok.at[b], tok.at[b], ss, rs_t.at[b], dev)
+
+        def wait_block(zb):
+            for h in range(2):
+                b = block_at(2 * zb + k, h, count)
+                remote(tok.at[b], tok.at[b], ss_p.at[h], rs_t.at[b], sib).wait_recv()
+
+        def send_up(j):
+            for h in range(2):
+                copy_block(z - j, h, ss_up.at[j, h], up).start()
+
+        def send_down(j):
+            for h in range(2):
+                copy_block(z + j, h, ss_dn.at[j, h], down).start()
+
+        def send_sib(zb):
+            for h in range(2):
+                copy_block(zb, h, ss_sib.at[zb, h], sib).start()
+
+        def w_forward(i):
+            shard = (f + 2) % 4
+            remote(wpart(wall, shard, i), wpart(wall, shard, i), ss_wx.at[i], rs_wx.at[i], xn).wait_recv()
+            remote(wpart(wall, shard, i), wpart(wall, shard, i), ss_wf.at[i], rs_wf.at[i], sib).start()
+
+        wait_block(z)
+
+        @pl.when(z < depth - 1)
+        def _():
+            send_up(0)
+
+        @pl.when(z > 0)
+        def _():
+            send_down(0)
+
+        send_sib(z)
+        for j in range(1, depth):
+            if j < pieces:
+                w_forward(j - 1)
+
+            @pl.when(z - j >= 0)
+            def _(j=j):
+                wait_block(z - j)
+
+                @pl.when(z < depth - 1)
+                def _():
+                    send_up(j)
+
+                send_sib(z - j)
+
+            @pl.when(z + j <= depth - 1)
+            def _(j=j):
+                wait_block(z + j)
+
+                @pl.when(z > 0)
+                def _():
+                    send_down(j)
+
+                send_sib(z + j)
+
+        for i in range(min(depth, pieces) - 1, pieces):
+            w_forward(i)
+
+        for zt in range(depth):
+            for h in range(2):
+                b = block_at(2 * zt + 1 - k, h, count)
+                remote(tok.at[b], tok.at[b], ss_p.at[h], rs_t.at[b], sib).wait_recv()
+                copy_block(zt, h, ss_sib.at[zt, h], sib).wait_send()
+        for ct in range(count):
+            remote(s_ref, st.at[ct], ss_s.at[0], rs_s.at[ct], sib).wait_recv()
+        for i in range(pieces):
+            shard = sib[1] + 2 - 4 * (sib[1] // 2)
+            remote(wpart(wall, shard, i), wpart(wall, shard, i), ss_wf.at[i], rs_wf.at[i], sib).wait_recv()
+            remote(wpart(wall, shard, i), wpart(wall, shard, i), ss_wf.at[i], rs_wf.at[i], sib).wait_send()
+            remote(w_ref.at[pl.ds(i * piece, piece)], wpart(wall, f, i), ss_wx.at[i], rs_wx.at[i], xn).wait_send()
+        remote(w_ref, wall.at[sib[1]], ss_ws, rs_ws, sib).wait()
+        pltpu.make_async_copy(w_ref, wall.at[f], loc).wait()
+
+        @pl.when(jnp.logical_not(holder))
+        def _():
+            for h in range(2):
+                send_in(h).wait_send()
+
+        for j in range(depth):
+
+            @pl.when((z < depth - 1) & (z - j >= 0))
+            def _(j=j):
+                for h in range(2):
+                    copy_block(z - j, h, ss_up.at[j, h], up).wait_send()
+
+            @pl.when((z > 0) & (z + j <= depth - 1))
+            def _(j=j):
+                for h in range(2):
+                    copy_block(z + j, h, ss_dn.at[j, h], down).wait_send()
+
+        for zt in range(depth):
+            for kt in range(2):
+                mine = holder & (z == zt) & (k == kt)
+
+                @pl.when(jnp.logical_not(mine))
+                def _(zt=zt, kt=kt):
+                    remote(s_ref, st.at[c], ss_s.at[2 * zt + kt], rs_s.at[c], sib).wait_send()
+
+    return pl.pallas_call(
+        kernel,
+        name="gather_stream",
+        out_shape=(
+            jax.ShapeDtypeStruct((2 * count,) + normed.shape[1:], normed.dtype),
+            jax.ShapeDtypeStruct((count,) + starts.shape, starts.dtype),
+            jax.ShapeDtypeStruct((4, rows, width), weight.dtype),
+        ),
+        in_specs=[ANY] * 3,
+        out_specs=(ANY,) * 3,
+        scratch_shapes=[
+            DMA((2 * count,)), DMA((2,)), DMA((depth, 2)), DMA((depth, 2)), DMA((depth, 2)),
+            DMA((count,)), DMA((count,)), DMA((pieces,)), DMA((pieces,)), DMA, DMA,
+            DMA((pieces,)), DMA((pieces,)), DMA,
+        ],
+        compiler_params=params(),
+    )(normed, starts, weight)
+
+
+def heads_to_tokens(arrays, name):
+    count = lax.axis_size("ctx")
+    number = len(arrays)
+    lanes = arrays[0].shape[2]
+    width = count * lanes
+
+    def kernel(*refs):
+        ins, (out, ss, rs) = refs[:number], refs[number:]
+        c, f, z, y, x, k = place()
+        pair = 2 * z + k
+        target = 2 * x + y
+
+        def there(half, a):
+            return out.at[half, :, pl.ds(pl.multiple_of(a * width + pair * lanes, lanes), lanes)]
+
+        def send(i, half, a):
+            ct = (c + i) % count
+            return remote(
+                ins[a].at[block_at(ct, half, count)], there(half, a), ss.at[i, half, a], rs.at[pair, half, a], (ct, target)
+            )
+
+        def own(half, a):
+            return pltpu.make_async_copy(ins[a].at[block_at(c, half, count)], there(half, a), rs.at[pair, half, a])
+
+        pieces = [(half, a) for a in range(number) for half in range(2)]
+        for i in [*range(1, count), 0]:
+            if i:
+                for half, a in pieces:
+                    send(i, half, a).start()
+            else:
+
+                @pl.when(k == y)
+                def _():
+                    for half, a in pieces:
+                        own(half, a).start()
+
+                @pl.when(k != y)
+                def _():
+                    for half, a in pieces:
+                        send(0, half, a).start()
+
+        for half, a in pieces:
+            for other in range(count):
+                cols = pl.ds(a * width + other * lanes, lanes)
+                remote(ins[a].at[0], out.at[half, :, cols], ss.at[0, half, a], rs.at[other, half, a], (c, f + 1 - 2 * k)).wait_recv()
+        for i in range(1, count):
+            for half, a in pieces:
+                send(i, half, a).wait_send()
+
+        @pl.when(k != y)
+        def _():
+            for half, a in pieces:
+                send(0, half, a).wait_send()
+
+    return pl.pallas_call(
+        kernel,
+        name=name,
+        out_shape=jax.ShapeDtypeStruct((2, arrays[0].shape[1], number * width), arrays[0].dtype),
+        in_specs=[ANY] * number,
+        out_specs=ANY,
+        scratch_shapes=[DMA((count, 2, number)), DMA((count, 2, number))],
+        compiler_params=params(),
+    )(*arrays)
+
+
+def tokens_to_heads(array, name):
+    count = lax.axis_size("ctx")
+    lanes = array.shape[2] // count
+
+    def kernel(a_ref, out, ss, rs):
+        c, f, z, y, x, k = place()
+
+        def part(half, pair):
+            return a_ref.at[half, :, pl.ds(pl.multiple_of(pair * lanes, lanes), lanes)]
+
+        def peer(i):
+            pair = (2 * z + k + i) % count
+            return pair, (2 * (pair // 2) + k, 2 * x + pair % 2)
+
+        def send(i, half):
+            pair, dev = peer(i)
+            b = block_at(c, half, count)
+            return remote(part(half, pair), out.at[b], ss.at[i, half], rs.at[b], dev)
+
+        for i in range(1, count):
+            for half in range(2):
+                send(i, half).start()
+
+        @pl.when(k == y)
+        def _():
+            for half in range(2):
+                b = block_at(c, half, count)
+                pltpu.make_async_copy(part(half, 2 * z + k), out.at[b], rs.at[b]).start()
+
+        @pl.when(k != y)
+        def _():
+            for half in range(2):
+                send(0, half).start()
+
+        for b in range(2 * count):
+            remote(part(0, 0), out.at[b], ss.at[0, 0], rs.at[b], (c, f + 1 - 2 * k)).wait_recv()
+        for i in range(1, count):
+            for half in range(2):
+                send(i, half).wait_send()
+
+        @pl.when(k != y)
+        def _():
+            for half in range(2):
+                send(0, half).wait_send()
+
+    return pl.pallas_call(
+        kernel,
+        name=name,
+        out_shape=jax.ShapeDtypeStruct((2 * count, array.shape[1], lanes), array.dtype),
+        in_specs=[ANY],
+        out_specs=ANY,
+        scratch_shapes=[DMA((count, 2)), DMA((2 * count,))],
+        compiler_params=params(),
+    )(array)
+
+
+TILE = 256
+
+
+def attend_forward(qkv, start_column, first_tile, scale):
+    length = qkv.shape[0]
+    tiles = length // TILE
+    lanes = 128
+    size = lanes // 2
+
+    def kernel(first, q_ref, k_ref, v_ref, s_ref, o32, o16, lse):
+        i = pl.program_id(0)
+        lane = lax.broadcasted_iota(jnp.int32, (TILE, lanes), 1)
+        query = q_ref[...]
+        zero = jnp.zeros_like(query)
+        heads = [jnp.where(lane < size, query, zero), jnp.where(lane >= size, query, zero)]
+        start = s_ref[...]
+        row = i * TILE + lax.broadcasted_iota(jnp.int32, (TILE, TILE), 0)
+        column = lax.broadcasted_iota(jnp.int32, (TILE, TILE), 1)
+
+        def step(j, carried):
+            at = pl.multiple_of(j * TILE, TILE)
+            keys = k_ref[pl.ds(at, TILE), :]
+            values = v_ref[pl.ds(at, TILE), :]
+            seen = (column + at <= row) & (column + at >= start)
+            out = []
+            for h in range(2):
+                top, total, mixed = carried[h]
+                score = lax.dot_general(heads[h], keys, (((1,), (1,)), ((), ())), preferred_element_type=F32) * scale
+                score = jnp.where(seen, score, NEGATIVE)
+                new_top = jnp.maximum(top, jnp.max(score, axis=1, keepdims=True))
+                weight = jnp.where(seen, jnp.exp(score - new_top), 0.0)
+                shrink = jnp.exp(top - new_top)
+                total = total * shrink + jnp.sum(weight, axis=1, keepdims=True)
+                mixed = mixed * shrink + jnp.dot(weight.astype(BF), values, preferred_element_type=F32)
+                out.append((new_top, total, mixed))
+            return tuple(out)
+
+        begin = (
+            jnp.full((TILE, 1), NEGATIVE, F32),
+            jnp.zeros((TILE, 1), F32),
+            jnp.zeros((TILE, lanes), F32),
+        )
+        done = lax.fori_loop(first[i], i + 1, step, (begin, begin))
+        ready = [mixed / total for _, total, mixed in done]
+        logs = [top + jnp.log(total) for top, total, _ in done]
+        mixed = jnp.where(lane < size, ready[0], ready[1])
+        o32[...] = mixed
+        o16[...] = mixed.astype(BF)
+        lse[...] = jnp.where(lane < size, logs[0], logs[1])
+
+    return pl.pallas_call(
+        kernel,
+        name="attend_forward",
+        grid_spec=pltpu.PrefetchScalarGridSpec(
+            num_scalar_prefetch=1,
+            grid=(tiles,),
+            in_specs=[
+                pl.BlockSpec((TILE, lanes), lambda i, first: (i, 0)),
+                pl.BlockSpec((length, lanes), lambda i, first: (0, 1)),
+                pl.BlockSpec((length, lanes), lambda i, first: (0, 2)),
+                pl.BlockSpec((TILE, 1), lambda i, first: (i, 0)),
+            ],
+            out_specs=[pl.BlockSpec((TILE, lanes), lambda i, first: (i, 0))] * 3,
+        ),
+        out_shape=(
+            jax.ShapeDtypeStruct((length, lanes), F32),
+            jax.ShapeDtypeStruct((length, lanes), BF),
+            jax.ShapeDtypeStruct((length, lanes), F32),
+        ),
+        compiler_params=params(False),
+    )(first_tile, qkv, qkv, qkv, start_column)
+
+
+def attend_backward(qkv, grad, start_row, log_rows, delta_rows, first_tile, scale):
+    length = qkv.shape[0]
+    tiles = length // TILE
+    lanes = 128
+    size = lanes // 2
+
+    def kernel(first, q_ref, k_ref, v_ref, g_ref, s_ref, l_ref, d_ref, dq, dk, dv, acc_k, acc_v):
+        i = pl.program_id(0)
+
+        @pl.when(i == 0)
+        def _():
+            acc_k[...] = jnp.zeros_like(acc_k)
+            acc_v[...] = jnp.zeros_like(acc_v)
+
+        lane = lax.broadcasted_iota(jnp.int32, (TILE, lanes), 1)
+
+        def split(value):
+            zero = jnp.zeros_like(value)
+            return [jnp.where(lane < size, value, zero), jnp.where(lane >= size, value, zero)]
+
+        queries, grads = split(q_ref[...]), split(g_ref[...])
+        start = s_ref[...]
+        key_row = lax.broadcasted_iota(jnp.int32, (TILE, TILE), 0)
+        query_column = i * TILE + lax.broadcasted_iota(jnp.int32, (TILE, TILE), 1)
+
+        def step(j, running):
+            at = pl.multiple_of(j * TILE, TILE)
+            keys = k_ref[pl.ds(at, TILE), :]
+            values = v_ref[pl.ds(at, TILE), :]
+            key_parts = split(keys)
+            seen = (key_row + at <= query_column) & (key_row + at >= start)
+            key_sum = jnp.zeros((TILE, lanes), F32)
+            value_sum = jnp.zeros((TILE, lanes), F32)
+            for h in range(2):
+                score = lax.dot_general(keys, queries[h], (((1,), (1,)), ((), ())), preferred_element_type=F32) * scale
+                weight = jnp.where(seen, jnp.exp(score - l_ref[h : h + 1, :]), 0.0)
+                grad_weight = lax.dot_general(
+                    values, grads[h], (((1,), (1,)), ((), ())), preferred_element_type=F32
+                )
+                grad_score = (weight * (grad_weight - d_ref[h : h + 1, :])).astype(BF)
+                value_sum += jnp.dot(weight.astype(BF), grads[h], preferred_element_type=F32)
+                key_sum += jnp.dot(grad_score, queries[h], preferred_element_type=F32)
+                running += lax.dot_general(
+                    grad_score, key_parts[h], (((0,), (0,)), ((), ())), preferred_element_type=F32
+                )
+            acc_k[pl.ds(at, TILE), :] += key_sum
+            acc_v[pl.ds(at, TILE), :] += value_sum
+            return running
+
+        total = lax.fori_loop(first[i], i + 1, step, jnp.zeros((TILE, lanes), F32))
+        dq[...] = (total * scale).astype(BF)
+
+        @pl.when(i == tiles - 1)
+        def _():
+            dk[...] = (acc_k[...] * scale).astype(BF)
+            dv[...] = acc_v[...].astype(BF)
+
+    return pl.pallas_call(
+        kernel,
+        name="attend_backward",
+        grid_spec=pltpu.PrefetchScalarGridSpec(
+            num_scalar_prefetch=1,
+            grid=(tiles,),
+            in_specs=[
+                pl.BlockSpec((TILE, lanes), lambda i, first: (i, 0)),
+                pl.BlockSpec((length, lanes), lambda i, first: (0, 1)),
+                pl.BlockSpec((length, lanes), lambda i, first: (0, 2)),
+                pl.BlockSpec((TILE, lanes), lambda i, first: (i, 0)),
+                pl.BlockSpec((1, TILE), lambda i, first: (0, i)),
+                pl.BlockSpec((2, TILE), lambda i, first: (0, i)),
+                pl.BlockSpec((2, TILE), lambda i, first: (0, i)),
+            ],
+            out_specs=[
+                pl.BlockSpec((TILE, lanes), lambda i, first: (i, 0)),
+                pl.BlockSpec((length, lanes), lambda i, first: (0, 0)),
+                pl.BlockSpec((length, lanes), lambda i, first: (0, 0)),
+            ],
+            scratch_shapes=[pltpu.VMEM((length, lanes), F32), pltpu.VMEM((length, lanes), F32)],
+        ),
+        out_shape=(jax.ShapeDtypeStruct((length, lanes), BF),) * 3,
+        compiler_params=params(False),
+    )(first_tile, qkv, qkv, qkv, grad, start_row, log_rows, delta_rows)
+
+
+def dispatch_rows(arrays):
+    count = lax.axis_size("ctx")
+    number = len(arrays)
+    _, own_experts, cap, width = arrays[0].shape
+
+    def kernel(*refs):
+        ins, outs = refs[:number], refs[number : 2 * number]
+        ss1, rs1, ssx, rsx, sss, rss, ssf, rsf = refs[2 * number :]
+        c, f, z, y, x, k = place()
+        sib = (c, f + 1 - 2 * k)
+        xn = (c, (f + 2) % 4)
+
+        def here(a, stream, source):
+            return outs[a].at[:, stream, source]
+
+        def first(a, i):
+            ct = (c + i) % count
+            return remote(ins[a].at[ct], here(a, f, c), ss1.at[a, i], rs1.at[a, c], (ct, f))
+
+        for a in range(number):
+            pltpu.make_async_copy(ins[a].at[c], here(a, f, c), rs1.at[a, c]).start()
+            for i in range(1, count):
+                first(a, i).start()
+
+        def hop(a, stream, source, ss, rs, dev):
+            return remote(here(a, stream, source), here(a, stream, source), ss.at[a, source], rs.at[a, source], dev)
+
+        other = (f + 2) % 4
+        for a in range(number):
+            for i in range(count):
+                cs = (c + i) % count
+                remote(here(a, f, cs), here(a, f, cs), ss1.at[a, 0], rs1.at[a, cs], sib).wait_recv()
+                hop(a, f, cs, ssx, rsx, xn).start()
+                hop(a, f, cs, sss, rss, sib).start()
+        for a in range(number):
+            for i in range(count):
+                cs = (c + i) % count
+                hop(a, other, cs, ssx, rsx, xn).wait_recv()
+                hop(a, other, cs, ssf, rsf, sib).start()
+        for a in range(number):
+            for i in range(count):
+                if i:
+                    first(a, i).wait_send()
+                cs = (c + i) % count
+                hop(a, f, cs, ssx, rsx, xn).wait_send()
+                hop(a, sib[1], cs, sss, rss, sib).wait()
+                hop(a, (sib[1] + 2) % 4, cs, ssf, rsf, sib).wait()
+
+    return pl.pallas_call(
+        kernel,
+        name="dispatch_rows",
+        out_shape=(jax.ShapeDtypeStruct((own_experts, 4, count, cap, width), arrays[0].dtype),) * number,
+        in_specs=[ANY] * number,
+        out_specs=(ANY,) * number,
+        scratch_shapes=[DMA((number, count))] * 8,
+        compiler_params=params(),
+    )(*arrays)
+
+
+def return_rows(arrays):
+    count = lax.axis_size("ctx")
+    number = len(arrays)
+    _, experts, _, cap, width = arrays[0].shape
+    groups = 2
+    chunk = experts // groups
+
+    def kernel(*refs):
+        ins, outs = refs[:number], refs[number : 2 * number]
+        near, far, got_near, got_far, got_x = refs[2 * number : 2 * number + 5]
+        ssn, rsn, ssf, rsf, ssx, rsx, sso, rso, loc = refs[2 * number + 5 :]
+        c, f, z, y, x, k = place()
+        sib = (c, f + 1 - 2 * k)
+        other = (f + 2) % 4
+        xn = (c, other)
+        sib_other = (sib[1] + 2) % 4
+
+        def to_near(a):
+            return remote(ins[a].at[sib[1]], got_near.at[a], ssn.at[a], rsn.at[a], sib)
+
+        def to_far(a):
+            return remote(ins[a].at[sib_other], got_far.at[a], ssf.at[a], rsf.at[a], sib)
+
+        def load(a, stream, buf, i):
+            return pltpu.make_async_copy(ins[a].at[stream], buf.at[a], loc.at[a, i])
+
+        for a in range(number):
+            to_far(a).start()
+            load(a, other, far, 0).start()
+        for a in range(number):
+            to_near(a).start()
+            load(a, f, near, 1).start()
+
+        def across(a, e):
+            return remote(far.at[a, e], got_x.at[a, e], ssx.at[a, e], rsx.at[a, e], xn)
+
+        for a in range(number):
+            load(a, other, far, 0).wait()
+            to_far(a).wait_recv()
+            for e in range(experts):
+                far[a, e] = (far[a, e].astype(F32) + got_far[a, e].astype(F32)).astype(BF)
+                across(a, e).start()
+
+        def home(a, g, i):
+            ct = (c + i) % count
+            return remote(
+                near.at[a, pl.ds(g * chunk, chunk), ct],
+                outs[a].at[c, pl.ds(g * chunk, chunk)],
+                sso.at[a, g, i],
+                rso.at[a, g, c],
+                (ct, f),
+            )
+
+        def stay(a, g):
+            return pltpu.make_async_copy(
+                near.at[a, pl.ds(g * chunk, chunk), c], outs[a].at[c, pl.ds(g * chunk, chunk)], rso.at[a, g, c]
+            )
+
+        for a in range(number):
+            load(a, f, near, 1).wait()
+            to_near(a).wait_recv()
+            for g in range(groups):
+                for e in range(g * chunk, (g + 1) * chunk):
+                    across(a, e).wait_recv()
+                    near[a, e] = (
+                        near[a, e].astype(F32) + got_near[a, e].astype(F32) + got_x[a, e].astype(F32)
+                    ).astype(BF)
+                for i in range(1, count):
+                    home(a, g, i).start()
+                stay(a, g).start()
+        for a in range(number):
+            to_far(a).wait_send()
+            to_near(a).wait_send()
+            for e in range(experts):
+                across(a, e).wait_send()
+            for g in range(groups):
+                for i in range(count):
+                    cs = (c + i) % count
+                    remote(
+                        near.at[a, pl.ds(g * chunk, chunk), cs],
+                        outs[a].at[cs, pl.ds(g * chunk, chunk)],
+                        sso.at[a, g, i],
+                        rso.at[a, g, cs],
+                        sib,
+                    ).wait_recv()
+                    if i:
+                        home(a, g, i).wait_send()
+
+    buffer = pltpu.VMEM((number, experts, count, cap, width), BF)
+    return pl.pallas_call(
+        kernel,
+        name="return_rows",
+        out_shape=(jax.ShapeDtypeStruct((count, experts, cap, width), BF),) * number,
+        in_specs=[ANY] * number,
+        out_specs=(ANY,) * number,
+        scratch_shapes=[buffer] * 5
+        + [DMA((number,))] * 4
+        + [DMA((number, experts))] * 2
+        + [DMA((number, groups, count))] * 2
+        + [DMA((number, 2))],
+        compiler_params=params(),
+    )(*arrays)
+
+
+ROOT = math.sqrt(2.0 / math.pi)
+CUBIC = 0.044715
+
+
+def experts_step(rows, grads, first_proj, second_proj):
+    number, count, width = rows.shape
+    units = first_proj.shape[2]
+    quarter = count // 4
+
+    def kernel(r_ref, g_ref, a_ref, b_ref, out, back, da, db):
+        row, grad = r_ref[0], g_ref[0]
+        first = a_ref[0].astype(BF)
+        second = b_ref[0].astype(BF)
+        hidden = jnp.dot(row, first, preferred_element_type=F32)
+        upstream = lax.dot_general(grad, second, (((1,), (1,)), ((), ())), preferred_element_type=F32)
+        bent = jnp.tanh(ROOT * (hidden + CUBIC * hidden * hidden * hidden))
+        active = (0.5 * hidden * (1.0 + bent)).astype(BF)
+        slope = 0.5 * (1.0 + bent) + 0.5 * hidden * (1.0 - bent * bent) * (ROOT * (1.0 + 3.0 * CUBIC * hidden * hidden))
+        grad_hidden = (upstream * slope).astype(BF)
+        term = lax.dot_general(grad_hidden, first, (((1,), (1,)), ((), ())), preferred_element_type=F32).astype(BF)
+        mixed = jnp.dot(active, second, preferred_element_type=F32).astype(BF)
+        for s in range(4):
+            back[s, 0] = term[s * quarter : (s + 1) * quarter]
+            out[s, 0] = mixed[s * quarter : (s + 1) * quarter]
+        da[0] = lax.dot_general(row, grad_hidden, (((0,), (0,)), ((), ())), preferred_element_type=F32)
+        db[0] = lax.dot_general(active, grad, (((0,), (0,)), ((), ())), preferred_element_type=F32)
+
+    whole = pl.BlockSpec((1, count, width), lambda e: (e, 0, 0))
+    left = pl.BlockSpec((1, width, units), lambda e: (e, 0, 0))
+    right = pl.BlockSpec((1, units, width), lambda e: (e, 0, 0))
+    parts = pl.BlockSpec((4, 1, quarter, width), lambda e: (0, e, 0, 0))
+    return pl.pallas_call(
+        kernel,
+        name="experts_step",
+        grid=(number,),
+        in_specs=[whole, whole, left, right],
+        out_specs=[parts, parts, left, right],
+        out_shape=(
+            jax.ShapeDtypeStruct((4, number, quarter, width), BF),
+            jax.ShapeDtypeStruct((4, number, quarter, width), BF),
+            jax.ShapeDtypeStruct(first_proj.shape, F32),
+            jax.ShapeDtypeStruct(second_proj.shape, F32),
+        ),
+        compiler_params=params(False),
+    )(rows, grads, first_proj, second_proj)
+
+
+def sum_weight_grads(parts):
+    count = lax.axis_size("ctx")
+    depth = count // 2
+    _, rows, wide = parts.shape
+    lanes = wide // 3
+    width = count * lanes
+
+    def kernel(p_ref, out, got, held, ss_r, rs_r, ss_up, ss_dn, rs_z, ss_a, ss_b, rs_o):
+        c, f, z, y, x, k = place()
+        peers = [
+            (2 * z + 1 - y, f, 2 * x + 1 - y),
+            (c, (f + 2) % 4, 2 * (1 - x) + y),
+            (2 * z + 1 - y, (f + 2) % 4, 2 * (1 - x) + 1 - y),
+        ]
+        sib = (c, f + 1 - 2 * k)
+        up = (c + 2, f)
+        down = (c - 2, f)
+
+        def scatter(d):
+            cp, fp, shard = peers[d]
+            return remote(p_ref.at[shard], got.at[d], ss_r.at[d], rs_r.at[d], (cp, fp))
+
+        for d in (2, 1, 0):
+            scatter(d).start()
+        total = p_ref[2 * x + y].astype(F32)
+        for d in range(3):
+            scatter(d).wait_recv()
+            total += got[d].astype(F32)
+        held[z] = total.astype(BF)
+
+        def chain(zb, ss, dev):
+            return remote(held.at[zb], held.at[zb], ss, rs_z.at[zb], dev)
+
+        def piece(zb, j):
+            return held.at[zb, :, pl.ds(j * lanes, lanes)]
+
+        def there(zb, j):
+            return out.at[:, pl.ds(pl.multiple_of(j * width + (2 * zb + k) * lanes, lanes), lanes)]
+
+        def own_column(zb, j):
+            return remote(piece(zb, j), there(zb, j), ss_a.at[zb, j], rs_o.at[2 * zb + k, j], (c, 2 * x + y))
+
+        def own_local(zb, j):
+            return pltpu.make_async_copy(piece(zb, j), there(zb, j), rs_o.at[2 * zb + k, j])
+
+        def next_column(zb, j):
+            return remote(
+                piece(zb, j), there(zb, j), ss_b.at[zb, j], rs_o.at[2 * zb + k, j], (2 * z + 1 - y, 2 * x + y)
+            )
+
+        def spread(zb):
+            for j in range(3):
+                next_column(zb, j).start()
+
+            @pl.when(k == y)
+            def _():
+                for j in range(3):
+                    own_local(zb, j).start()
+
+            @pl.when(k != y)
+            def _():
+                for j in range(3):
+                    own_column(zb, j).start()
+
+        @pl.when(z < depth - 1)
+        def _():
+            chain(z, ss_up.at[0], up).start()
+
+        @pl.when(z > 0)
+        def _():
+            chain(z, ss_dn.at[0], down).start()
+
+        spread(z)
+        for j in range(1, depth):
+
+            @pl.when(z - j >= 0)
+            def _(j=j):
+                chain(z - j, ss_up.at[j], sib).wait_recv()
+
+                @pl.when(z < depth - 1)
+                def _():
+                    chain(z - j, ss_up.at[j], up).start()
+
+                spread(z - j)
+
+            @pl.when(z + j <= depth - 1)
+            def _(j=j):
+                chain(z + j, ss_dn.at[j], sib).wait_recv()
+
+                @pl.when(z > 0)
+                def _():
+                    chain(z + j, ss_dn.at[j], down).start()
+
+                spread(z + j)
+
+        for d in range(3):
+            scatter(d).wait_send()
+        for pair in range(count):
+            for j in range(3):
+                remote(
+                    piece(0, j), out.at[:, pl.ds(j * width + pair * lanes, lanes)], ss_a.at[0, j], rs_o.at[pair, j], sib
+                ).wait_recv()
+        for j in range(depth):
+
+            @pl.when((z < depth - 1) & (z - j >= 0))
+            def _(j=j):
+                chain(z - j, ss_up.at[j], up).wait_send()
+
+            @pl.when((z > 0) & (z + j <= depth - 1))
+            def _(j=j):
+                chain(z + j, ss_dn.at[j], down).wait_send()
+
+        for zb in range(depth):
+            for j in range(3):
+                next_column(zb, j).wait_send()
+
+        @pl.when(k != y)
+        def _():
+            for zb in range(depth):
+                for j in range(3):
+                    own_column(zb, j).wait_send()
+
+    return pl.pallas_call(
+        kernel,
+        name="sum_weight_grads",
+        out_shape=jax.ShapeDtypeStruct((rows, 3 * width), BF),
+        in_specs=[pl.BlockSpec(memory_space=pltpu.VMEM)],
+        out_specs=ANY,
+        scratch_shapes=[
+            pltpu.VMEM((3, rows, wide), BF),
+            pltpu.VMEM((depth, rows, wide), BF),
+            DMA((3,)), DMA((3,)), DMA((depth,)), DMA((depth,)), DMA((depth,)),
+            DMA((depth, 3)), DMA((depth, 3)), DMA((count, 3)),
+        ],
+        compiler_params=params(),
+    )(parts)
+
+
+def slots_of(routes):
+    tokens = routes.shape[0]
+    chosen = routes[:, None] == jnp.arange(EXPERTS, dtype=jnp.int32)[None, :]
+    earlier = (jnp.arange(tokens)[:, None] >= jnp.arange(tokens)[None, :]).astype(BF)
+    running = jnp.dot(earlier, chosen.astype(BF), preferred_element_type=F32)
+    rank = jnp.sum(jnp.where(chosen, running, 0.0), axis=1).astype(jnp.int32) - 1
+    slot = routes * CAP + rank
+    return (jnp.arange(EXPERTS * CAP, dtype=jnp.int32)[:, None] == slot[None, :]).astype(BF)
+
+
+def by_head_pairs(
+    tokens, doc_starts, expert_ids, query_key_value_weight, output_weight_matrix, expert_in, expert_out, gain_one, gain_two, grad_output
+):
+    half_rows = tokens.shape[3]
+    width = tokens.shape[4]
+    count = lax.axis_size("ctx")
+    rows = 2 * half_rows
+    length = count * rows
+    scale = (width // HEADS) ** (-0.5)
+    c, f, z, y, x, k = place()
+    pair = 2 * z + k
+    lanes = 2 * (width // HEADS)
+    start_x = tokens.reshape(rows, width).astype(F32)
+    cotangent = grad_output.reshape(rows, width)
+    qkv_low = query_key_value_weight.astype(BF)
+    out_proj = lax.all_gather(output_weight_matrix.astype(BF), "fsdp", axis=0, tiled=True)
+    first_normed, hat_one, inverse_one = norm_forward(start_x, gain_one)
+    normed = first_normed.astype(BF)
+    stream, starts, projection = gather_stream(
+        normed.reshape(2, half_rows, width), doc_starts.reshape(2, half_rows), qkv_low
+    )
+    stream = stream.reshape(length, width)
+    projection = projection.reshape(width, 3 * width)
+    own_columns = jnp.concatenate(
+        [lax.dynamic_slice(projection, (0, j * width + pair * lanes), (width, lanes)) for j in range(3)], axis=1
+    )
+    qkv = jnp.dot(stream, own_columns, preferred_element_type=F32).astype(BF)
+    start_line = jnp.concatenate([starts[:, 0].reshape(-1), starts[::-1, 1].reshape(-1)])
+    first_tile = jnp.min(start_line.reshape(-1, TILE), axis=1) // TILE
+    mixed32, mixed16, logs = attend_forward(qkv, start_line[:, None], first_tile, scale)
+    mixed = heads_to_tokens([mixed16.reshape(2 * count, half_rows, lanes)], "mixed_to_tokens").reshape(rows, width)
+    middle = start_x + jnp.dot(mixed, out_proj, preferred_element_type=F32)
+    normed_two, hat_two, inverse_two = norm_forward(middle, gain_two)
+    routed = normed_two.astype(BF)
+    dispatch = slots_of(expert_ids.reshape(rows))
+    own_experts = EXPERTS // count
+    shape = (count, own_experts, CAP, width)
+    send_rows = jnp.dot(dispatch, routed, preferred_element_type=F32).astype(BF).reshape(shape)
+    send_grads = jnp.dot(dispatch, cotangent, preferred_element_type=F32).astype(BF).reshape(shape)
+    all_rows, all_grads = dispatch_rows([send_rows, send_grads])
+    flat = (own_experts, 4 * count * CAP, width)
+    out_terms, back_terms, grad_in, grad_outw = experts_step(
+        all_rows.reshape(flat), all_grads.reshape(flat), expert_in, expert_out
+    )
+    folded = (4, own_experts, count, CAP, width)
+    returned, back_rows = return_rows([back_terms.reshape(folded), out_terms.reshape(folded)])
+    slots = (EXPERTS * CAP, width)
+    pick = (((0,), (0,)), ((), ()))
+    grad_routed = lax.dot_general(dispatch, returned.reshape(slots), pick, preferred_element_type=F32)
+    expert_sum = lax.dot_general(dispatch, back_rows.reshape(slots), pick, preferred_element_type=F32)
+    block_out = (middle + expert_sum).astype(BF)
+    grad_mid_norm, grad_gain_two = norm_backward(grad_routed[None], hat_two[None], inverse_two[None], gain_two)
+    grad_middle = cotangent.astype(F32) + grad_mid_norm[0]
+    grad_attn = grad_middle.astype(BF)
+    grad_outproj = lax.dot_general(mixed, grad_attn, pick, preferred_element_type=F32)
+    grad_mixed = lax.dot_general(grad_attn, out_proj, (((1,), (1,)), ((), ())), preferred_element_type=F32).astype(BF)
+    grad_heads = tokens_to_heads(grad_mixed.reshape(2, half_rows, width), "grad_to_heads").reshape(length, lanes)
+    delta = jnp.sum((grad_heads.astype(F32) * mixed32).reshape(length, 2, lanes // 2), axis=2).T
+    log_rows = logs[:, :: lanes // 2].T
+    grad_q, grad_k, grad_v = attend_backward(qkv, grad_heads, start_line[None], log_rows, delta, first_tile, scale)
+    blocks = (2 * count, half_rows, lanes)
+    grad_projected = heads_to_tokens(
+        [grad_q.reshape(blocks), grad_k.reshape(blocks), grad_v.reshape(blocks)], "grad_to_tokens"
+    ).reshape(rows, 3 * width)
+    own_grads = jnp.concatenate([grad_q, grad_k, grad_v], axis=1)
+    parts = lax.dot_general(stream, own_grads, pick, preferred_element_type=F32).astype(BF)
+    shard_rows = width // 4
+    weight_grad = sum_weight_grads(parts.reshape(4, shard_rows, 3 * lanes)).astype(F32)
+    grad_normed = lax.dot_general(grad_projected, projection, (((1,), (1,)), ((), ())), preferred_element_type=F32)
+    grad_in_norm, _ = norm_backward(grad_normed[None], hat_one[None], inverse_one[None], gain_one)
+    grad_start = grad_middle + grad_in_norm[0]
+    own_gain = lax.dynamic_slice(gain_one, (f * shard_rows,), (shard_rows,))
+    shard_gain_one = jnp.sum(weight_grad * qkv_low.astype(F32), axis=1) / own_gain
+    summed_gain = lax.psum(grad_gain_two, ("ctx", "fsdp"))
+    shard_gain_two = lax.dynamic_slice(summed_gain, (f * shard_rows,), (shard_rows,))
+    shard_out = lax.psum_scatter(grad_outproj.astype(BF), "fsdp", scatter_dimension=0, tiled=True)
+    shard_out = lax.psum(shard_out, "ctx").astype(F32)
+    return (
+        block_out.reshape(tokens.shape),
+        grad_start.reshape(tokens.shape),
+        weight_grad,
+        shard_out,
+        grad_in,
+        grad_outw,
+        shard_gain_one,
+        shard_gain_two,
+    )
+
+
 def solution(mesh):
+    pairs = mesh.shape["ctx"] * 2 == HEADS and mesh.shape["fsdp"] == 4
     return jax.shard_map(
-        shards,
+        by_head_pairs if pairs else shards,
         mesh=mesh,
         in_specs=(
             P("fsdp", "ctx", None, None, None),

time: 1300 us -> 634 us (0.49)
  waiting for transfers between devices: 609 us -> 79.1 us
  Pallas kernels: 0 us -> 438 us
  matrix products: 309 us -> 30.1 us
  blocking collectives: 227 us -> 37.3 us
  local copies, waits for them, and re-layouts: 72.5 us -> 12.6 us
  other arithmetic: 42.3 us -> 18.7 us
    pallas_call x0 -> x10, Pallas kernels: none -> 438 us  [the longest x1 87.8 us: return_rows(): pl.pallas_call(kernel, name='return_rows', out_shape=(jax.ShapeDtypeStruc...]
    reduce_scatter x3 -> x1, waiting for transfers between devices: 289 us -> 0.01 us  [by_head_pairs(): lax.psum_scatter(grad_outproj.astype(BF), 'fsdp', scatter_dimension=0, ti...]
    dot_general x52 -> x11, matrix products: 309 us -> 30.1 us  [the longest x1 5.68 us: by_head_pairs(): qkv = jnp.dot(stream, own_columns, preferred_element_type=F32).astype(BF)]
    all_gather x6 -> x1, waiting for transfers between devices: 182 us -> 0.01 us  [by_head_pairs(): lax.all_gather(output_weight_matrix.astype(BF), 'fsdp', axis=0, tiled=True)]
    unnamed x2 -> x0, blocking collectives: 152 us -> none
    unnamed x12 -> x3, waiting for transfers between devices: 60.4 us -> 0.05 us
    all_to_all x2 -> x0, blocking collectives: 57.2 us -> none  [the longest x1 28.8 us: shards(): lax.all_to_all(send_grads, 'ctx', split_axis=0, concat_axis=0, tiled=True)]
    dynamic_update_slice x8 -> x0, local copies, waits for them, and re-layouts: 40.3 us -> none  [shards(): lax.map(one_piece, jnp.arange(local_rows * lax.axis_size('ctx') // sub_ro...]
  transfers between devices with their start and end apart: 13 -> 3, of which waited for: 11 -> 1; matrix products, arithmetic and copies ran while one was open for 17% -> 7% of each run, Pallas kernels for 0% -> 36%
where the time goes in v1:
time: 634 us; the launch traced here: 630 us
  Pallas kernels  438 us (69%)
  waiting for transfers between devices  79.1 us (12%)
  blocking collectives  37.3 us (6%)
  matrix products  30.1 us (5%)
  other arithmetic  18.7 us (3%)
  between operations  14.1 us (2%)
  local copies, waits for them, and re-layouts  12.6 us (2%)
    pallas_call x1, Pallas kernels, return_rows(): pl.pallas_call(kernel, name='return_rows', out_shape=(jax.ShapeDtypeStruc...  87.8 us
    psum x1, waiting for transfers between devices, by_head_pairs(): shard_out = lax.psum(shard_out, 'ctx').astype(F32)  79 us
    pallas_call x2, Pallas kernels, heads_to_tokens(): pl.pallas_call(kernel, name=name, out_shape=jax.ShapeDtypeStruct((2, arra...  66 us
    pallas_call x1, Pallas kernels, dispatch_rows(): pl.pallas_call(kernel, name='dispatch_rows', out_shape=(jax.ShapeDtypeStr...  64.6 us
    pallas_call x1, Pallas kernels, gather_stream(): pl.pallas_call(kernel, name='gather_stream', out_shape=(jax.ShapeDtypeStr...  60.6 us
    pallas_call x1, Pallas kernels, experts_step(): pl.pallas_call(kernel, name='experts_step', grid=(number,), in_specs=[who...  56.9 us
    pallas_call x1, Pallas kernels, sum_weight_grads(): pl.pallas_call(kernel, name='sum_weight_grads', out_shape=jax.ShapeDtypeS...  42.3 us
    psum x1, blocking collectives, by_head_pairs(): summed_gain = lax.psum(grad_gain_two, ('ctx', 'fsdp'))  37.3 us
  transfers between devices with their start and end apart: 3, of which 1 were waited for; matrix products, arithmetic and copies ran while one was open for 7% of the time, Pallas kernels for 36%

profile of v1, /device:TPU:1, one launch (start us, length us, event | category | flops | bytes accessed | tf_op | source)
XLA Modules:
  0.0 630.0 jit_solution(3548240018108860607)
XLA Ops:
  7.2 2.1 convert_element_type.93
  9.5 3.3 convert_element_type.91.w_ref
  14.3 60.6 %gather_stream.1 = (bf16[16,128,1024]{2,1,0:T(8,128)(2,1)}, s32[8,2,128]{2,1,0:T(2,128)}, bf16[4,256,3072]{2,1,0:T(8,128)(2,1)}) custom-call(bf16[2,128,1024]{2,1,0:T(8,128)(2,1)} %fusion.13.n_ref, s32[2,128]{1,0:T(2,128)} %bitcast.105, bf16[256,3072]{1,0:T(8,128)(2,1)} %convert_element_type.91.w_ref), custom_call_target="tpu_custom_call" | custom-call | tf_op jit(solution)/shard_map/gather_stream/pallas_call | solution.py:636
  75.7 1.3 copy.19.s_ref
  78.9 5.7 convolution_convert_fusion.q_ref.k_ref.v_ref
  84.6 19.2 %attend_forward.1 = (f32[2048,128]{1,0:T(8,128)}, bf16[2048,128]{1,0:T(8,128)(2,1)}, f32[2048,128]{1,0:T(8,128)}) custom-call(s32[8]{0:T(128)} %and_select_fusion.first, bf16[2048,384]{1,0:T(8,128)(2,1)} %convolution_convert_fusion.q_ref.k_ref.v_ref, bf16[2048,384]{1,0:T(8,128)(2,1)} %convolution_convert_fusion.q_ref.k_ref.v_ref, ...), custom_call_target="tpu_custom_call" | custom-call | tf_op jit(solution)/shard_map/attend_forward/pallas_call | solution.py:826
  103.8 32.8 %mixed_to_tokens.1 = bf16[2,128,1024]{2,1,0:T(8,128)(2,1)} custom-call(bf16[16,128,128]{2,1,0:T(8,128)(2,1)} %bitcast.92), custom_call_target="tpu_custom_call" | custom-call | tf_op jit(solution)/shard_map/mixed_to_tokens/pallas_call | solution.py:709
  136.9 1.4 convolution_convert_fusion.2
  138.3 2.6 fusion.42
  141.2 1.6 convolution_convert_fusion.3
  142.7 64.6 %dispatch_rows.1 = (bf16[8,4,8,8,1024]{4,3,2,1,0:T(8,128)(2,1)}, bf16[8,4,8,8,1024]{4,3,2,1,0:T(8,128)(2,1)}) custom-call(bf16[8,8,8,1024]{3,2,1,0:T(8,128)(2,1)} %bitcast.87, bf16[8,8,8,1024]{3,2,1,0:T(8,128)(2,1)} %bitcast.86), custom_call_target="tpu_custom_call" | custom-call | tf_op jit(solution)/shard_map/dispatch_rows/pallas_call | solution.py:981
  207.3 56.9 %experts_step.1 = (bf16[4,8,64,1024]{3,2,1,0:T(8,128)(2,1)}, bf16[4,8,64,1024]{3,2,1,0:T(8,128)(2,1)}, f32[8,1024,1024]{2,1,0:T(8,128)}, f32[8,1024,1024]{2,1,0:T(8,128)}) custom-call(bf16[8,256,1024]{2,1,0:T(8,128)(2,1)} %bitcast.80, bf16[8,256,1024]{2,1,0:T(8,128)(2,1)} %bitcast.81, f32[8,1024,1024]{2,1,0:T(8,128)} %a_ref.1, f32[8,1024,1024]{2,1,0:T(8,128)} %b_ref.1), custom_call_target="tpu_custom_call" | custom-call | tf_op jit(solution)/shard_map/experts_step/pallas_call | solution.py:1127
  264.2 87.8 %return_rows.1 = (bf16[8,8,8,1024]{3,2,1,0:T(8,128)(2,1)}, bf16[8,8,8,1024]{3,2,1,0:T(8,128)(2,1)}) custom-call(bf16[4,8,8,8,1024]{4,3,2,1,0:T(8,128)(2,1)} %bitcast.84, bf16[4,8,8,8,1024]{4,3,2,1,0:T(8,128)(2,1)} %bitcast.83), custom_call_target="tpu_custom_call" | custom-call | tf_op jit(solution)/shard_map/return_rows/pallas_call | solution.py:1081
  352.0 2.0 multiply_reduce_fusion.1
  355.3 2.0 convolution_convert_fusion.1
  357.5 2.5 copy.20
  360.0 1.8 slice.11
  361.8 3.4 convolution_convert_fusion.4
  365.2 23.2 %grad_to_heads.1 = bf16[16,128,128]{2,1,0:T(8,128)(2,1)} custom-call(bf16[2,128,1024]{2,1,0:T(8,128)(2,1)} %bitcast.93), custom_call_target="tpu_custom_call" | custom-call | tf_op jit(solution)/shard_map/grad_to_heads/pallas_call | solution.py:765
  388.4 2.1 convert_multiply_fusion
  390.5 2.5 copy.21
  393.0 2.1 bitcast_reduce_fusion
  395.1 17.5 %attend_backward.1 = (bf16[2048,128]{1,0:T(8,128)(2,1)}, bf16[2048,128]{1,0:T(8,128)(2,1)}, bf16[2048,128]{1,0:T(8,128)(2,1)}) custom-call(s32[8]{0:T(128)} %and_select_fusion.first, bf16[2048,384]{1,0:T(8,128)(2,1)} %convolution_convert_fusion.q_ref.k_ref.v_ref, bf16[2048,384]{1,0:T(8,128)(2,1)} %convolution_convert_fusion.q_ref.k_ref.v_ref, ...), custom_call_target="tpu_custom_call" | custom-call | tf_op jit(solution)/shard_map/attend_backward/pallas_call | solution.py:906
  412.5 4.6 fusion.6
  417.1 42.3 %sum_weight_grads.1 = bf16[256,3072]{1,0:T(8,128)(2,1)} custom-call(bf16[4,256,384]{2,1,0:T(8,128)(2,1)} %bitcast.90), custom_call_target="tpu_custom_call" | custom-call | tf_op jit(solution)/shard_map/sum_weight_grads/pallas_call | solution.py:1265
  459.5 37.3 %psum.15 = f32[1024]{0:T(1024)S(1)} all-reduce(f32[1024]{0:T(1024)S(1)} %get-tuple-element.42), channel_id=1, replica_groups=mesh['ctx'=8,'fsdp'=4] {'ctx','fsdp'}, use_global_device_ids=true, to_apply=%region_15.16 | all-reduce | flops 1024 | bytes 8192 | tf_op jit(solution)/shard_map/psum | solution.py:1364
  497.4 33.2 %grad_to_tokens.1 = bf16[2,128,3072]{2,1,0:T(8,128)(2,1)} custom-call(bf16[16,128,128]{2,1,0:T(8,128)(2,1)} %bitcast.94, bf16[16,128,128]{2,1,0:T(8,128)(2,1)} %bitcast.95, bf16[16,128,128]{2,1,0:T(8,128)(2,1)} %bitcast.96), custom_call_target="tpu_custom_call" | custom-call | tf_op jit(solution)/shard_map/grad_to_tokens/pallas_call | solution.py:709
  530.6 5.3 fusion.40
  536.0 1.3 fusion.9
  538.5 2.0 multiply_reduce_fusion
  542.3 79.0 %all-reduce.2.cloned.1.call-done = bf16[256,1024]{1,0:T(8,128)(2,1)} async-done(((bf16[256,1024]{1,0:T(8,128)(2,1)}), bf16[256,1024]{1,0:T(8,128)(2,1)}) %all-reduce.2.cloned.1.call-update) | async-done | bytes 524304 | tf_op jit(solution)/shard_map/psum | solution.py:1367
  621.4 2.1 convert_element_type.107
  (61 shorter events, 9.8 us)
Async XLA Ops:
  7.2 5.6 copy-start
  7.2 131.1 %all-gather.2.cloned.1.call-start = ((), (), s32[]{:S(2)}) async-start(), calls=%async_computation.1 | async-start | bytes 2621440 | tf_op jit(solution)/shard_map/all_gather | solution.py:1306
  9.4 3.8 copy-start.10
  9.4 531.1 %reduce-scatter.2.cloned.1.call-start = ((), (), s32[]{:S(2)}) async-start(), calls=%async_computation.2 | async-start | bytes 2621440 | tf_op jit(solution)/shard_map/reduce_scatter | solution.py:1366
  75.7 8.9 %copy-start.8 = (s32[2048]{0:T(1024)}, s32[2048]{0:T(1024)S(1)}, u32[]{:S(2)}) copy-start(s32[2048]{0:T(1024)S(1)} %pad_add_fusion) | copy-start | bytes 24580
  84.6 52.0 %copy-start.11 = (s32[1,1,2,128,1]{3,4,2,1,0:T(1,128)S(1)}, s32[1,1,2,128,1]{3,4,2,1,0:T(1,128)}, u32[]{:S(2)}) copy-start(s32[1,1,2,128,1]{3,4,2,1,0:T(1,128)} %param.12) | copy-start | bytes 3076
  84.6 52.3 %copy-start.4 = (bf16[1,1,2,128,1024]{4,3,2,1,0:T(8,128)(2,1)S(1)}, bf16[1,1,2,128,1024]{4,3,2,1,0:T(8,128)(2,1)}, u32[]{:S(2)}) copy-start(bf16[1,1,2,128,1024]{4,3,2,1,0:T(8,128)(2,1)} %param.19) | copy-start | bytes 1572868
  136.9 4.3 copy-start.9
  352.0 3.3 copy-start.3
  354.5 0.8 copy-start.5
  357.4 263.9 %all-reduce.2.cloned.1.call-start = ((), (), s32[]{:S(2)}) async-start(), calls=%async_computation.3 | async-start | bytes 1048576 | tf_op jit(solution)/shard_map/psum | solution.py:1367
  361.8 26.5 %copy-start.7 = (f32[2048,128]{1,0:T(8,128)S(1)}, f32[2048,128]{1,0:T(8,128)}, u32[]{:S(2)}) copy-start(f32[2048,128]{1,0:T(8,128)} %get-tuple-element.36) | copy-start | bytes 3145732
  393.0 19.5 %copy-start.12 = (bf16[16,128,1024]{2,1,0:T(8,128)(2,1)S(1)}, bf16[16,128,1024]{2,1,0:T(8,128)(2,1)}, u32[]{:S(2)}) copy-start(bf16[16,128,1024]{2,1,0:T(8,128)(2,1)} %get-tuple-element.26) | copy-start | bytes 12582916
  530.6 5.4 copy-start.6
  535.9 2.1 copy-start.1
  536.0 2.5 copy-start.2
Sparse Core Ops, SparseCore 0:
  10.1 34.6 all-gather.1
  357.5 35.6 reduce-scatter.1
  540.6 80.7 all-reduce.1

commit v2 on v1

--- a/solution.py
+++ b/solution.py
@@ -776,53 +776,66 @@
 TILE = 256
 
 
-def attend_forward(qkv, start_column, first_tile, scale):
-    length = qkv.shape[0]
+def halves(value, axis):
+    size = value.shape[axis] // 2
+    at = lax.broadcasted_iota(jnp.int32, value.shape, axis)
+    zero = jnp.zeros_like(value)
+    return [jnp.where(at < size, value, zero), jnp.where(at >= size, value, zero)]
+
+
+def attend_forward(stream, projection, start_row, numbers, scale):
+    length, width = stream.shape
     tiles = length // TILE
     lanes = 128
     size = lanes // 2
 
-    def kernel(first, q_ref, k_ref, v_ref, s_ref, o32, o16, lse):
+    def kernel(first, x_ref, wq_ref, wk_ref, wv_ref, s_ref, q_out, k_out, v_out, m16, m32, lse, v_turned):
         i = pl.program_id(0)
-        lane = lax.broadcasted_iota(jnp.int32, (TILE, lanes), 1)
-        query = q_ref[...]
-        zero = jnp.zeros_like(query)
-        heads = [jnp.where(lane < size, query, zero), jnp.where(lane >= size, query, zero)]
+        own = pl.ds(pl.multiple_of(i * TILE, TILE), TILE)
+        rows = x_ref[...]
+        query = jnp.dot(rows, wq_ref[...], preferred_element_type=F32).astype(BF)
+        key = jnp.dot(rows, wk_ref[...], preferred_element_type=F32).astype(BF)
+        value = jnp.dot(rows, wv_ref[...], preferred_element_type=F32).astype(BF)
+        q_out[...] = query
+        k_out[own, :] = key
+        v_out[...] = value
+        v_turned[:, own] = value.T
+        queries = halves((query * scale).T, 0)
         start = s_ref[...]
-        row = i * TILE + lax.broadcasted_iota(jnp.int32, (TILE, TILE), 0)
-        column = lax.broadcasted_iota(jnp.int32, (TILE, TILE), 1)
+        key_row = lax.broadcasted_iota(jnp.int32, (TILE, TILE), 0)
+        query_column = i * TILE + lax.broadcasted_iota(jnp.int32, (TILE, TILE), 1)
 
         def step(j, carried):
             at = pl.multiple_of(j * TILE, TILE)
-            keys = k_ref[pl.ds(at, TILE), :]
-            values = v_ref[pl.ds(at, TILE), :]
-            seen = (column + at <= row) & (column + at >= start)
+            keys = k_out[pl.ds(at, TILE), :]
+            seen = (key_row + at <= query_column) & (key_row + at >= start)
             out = []
             for h in range(2):
                 top, total, mixed = carried[h]
-                score = lax.dot_general(heads[h], keys, (((1,), (1,)), ((), ())), preferred_element_type=F32) * scale
-                score = jnp.where(seen, score, NEGATIVE)
-                new_top = jnp.maximum(top, jnp.max(score, axis=1, keepdims=True))
-                weight = jnp.where(seen, jnp.exp(score - new_top), 0.0)
+                score = jnp.where(seen, jnp.dot(keys, queries[h], preferred_element_type=F32), NEGATIVE)
+                new_top = jnp.maximum(top, jnp.max(score, axis=0, keepdims=True))
+                weight = jnp.exp(score - new_top)
                 shrink = jnp.exp(top - new_top)
-                total = total * shrink + jnp.sum(weight, axis=1, keepdims=True)
-                mixed = mixed * shrink + jnp.dot(weight.astype(BF), values, preferred_element_type=F32)
+                total = total * shrink + jnp.sum(weight, axis=0, keepdims=True)
+                values = v_turned[h * size : (h + 1) * size, pl.ds(at, TILE)]
+                mixed = mixed * shrink + jnp.dot(values, weight.astype(BF), preferred_element_type=F32)
                 out.append((new_top, total, mixed))
             return tuple(out)
 
         begin = (
-            jnp.full((TILE, 1), NEGATIVE, F32),
-            jnp.zeros((TILE, 1), F32),
-            jnp.zeros((TILE, lanes), F32),
+            jnp.full((1, TILE), NEGATIVE, F32),
+            jnp.zeros((1, TILE), F32),
+            jnp.zeros((size, TILE), F32),
         )
         done = lax.fori_loop(first[i], i + 1, step, (begin, begin))
-        ready = [mixed / total for _, total, mixed in done]
-        logs = [top + jnp.log(total) for top, total, _ in done]
-        mixed = jnp.where(lane < size, ready[0], ready[1])
-        o32[...] = mixed
-        o16[...] = mixed.astype(BF)
-        lse[...] = jnp.where(lane < size, logs[0], logs[1])
-
+        mixed = jnp.concatenate([part / total for _, total, part in done], axis=0)
+        m32[...] = mixed
+        m16[...] = mixed.T.astype(BF)
+        lse[...] = jnp.concatenate([top + jnp.log(total) for top, total, _ in done], axis=0)
+
+    groups = width // lanes
+    tile = pl.BlockSpec((TILE, lanes), lambda i, n: (i, 0))
+    turned = pl.BlockSpec((lanes, TILE), lambda i, n: (0, i))
     return pl.pallas_call(
         kernel,
         name="attend_forward",
@@ -830,43 +843,57 @@
             num_scalar_prefetch=1,
             grid=(tiles,),
             in_specs=[
-                pl.BlockSpec((TILE, lanes), lambda i, first: (i, 0)),
-                pl.BlockSpec((length, lanes), lambda i, first: (0, 1)),
-                pl.BlockSpec((length, lanes), lambda i, first: (0, 2)),
-                pl.BlockSpec((TILE, 1), lambda i, first: (i, 0)),
+                pl.BlockSpec((TILE, width), lambda i, n: (i, 0)),
+                pl.BlockSpec((width, lanes), lambda i, n: (0, n[tiles])),
+                pl.BlockSpec((width, lanes), lambda i, n: (0, groups + n[tiles])),
+                pl.BlockSpec((width, lanes), lambda i, n: (0, 2 * groups + n[tiles])),
+                pl.BlockSpec((1, TILE), lambda i, n: (0, i)),
             ],
-            out_specs=[pl.BlockSpec((TILE, lanes), lambda i, first: (i, 0))] * 3,
+            out_specs=[
+                tile,
+                pl.BlockSpec((length, lanes), lambda i, n: (0, 0)),
+                tile,
+                tile,
+                turned,
+                pl.BlockSpec((2, TILE), lambda i, n: (0, i)),
+            ],
+            scratch_shapes=[pltpu.VMEM((lanes, length), BF)],
         ),
         out_shape=(
-            jax.ShapeDtypeStruct((length, lanes), F32),
             jax.ShapeDtypeStruct((length, lanes), BF),
-            jax.ShapeDtypeStruct((length, lanes), F32),
+            jax.ShapeDtypeStruct((length, lanes), BF),
+            jax.ShapeDtypeStruct((length, lanes), BF),
+            jax.ShapeDtypeStruct((length, lanes), BF),
+            jax.ShapeDtypeStruct((lanes, length), F32),
+            jax.ShapeDtypeStruct((2, length), F32),
         ),
         compiler_params=params(False),
-    )(first_tile, qkv, qkv, qkv, start_column)
-
-
-def attend_backward(qkv, grad, start_row, log_rows, delta_rows, first_tile, scale):
-    length = qkv.shape[0]
+    )(numbers, stream, projection, projection, projection, start_row)
+
+
+def attend_backward(query, key, value, grad, mixed, logs, start_row, numbers, scale):
+    length, lanes = query.shape
     tiles = length // TILE
-    lanes = 128
     size = lanes // 2
 
-    def kernel(first, q_ref, k_ref, v_ref, g_ref, s_ref, l_ref, d_ref, dq, dk, dv, acc_k, acc_v):
+    def kernel(first, q_ref, k_ref, v_ref, g_ref, m_ref, l_ref, s_ref, dq, dk, dv, acc_k, acc_v, k_turned):
         i = pl.program_id(0)
 
         @pl.when(i == 0)
         def _():
             acc_k[...] = jnp.zeros_like(acc_k)
             acc_v[...] = jnp.zeros_like(acc_v)
-
-        lane = lax.broadcasted_iota(jnp.int32, (TILE, lanes), 1)
-
-        def split(value):
-            zero = jnp.zeros_like(value)
-            return [jnp.where(lane < size, value, zero), jnp.where(lane >= size, value, zero)]
-
-        queries, grads = split(q_ref[...]), split(g_ref[...])
+            for t in range(tiles):
+                k_turned[:, t * TILE : (t + 1) * TILE] = k_ref[t * TILE : (t + 1) * TILE, :].T
+
+        scaled = q_ref[...] * scale
+        grads = g_ref[...]
+        turned = grads.T
+        queries, queries_turned = halves(scaled, 1), halves(scaled.T, 0)
+        grad_rows, grads_turned = halves(grads, 1), halves(turned, 0)
+        product = turned.astype(F32) * m_ref[...]
+        deltas = [jnp.sum(product[h * size : (h + 1) * size], axis=0, keepdims=True) for h in range(2)]
+        logs_row = [l_ref[h : h + 1, :] for h in range(2)]
         start = s_ref[...]
         key_row = lax.broadcasted_iota(jnp.int32, (TILE, TILE), 0)
         query_column = i * TILE + lax.broadcasted_iota(jnp.int32, (TILE, TILE), 1)
@@ -875,34 +902,34 @@
             at = pl.multiple_of(j * TILE, TILE)
             keys = k_ref[pl.ds(at, TILE), :]
             values = v_ref[pl.ds(at, TILE), :]
-            key_parts = split(keys)
             seen = (key_row + at <= query_column) & (key_row + at >= start)
             key_sum = jnp.zeros((TILE, lanes), F32)
             value_sum = jnp.zeros((TILE, lanes), F32)
+            out = []
             for h in range(2):
-                score = lax.dot_general(keys, queries[h], (((1,), (1,)), ((), ())), preferred_element_type=F32) * scale
-                weight = jnp.where(seen, jnp.exp(score - l_ref[h : h + 1, :]), 0.0)
-                grad_weight = lax.dot_general(
-                    values, grads[h], (((1,), (1,)), ((), ())), preferred_element_type=F32
-                )
-                grad_score = (weight * (grad_weight - d_ref[h : h + 1, :])).astype(BF)
-                value_sum += jnp.dot(weight.astype(BF), grads[h], preferred_element_type=F32)
+                score = jnp.dot(keys, queries_turned[h], preferred_element_type=F32)
+                weight = jnp.exp(jnp.where(seen, score - logs_row[h], NEGATIVE))
+                grad_weight = jnp.dot(values, grads_turned[h], preferred_element_type=F32)
+                grad_score = (weight * (grad_weight - deltas[h])).astype(BF)
+                value_sum += jnp.dot(weight.astype(BF), grad_rows[h], preferred_element_type=F32)
                 key_sum += jnp.dot(grad_score, queries[h], preferred_element_type=F32)
-                running += lax.dot_general(
-                    grad_score, key_parts[h], (((0,), (0,)), ((), ())), preferred_element_type=F32
-                )
+                part = k_turned[h * size : (h + 1) * size, pl.ds(at, TILE)]
+                out.append(running[h] + jnp.dot(part, grad_score, preferred_element_type=F32))
             acc_k[pl.ds(at, TILE), :] += key_sum
             acc_v[pl.ds(at, TILE), :] += value_sum
-            return running
-
-        total = lax.fori_loop(first[i], i + 1, step, jnp.zeros((TILE, lanes), F32))
-        dq[...] = (total * scale).astype(BF)
+            return tuple(out)
+
+        zero = jnp.zeros((size, TILE), F32)
+        total = lax.fori_loop(first[i], i + 1, step, (zero, zero))
+        dq[...] = (jnp.concatenate(total, axis=0) * scale).T.astype(BF)
 
         @pl.when(i == tiles - 1)
         def _():
-            dk[...] = (acc_k[...] * scale).astype(BF)
+            dk[...] = acc_k[...].astype(BF)
             dv[...] = acc_v[...].astype(BF)
 
+    tile = pl.BlockSpec((TILE, lanes), lambda i, n: (i, 0))
+    full = pl.BlockSpec((length, lanes), lambda i, n: (0, 0))
     return pl.pallas_call(
         kernel,
         name="attend_backward",
@@ -910,24 +937,24 @@
             num_scalar_prefetch=1,
             grid=(tiles,),
             in_specs=[
-                pl.BlockSpec((TILE, lanes), lambda i, first: (i, 0)),
-                pl.BlockSpec((length, lanes), lambda i, first: (0, 1)),
-                pl.BlockSpec((length, lanes), lambda i, first: (0, 2)),
-                pl.BlockSpec((TILE, lanes), lambda i, first: (i, 0)),
-                pl.BlockSpec((1, TILE), lambda i, first: (0, i)),
-                pl.BlockSpec((2, TILE), lambda i, first: (0, i)),
-                pl.BlockSpec((2, TILE), lambda i, first: (0, i)),
+                tile,
+                full,
+                full,
+                tile,
+                pl.BlockSpec((lanes, TILE), lambda i, n: (0, i)),
+                pl.BlockSpec((2, TILE), lambda i, n: (0, i)),
+                pl.BlockSpec((1, TILE), lambda i, n: (0, i)),
             ],
-            out_specs=[
-                pl.BlockSpec((TILE, lanes), lambda i, first: (i, 0)),
-                pl.BlockSpec((length, lanes), lambda i, first: (0, 0)),
-                pl.BlockSpec((length, lanes), lambda i, first: (0, 0)),
+            out_specs=[tile, full, full],
+            scratch_shapes=[
+                pltpu.VMEM((length, lanes), F32),
+                pltpu.VMEM((length, lanes), F32),
+                pltpu.VMEM((lanes, length), BF),
             ],
-            scratch_shapes=[pltpu.VMEM((length, lanes), F32), pltpu.VMEM((length, lanes), F32)],
         ),
         out_shape=(jax.ShapeDtypeStruct((length, lanes), BF),) * 3,
         compiler_params=params(False),
-    )(first_tile, qkv, qkv, qkv, grad, start_row, log_rows, delta_rows)
+    )(numbers, query, key, value, grad, mixed, logs, start_row)
 
 
 def dispatch_rows(arrays):
@@ -1140,23 +1167,51 @@
     )(rows, grads, first_proj, second_proj)
 
 
-def sum_weight_grads(parts):
+def finish_exchange(arrays, parts, out_parts, gain_part):
     count = lax.axis_size("ctx")
     depth = count // 2
+    number = len(arrays)
+    lanes = arrays[0].shape[2]
+    width = count * lanes
     _, rows, wide = parts.shape
-    lanes = wide // 3
-    width = count * lanes
-
-    def kernel(p_ref, out, got, held, ss_r, rs_r, ss_up, ss_dn, rs_z, ss_a, ss_b, rs_o):
+    slab = rows // count
+
+    def kernel(*refs):
+        ins, (p_ref, o_ref, g_ref), (tok_out, w_out, o_out, g_out) = (
+            refs[:number],
+            refs[number : number + 3],
+            refs[number + 3 : number + 7],
+        )
+        (
+            got, held, got_a, far, got_x, mine, got_c, slab_out, got_g, sum_g, got_gc,
+            ss, rs, ss_r, rs_r, ss_up, ss_dn, rs_z, ss_a, ss_b, rs_o,
+            ss_oa, rs_oa, ss_ox, rs_ox, ss_oc, rs_oc, ss_of, rs_of, ss_g, rs_g, ss_gc, rs_gc,
+        ) = refs[number + 7 :]
         c, f, z, y, x, k = place()
+        pair = 2 * z + k
+        target = 2 * x + y
+        sib = (c, f + 1 - 2 * k)
+        xn = (c, (f + 2) % 4)
+        up = (c + 2, f)
+        down = (c - 2, f)
+
+        def core_send(j):
+            shard = 2 * (1 - x) + 1 - k if j == 0 else 2 * x + 1 - k
+            return remote(o_ref.at[shard], got_a.at[j], ss_oa.at[j], rs_oa.at[j], sib)
+
+        def gain_send(j):
+            return remote(sum_g.at[j], got_g.at[j], ss_g.at[j], rs_g.at[j], sib if j == 0 else xn)
+
+        core_send(0).start()
+        core_send(1).start()
+        sum_g[0] = g_ref[...]
+        gain_send(0).start()
+
         peers = [
             (2 * z + 1 - y, f, 2 * x + 1 - y),
             (c, (f + 2) % 4, 2 * (1 - x) + y),
             (2 * z + 1 - y, (f + 2) % 4, 2 * (1 - x) + 1 - y),
         ]
-        sib = (c, f + 1 - 2 * k)
-        up = (c + 2, f)
-        down = (c - 2, f)
 
         def scatter(d):
             cp, fp, shard = peers[d]
@@ -1164,31 +1219,65 @@
 
         for d in (2, 1, 0):
             scatter(d).start()
+
+        def there(half, a):
+            return tok_out.at[half, :, pl.ds(pl.multiple_of(a * width + pair * lanes, lanes), lanes)]
+
+        def send(i, half, a):
+            ct = (c + i) % count
+            return remote(
+                ins[a].at[block_at(ct, half, count)], there(half, a), ss.at[i, half, a], rs.at[pair, half, a], (ct, target)
+            )
+
+        def own(half, a):
+            return pltpu.make_async_copy(ins[a].at[block_at(c, half, count)], there(half, a), rs.at[pair, half, a])
+
+        pieces = [(half, a) for a in range(number) for half in range(2)]
+        for i in range(1, count):
+            for half, a in pieces:
+                send(i, half, a).start()
+
+        @pl.when(k == y)
+        def _():
+            for half, a in pieces:
+                own(half, a).start()
+
+        @pl.when(k != y)
+        def _():
+            for half, a in pieces:
+                send(0, half, a).start()
+
+        across = remote(far, got_x, ss_ox, rs_ox, xn)
+        core_send(0).wait_recv()
+        far[...] = (o_ref[2 * (1 - x) + k].astype(F32) + got_a[0].astype(F32)).astype(BF)
+        across.start()
+        gain_send(0).wait_recv()
+        sum_g[1] = sum_g[0] + got_g[0]
+        gain_send(1).start()
+
         total = p_ref[2 * x + y].astype(F32)
         for d in range(3):
             scatter(d).wait_recv()
             total += got[d].astype(F32)
         held[z] = total.astype(BF)
 
-        def chain(zb, ss, dev):
-            return remote(held.at[zb], held.at[zb], ss, rs_z.at[zb], dev)
+        def chain(zb, sem, dev):
+            return remote(held.at[zb], held.at[zb], sem, rs_z.at[zb], dev)
 
         def piece(zb, j):
             return held.at[zb, :, pl.ds(j * lanes, lanes)]
 
-        def there(zb, j):
-            return out.at[:, pl.ds(pl.multiple_of(j * width + (2 * zb + k) * lanes, lanes), lanes)]
+        def goal(zb, j):
+            return w_out.at[:, pl.ds(pl.multiple_of(j * width + (2 * zb + k) * lanes, lanes), lanes)]
 
         def own_column(zb, j):
-            return remote(piece(zb, j), there(zb, j), ss_a.at[zb, j], rs_o.at[2 * zb + k, j], (c, 2 * x + y))
+            return remote(piece(zb, j), goal(zb, j), ss_a.at[zb, j], rs_o.at[2 * zb + k, j], (c, target))
 
         def own_local(zb, j):
-            return pltpu.make_async_copy(piece(zb, j), there(zb, j), rs_o.at[2 * zb + k, j])
+            return pltpu.make_async_copy(piece(zb, j), goal(zb, j), rs_o.at[2 * zb + k, j])
 
         def next_column(zb, j):
-            return remote(
-                piece(zb, j), there(zb, j), ss_b.at[zb, j], rs_o.at[2 * zb + k, j], (2 * z + 1 - y, 2 * x + y)
-            )
+            return remote(piece(zb, j), goal(zb, j), ss_b.at[zb, j], rs_o.at[2 * zb + k, j], (2 * z + 1 - y, target))
 
         def spread(zb):
             for j in range(3):
@@ -1213,6 +1302,28 @@
             chain(z, ss_dn.at[0], down).start()
 
         spread(z)
+
+        core_send(1).wait_recv()
+        across.wait_recv()
+        for b in range(count):
+            at = pl.ds(b * slab, slab)
+            mine[b] = (
+                o_ref[2 * x + k, at, :].astype(F32) + got_a[1, at, :].astype(F32) + got_x[at, :].astype(F32)
+            ).astype(BF)
+        gain_send(1).wait_recv()
+        sum_g[2] = sum_g[1] + got_g[1]
+
+        def slab_send(i):
+            ct = (c + i) % count
+            return remote(mine.at[ct], got_c.at[c], ss_oc.at[i], rs_oc.at[c], (ct, f))
+
+        def gain_spread(i):
+            return remote(sum_g.at[2], got_gc.at[c], ss_gc.at[i], rs_gc.at[c], ((c + i) % count, f))
+
+        for i in range(1, count):
+            slab_send(i).start()
+            gain_spread(i).start()
+
         for j in range(1, depth):
 
             @pl.when(z - j >= 0)
@@ -1235,12 +1346,58 @@
 
                 spread(z + j)
 
+        sum_o = mine[c].astype(F32)
+        total_g = sum_g[2]
+        for i in range(1, count):
+            cs = (c + i) % count
+            remote(mine.at[cs], got_c.at[cs], ss_oc.at[i], rs_oc.at[cs], sib).wait_recv()
+            remote(sum_g.at[2], got_gc.at[cs], ss_gc.at[i], rs_gc.at[cs], sib).wait_recv()
+            sum_o += got_c[cs].astype(F32)
+            total_g += got_gc[cs]
+        g_out[...] = total_g
+        slab_out[...] = sum_o.astype(BF)
+
+        def slab_spread(i):
+            return remote(slab_out, o_out.at[c], ss_of.at[i], rs_of.at[c], ((c + i) % count, f))
+
+        slab_own = pltpu.make_async_copy(slab_out, o_out.at[c], rs_of.at[c])
+        for i in range(1, count):
+            slab_spread(i).start()
+        slab_own.start()
+
+        core_send(0).wait_send()
+        core_send(1).wait_send()
+        gain_send(0).wait_send()
+        gain_send(1).wait_send()
+        across.wait_send()
         for d in range(3):
             scatter(d).wait_send()
-        for pair in range(count):
+        for half, a in pieces:
+            for other in range(count):
+                cols = pl.ds(a * width + other * lanes, lanes)
+                remote(ins[a].at[0], tok_out.at[half, :, cols], ss.at[0, half, a], rs.at[other, half, a], sib).wait_recv()
+        for i in range(1, count):
+            for half, a in pieces:
+                send(i, half, a).wait_send()
+            slab_send(i).wait_send()
+            gain_spread(i).wait_send()
+            slab_spread(i).wait_send()
+            cs = (c + i) % count
+            remote(slab_out, o_out.at[cs], ss_of.at[i], rs_of.at[cs], sib).wait_recv()
+        slab_own.wait()
+
+        @pl.when(k != y)
+        def _():
+            for half, a in pieces:
+                send(0, half, a).wait_send()
+            for zb in range(depth):
+                for j in range(3):
+                    own_column(zb, j).wait_send()
+
+        for other in range(count):
             for j in range(3):
                 remote(
-                    piece(0, j), out.at[:, pl.ds(j * width + pair * lanes, lanes)], ss_a.at[0, j], rs_o.at[pair, j], sib
+                    piece(0, j), w_out.at[:, pl.ds(j * width + other * lanes, lanes)], ss_a.at[0, j], rs_o.at[other, j], sib
                 ).wait_recv()
         for j in range(depth):
 
@@ -1256,26 +1413,39 @@
             for j in range(3):
                 next_column(zb, j).wait_send()
 
-        @pl.when(k != y)
-        def _():
-            for zb in range(depth):
-                for j in range(3):
-                    own_column(zb, j).wait_send()
-
+    vmem = pl.BlockSpec(memory_space=pltpu.VMEM)
+    eighth = gain_part.shape
     return pl.pallas_call(
         kernel,
-        name="sum_weight_grads",
-        out_shape=jax.ShapeDtypeStruct((rows, 3 * width), BF),
-        in_specs=[pl.BlockSpec(memory_space=pltpu.VMEM)],
-        out_specs=ANY,
+        name="finish_exchange",
+        out_shape=(
+            jax.ShapeDtypeStruct((2, arrays[0].shape[1], number * width), BF),
+            jax.ShapeDtypeStruct((rows, 3 * width), BF),
+            jax.ShapeDtypeStruct((count, slab, width), BF),
+            jax.ShapeDtypeStruct(eighth, F32),
+        ),
+        in_specs=[ANY] * number + [vmem] * 3,
+        out_specs=(ANY, ANY, ANY, vmem),
         scratch_shapes=[
             pltpu.VMEM((3, rows, wide), BF),
             pltpu.VMEM((depth, rows, wide), BF),
+            pltpu.VMEM((2, rows, width), BF),
+            pltpu.VMEM((rows, width), BF),
+            pltpu.VMEM((rows, width), BF),
+            pltpu.VMEM((count, slab, width), BF),
+            pltpu.VMEM((count, slab, width), BF),
+            pltpu.VMEM((slab, width), BF),
+            pltpu.VMEM((2,) + eighth, F32),
+            pltpu.VMEM((3,) + eighth, F32),
+            pltpu.VMEM((count,) + eighth, F32),
+            DMA((count, 2, number)), DMA((count, 2, number)),
             DMA((3,)), DMA((3,)), DMA((depth,)), DMA((depth,)), DMA((depth,)),
             DMA((depth, 3)), DMA((depth, 3)), DMA((count, 3)),
+            DMA((2,)), DMA((2,)), DMA, DMA, DMA((count,)), DMA((count,)), DMA((count,)), DMA((count,)),
+            DMA((2,)), DMA((2,)), DMA((count,)), DMA((count,)),
         ],
         compiler_params=params(),
-    )(parts)
+    )(*arrays, parts, out_parts, gain_part)
 
 
 def slots_of(routes):
@@ -1311,13 +1481,9 @@
     )
     stream = stream.reshape(length, width)
     projection = projection.reshape(width, 3 * width)
-    own_columns = jnp.concatenate(
-        [lax.dynamic_slice(projection, (0, j * width + pair * lanes), (width, lanes)) for j in range(3)], axis=1
-    )
-    qkv = jnp.dot(stream, own_columns, preferred_element_type=F32).astype(BF)
-    start_line = jnp.concatenate([starts[:, 0].reshape(-1), starts[::-1, 1].reshape(-1)])
-    first_tile = jnp.min(start_line.reshape(-1, TILE), axis=1) // TILE
-    mixed32, mixed16, logs = attend_forward(qkv, start_line[:, None], first_tile, scale)
+    start_row = jnp.concatenate([starts[:, 0].reshape(-1), starts[::-1, 1].reshape(-1)])[None]
+    numbers = jnp.concatenate([jnp.min(start_row.reshape(-1, TILE), axis=1) // TILE, pair[None]])
+    query, key, value, mixed16, mixed32, logs = attend_forward(stream, projection, start_row, numbers, scale)
     mixed = heads_to_tokens([mixed16.reshape(2 * count, half_rows, lanes)], "mixed_to_tokens").reshape(rows, width)
     middle = start_x + jnp.dot(mixed, out_proj, preferred_element_type=F32)
     normed_two, hat_two, inverse_two = norm_forward(middle, gain_two)
@@ -1342,29 +1508,31 @@
     grad_mid_norm, grad_gain_two = norm_backward(grad_routed[None], hat_two[None], inverse_two[None], gain_two)
     grad_middle = cotangent.astype(F32) + grad_mid_norm[0]
     grad_attn = grad_middle.astype(BF)
-    grad_outproj = lax.dot_general(mixed, grad_attn, pick, preferred_element_type=F32)
+    grad_outproj = lax.dot_general(mixed, grad_attn, pick, preferred_element_type=F32).astype(BF)
     grad_mixed = lax.dot_general(grad_attn, out_proj, (((1,), (1,)), ((), ())), preferred_element_type=F32).astype(BF)
     grad_heads = tokens_to_heads(grad_mixed.reshape(2, half_rows, width), "grad_to_heads").reshape(length, lanes)
-    delta = jnp.sum((grad_heads.astype(F32) * mixed32).reshape(length, 2, lanes // 2), axis=2).T
-    log_rows = logs[:, :: lanes // 2].T
-    grad_q, grad_k, grad_v = attend_backward(qkv, grad_heads, start_line[None], log_rows, delta, first_tile, scale)
+    grad_q, grad_k, grad_v = attend_backward(
+        query, key, value, grad_heads, mixed32, logs, start_row, numbers, scale
+    )
     blocks = (2 * count, half_rows, lanes)
-    grad_projected = heads_to_tokens(
-        [grad_q.reshape(blocks), grad_k.reshape(blocks), grad_v.reshape(blocks)], "grad_to_tokens"
-    ).reshape(rows, 3 * width)
     own_grads = jnp.concatenate([grad_q, grad_k, grad_v], axis=1)
     parts = lax.dot_general(stream, own_grads, pick, preferred_element_type=F32).astype(BF)
     shard_rows = width // 4
-    weight_grad = sum_weight_grads(parts.reshape(4, shard_rows, 3 * lanes)).astype(F32)
+    grad_projected, weight_grad, shard_out, gain_sum = finish_exchange(
+        [grad_q.reshape(blocks), grad_k.reshape(blocks), grad_v.reshape(blocks)],
+        parts.reshape(4, shard_rows, 3 * lanes),
+        grad_outproj.reshape(4, shard_rows, width),
+        grad_gain_two.reshape(8, width // 8),
+    )
+    grad_projected = grad_projected.reshape(rows, 3 * width)
+    weight_grad = weight_grad.astype(F32)
+    shard_out = shard_out.reshape(shard_rows, width).astype(F32)
     grad_normed = lax.dot_general(grad_projected, projection, (((1,), (1,)), ((), ())), preferred_element_type=F32)
     grad_in_norm, _ = norm_backward(grad_normed[None], hat_one[None], inverse_one[None], gain_one)
     grad_start = grad_middle + grad_in_norm[0]
     own_gain = lax.dynamic_slice(gain_one, (f * shard_rows,), (shard_rows,))
     shard_gain_one = jnp.sum(weight_grad * qkv_low.astype(F32), axis=1) / own_gain
-    summed_gain = lax.psum(grad_gain_two, ("ctx", "fsdp"))
-    shard_gain_two = lax.dynamic_slice(summed_gain, (f * shard_rows,), (shard_rows,))
-    shard_out = lax.psum_scatter(grad_outproj.astype(BF), "fsdp", scatter_dimension=0, tiled=True)
-    shard_out = lax.psum(shard_out, "ctx").astype(F32)
+    shard_gain_two = lax.dynamic_slice(gain_sum.reshape(width), (f * shard_rows,), (shard_rows,))
     return (
         block_out.reshape(tokens.shape),
         grad_start.reshape(tokens.shape),

time: 634 us -> 511 us (0.81)
  waiting for transfers between devices: 79.1 us -> 0.02 us
  blocking collectives: 37.3 us -> 0 us
  Pallas kernels: 438 us -> 453 us
  local copies, waits for them, and re-layouts: 12.6 us -> 2.28 us
    psum x1 -> x0, waiting for transfers between devices: 79 us -> none  [by_head_pairs(): shard_out = lax.psum(shard_out, 'ctx').astype(F32)]
    pallas_call x1, Pallas kernels: 42.3 us -> 90.9 us  [finish_exchange(): pl.pallas_call(kernel, name='finish_exchange', out_shape=(jax.ShapeDtypeS...]
    psum x1 -> x0, blocking collectives: 37.3 us -> none  [by_head_pairs(): summed_gain = lax.psum(grad_gain_two, ('ctx', 'fsdp'))]
    pallas_call x2 -> x1, Pallas kernels: 66 us -> 31.4 us  [heads_to_tokens(): pl.pallas_call(kernel, name=name, out_shape=jax.ShapeDtypeStruct((2, arra...]
  transfers between devices with their start and end apart: 3 -> 1, of which waited for: 1 -> 0; matrix products, arithmetic and copies ran while one was open for 7% -> 2% of each run, Pallas kernels for 36% -> 22%
where the time goes in v2:
time: 511 us; the launch traced here: 509 us
  Pallas kernels  453 us (89%)
  matrix products  24.1 us (5%)
  other arithmetic  15.2 us (3%)
  between operations  14.3 us (3%)
    pallas_call x1, Pallas kernels, finish_exchange(): pl.pallas_call(kernel, name='finish_exchange', out_shape=(jax.ShapeDtypeS...  90.9 us
    pallas_call x1, Pallas kernels, return_rows(): pl.pallas_call(kernel, name='return_rows', out_shape=(jax.ShapeDtypeStruc...  88 us
    pallas_call x1, Pallas kernels, dispatch_rows(): pl.pallas_call(kernel, name='dispatch_rows', out_shape=(jax.ShapeDtypeStr...  64.6 us
    pallas_call x1, Pallas kernels, gather_stream(): pl.pallas_call(kernel, name='gather_stream', out_shape=(jax.ShapeDtypeStr...  60.6 us
    pallas_call x1, Pallas kernels, experts_step(): pl.pallas_call(kernel, name='experts_step', grid=(number,), in_specs=[who...  56.9 us
    pallas_call x1, Pallas kernels, heads_to_tokens(): pl.pallas_call(kernel, name=name, out_shape=jax.ShapeDtypeStruct((2, arra...  31.4 us
    pallas_call x1, Pallas kernels, tokens_to_heads(): pl.pallas_call(kernel, name=name, out_shape=jax.ShapeDtypeStruct((2 * cou...  22.8 us
    pallas_call x1, Pallas kernels, attend_forward(): pl.pallas_call(kernel, name='attend_forward', grid_spec=pltpu.PrefetchSca...  21.3 us
  transfers between devices with their start and end apart: 1, of which 0 were waited for; matrix products, arithmetic and copies ran while one was open for 2% of the time, Pallas kernels for 22%

profile of v2, /device:TPU:1, one launch (start us, length us, event | category | flops | bytes accessed | tf_op | source)
XLA Modules:
  0.0 509.1 jit_solution(7498733362530362872)
XLA Ops:
  7.2 2.1 convert_element_type.89
  9.4 3.3 convert_element_type.88.w_ref
  12.8 0.3 fusion.21
  13.1 1.1 fusion.13.n_ref
  14.2 60.6 %gather_stream.1 = (bf16[16,128,1024]{2,1,0:T(8,128)(2,1)}, s32[8,2,128]{2,1,0:T(2,128)}, bf16[4,256,3072]{2,1,0:T(8,128)(2,1)}) custom-call(bf16[2,128,1024]{2,1,0:T(8,128)(2,1)} %fusion.13.n_ref, s32[2,128]{1,0:T(2,128)} %bitcast.110, bf16[256,3072]{1,0:T(8,128)(2,1)} %convert_element_type.88.w_ref), custom_call_target="tpu_custom_call" | custom-call | tf_op jit(solution)/shard_map/gather_stream/pallas_call | solution.py:636
  74.8 0.8 fusion.35
  75.8 0.6 pad_add_fusion.1.first
  76.4 0.6 pad_add_fusion
  77.0 21.3 %attend_forward.1 = (bf16[2048,128]{1,0:T(8,128)(2,1)}, bf16[2048,128]{1,0:T(8,128)(2,1)}, bf16[2048,128]{1,0:T(8,128)(2,1)}, bf16[2048,128]{1,0:T(8,128)(2,1)}, f32[128,2048]{1,0:T(8,128)}, /*index=5*/f32[2,2048]{1,0:T(2,128)}) custom-call(s32[9]{0:T(128)} %pad_add_fusion.1.first, bf16[2048,1024]{1,0:T(8,128)(2,1)} %bitcast.94, ...), custom_call_target="tpu_custom_call" | custom-call | tf_op jit(solution)/shard_map/attend_forward/pallas_call | solution.py:839
  98.3 31.4 %mixed_to_tokens.1 = bf16[2,128,1024]{2,1,0:T(8,128)(2,1)} custom-call(bf16[16,128,128]{2,1,0:T(8,128)(2,1)} %bitcast.103), custom_call_target="tpu_custom_call" | custom-call | tf_op jit(solution)/shard_map/mixed_to_tokens/pallas_call | solution.py:709
  130.0 1.4 convolution_convert_fusion.1
  131.4 2.6 fusion.36
  134.3 1.6 convolution_convert_fusion.2
  135.8 64.6 %dispatch_rows.1 = (bf16[8,4,8,8,1024]{4,3,2,1,0:T(8,128)(2,1)}, bf16[8,4,8,8,1024]{4,3,2,1,0:T(8,128)(2,1)}) custom-call(bf16[8,8,8,1024]{3,2,1,0:T(8,128)(2,1)} %bitcast.93, bf16[8,8,8,1024]{3,2,1,0:T(8,128)(2,1)} %bitcast.92), custom_call_target="tpu_custom_call" | custom-call | tf_op jit(solution)/shard_map/dispatch_rows/pallas_call | solution.py:1008
  200.4 56.9 %experts_step.1 = (bf16[4,8,64,1024]{3,2,1,0:T(8,128)(2,1)}, bf16[4,8,64,1024]{3,2,1,0:T(8,128)(2,1)}, f32[8,1024,1024]{2,1,0:T(8,128)}, f32[8,1024,1024]{2,1,0:T(8,128)}) custom-call(bf16[8,256,1024]{2,1,0:T(8,128)(2,1)} %bitcast.86, bf16[8,256,1024]{2,1,0:T(8,128)(2,1)} %bitcast.87, f32[8,1024,1024]{2,1,0:T(8,128)} %a_ref.1, f32[8,1024,1024]{2,1,0:T(8,128)} %b_ref.1), custom_call_target="tpu_custom_call" | custom-call | tf_op jit(solution)/shard_map/experts_step/pallas_call | solution.py:1154
  257.3 88.0 %return_rows.1 = (bf16[8,8,8,1024]{3,2,1,0:T(8,128)(2,1)}, bf16[8,8,8,1024]{3,2,1,0:T(8,128)(2,1)}) custom-call(bf16[4,8,8,8,1024]{4,3,2,1,0:T(8,128)(2,1)} %bitcast.90, bf16[4,8,8,8,1024]{4,3,2,1,0:T(8,128)(2,1)} %bitcast.89), custom_call_target="tpu_custom_call" | custom-call | tf_op jit(solution)/shard_map/return_rows/pallas_call | solution.py:1108
  345.3 2.5 fusion.9
  347.8 2.6 multiply_reduce_fusion.1
  350.4 1.4 add_convert_fusion
  351.8 2.1 convolution_convert_fusion
  353.9 1.6 convolution_convert_fusion.3
  355.5 22.8 %grad_to_heads.1 = bf16[16,128,128]{2,1,0:T(8,128)(2,1)} custom-call(bf16[2,128,1024]{2,1,0:T(8,128)(2,1)} %bitcast.104), custom_call_target="tpu_custom_call" | custom-call | tf_op jit(solution)/shard_map/grad_to_heads/pallas_call | solution.py:765
  378.3 16.7 %attend_backward.1 = (bf16[2048,128]{1,0:T(8,128)(2,1)}, bf16[2048,128]{1,0:T(8,128)(2,1)}, bf16[2048,128]{1,0:T(8,128)(2,1)}) custom-call(s32[9]{0:T(128)} %pad_add_fusion.1.first, bf16[2048,128]{1,0:T(8,128)(2,1)} %get-tuple-element.42.q_ref, bf16[2048,128]{1,0:T(8,128)(2,1)} %get-tuple-element.43.k_ref, bf16[2048,128]{1,0:T(8,128)(2,1)} %get-tuple-element.44.v_ref, ...), custom_call_target="tpu_custom_call" | custom-call | tf_op jit(solution)/shard_map/attend_backward/pallas_call | solution.py:933
  395.0 6.0 %fusion.6 = bf16[1024,384]{1,0:T(8,128)(2,1)} fusion(bf16[2048,1024]{1,0:T(8,128)(2,1)} %bitcast.95, bf16[2048,128]{1,0:T(8,128)(2,1)} %get-tuple-element.49, bf16[2048,128]{1,0:T(8,128)(2,1)} %get-tuple-element.48, bf16[2048,128]{1,0:T(8,128)(2,1)} %get-tuple-element.47), kind=kOutput, calls=%fused_computation.10 | convolution fusion | flops 1615724544 | bytes 6553600 | tf_op jit(solution)/shard_map/dot_general | solution.py:1519
  401.0 90.9 %finish_exchange.1 = (bf16[2,128,3072]{2,1,0:T(8,128)(2,1)}, bf16[256,3072]{1,0:T(8,128)(2,1)}, bf16[8,32,1024]{2,1,0:T(8,128)(2,1)}, f32[8,128]{1,0:T(8,128)}) custom-call(bf16[16,128,128]{2,1,0:T(8,128)(2,1)} %bitcast.100, bf16[16,128,128]{2,1,0:T(8,128)(2,1)} %bitcast.101, bf16[16,128,128]{2,1,0:T(8,128)(2,1)} %bitcast.102, ...), custom_call_target="tpu_custom_call" | custom-call | tf_op jit(solution)/shard_map/finish_exchange/pallas_call | solution.py:1418
  491.9 3.6 fusion.34
  495.5 1.1 bitcast_convert_fusion
  496.7 2.0 multiply_reduce_fusion
  498.6 1.4 dynamic_slice.7
  500.0 0.6 dynamic-slice_divide_fusion
  500.7 0.3 fusion.19
  501.0 1.2 add_add_fusion
  (47 shorter events, 0.9 us)
Async XLA Ops:
  7.2 5.5 %copy-start = (bf16[1,1,2,128,1024]{4,3,2,1,0:T(8,128)(2,1)S(1)}, bf16[1,1,2,128,1024]{4,3,2,1,0:T(8,128)(2,1)}, u32[]{:S(2)}) copy-start(bf16[1,1,2,128,1024]{4,3,2,1,0:T(8,128)(2,1)} %param.10) | copy-start | bytes 1572868
  7.2 124.2 %all-gather.2.cloned.1.call-start = ((), (), s32[]{:S(2)}) async-start(), calls=%async_computation | async-start | bytes 2621440 | tf_op jit(solution)/shard_map/all_gather | solution.py:1476
  9.4 3.8 copy-start.9
  77.0 52.8 %copy-start.10 = (s32[1,1,2,128,1]{3,4,2,1,0:T(1,128)S(1)}, s32[1,1,2,128,1]{3,4,2,1,0:T(1,128)}, u32[]{:S(2)}) copy-start(s32[1,1,2,128,1]{3,4,2,1,0:T(1,128)} %param.12) | copy-start | bytes 3076
  77.0 53.0 %copy-start.3 = (bf16[1,1,2,128,1024]{4,3,2,1,0:T(8,128)(2,1)S(1)}, bf16[1,1,2,128,1024]{4,3,2,1,0:T(8,128)(2,1)}, u32[]{:S(2)}) copy-start(bf16[1,1,2,128,1024]{4,3,2,1,0:T(8,128)(2,1)} %param.19) | copy-start | bytes 1572868
  130.0 4.3 copy-start.8
  347.8 4.0 copy-start.2
  350.4 3.5 copy-start.5
  395.0 96.9 %slice-start = ((s8[6291456]{0:T(1024)(128)(4,1)}), s8[4194304]{0:T(1024)(128)(4,1)S(1)}, s32[]{:S(2)}) async-start(s8[6291456]{0:T(1024)(128)(4,1)} %bitcast.78), calls=%async_computation.1 | async-start | bytes 8388608
  395.0 96.9 %slice-start.1 = ((s8[6291456]{0:T(1024)(128)(4,1)}), s8[2097152]{0:T(1024)(128)(4,1)S(1)}, s32[]{:S(2)}) async-start(s8[6291456]{0:T(1024)(128)(4,1)} %bitcast.78), calls=%async_computation.2 | async-start | bytes 4194304
  491.9 3.6 copy-start.7
  491.9 4.7 copy-start.1
  491.9 4.7 copy-start.6
  498.6 2.4 copy-start.4
Sparse Core Ops, SparseCore 0:
  10.1 34.7 all-gather.1

commit v3 on v2

--- a/solution.py
+++ b/solution.py
@@ -466,6 +466,19 @@
     return c if half == 0 else 2 * count - 1 - c
 
 
+def relative(a, b):
+    return (a // 2 + b // 2) % 2 * 2 + (a + b) % 2
+
+
+def swap(value, axis, bit):
+    size = lax.axis_size(axis)
+    return lax.ppermute(value, axis, [(i, i ^ bit) for i in range(size)])
+
+
+def lasting(microseconds):
+    return pl.CostEstimate(flops=0, bytes_accessed=int(microseconds * 3.3e6), transcendentals=0)
+
+
 def params(side=True):
     return pltpu.CompilerParams(has_side_effects=side, vmem_limit_bytes=VMEM_CAP)
 
@@ -473,34 +486,24 @@
 def gather_stream(normed, starts, weight):
     count = lax.axis_size("ctx")
     depth = count // 2
-    rows, width = weight.shape
-    pieces = 4
-    piece = rows // pieces
-
-    def kernel(n_ref, s_ref, w_ref, tok, st, wall, rs_t, ss_p, ss_up, ss_dn, ss_sib, rs_s, ss_s, rs_wx, ss_wx, rs_ws, ss_ws, rs_wf, ss_wf, loc):
+    rows, wide = weight.shape
+    lanes = wide // 3 // count
+
+    def kernel(n_ref, s_ref, w_ref, tok, st, cols, rs_t, ss_p, ss_up, ss_dn, ss_sib, rs_s, ss_s, rs_w, ss_w):
         c, f, z, y, x, k = place()
         sib = (c, f + 1 - 2 * k)
-        xn = (c, (f + 2) % 4)
         partner = (c + 1 - 2 * y, f + 1 - 2 * k)
         up = (c + 2, f)
         down = (c - 2, f)
         holder = k == y
 
-        def wpart(ref, shard, i):
-            return ref.at[shard, pl.ds(i * piece, piece)]
-
-        for i in range(pieces):
-            remote(w_ref.at[pl.ds(i * piece, piece)], wpart(wall, f, i), ss_wx.at[i], rs_wx.at[i], xn).start()
-
         def send_in(h):
-            return remote(
-                n_ref.at[h], tok.at[block_at(c, h, count)], ss_p.at[h], rs_t.at[block_at(c, h, count)], partner
-            )
+            b = block_at(c, h, count)
+            return remote(n_ref.at[h], tok.at[b], ss_p.at[h], rs_t.at[b], partner)
 
         def local_in(h):
-            return pltpu.make_async_copy(
-                n_ref.at[h], tok.at[block_at(c, h, count)], rs_t.at[block_at(c, h, count)]
-            )
+            b = block_at(c, h, count)
+            return pltpu.make_async_copy(n_ref.at[h], tok.at[b], rs_t.at[b])
 
         @pl.when(holder)
         def _():
@@ -514,84 +517,72 @@
 
         for zt in range(depth):
             for kt in range(2):
-                dev = (2 * zt + k, 2 * x + kt)
-                slot = 2 * zt + kt
                 mine = holder & (z == zt) & (k == kt)
 
                 @pl.when(mine)
-                def _(dev=dev, slot=slot):
+                def _():
                     pltpu.make_async_copy(s_ref, st.at[c], rs_s.at[c]).start()
 
                 @pl.when(jnp.logical_not(mine))
-                def _(dev=dev, slot=slot):
-                    remote(s_ref, st.at[c], ss_s.at[slot], rs_s.at[c], dev).start()
-
-        remote(w_ref, wall.at[f], ss_ws, rs_ws, sib).start()
-        pltpu.make_async_copy(w_ref, wall.at[f], loc).start()
+                def _(zt=zt, kt=kt):
+                    remote(s_ref, st.at[c], ss_s.at[2 * zt + kt], rs_s.at[c], (2 * zt + k, 2 * x + kt)).start()
+
+        goals = [(2 * z + k, (c, (f + 2) % 4)), (2 * z + 1 - k, (c, (sib[1] + 2) % 4)), (2 * z + 1 - k, sib)]
+
+        def columns(pair, j):
+            return w_ref.at[:, pl.ds(pl.multiple_of(j * count * lanes + pair * lanes, lanes), lanes)]
+
+        def weight_place(shard, j):
+            return cols.at[j, pl.ds(pl.multiple_of(shard * rows, rows), rows)]
+
+        def weight_send(t, j):
+            pair, dev = goals[t]
+            return remote(columns(pair, j), weight_place(f, j), ss_w.at[t, j], rs_w.at[f, j], dev)
+
+        for j in range(3):
+            for t in range(3):
+                weight_send(t, j).start()
+            pltpu.make_async_copy(columns(2 * z + k, j), weight_place(f, j), rs_w.at[f, j]).start()
 
         def copy_block(zb, h, ss, dev):
             b = block_at(2 * zb + k, h, count)
             return remote(tok.at[b], tok.at[b], ss, rs_t.at[b], dev)
 
-        def wait_block(zb):
+        for j in range(depth):
             for h in range(2):
-                b = block_at(2 * zb + k, h, count)
-                remote(tok.at[b], tok.at[b], ss_p.at[h], rs_t.at[b], sib).wait_recv()
-
-        def send_up(j):
-            for h in range(2):
-                copy_block(z - j, h, ss_up.at[j, h], up).start()
-
-        def send_down(j):
-            for h in range(2):
-                copy_block(z + j, h, ss_dn.at[j, h], down).start()
-
-        def send_sib(zb):
-            for h in range(2):
-                copy_block(zb, h, ss_sib.at[zb, h], sib).start()
-
-        def w_forward(i):
-            shard = (f + 2) % 4
-            remote(wpart(wall, shard, i), wpart(wall, shard, i), ss_wx.at[i], rs_wx.at[i], xn).wait_recv()
-            remote(wpart(wall, shard, i), wpart(wall, shard, i), ss_wf.at[i], rs_wf.at[i], sib).start()
-
-        wait_block(z)
-
-        @pl.when(z < depth - 1)
-        def _():
-            send_up(0)
-
-        @pl.when(z > 0)
-        def _():
-            send_down(0)
-
-        send_sib(z)
-        for j in range(1, depth):
-            if j < pieces:
-                w_forward(j - 1)
-
-            @pl.when(z - j >= 0)
-            def _(j=j):
-                wait_block(z - j)
-
-                @pl.when(z < depth - 1)
-                def _():
-                    send_up(j)
-
-                send_sib(z - j)
-
-            @pl.when(z + j <= depth - 1)
-            def _(j=j):
-                wait_block(z + j)
-
-                @pl.when(z > 0)
-                def _():
-                    send_down(j)
-
-                send_sib(z + j)
-
-        for i in range(min(depth, pieces) - 1, pieces):
-            w_forward(i)
+                if j == 0:
+                    copy_block(z, h, ss_p.at[h], sib).wait_recv()
+
+                    @pl.when(z < depth - 1)
+                    def _(h=h):
+                        copy_block(z, h, ss_up.at[0, h], up).start()
+
+                    @pl.when(z > 0)
+                    def _(h=h):
+                        copy_block(z, h, ss_dn.at[0, h], down).start()
+
+                    copy_block(z, h, ss_sib.at[z, h], sib).start()
+                    continue
+
+                @pl.when(z - j >= 0)
+                def _(j=j, h=h):
+                    copy_block(z - j, h, ss_p.at[h], sib).wait_recv()
+
+                    @pl.when(z < depth - 1)
+                    def _():
+                        copy_block(z - j, h, ss_up.at[j, h], up).start()
+
+                    copy_block(z - j, h, ss_sib.at[z - j, h], sib).start()
+
+                @pl.when(z + j <= depth - 1)
+                def _(j=j, h=h):
+                    copy_block(z + j, h, ss_p.at[h], sib).wait_recv()
+
+                    @pl.when(z > 0)
+                    def _():
+                        copy_block(z + j, h, ss_dn.at[j, h], down).start()
+
+                    copy_block(z + j, h, ss_sib.at[z + j, h], sib).start()
 
         for zt in range(depth):
             for h in range(2):
@@ -600,13 +591,11 @@
                 copy_block(zt, h, ss_sib.at[zt, h], sib).wait_send()
         for ct in range(count):
             remote(s_ref, st.at[ct], ss_s.at[0], rs_s.at[ct], sib).wait_recv()
-        for i in range(pieces):
-            shard = sib[1] + 2 - 4 * (sib[1] // 2)
-            remote(wpart(wall, shard, i), wpart(wall, shard, i), ss_wf.at[i], rs_wf.at[i], sib).wait_recv()
-            remote(wpart(wall, shard, i), wpart(wall, shard, i), ss_wf.at[i], rs_wf.at[i], sib).wait_send()
-            remote(w_ref.at[pl.ds(i * piece, piece)], wpart(wall, f, i), ss_wx.at[i], rs_wx.at[i], xn).wait_send()
-        remote(w_ref, wall.at[sib[1]], ss_ws, rs_ws, sib).wait()
-        pltpu.make_async_copy(w_ref, wall.at[f], loc).wait()
+        for j in range(3):
+            for shard in range(4):
+                remote(columns(0, j), weight_place(shard, j), ss_w.at[0, j], rs_w.at[shard, j], sib).wait_recv()
+            for t in range(3):
+                weight_send(t, j).wait_send()
 
         @pl.when(jnp.logical_not(holder))
         def _():
@@ -636,141 +625,20 @@
     return pl.pallas_call(
         kernel,
         name="gather_stream",
+        cost_estimate=lasting(50),
         out_shape=(
             jax.ShapeDtypeStruct((2 * count,) + normed.shape[1:], normed.dtype),
             jax.ShapeDtypeStruct((count,) + starts.shape, starts.dtype),
-            jax.ShapeDtypeStruct((4, rows, width), weight.dtype),
+            jax.ShapeDtypeStruct((3, 4 * rows, lanes), weight.dtype),
         ),
         in_specs=[ANY] * 3,
         out_specs=(ANY,) * 3,
         scratch_shapes=[
             DMA((2 * count,)), DMA((2,)), DMA((depth, 2)), DMA((depth, 2)), DMA((depth, 2)),
-            DMA((count,)), DMA((count,)), DMA((pieces,)), DMA((pieces,)), DMA, DMA,
-            DMA((pieces,)), DMA((pieces,)), DMA,
+            DMA((count,)), DMA((count,)), DMA((4, 3)), DMA((3, 3)),
         ],
         compiler_params=params(),
     )(normed, starts, weight)
-
-
-def heads_to_tokens(arrays, name):
-    count = lax.axis_size("ctx")
-    number = len(arrays)
-    lanes = arrays[0].shape[2]
-    width = count * lanes
-
-    def kernel(*refs):
-        ins, (out, ss, rs) = refs[:number], refs[number:]
-        c, f, z, y, x, k = place()
-        pair = 2 * z + k
-        target = 2 * x + y
-
-        def there(half, a):
-            return out.at[half, :, pl.ds(pl.multiple_of(a * width + pair * lanes, lanes), lanes)]
-
-        def send(i, half, a):
-            ct = (c + i) % count
-            return remote(
-                ins[a].at[block_at(ct, half, count)], there(half, a), ss.at[i, half, a], rs.at[pair, half, a], (ct, target)
-            )
-
-        def own(half, a):
-            return pltpu.make_async_copy(ins[a].at[block_at(c, half, count)], there(half, a), rs.at[pair, half, a])
-
-        pieces = [(half, a) for a in range(number) for half in range(2)]
-        for i in [*range(1, count), 0]:
-            if i:
-                for half, a in pieces:
-                    send(i, half, a).start()
-            else:
-
-                @pl.when(k == y)
-                def _():
-                    for half, a in pieces:
-                        own(half, a).start()
-
-                @pl.when(k != y)
-                def _():
-                    for half, a in pieces:
-                        send(0, half, a).start()
-
-        for half, a in pieces:
-            for other in range(count):
-                cols = pl.ds(a * width + other * lanes, lanes)
-                remote(ins[a].at[0], out.at[half, :, cols], ss.at[0, half, a], rs.at[other, half, a], (c, f + 1 - 2 * k)).wait_recv()
-        for i in range(1, count):
-            for half, a in pieces:
-                send(i, half, a).wait_send()
-
-        @pl.when(k != y)
-        def _():
-            for half, a in pieces:
-                send(0, half, a).wait_send()
-
-    return pl.pallas_call(
-        kernel,
-        name=name,
-        out_shape=jax.ShapeDtypeStruct((2, arrays[0].shape[1], number * width), arrays[0].dtype),
-        in_specs=[ANY] * number,
-        out_specs=ANY,
-        scratch_shapes=[DMA((count, 2, number)), DMA((count, 2, number))],
-        compiler_params=params(),
-    )(*arrays)
-
-
-def tokens_to_heads(array, name):
-    count = lax.axis_size("ctx")
-    lanes = array.shape[2] // count
-
-    def kernel(a_ref, out, ss, rs):
-        c, f, z, y, x, k = place()
-
-        def part(half, pair):
-            return a_ref.at[half, :, pl.ds(pl.multiple_of(pair * lanes, lanes), lanes)]
-
-        def peer(i):
-            pair = (2 * z + k + i) % count
-            return pair, (2 * (pair // 2) + k, 2 * x + pair % 2)
-
-        def send(i, half):
-            pair, dev = peer(i)
-            b = block_at(c, half, count)
-            return remote(part(half, pair), out.at[b], ss.at[i, half], rs.at[b], dev)
-
-        for i in range(1, count):
-            for half in range(2):
-                send(i, half).start()
-
-        @pl.when(k == y)
-        def _():
-            for half in range(2):
-                b = block_at(c, half, count)
-                pltpu.make_async_copy(part(half, 2 * z + k), out.at[b], rs.at[b]).start()
-
-        @pl.when(k != y)
-        def _():
-            for half in range(2):
-                send(0, half).start()
-
-        for b in range(2 * count):
-            remote(part(0, 0), out.at[b], ss.at[0, 0], rs.at[b], (c, f + 1 - 2 * k)).wait_recv()
-        for i in range(1, count):
-            for half in range(2):
-                send(i, half).wait_send()
-
-        @pl.when(k != y)
-        def _():
-            for half in range(2):
-                send(0, half).wait_send()
-
-    return pl.pallas_call(
-        kernel,
-        name=name,
-        out_shape=jax.ShapeDtypeStruct((2 * count, array.shape[1], lanes), array.dtype),
-        in_specs=[ANY],
-        out_specs=ANY,
-        scratch_shapes=[DMA((count, 2)), DMA((2 * count,))],
-        compiler_params=params(),
-    )(array)
 
 
 TILE = 256
@@ -783,19 +651,17 @@
     return [jnp.where(at < size, value, zero), jnp.where(at >= size, value, zero)]
 
 
-def attend_forward(stream, projection, start_row, numbers, scale):
+def attend_forward(stream, columns, start_row, numbers, scale):
     length, width = stream.shape
     tiles = length // TILE
     lanes = 128
     size = lanes // 2
 
-    def kernel(first, x_ref, wq_ref, wk_ref, wv_ref, s_ref, q_out, k_out, v_out, m16, m32, lse, v_turned):
+    def kernel(first, x_ref, w_ref, s_ref, q_out, k_out, v_out, m16, m32, lse, v_turned):
         i = pl.program_id(0)
         own = pl.ds(pl.multiple_of(i * TILE, TILE), TILE)
         rows = x_ref[...]
-        query = jnp.dot(rows, wq_ref[...], preferred_element_type=F32).astype(BF)
-        key = jnp.dot(rows, wk_ref[...], preferred_element_type=F32).astype(BF)
-        value = jnp.dot(rows, wv_ref[...], preferred_element_type=F32).astype(BF)
+        query, key, value = [jnp.dot(rows, w_ref[j], preferred_element_type=F32).astype(BF) for j in range(3)]
         q_out[...] = query
         k_out[own, :] = key
         v_out[...] = value
@@ -833,20 +699,18 @@
         m16[...] = mixed.T.astype(BF)
         lse[...] = jnp.concatenate([top + jnp.log(total) for top, total, _ in done], axis=0)
 
-    groups = width // lanes
     tile = pl.BlockSpec((TILE, lanes), lambda i, n: (i, 0))
     turned = pl.BlockSpec((lanes, TILE), lambda i, n: (0, i))
     return pl.pallas_call(
         kernel,
         name="attend_forward",
+        cost_estimate=lasting(22),
         grid_spec=pltpu.PrefetchScalarGridSpec(
             num_scalar_prefetch=1,
             grid=(tiles,),
             in_specs=[
                 pl.BlockSpec((TILE, width), lambda i, n: (i, 0)),
-                pl.BlockSpec((width, lanes), lambda i, n: (0, n[tiles])),
-                pl.BlockSpec((width, lanes), lambda i, n: (0, groups + n[tiles])),
-                pl.BlockSpec((width, lanes), lambda i, n: (0, 2 * groups + n[tiles])),
+                pl.BlockSpec((3, width, lanes), lambda i, n: (0, 0, 0)),
                 pl.BlockSpec((1, TILE), lambda i, n: (0, i)),
             ],
             out_specs=[
@@ -868,7 +732,7 @@
             jax.ShapeDtypeStruct((2, length), F32),
         ),
         compiler_params=params(False),
-    )(numbers, stream, projection, projection, projection, start_row)
+    )(numbers, stream, columns, start_row)
 
 
 def attend_backward(query, key, value, grad, mixed, logs, start_row, numbers, scale):
@@ -933,6 +797,7 @@
     return pl.pallas_call(
         kernel,
         name="attend_backward",
+        cost_estimate=lasting(19),
         grid_spec=pltpu.PrefetchScalarGridSpec(
             num_scalar_prefetch=1,
             grid=(tiles,),
@@ -957,217 +822,417 @@
     )(numbers, query, key, value, grad, mixed, logs, start_row)
 
 
-def dispatch_rows(arrays):
+def statistics(value):
+    row_mean = jnp.mean(value, axis=1, keepdims=True)
+    centred = value - row_mean
+    inverse = lax.rsqrt(jnp.mean(centred * centred, axis=1, keepdims=True) + EPS)
+    return centred * inverse, inverse
+
+
+def route_rows(by_head, out_proj, tokens, dispatch, gain):
     count = lax.axis_size("ctx")
-    number = len(arrays)
-    _, own_experts, cap, width = arrays[0].shape
-
-    def kernel(*refs):
-        ins, outs = refs[:number], refs[number : 2 * number]
-        ss1, rs1, ssx, rsx, sss, rss, ssf, rsf = refs[2 * number :]
+    early = count // 2
+    lanes = by_head.shape[2]
+    half_rows = by_head.shape[1]
+    rows, width = tokens.shape
+    experts = EXPERTS // count
+
+    def kernel(
+        a_ref, w_ref, x_ref, d_ref, g_ref, mixed, middle, out, routed, slots, mirror,
+        ss, rs, ss1, rs1, ssm, rsm, ss2, rs2, sse, ssx, sss, rss, ssf, rsf,
+    ):
         c, f, z, y, x, k = place()
         sib = (c, f + 1 - 2 * k)
         xn = (c, (f + 2) % 4)
-
-        def here(a, stream, source):
-            return outs[a].at[:, stream, source]
-
-        def first(a, i):
+        pair = 2 * z + k
+        target = 2 * x + y
+
+        def there(half):
+            column = (2 * relative(z, target) + k) * lanes
+            return mixed.at[half, :, pl.ds(pl.multiple_of(column, lanes), lanes)]
+
+        def send(i, half):
             ct = (c + i) % count
-            return remote(ins[a].at[ct], here(a, f, c), ss1.at[a, i], rs1.at[a, c], (ct, f))
-
-        for a in range(number):
-            pltpu.make_async_copy(ins[a].at[c], here(a, f, c), rs1.at[a, c]).start()
+            return remote(a_ref.at[block_at(ct, half, count)], there(half), ss.at[i, half], rs.at[pair, half], (ct, target))
+
+        def keep(half):
+            return pltpu.make_async_copy(a_ref.at[block_at(c, half, count)], there(half), rs.at[pair, half])
+
+        for half in range(2):
             for i in range(1, count):
-                first(a, i).start()
-
-        def hop(a, stream, source, ss, rs, dev):
-            return remote(here(a, stream, source), here(a, stream, source), ss.at[a, source], rs.at[a, source], dev)
-
-        other = (f + 2) % 4
-        for a in range(number):
-            for i in range(count):
-                cs = (c + i) % count
-                remote(here(a, f, cs), here(a, f, cs), ss1.at[a, 0], rs1.at[a, cs], sib).wait_recv()
-                hop(a, f, cs, ssx, rsx, xn).start()
-                hop(a, f, cs, sss, rss, sib).start()
-        for a in range(number):
-            for i in range(count):
-                cs = (c + i) % count
-                hop(a, other, cs, ssx, rsx, xn).wait_recv()
-                hop(a, other, cs, ssf, rsf, sib).start()
-        for a in range(number):
-            for i in range(count):
-                if i:
-                    first(a, i).wait_send()
-                cs = (c + i) % count
-                hop(a, f, cs, ssx, rsx, xn).wait_send()
-                hop(a, sib[1], cs, sss, rss, sib).wait()
-                hop(a, (sib[1] + 2) % 4, cs, ssf, rsf, sib).wait()
-
+                send(i, half).start()
+
+            @pl.when(k == y)
+            def _(half=half):
+                keep(half).start()
+
+            @pl.when(k != y)
+            def _(half=half):
+                send(0, half).start()
+
+        for half in range(2):
+            for other in range(count):
+                column = (2 * relative(other // 2, f) + other % 2) * lanes
+                cols = pl.ds(pl.multiple_of(column, lanes), lanes)
+                remote(a_ref.at[0], mixed.at[half, :, cols], ss.at[0, half], rs.at[other, half], sib).wait_recv()
+            here = pl.ds(half * half_rows, half_rows)
+            value = x_ref[here, :].astype(F32) + jnp.dot(mixed[half], w_ref[...], preferred_element_type=F32)
+            middle[here, :] = value
+            hat, _ = statistics(value)
+            routed[here, :] = (hat * g_ref[...]).astype(BF)
+        slots[...] = jnp.dot(d_ref[...], routed[...], preferred_element_type=F32).astype(BF).reshape(slots.shape)
+
+        def owner(i):
+            return (c + i) % count
+
+        def straight(i):
+            return remote(slots.at[owner(i)], out.at[0, c], ss1.at[i], rs1.at[c], (owner(i), f))
+
+        def over(i):
+            return remote(slots.at[owner(i)], mirror.at[i], ssm.at[i], rsm.at[i], xn)
+
+        def onward(i):
+            return remote(mirror.at[i], out.at[2, c], sse.at[i], rs2.at[c], (owner(i), f))
+
+        own = pltpu.make_async_copy(slots.at[c], out.at[0, c], rs1.at[c])
+        beside = remote(slots.at[c], out.at[2, c], ss2, rs2.at[c], xn)
+        beside.start()
+        for i in range(1, early):
+            over(i).start()
+        own.start()
+        for i in [*range(early, count), *range(1, early)]:
+            straight(i).start()
+
+        def hop(source, send_sem, recv_sem, first, dst, dev):
+            return remote(out.at[first, source], out.at[dst, source], send_sem.at[source], recv_sem.at[source], dev)
+
+        def across(source):
+            return hop(source, ssx, rs2, 0, 2, xn)
+
+        def share(source):
+            return hop(source, sss, rss, 0, 1, sib)
+
+        def share_other(source):
+            return hop(source, ssf, rsf, 2, 3, sib)
+
+        def arrived(rel, source, recv_sem):
+            remote(out.at[rel, source], out.at[rel, source], ss2, recv_sem.at[source], sib).wait_recv()
+
+        def source_of(i):
+            return (c + count - i) % count
+
+        arrived(0, c, rs1)
+        share(c).start()
+        for i in range(early, count):
+            arrived(0, source_of(i), rs1)
+            across(source_of(i)).start()
+            share(source_of(i)).start()
+            j = i - early + 1
+            if j < early:
+                over(j).wait_recv()
+                onward(j).start()
+        for i in range(1, early):
+            arrived(0, source_of(i), rs1)
+            share(source_of(i)).start()
+        for i in range(count):
+            arrived(2, source_of(i), rs2)
+            share_other(source_of(i)).start()
+        for i in range(count):
+            cs = source_of(i)
+            share(cs).wait_send()
+            share_other(cs).wait_send()
+            arrived(1, cs, rss)
+            arrived(3, cs, rsf)
+            if i:
+                straight(i).wait_send()
+            if 1 <= i < early:
+                over(i).wait_send()
+                onward(i).wait_send()
+            if i >= early:
+                across(cs).wait_send()
+        beside.wait_send()
+        for i in range(1, count):
+            for half in range(2):
+                send(i, half).wait_send()
+
+        @pl.when(k != y)
+        def _():
+            for half in range(2):
+                send(0, half).wait_send()
+
+    vmem = pl.BlockSpec(memory_space=pltpu.VMEM)
+    block = (experts, CAP, width)
     return pl.pallas_call(
         kernel,
-        name="dispatch_rows",
-        out_shape=(jax.ShapeDtypeStruct((own_experts, 4, count, cap, width), arrays[0].dtype),) * number,
-        in_specs=[ANY] * number,
-        out_specs=(ANY,) * number,
-        scratch_shapes=[DMA((number, count))] * 8,
+        name="route_rows",
+        cost_estimate=lasting(50),
+        out_shape=(
+            jax.ShapeDtypeStruct((2, half_rows, width), BF),
+            jax.ShapeDtypeStruct((rows, width), F32),
+            jax.ShapeDtypeStruct((4, count) + block, BF),
+        ),
+        in_specs=[ANY] + [vmem] * 4,
+        out_specs=(vmem, vmem, ANY),
+        scratch_shapes=[
+            pltpu.VMEM((rows, width), BF),
+            pltpu.VMEM((count,) + block, BF),
+            pltpu.VMEM((early,) + block, BF),
+            DMA((count, 2)), DMA((count, 2)),
+            DMA((count,)), DMA((count,)), DMA((early,)), DMA((early,)), DMA, DMA((count,)), DMA((early,)),
+            DMA((count,)), DMA((count,)), DMA((count,)), DMA((count,)), DMA((count,)),
+        ],
         compiler_params=params(),
-    )(*arrays)
-
-
-def return_rows(arrays):
+    )(by_head, out_proj, tokens, dispatch, gain)
+
+
+def return_grads(own, near, far, ready, dispatch, cotangent, middle, mixed, out_proj, gain):
     count = lax.axis_size("ctx")
-    number = len(arrays)
-    _, experts, _, cap, width = arrays[0].shape
-    groups = 2
-    chunk = experts // groups
-
-    def kernel(*refs):
-        ins, outs = refs[:number], refs[number : 2 * number]
-        near, far, got_near, got_far, got_x = refs[2 * number : 2 * number + 5]
-        ssn, rsn, ssf, rsf, ssx, rsx, sso, rso, loc = refs[2 * number + 5 :]
+    lanes = width_of_pair = out_proj.shape[1] // count
+    rows, width = middle.shape
+    half_rows = rows // 2
+    quarter = width // 4
+
+    def kernel(
+        o_ref, n_ref, f_ref, z_ref, d_ref, c_ref, m_ref, a_ref, w_ref, g_ref, heads, grad_middle, gain_out, shard,
+        own_v, near_v, total, got, back, parts, got_near, far_v, got_far,
+        loc, ss, rs, ss_h, rs_h, ss_n, rs_n, ss_f, rs_f,
+    ):
         c, f, z, y, x, k = place()
         sib = (c, f + 1 - 2 * k)
-        other = (f + 2) % 4
-        xn = (c, other)
-        sib_other = (sib[1] + 2) % 4
-
-        def to_near(a):
-            return remote(ins[a].at[sib[1]], got_near.at[a], ssn.at[a], rsn.at[a], sib)
-
-        def to_far(a):
-            return remote(ins[a].at[sib_other], got_far.at[a], ssf.at[a], rsf.at[a], sib)
-
-        def load(a, stream, buf, i):
-            return pltpu.make_async_copy(ins[a].at[stream], buf.at[a], loc.at[a, i])
-
-        for a in range(number):
-            to_far(a).start()
-            load(a, other, far, 0).start()
-        for a in range(number):
-            to_near(a).start()
-            load(a, f, near, 1).start()
-
-        def across(a, e):
-            return remote(far.at[a, e], got_x.at[a, e], ssx.at[a, e], rsx.at[a, e], xn)
-
-        for a in range(number):
-            load(a, other, far, 0).wait()
-            to_far(a).wait_recv()
-            for e in range(experts):
-                far[a, e] = (far[a, e].astype(F32) + got_far[a, e].astype(F32)).astype(BF)
-                across(a, e).start()
-
-        def home(a, g, i):
+        xn = (c, (f + 2) % 4)
+        loads = [
+            pltpu.make_async_copy(o_ref.at[0], own_v, loc.at[0]),
+            pltpu.make_async_copy(n_ref.at[0], near_v, loc.at[1]),
+        ]
+        for load in loads:
+            load.start()
+        for load in loads:
+            load.wait()
+
+        def home(i):
             ct = (c + i) % count
-            return remote(
-                near.at[a, pl.ds(g * chunk, chunk), ct],
-                outs[a].at[c, pl.ds(g * chunk, chunk)],
-                sso.at[a, g, i],
-                rso.at[a, g, c],
-                (ct, f),
-            )
-
-        def stay(a, g):
-            return pltpu.make_async_copy(
-                near.at[a, pl.ds(g * chunk, chunk), c], outs[a].at[c, pl.ds(g * chunk, chunk)], rso.at[a, g, c]
-            )
-
-        for a in range(number):
-            load(a, f, near, 1).wait()
-            to_near(a).wait_recv()
-            for g in range(groups):
-                for e in range(g * chunk, (g + 1) * chunk):
-                    across(a, e).wait_recv()
-                    near[a, e] = (
-                        near[a, e].astype(F32) + got_near[a, e].astype(F32) + got_x[a, e].astype(F32)
-                    ).astype(BF)
-                for i in range(1, count):
-                    home(a, g, i).start()
-                stay(a, g).start()
-        for a in range(number):
-            to_far(a).wait_send()
-            to_near(a).wait_send()
-            for e in range(experts):
-                across(a, e).wait_send()
-            for g in range(groups):
-                for i in range(count):
-                    cs = (c + i) % count
-                    remote(
-                        near.at[a, pl.ds(g * chunk, chunk), cs],
-                        outs[a].at[cs, pl.ds(g * chunk, chunk)],
-                        sso.at[a, g, i],
-                        rso.at[a, g, cs],
-                        sib,
-                    ).wait_recv()
-                    if i:
-                        home(a, g, i).wait_send()
-
-    buffer = pltpu.VMEM((number, experts, count, cap, width), BF)
+            return remote(total.at[ct], got.at[c], ss.at[i], rs.at[c], (ct, f))
+
+        zero = z_ref[0:1, 0:1]
+        for i in [*range(1, count), 0]:
+            ct = (c + i) % count
+            value = own_v[ct].astype(F32) + near_v[ct].astype(F32) + f_ref[ct].astype(F32) + zero
+            if i:
+                total[ct] = value.astype(BF)
+                home(i).start()
+            else:
+                got[c] = value.astype(BF)
+        hat, inverse = statistics(m_ref[...])
+        for i in range(1, count):
+            cs = (c + i) % count
+            remote(total.at[cs], got.at[cs], ss.at[i], rs.at[cs], sib).wait_recv()
+        routed = lax.dot_general(
+            d_ref[...], got[...].reshape(-1, width), (((0,), (0,)), ((), ())), preferred_element_type=F32
+        )
+        scaled = routed * g_ref[...]
+        mean_grad = jnp.mean(scaled, axis=1, keepdims=True)
+        mean_proj = jnp.mean(scaled * hat, axis=1, keepdims=True)
+        gain_out[...] = jnp.sum(routed * hat, axis=0, keepdims=True)
+        grad = c_ref[...].astype(F32) + inverse * (scaled - mean_grad - hat * mean_proj)
+        grad_middle[...] = grad
+        low = grad.astype(BF)
+        back[...] = (
+            lax.dot_general(low, w_ref[...], (((1,), (1,)), ((), ())), preferred_element_type=F32)
+            .astype(BF)
+            .reshape(back.shape)
+        )
+
+        def part(half, pair):
+            column = (2 * relative(pair // 2, f) + pair % 2) * lanes
+            return back.at[half, :, pl.ds(pl.multiple_of(column, lanes), lanes)]
+
+        def send(i, half):
+            pair = (2 * z + k + i) % count
+            b = block_at(c, half, count)
+            dev = (2 * (pair // 2) + k, 2 * x + pair % 2)
+            return remote(part(half, pair), heads.at[b], ss_h.at[i, half], rs_h.at[b], dev)
+
+        for i in range(1, count):
+            for half in range(2):
+                send(i, half).start()
+
+        @pl.when(k == y)
+        def _():
+            for half in range(2):
+                b = block_at(c, half, count)
+                pltpu.make_async_copy(part(half, 2 * z + k), heads.at[b], rs_h.at[b]).start()
+
+        @pl.when(k != y)
+        def _():
+            for half in range(2):
+                send(0, half).start()
+
+        def term(j):
+            return lax.dot_general(
+                a_ref[:, j * quarter : (j + 1) * quarter], low, (((0,), (0,)), ((), ())), preferred_element_type=F32
+            ).astype(BF)
+
+        def core_send(j):
+            return remote(parts.at[2 * j + 1], got_near.at[j], ss_n.at[j], rs_n.at[j], sib)
+
+        across = remote(far_v, got_far, ss_f, rs_f, xn)
+        for j in (1, 0):
+            parts[2 * j + 1] = term(2 * j + 1)
+            core_send(j).start()
+        parts[2] = term(2)
+        core_send(1).wait_recv()
+        far_v[...] = (parts[2].astype(F32) + got_near[1].astype(F32)).astype(BF)
+        across.start()
+        parts[0] = term(0)
+        core_send(0).wait_recv()
+        across.wait_recv()
+        shard[...] = (parts[0].astype(F32) + got_near[0].astype(F32) + got_far[...].astype(F32)).astype(BF)
+
+        for b in range(2 * count):
+            remote(part(0, 0), heads.at[b], ss_h.at[0, 0], rs_h.at[b], sib).wait_recv()
+        for i in range(1, count):
+            home(i).wait_send()
+            for half in range(2):
+                send(i, half).wait_send()
+
+        @pl.when(k != y)
+        def _():
+            for half in range(2):
+                send(0, half).wait_send()
+
+        core_send(0).wait_send()
+        core_send(1).wait_send()
+        across.wait_send()
+
+    vmem = pl.BlockSpec(memory_space=pltpu.VMEM)
+    slots = pltpu.VMEM(far.shape, BF)
+    shard_shape = pltpu.VMEM((quarter, width), BF)
     return pl.pallas_call(
         kernel,
-        name="return_rows",
-        out_shape=(jax.ShapeDtypeStruct((count, experts, cap, width), BF),) * number,
-        in_specs=[ANY] * number,
-        out_specs=(ANY,) * number,
-        scratch_shapes=[buffer] * 5
-        + [DMA((number,))] * 4
-        + [DMA((number, experts))] * 2
-        + [DMA((number, groups, count))] * 2
-        + [DMA((number, 2))],
+        name="return_grads",
+        cost_estimate=lasting(35),
+        out_shape=(
+            jax.ShapeDtypeStruct((2 * count, half_rows, width_of_pair), BF),
+            jax.ShapeDtypeStruct((rows, width), F32),
+            jax.ShapeDtypeStruct((1, width), F32),
+            jax.ShapeDtypeStruct((quarter, width), BF),
+        ),
+        in_specs=[ANY, ANY] + [vmem] * 8,
+        out_specs=(ANY, vmem, vmem, vmem),
+        scratch_shapes=[
+            slots, slots, slots, slots,
+            pltpu.VMEM((2, half_rows, width), BF),
+            pltpu.VMEM((4, quarter, width), BF),
+            pltpu.VMEM((2, quarter, width), BF),
+            shard_shape, shard_shape,
+            DMA((2,)), DMA((count,)), DMA((count,)), DMA((count, 2)), DMA((2 * count,)), DMA((2,)), DMA((2,)), DMA, DMA,
+        ],
         compiler_params=params(),
-    )(*arrays)
+    )(own, near, far, ready, dispatch, cotangent, middle, mixed, out_proj, gain)
 
 
 ROOT = math.sqrt(2.0 / math.pi)
 CUBIC = 0.044715
 
 
-def experts_step(rows, grads, first_proj, second_proj):
-    number, count, width = rows.shape
+def stacked(ref):
+    return ref[...].reshape(-1, ref.shape[-1])
+
+
+def experts_rows(rows, near, far, beside, first_proj, second_proj):
+    _, count, number, cap, width = rows.shape
     units = first_proj.shape[2]
-    quarter = count // 4
-
-    def kernel(r_ref, g_ref, a_ref, b_ref, out, back, da, db):
-        row, grad = r_ref[0], g_ref[0]
-        first = a_ref[0].astype(BF)
-        second = b_ref[0].astype(BF)
+    total = 4 * count * cap
+
+    def kernel(r_ref, n_ref, f_ref, b_ref, w1, w2, back, back_odd, out, out_odd, active_out, hidden_out, grad_out):
+        row = stacked(r_ref)
+        grad = jnp.concatenate(
+            [stacked(n_ref), b_ref[0].reshape(-1, width), stacked(f_ref), b_ref[1].reshape(-1, width)], axis=0
+        )
+        grad_out[0] = grad
+        first = w1[0].astype(BF)
+        second = w2[0].astype(BF)
         hidden = jnp.dot(row, first, preferred_element_type=F32)
         upstream = lax.dot_general(grad, second, (((1,), (1,)), ((), ())), preferred_element_type=F32)
         bent = jnp.tanh(ROOT * (hidden + CUBIC * hidden * hidden * hidden))
         active = (0.5 * hidden * (1.0 + bent)).astype(BF)
         slope = 0.5 * (1.0 + bent) + 0.5 * hidden * (1.0 - bent * bent) * (ROOT * (1.0 + 3.0 * CUBIC * hidden * hidden))
         grad_hidden = (upstream * slope).astype(BF)
-        term = lax.dot_general(grad_hidden, first, (((1,), (1,)), ((), ())), preferred_element_type=F32).astype(BF)
-        mixed = jnp.dot(active, second, preferred_element_type=F32).astype(BF)
-        for s in range(4):
-            back[s, 0] = term[s * quarter : (s + 1) * quarter]
-            out[s, 0] = mixed[s * quarter : (s + 1) * quarter]
-        da[0] = lax.dot_general(row, grad_hidden, (((0,), (0,)), ((), ())), preferred_element_type=F32)
-        db[0] = lax.dot_general(active, grad, (((0,), (0,)), ((), ())), preferred_element_type=F32)
-
-    whole = pl.BlockSpec((1, count, width), lambda e: (e, 0, 0))
+        active_out[0] = active
+        hidden_out[0] = grad_hidden
+        term = lax.dot_general(grad_hidden, first, (((1,), (1,)), ((), ())), preferred_element_type=F32)
+        result = jnp.dot(active, second, preferred_element_type=F32)
+        for j in range(4):
+            here = slice(j * total // 4, (j + 1) * total // 4)
+            (back_odd if j % 2 else back)[j // 2] = term[here].astype(BF).reshape(back.shape[1:])
+            (out_odd if j % 2 else out)[j // 2] = result[here].astype(BF).reshape(out.shape[1:])
+
+    parts = pl.BlockSpec((4, count, 1, cap, width), lambda e: (0, 0, e, 0, 0))
+    quarter = pl.BlockSpec((count, 1, cap, width), lambda e: (0, e, 0, 0))
+    pair = pl.BlockSpec((2, count, 1, cap, width), lambda e: (0, 0, e, 0, 0))
     left = pl.BlockSpec((1, width, units), lambda e: (e, 0, 0))
     right = pl.BlockSpec((1, units, width), lambda e: (e, 0, 0))
-    parts = pl.BlockSpec((4, 1, quarter, width), lambda e: (0, e, 0, 0))
+    wide = pl.BlockSpec((1, total, units), lambda e: (e, 0, 0))
+    flat = pl.BlockSpec((1, total, width), lambda e: (e, 0, 0))
     return pl.pallas_call(
         kernel,
-        name="experts_step",
+        name="experts_rows",
         grid=(number,),
-        in_specs=[whole, whole, left, right],
-        out_specs=[parts, parts, left, right],
+        in_specs=[parts, quarter, quarter, pair, left, right],
+        out_specs=[pair] * 4 + [wide, wide, flat],
         out_shape=(
-            jax.ShapeDtypeStruct((4, number, quarter, width), BF),
-            jax.ShapeDtypeStruct((4, number, quarter, width), BF),
-            jax.ShapeDtypeStruct(first_proj.shape, F32),
-            jax.ShapeDtypeStruct(second_proj.shape, F32),
+            *[jax.ShapeDtypeStruct((2,) + rows.shape[1:], BF)] * 4,
+            jax.ShapeDtypeStruct((number, total, units), BF),
+            jax.ShapeDtypeStruct((number, total, units), BF),
+            jax.ShapeDtypeStruct((number, total, width), BF),
+        ),
+        cost_estimate=pl.CostEstimate(
+            flops=8 * number * total * units * width, bytes_accessed=8 * number * units * width, transcendentals=0
         ),
         compiler_params=params(False),
-    )(rows, grads, first_proj, second_proj)
-
-
-def finish_exchange(arrays, parts, out_parts, gain_part):
+    )(rows, near, far, beside, first_proj, second_proj)
+
+
+def experts_weights(rows, grads, active, grad_hidden):
+    _, count, number, cap, width = rows.shape
+    total, units = active.shape[1:]
+
+    def kernel(r_ref, g_ref, a_ref, h_ref, da, db, done):
+        done[...] = jnp.zeros_like(done)
+        turn = (((0,), (0,)), ((), ()))
+        da[0] = lax.dot_general(stacked(r_ref), h_ref[0], turn, preferred_element_type=F32)
+        db[0] = lax.dot_general(a_ref[0], g_ref[0], turn, preferred_element_type=F32)
+
+    parts = pl.BlockSpec((4, count, 1, cap, width), lambda e: (0, 0, e, 0, 0))
+    wide = pl.BlockSpec((1, total, units), lambda e: (e, 0, 0))
+    flat = pl.BlockSpec((1, total, width), lambda e: (e, 0, 0))
+    return pl.pallas_call(
+        kernel,
+        name="experts_weights",
+        grid=(number,),
+        in_specs=[parts, flat, wide, wide],
+        out_specs=[
+            pl.BlockSpec((1, width, units), lambda e: (e, 0, 0)),
+            pl.BlockSpec((1, units, width), lambda e: (e, 0, 0)),
+            pl.BlockSpec((8, 128), lambda e: (0, 0)),
+        ],
+        out_shape=(
+            jax.ShapeDtypeStruct((number, width, units), F32),
+            jax.ShapeDtypeStruct((number, units, width), F32),
+            jax.ShapeDtypeStruct((8, 128), F32),
+        ),
+        cost_estimate=pl.CostEstimate(
+            flops=4 * number * total * units * width, bytes_accessed=12 * number * units * width, transcendentals=0
+        ),
+        compiler_params=params(False),
+    )(rows, grads, active, grad_hidden)
+
+
+def after(value, *others):
+    return lax.optimization_barrier((value,) + others)[0]
+
+
+def finish_exchange(arrays, parts, out_slab, gain_part, weight):
     count = lax.axis_size("ctx")
     depth = count // 2
     number = len(arrays)
@@ -1175,18 +1240,20 @@
     width = count * lanes
     _, rows, wide = parts.shape
     slab = rows // count
+    pieces_w = 4
+    piece_w = rows // pieces_w
 
     def kernel(*refs):
-        ins, (p_ref, o_ref, g_ref), (tok_out, w_out, o_out, g_out) = (
+        ins, (p_ref, o_ref, g_ref, w_ref), (tok_out, w_out, o_out, g_out, w_all) = (
             refs[:number],
-            refs[number : number + 3],
-            refs[number + 3 : number + 7],
+            refs[number : number + 4],
+            refs[number + 4 : number + 9],
         )
         (
-            got, held, got_a, far, got_x, mine, got_c, slab_out, got_g, sum_g, got_gc,
+            got, held, got_g, sum_g, got_gc,
             ss, rs, ss_r, rs_r, ss_up, ss_dn, rs_z, ss_a, ss_b, rs_o,
-            ss_oa, rs_oa, ss_ox, rs_ox, ss_oc, rs_oc, ss_of, rs_of, ss_g, rs_g, ss_gc, rs_gc,
-        ) = refs[number + 7 :]
+            ss_of, rs_of, ss_g, rs_g, ss_gc, rs_gc, ss_wx, rs_wx, ss_ws, rs_ws, ss_wf, rs_wf, loc,
+        ) = refs[number + 9 :]
         c, f, z, y, x, k = place()
         pair = 2 * z + k
         target = 2 * x + y
@@ -1195,17 +1262,28 @@
         up = (c + 2, f)
         down = (c - 2, f)
 
-        def core_send(j):
-            shard = 2 * (1 - x) + 1 - k if j == 0 else 2 * x + 1 - k
-            return remote(o_ref.at[shard], got_a.at[j], ss_oa.at[j], rs_oa.at[j], sib)
-
         def gain_send(j):
             return remote(sum_g.at[j], got_g.at[j], ss_g.at[j], rs_g.at[j], sib if j == 0 else xn)
 
-        core_send(0).start()
-        core_send(1).start()
         sum_g[0] = g_ref[...]
         gain_send(0).start()
+
+        def slab_spread(i):
+            return remote(o_ref, o_out.at[c], ss_of.at[i], rs_of.at[c], ((c + i) % count, f))
+
+        slab_own = pltpu.make_async_copy(o_ref, o_out.at[c], rs_of.at[c])
+
+        def weight_part(shard, i):
+            return w_all.at[shard, pl.ds(i * piece_w, piece_w)]
+
+        def weight_across(i):
+            return remote(w_ref.at[pl.ds(i * piece_w, piece_w)], weight_part(f, i), ss_wx.at[i], rs_wx.at[i], xn)
+
+        def weight_on(i, shard):
+            return remote(weight_part(shard, i), weight_part(shard, i), ss_wf.at[i], rs_wf.at[i], sib)
+
+        weight_share = remote(w_ref, w_all.at[f], ss_ws, rs_ws, sib)
+        weight_own = pltpu.make_async_copy(w_ref, w_all.at[f], loc)
 
         peers = [
             (2 * z + 1 - y, f, 2 * x + 1 - y),
@@ -1247,10 +1325,11 @@
             for half, a in pieces:
                 send(0, half, a).start()
 
-        across = remote(far, got_x, ss_ox, rs_ox, xn)
-        core_send(0).wait_recv()
-        far[...] = (o_ref[2 * (1 - x) + k].astype(F32) + got_a[0].astype(F32)).astype(BF)
-        across.start()
+        for i in range(pieces_w):
+            weight_across(i).start()
+        weight_share.start()
+        weight_own.start()
+        slab_own.start()
         gain_send(0).wait_recv()
         sum_g[1] = sum_g[0] + got_g[0]
         gain_send(1).start()
@@ -1303,26 +1382,20 @@
 
         spread(z)
 
-        core_send(1).wait_recv()
-        across.wait_recv()
-        for b in range(count):
-            at = pl.ds(b * slab, slab)
-            mine[b] = (
-                o_ref[2 * x + k, at, :].astype(F32) + got_a[1, at, :].astype(F32) + got_x[at, :].astype(F32)
-            ).astype(BF)
         gain_send(1).wait_recv()
         sum_g[2] = sum_g[1] + got_g[1]
 
-        def slab_send(i):
-            ct = (c + i) % count
-            return remote(mine.at[ct], got_c.at[c], ss_oc.at[i], rs_oc.at[c], (ct, f))
-
         def gain_spread(i):
             return remote(sum_g.at[2], got_gc.at[c], ss_gc.at[i], rs_gc.at[c], ((c + i) % count, f))
 
         for i in range(1, count):
-            slab_send(i).start()
             gain_spread(i).start()
+            slab_spread(i).start()
+
+        def weight_pass(i):
+            shard = (f + 2) % 4
+            remote(weight_part(shard, i), weight_part(shard, i), ss_wf.at[i], rs_wx.at[i], sib).wait_recv()
+            weight_on(i, shard).start()
 
         for j in range(1, depth):
 
@@ -1346,30 +1419,25 @@
 
                 spread(z + j)
 
-        sum_o = mine[c].astype(F32)
+            weight_pass(j - 1)
+        for i in range(depth - 1, pieces_w):
+            weight_pass(i)
+
         total_g = sum_g[2]
         for i in range(1, count):
             cs = (c + i) % count
-            remote(mine.at[cs], got_c.at[cs], ss_oc.at[i], rs_oc.at[cs], sib).wait_recv()
             remote(sum_g.at[2], got_gc.at[cs], ss_gc.at[i], rs_gc.at[cs], sib).wait_recv()
-            sum_o += got_c[cs].astype(F32)
             total_g += got_gc[cs]
         g_out[...] = total_g
-        slab_out[...] = sum_o.astype(BF)
-
-        def slab_spread(i):
-            return remote(slab_out, o_out.at[c], ss_of.at[i], rs_of.at[c], ((c + i) % count, f))
-
-        slab_own = pltpu.make_async_copy(slab_out, o_out.at[c], rs_of.at[c])
-        for i in range(1, count):
-            slab_spread(i).start()
-        slab_own.start()
-
-        core_send(0).wait_send()
-        core_send(1).wait_send()
+
         gain_send(0).wait_send()
         gain_send(1).wait_send()
-        across.wait_send()
+        for i in range(pieces_w):
+            weight_across(i).wait_send()
+            weight_on(i, (f + 2) % 4).wait_send()
+            remote(weight_part(0, i), weight_part(0, i), ss_wf.at[i], rs_wf.at[i], sib).wait_recv()
+        weight_share.wait()
+        weight_own.wait()
         for d in range(3):
             scatter(d).wait_send()
         for half, a in pieces:
@@ -1379,11 +1447,10 @@
         for i in range(1, count):
             for half, a in pieces:
                 send(i, half, a).wait_send()
-            slab_send(i).wait_send()
             gain_spread(i).wait_send()
             slab_spread(i).wait_send()
             cs = (c + i) % count
-            remote(slab_out, o_out.at[cs], ss_of.at[i], rs_of.at[cs], sib).wait_recv()
+            remote(o_ref, o_out.at[cs], ss_of.at[i], rs_of.at[cs], sib).wait_recv()
         slab_own.wait()
 
         @pl.when(k != y)
@@ -1418,34 +1485,30 @@
     return pl.pallas_call(
         kernel,
         name="finish_exchange",
+        cost_estimate=lasting(70),
         out_shape=(
             jax.ShapeDtypeStruct((2, arrays[0].shape[1], number * width), BF),
             jax.ShapeDtypeStruct((rows, 3 * width), BF),
             jax.ShapeDtypeStruct((count, slab, width), BF),
             jax.ShapeDtypeStruct(eighth, F32),
+            jax.ShapeDtypeStruct((4,) + weight.shape, BF),
         ),
-        in_specs=[ANY] * number + [vmem] * 3,
-        out_specs=(ANY, ANY, ANY, vmem),
+        in_specs=[ANY] * number + [vmem, ANY, vmem, ANY],
+        out_specs=(ANY, ANY, ANY, vmem, ANY),
         scratch_shapes=[
             pltpu.VMEM((3, rows, wide), BF),
             pltpu.VMEM((depth, rows, wide), BF),
-            pltpu.VMEM((2, rows, width), BF),
-            pltpu.VMEM((rows, width), BF),
-            pltpu.VMEM((rows, width), BF),
-            pltpu.VMEM((count, slab, width), BF),
-            pltpu.VMEM((count, slab, width), BF),
-            pltpu.VMEM((slab, width), BF),
             pltpu.VMEM((2,) + eighth, F32),
             pltpu.VMEM((3,) + eighth, F32),
             pltpu.VMEM((count,) + eighth, F32),
             DMA((count, 2, number)), DMA((count, 2, number)),
             DMA((3,)), DMA((3,)), DMA((depth,)), DMA((depth,)), DMA((depth,)),
             DMA((depth, 3)), DMA((depth, 3)), DMA((count, 3)),
-            DMA((2,)), DMA((2,)), DMA, DMA, DMA((count,)), DMA((count,)), DMA((count,)), DMA((count,)),
-            DMA((2,)), DMA((2,)), DMA((count,)), DMA((count,)),
+            DMA((count,)), DMA((count,)), DMA((2,)), DMA((2,)), DMA((count,)), DMA((count,)),
+            DMA((pieces_w,)), DMA((pieces_w,)), DMA, DMA, DMA((pieces_w,)), DMA((pieces_w,)), DMA,
         ],
         compiler_params=params(),
-    )(*arrays, parts, out_parts, gain_part)
+    )(*arrays, parts, out_slab, gain_part, weight)
 
 
 def slots_of(routes):
@@ -1467,67 +1530,84 @@
     rows = 2 * half_rows
     length = count * rows
     scale = (width // HEADS) ** (-0.5)
-    c, f, z, y, x, k = place()
-    pair = 2 * z + k
+    f = lax.axis_index("fsdp")
     lanes = 2 * (width // HEADS)
+    shard_rows = width // 4
+    pick = (((0,), (0,)), ((), ()))
+    turn = (((1,), (1,)), ((), ()))
     start_x = tokens.reshape(rows, width).astype(F32)
     cotangent = grad_output.reshape(rows, width)
     qkv_low = query_key_value_weight.astype(BF)
-    out_proj = lax.all_gather(output_weight_matrix.astype(BF), "fsdp", axis=0, tiled=True)
     first_normed, hat_one, inverse_one = norm_forward(start_x, gain_one)
     normed = first_normed.astype(BF)
-    stream, starts, projection = gather_stream(
+    stream, starts, columns = gather_stream(
         normed.reshape(2, half_rows, width), doc_starts.reshape(2, half_rows), qkv_low
     )
-    stream = stream.reshape(length, width)
-    projection = projection.reshape(width, 3 * width)
-    start_row = jnp.concatenate([starts[:, 0].reshape(-1), starts[::-1, 1].reshape(-1)])[None]
-    numbers = jnp.concatenate([jnp.min(start_row.reshape(-1, TILE), axis=1) // TILE, pair[None]])
-    query, key, value, mixed16, mixed32, logs = attend_forward(stream, projection, start_row, numbers, scale)
-    mixed = heads_to_tokens([mixed16.reshape(2 * count, half_rows, lanes)], "mixed_to_tokens").reshape(rows, width)
-    middle = start_x + jnp.dot(mixed, out_proj, preferred_element_type=F32)
-    normed_two, hat_two, inverse_two = norm_forward(middle, gain_two)
-    routed = normed_two.astype(BF)
     dispatch = slots_of(expert_ids.reshape(rows))
     own_experts = EXPERTS // count
     shape = (count, own_experts, CAP, width)
-    send_rows = jnp.dot(dispatch, routed, preferred_element_type=F32).astype(BF).reshape(shape)
     send_grads = jnp.dot(dispatch, cotangent, preferred_element_type=F32).astype(BF).reshape(shape)
-    all_rows, all_grads = dispatch_rows([send_rows, send_grads])
-    flat = (own_experts, 4 * count * CAP, width)
-    out_terms, back_terms, grad_in, grad_outw = experts_step(
-        all_rows.reshape(flat), all_grads.reshape(flat), expert_in, expert_out
-    )
-    folded = (4, own_experts, count, CAP, width)
-    returned, back_rows = return_rows([back_terms.reshape(folded), out_terms.reshape(folded)])
+    grads_near = lax.all_to_all(send_grads, "ctx", split_axis=0, concat_axis=0, tiled=True)
+    grads_near = after(grads_near, stream)
+    out_own = output_weight_matrix.astype(BF)
+    grads_far = swap(grads_near, "fsdp", 2)
+    out_far = swap(after(out_own, stream), "fsdp", 2)
+    stream = stream.reshape(length, width)
+    start_row = jnp.concatenate([starts[:, 0].reshape(-1), starts[::-1, 1].reshape(-1)])[None]
+    numbers = jnp.min(start_row.reshape(-1, TILE), axis=1) // TILE
+    query, key, value, mixed16, mixed32, logs = attend_forward(stream, columns, start_row, numbers, scale)
+    grads_far, out_far = after(grads_far, mixed16), after(out_far, mixed16)
+    grads_beside = swap(jnp.stack([grads_near, grads_far]), "fsdp", 1)
+    out_beside = swap(jnp.stack([out_own, out_far]), "fsdp", 1)
+    out_proj = jnp.concatenate([out_own, out_beside[0], out_far, out_beside[1]], axis=0)
+    gain_row = gain_two.reshape(1, width)
+    mixed, middle, all_rows = route_rows(
+        mixed16.reshape(2 * count, half_rows, lanes), out_proj, tokens.reshape(rows, width), dispatch, gain_row
+    )
+    mixed = mixed.reshape(rows, width)
+    back_terms, back_odd, out_terms, out_odd, active, grad_hidden, all_grads = experts_rows(
+        all_rows, grads_near, grads_far, after(grads_beside, all_rows), expert_in, expert_out
+    )
     slots = (EXPERTS * CAP, width)
-    pick = (((0,), (0,)), ((), ()))
-    grad_routed = lax.dot_general(dispatch, returned.reshape(slots), pick, preferred_element_type=F32)
-    expert_sum = lax.dot_general(dispatch, back_rows.reshape(slots), pick, preferred_element_type=F32)
-    block_out = (middle + expert_sum).astype(BF)
-    grad_mid_norm, grad_gain_two = norm_backward(grad_routed[None], hat_two[None], inverse_two[None], gain_two)
-    grad_middle = cotangent.astype(F32) + grad_mid_norm[0]
-    grad_attn = grad_middle.astype(BF)
-    grad_outproj = lax.dot_general(mixed, grad_attn, pick, preferred_element_type=F32).astype(BF)
-    grad_mixed = lax.dot_general(grad_attn, out_proj, (((1,), (1,)), ((), ())), preferred_element_type=F32).astype(BF)
-    grad_heads = tokens_to_heads(grad_mixed.reshape(2, half_rows, width), "grad_to_heads").reshape(length, lanes)
+    back_near = swap(back_odd, "fsdp", 1)
+    back_send = (back_terms[1].astype(F32) + back_near[1].astype(F32)).astype(BF)
+    back_far = swap(back_send, "fsdp", 2)
+    grad_in, grad_outw, done = experts_weights(after(all_rows, back_send), all_grads, active, grad_hidden)
+    out_near = swap(after(out_odd, back_send), "fsdp", 1)
+    out_send = (out_terms[1].astype(F32) + out_near[1].astype(F32) + done[0, 0]).astype(BF)
+    out_far_rows = swap(out_send, "fsdp", 2)
+    grad_heads, grad_middle, grad_gain_two, out_shard = return_grads(
+        back_terms, back_near, back_far, after(done, out_send), dispatch, cotangent, middle, mixed, out_proj, gain_row
+    )
+    out_far_rows = after(out_far_rows, grad_heads)
+    out_sum = (out_terms[0].astype(F32) + out_near[0].astype(F32) + out_far_rows.astype(F32)).astype(BF)
+    out_slabs = lax.all_to_all(
+        out_shard.reshape(count, shard_rows // count, width), "ctx", split_axis=0, concat_axis=0, tiled=True
+    )
+    back_rows = lax.all_to_all(out_sum, "ctx", split_axis=0, concat_axis=0, tiled=True)
     grad_q, grad_k, grad_v = attend_backward(
-        query, key, value, grad_heads, mixed32, logs, start_row, numbers, scale
-    )
+        query, key, value, after(grad_heads, out_sum).reshape(length, lanes), mixed32, logs, start_row, numbers, scale
+    )
+    out_slabs, back_rows = after(out_slabs, grad_q), after(back_rows, grad_q)
+    out_slab = jnp.sum(out_slabs.astype(F32), axis=0).astype(BF)
     blocks = (2 * count, half_rows, lanes)
     own_grads = jnp.concatenate([grad_q, grad_k, grad_v], axis=1)
     parts = lax.dot_general(stream, own_grads, pick, preferred_element_type=F32).astype(BF)
-    shard_rows = width // 4
-    grad_projected, weight_grad, shard_out, gain_sum = finish_exchange(
+    grad_projected, weight_grad, shard_out, gain_sum, projection = finish_exchange(
         [grad_q.reshape(blocks), grad_k.reshape(blocks), grad_v.reshape(blocks)],
         parts.reshape(4, shard_rows, 3 * lanes),
-        grad_outproj.reshape(4, shard_rows, width),
-        grad_gain_two.reshape(8, width // 8),
+        out_slab,
+        grad_gain_two,
+        qkv_low,
     )
     grad_projected = grad_projected.reshape(rows, 3 * width)
+    projection = projection.reshape(width, 3 * width)
+    back_rows = after(back_rows, weight_grad)
+    expert_sum = lax.dot_general(dispatch, back_rows.reshape(slots), pick, preferred_element_type=F32)
+    block_out = (middle + expert_sum).astype(BF)
     weight_grad = weight_grad.astype(F32)
     shard_out = shard_out.reshape(shard_rows, width).astype(F32)
-    grad_normed = lax.dot_general(grad_projected, projection, (((1,), (1,)), ((), ())), preferred_element_type=F32)
+    grad_normed = lax.dot_general(grad_projected, projection, turn, preferred_element_type=F32)
     grad_in_norm, _ = norm_backward(grad_normed[None], hat_one[None], inverse_one[None], gain_one)
     grad_start = grad_middle + grad_in_norm[0]
     own_gain = lax.dynamic_slice(gain_one, (f * shard_rows,), (shard_rows,))

time: 511 us -> 453 us (0.89)
  Pallas kernels: 453 us -> 354 us
  starting transfers between devices: 0.04 us -> 30.8 us
  other arithmetic: 15.2 us -> 32 us
  between operations: 14.3 us -> 0.86 us
  waiting for transfers between devices: 0.02 us -> 13.2 us
  matrix products: 24.1 us -> 15.4 us
    pallas_call x9 -> x8, Pallas kernels: 453 us -> 354 us  [the longest x1 88.4 us: finish_exchange(): pl.pallas_call(kernel, name='finish_exchange', cost_estimate=lasting(70),...]
    all_to_all x0 -> x3, starting transfers between devices: none -> 25.7 us  [the longest x1 13.8 us: by_head_pairs(): lax.all_to_all(out_shard.reshape(count, shard_rows // count, width), 'ctx...]
    ppermute x0 -> x8, waiting for transfers between devices: none -> 13.2 us  [swap(): return lax.ppermute(value, axis, [(i, i ^ bit) for i in range(size)])]
    dot_general x6 -> x1, matrix products: 13.9 us -> 3.47 us  [by_head_pairs(): lax.dot_general(grad_projected, projection, turn, preferred_element_type=...]
    convert_element_type x2 -> x5, other arithmetic: 3.54 us -> 13 us  [the longest x1 3.48 us: by_head_pairs(): (out_terms[0].astype(F32) + out_near[0].astype(F32) + out_far_rows.astype...]
    ppermute x0 -> x8, starting transfers between devices: none -> 5.14 us  [swap(): return lax.ppermute(value, axis, [(i, i ^ bit) for i in range(size)])]
  transfers between devices with their start and end apart: 1 -> 11, of which waited for: 0 -> 3; matrix products, arithmetic and copies ran while one was open for 2% -> 9% of each run, Pallas kernels for 22% -> 71%
where the time goes in v3:
time: 453 us; the launch traced here: 452 us
  Pallas kernels  354 us (78%)
  other arithmetic  32 us (7%)
  starting transfers between devices  30.8 us (7%)
  matrix products  15.4 us (3%)
  waiting for transfers between devices  13.2 us (3%)
  local copies, waits for them, and re-layouts  5.03 us (1%)
    pallas_call x1, Pallas kernels, finish_exchange(): pl.pallas_call(kernel, name='finish_exchange', cost_estimate=lasting(70),...  88.4 us
    pallas_call x1, Pallas kernels, route_rows(): pl.pallas_call(kernel, name='route_rows', cost_estimate=lasting(50), out_...  60.3 us
    pallas_call x1, Pallas kernels, gather_stream(): pl.pallas_call(kernel, name='gather_stream', cost_estimate=lasting(50), o...  59.6 us
    pallas_call x1, Pallas kernels, return_grads(): pl.pallas_call(kernel, name='return_grads', cost_estimate=lasting(35), ou...  49.7 us
    pallas_call x1, Pallas kernels, experts_rows(): pl.pallas_call(kernel, name='experts_rows', grid=(number,), in_specs=[par...  32.6 us
    pallas_call x1, Pallas kernels, experts_weights(): pl.pallas_call(kernel, name='experts_weights', grid=(number,), in_specs=[...  27.4 us
    pallas_call x1, Pallas kernels, attend_forward(): pl.pallas_call(kernel, name='attend_forward', cost_estimate=lasting(22),...  20.4 us
    pallas_call x1, Pallas kernels, attend_backward(): pl.pallas_call(kernel, name='attend_backward', cost_estimate=lasting(19),...  16.1 us
  transfers between devices with their start and end apart: 11, of which 3 were waited for; matrix products, arithmetic and copies ran while one was open for 9% of the time, Pallas kernels for 71%

profile of v3, /device:TPU:1, one launch (start us, length us, event | category | flops | bytes accessed | tf_op | source)
XLA Modules:
  0.0 451.7 jit_solution(1453488919239481043)
XLA Ops:
  2.4 2.5 convolution_convert_fusion
  4.8 6.4 %all-to-all-start = ((bf16[8,8,8,1024]{3,2,1,0:T(8,128)(2,1)}), bf16[8,8,8,1024]{3,2,1,0:T(8,128)(2,1)}, u32[]{:S(2)}, u32[]{:S(2)}) async-start(bf16[8,8,8,1024]{3,2,1,0:T(8,128)(2,1)} %bitcast.69), calls=%async_computation | async-start | bytes 2097152 | tf_op jit(solution)/shard_map/all_to_all | solution.py:1550
  11.3 1.4 convert_element_type.104.w_ref.refs_6_
  14.2 59.6 %gather_stream.1 = (bf16[16,128,1024]{2,1,0:T(8,128)(2,1)}, s32[8,2,128]{2,1,0:T(2,128)}, bf16[3,1024,128]{2,1,0:T(8,128)(2,1)}) custom-call(bf16[2,128,1024]{2,1,0:T(8,128)(2,1)} %fusion.15.n_ref, s32[2,128]{1,0:T(2,128)} %bitcast.88, bf16[256,3072]{1,0:T(8,128)(2,1)} %convert_element_type.104.w_ref.refs_6_), custom_call_target="tpu_custom_call" | custom-call | bytes 165000000 | tf_op jit(solution)/shard_map/gather_stream/pallas_call | solution.py:625
  73.9 1.3 collective-permute-start.2
  75.1 2.1 convert_element_type.105
  79.6 20.4 %attend_forward.1 = (bf16[2048,128]{1,0:T(8,128)(2,1)}, bf16[2048,128]{1,0:T(8,128)(2,1)}, bf16[2048,128]{1,0:T(8,128)(2,1)}, bf16[2048,128]{1,0:T(8,128)(2,1)}, f32[128,2048]{1,0:T(8,128)}, /*index=5*/f32[2,2048]{1,0:T(2,128)}) custom-call(s32[8]{0:T(128)} %and_select_fusion.first, bf16[2048,1024]{1,0:T(8,128)(2,1)} %bitcast.67, ...), custom_call_target="tpu_custom_call" | custom-call | bytes 72600000 | tf_op jit(solution)/shard_map/attend_forward/pallas_call | solution.py:704
  100.0 1.8 pad_maximum_fusion.1
  102.7 7.4 %collective-permute-done = bf16[256,1024]{1,0:T(8,128)(2,1)} collective-permute-done((bf16[256,1024]{1,0:T(8,128)(2,1)}, bf16[256,1024]{1,0:T(8,128)(2,1)}, u32[]{:S(2)}, u32[]{:S(2)}) %collective-permute-start) | collective-permute-done | bytes 524320 | tf_op jit(solution)/shard_map/ppermute | solution.py:475
  113.1 1.5 collective-permute-done.1
  114.6 2.7 pad_maximum_fusion.w_ref
  117.3 60.3 %route_rows.1 = (bf16[2,128,1024]{2,1,0:T(8,128)(2,1)}, f32[256,1024]{1,0:T(8,128)}, bf16[4,8,8,8,1024]{4,3,2,1,0:T(8,128)(2,1)}) custom-call(bf16[16,128,128]{2,1,0:T(8,128)(2,1)} %bitcast.81, bf16[1024,1024]{1,0:T(8,128)(2,1)} %pad_maximum_fusion.w_ref, bf16[256,1024]{1,0:T(8,128)(2,1)} %bitcast.66, bf16[512,256]{1,0:T(8,128)(2,1)} %fusion.20.d_ref, ...), custom_call_target="tpu_custom_call" | custom-call | bytes 165000000 | tf_op jit(solution)/shard_map/route_rows/pallas_call | solution.py:965
  177.7 1.3 copy-done.6
  179.0 32.6 %experts_rows.1 = (bf16[2,8,8,8,1024]{4,3,2,1,0:T(8,128)(2,1)}, bf16[2,8,8,8,1024]{4,3,2,1,0:T(8,128)(2,1)}, bf16[2,8,8,8,1024]{4,3,2,1,0:T(8,128)(2,1)}, bf16[2...) custom-call(bf16[4,8,8,8,1024]{4,3,2,1,0:T(8,128)(2,1)} %get-tuple-e, ...), custom_call_target="tpu_custom_call" | custom-call | flops 17179869184 | bytes 67108864 | tf_op jit(solution)/shard_map/experts_rows/pallas_call | solution.py:1177
  211.8 4.2 collective-permute-done.4.n_ref
  216.0 3.4 fusion.18
  220.7 27.4 %experts_weights.1 = (f32[8,1024,1024]{2,1,0:T(8,128)}, f32[8,1024,1024]{2,1,0:T(8,128)}, f32[8,128]{1,0:T(8,128)}) custom-call(bf16[4,8,8,8,1024]{4,3,2,1,0:T(8,128)(2,1)} %get-tuple-element.71.r_ref, bf16[8,256,1024]{2,1,0:T(8,128)(2,1)} %get-tuple-element.72.g_ref, bf16[8,256,1024]{2,1,0:T(8,128)(2,1)} %get-tuple-element.73.a_ref, ...), custom_call_target="tpu_custom_call" | custom-call | flops 8589934592 | bytes 100663296 | tf_op jit(solution)/shard_map/experts_weights/pallas_call | solution.py:1209
  248.1 1.2 slice.43
  249.3 3.3 fusion.19
  252.9 49.7 %return_grads.1 = (bf16[16,128,128]{2,1,0:T(8,128)(2,1)}, f32[256,1024]{1,0:T(8,128)}, f32[1,1024]{1,0:T(1,128)}, bf16[256,1024]{1,0:T(8,128)(2,1)}) custom-call(bf16[2,8,8,8,1024]{4,3,2,1,0:T(8,128)(2,1)} %get-tuple-element.68.o_ref, bf16[2,8,8,8,1024]{4,3,2,1,0:T(8,128)(2,1)} %copy-done.3, bf16[8,8,8,1024]{3,2,1,0:T(8,128)(2,1)} %collective-permute-done.7.f_ref, ...), custom_call_target="tpu_custom_call" | custom-call | bytes 115500000 | tf_op jit(solution)/shard_map/return_grads/pallas_call | solution.py:1110
  302.6 13.8 %all-to-all-start.2 = ((bf16[8,32,1024]{2,1,0:T(8,128)(2,1)}), bf16[8,32,1024]{2,1,0:T(8,128)(2,1)}, u32[]{:S(2)}, u32[]{:S(2)}) async-start(bf16[8,32,1024]{2,1,0:T(8,128)(2,1)} %bitcast.79), calls=%async_computation.2 | async-start | bytes 1048576 | tf_op jit(solution)/shard_map/all_to_all | solution.py:1584
  316.4 3.5 fusion
  319.9 16.1 %attend_backward.1 = (bf16[2048,128]{1,0:T(8,128)(2,1)}, bf16[2048,128]{1,0:T(8,128)(2,1)}, bf16[2048,128]{1,0:T(8,128)(2,1)}) custom-call(s32[8]{0:T(128)} %and_select_fusion.first, bf16[2048,128]{1,0:T(8,128)(2,1)} %get-tuple-element.80.q_ref, bf16[2048,128]{1,0:T(8,128)(2,1)} %get-tuple-element.81.k_ref, bf16[2048,128]{1,0:T(8,128)(2,1)} %get-tuple-element.82.v_ref, ...), custom_call_target="tpu_custom_call" | custom-call | bytes 62700000 | tf_op jit(solution)/shard_map/attend_backward/pallas_call | solution.py:797
  336.0 5.4 %all-to-all-start.1 = ((bf16[8,8,8,1024]{3,2,1,0:T(8,128)(2,1)}), bf16[8,8,8,1024]{3,2,1,0:T(8,128)(2,1)}, u32[]{:S(2)}, u32[]{:S(2)}) async-start(bf16[8,8,8,1024]{3,2,1,0:T(8,128)(2,1)} %fusion), calls=%async_computation.1 | async-start | bytes 2097152 | tf_op jit(solution)/shard_map/all_to_all | solution.py:1587
  341.4 1.8 reduce_sum.69.refs_4_
  343.2 5.9 %fusion.7 = bf16[1024,384]{1,0:T(8,128)(2,1)} fusion(bf16[2048,1024]{1,0:T(8,128)(2,1)} %bitcast.68, bf16[2048,128]{1,0:T(8,128)(2,1)} %get-tuple-element.89, bf16[2048,128]{1,0:T(8,128)(2,1)} %get-tuple-element.88, bf16[2048,128]{1,0:T(8,128)(2,1)} %get-tuple-element.86), kind=kOutput, calls=%fused_computation.17 | convolution fusion | flops 1615724544 | bytes 6553600 | tf_op jit(solution)/shard_map/dot_general | solution.py:1595
  349.0 88.4 %finish_exchange.1 = (bf16[2,128,3072]{2,1,0:T(8,128)(2,1)}, bf16[256,3072]{1,0:T(8,128)(2,1)}, bf16[8,32,1024]{2,1,0:T(8,128)(2,1)}, f32[1,1024]{1,0:T(1,128)}, bf16[4,256,3072]{2,1,0:T(8,128)(2,1)}) custom-call(bf16[16,128,128]{2,1,0:T(8,128)(2,1)} %bitcast.75, bf16[16,128,128]{2,1,0:T(8,128)(2,1)} %bitcast.76, bf16[16,128,128]{2,1,0:T(8,128)(2,1)} %bitcast.77, ...), custom_call_target="tpu_custom_call" | custom-call | bytes 231000000 | tf_op jit(solution)/shard_map/finish_exchange/pallas_call | solution.py:1485
  437.4 3.5 multiply_reduce_fusion
  441.0 1.2 constant_dynamic-slice_fusion
  442.8 3.5 fusion.27
  447.8 1.3 multiply_add_fusion
  449.2 2.5 fusion.10
  (60 shorter events, 13.5 us)
Async XLA Ops:
  0.6 10.6 %copy-start.2 = (f32[256,3072]{1,0:T(8,128)S(1)}, f32[256,3072]{1,0:T(8,128)}, u32[]{:S(2)}) copy-start(f32[256,3072]{1,0:T(8,128)} %param.13) | copy-start | bytes 9437188
  4.8 69.0 %all-to-all-start = ((bf16[8,8,8,1024]{3,2,1,0:T(8,128)(2,1)}), bf16[8,8,8,1024]{3,2,1,0:T(8,128)(2,1)}, u32[]{:S(2)}, u32[]{:S(2)}) async-start(bf16[8,8,8,1024]{3,2,1,0:T(8,128)(2,1)} %bitcast.69), calls=%async_computation | async-start | bytes 2097152 | tf_op jit(solution)/shard_map/all_to_all | solution.py:1550
  11.2 1.4 copy-start
  11.2 1.9 copy-start.10
  73.9 26.1 %collective-permute-start.2 = (bf16[8,8,8,1024]{3,2,1,0:T(8,128)(2,1)}, bf16[8,8,8,1024]{3,2,1,0:T(8,128)(2,1)}, u32[]{:S(2)}, u32[]{:S(2)}) collective-permute-start(bf16[8,8,8,1024]{3,2,1,0:T(8,128)(2,1)} %all-to-all-done.n_ref), channel_id=1, source_target_pairs={{0,2},{1,3},{2,0},{3,1},{4,6},{5,7},{6,4},{7,5},{8,10},{9,11},{10,... | collective-permute-start | bytes 3145736 | tf_op jit(solution)/shard_map/ppermute | solution.py:475
  77.2 32.9 %collective-permute-start = (bf16[256,1024]{1,0:T(8,128)(2,1)}, bf16[256,1024]{1,0:T(8,128)(2,1)}, u32[]{:S(2)}, u32[]{:S(2)}) collective-permute-start(bf16[256,1024]{1,0:T(8,128)(2,1)} %convert_element_type.105), channel_id=1, source_target_pairs={{0,2},{1,3},{2,0},{3,1},{4,6},{5,7},{6,4},{7,5},{8,10},{9,11},{10,... | collective-permute-start | bytes 1572872 | tf_op jit(solution)/shard_map/ppermute | solution.py:475
  100.0 2.6 copy-start.4
  101.8 75.8 %collective-permute-start.3 = (bf16[2,8,8,8,1024]{4,3,2,1,0:T(8,128)(2,1)S(1)}, bf16[2,8,8,8,1024]{4,3,2,1,0:T(8,128)(2,1)S(1)}, u32[]{:S(2)}, u32[]{:S(2)}) collective-permute-start(bf16[2,8,8,8,1024]{4,3,2,1,0:T(8,128)(2,1)S(1)} %pad_maximum_fusion.1), channel_id=1, source_target_pairs={{0,1},{1,0},{2,3},{3,2},{4,5},{5,4},{6,7},{7,6},{8,9},{9,8},{10,11... | collective-permute-start | bytes 6291464 | tf_op jit(solution)/shard_map/ppermute | solution.py:475
  111.3 3.3 collective-permute-start.1
  177.7 1.3 copy-start.6
  211.6 4.4 collective-permute-start.4
  216.0 32.1 %copy-start.3 = (bf16[2,8,8,8,1024]{4,3,2,1,0:T(8,128)(2,1)}, bf16[2,8,8,8,1024]{4,3,2,1,0:T(8,128)(2,1)S(1)}, u32[]{:S(2)}) copy-start(bf16[2,8,8,8,1024]{4,3,2,1,0:T(8,128)(2,1)S(1)} %collective-permute-done.4.n_ref) | copy-start | bytes 6291460
  219.4 29.9 %collective-permute-start.5 = (bf16[2,8,8,8,1024]{4,3,2,1,0:T(8,128)(2,1)}, bf16[2,8,8,8,1024]{4,3,2,1,0:T(8,128)(2,1)}, u32[]{:S(2)}, u32[]{:S(2)}) collective-permute-start(bf16[2,8,8,8,1024]{4,3,2,1,0:T(8,128)(2,1)} %get-tuple-element.70), channel_id=1, source_target_pairs={{0,1},{1,0},{2,3},{3,2},{4,5},{5,4},{6,7},{7,6},{8,9},{9,8},{10,11... | collective-permute-start | bytes 6291464 | tf_op jit(solution)/shard_map/ppermute | solution.py:475
  219.5 33.3 %collective-permute-start.7 = (bf16[8,8,8,1024]{3,2,1,0:T(8,128)(2,1)}, bf16[8,8,8,1024]{3,2,1,0:T(8,128)(2,1)}, u32[]{:S(2)}, u32[]{:S(2)}) collective-permute-start(bf16[8,8,8,1024]{3,2,1,0:T(8,128)(2,1)} %fusion.18), channel_id=1, source_target_pairs={{0,2},{1,3},{2,0},{3,1},{4,6},{5,7},{6,4},{7,5},{8,10},{9,11},{10,... | collective-permute-start | bytes 3145736 | tf_op jit(solution)/shard_map/ppermute | solution.py:475
  220.7 28.6 %copy-start.7 = (bf16[2,8,8,8,1024]{4,3,2,1,0:T(8,128)(2,1)S(1)}, bf16[2,8,8,8,1024]{4,3,2,1,0:T(8,128)(2,1)}, u32[]{:S(2)}) copy-start(bf16[2,8,8,8,1024]{4,3,2,1,0:T(8,128)(2,1)} %get-tuple-element.66) | copy-start | bytes 6291460
  252.6 63.8 %collective-permute-start.6 = (bf16[8,8,8,1024]{3,2,1,0:T(8,128)(2,1)}, bf16[8,8,8,1024]{3,2,1,0:T(8,128)(2,1)}, u32[]{:S(2)}, u32[]{:S(2)}) collective-permute-start(bf16[8,8,8,1024]{3,2,1,0:T(8,128)(2,1)} %fusion.19), channel_id=1, source_target_pairs={{0,2},{1,3},{2,0},{3,1},{4,6},{5,7},{6,4},{7,5},{8,10},{9,11},{10,... | collective-permute-start | bytes 3145736 | tf_op jit(solution)/shard_map/ppermute | solution.py:475
  302.6 33.4 %all-to-all-start.2 = ((bf16[8,32,1024]{2,1,0:T(8,128)(2,1)}), bf16[8,32,1024]{2,1,0:T(8,128)(2,1)}, u32[]{:S(2)}, u32[]{:S(2)}) async-start(bf16[8,32,1024]{2,1,0:T(8,128)(2,1)} %bitcast.79), calls=%async_computation.2 | async-start | bytes 1048576 | tf_op jit(solution)/shard_map/all_to_all | solution.py:1584
  336.0 113.2 %all-to-all-start.1 = ((bf16[8,8,8,1024]{3,2,1,0:T(8,128)(2,1)}), bf16[8,8,8,1024]{3,2,1,0:T(8,128)(2,1)}, u32[]{:S(2)}, u32[]{:S(2)}) async-start(bf16[8,8,8,1024]{3,2,1,0:T(8,128)(2,1)} %fusion), calls=%async_computation.1 | async-start | bytes 2097152 | tf_op jit(solution)/shard_map/all_to_all | solution.py:1587
  437.4 5.4 %copy-start.1 = (bf16[1,1,2,128,1024]{4,3,2,1,0:T(8,128)(2,1)S(1)}, bf16[1,1,2,128,1024]{4,3,2,1,0:T(8,128)(2,1)}, u32[]{:S(2)}) copy-start(bf16[1,1,2,128,1024]{4,3,2,1,0:T(8,128)(2,1)} %param.10) | copy-start | bytes 1572868
  437.4 5.4 %copy-start.11 = (bf16[4,256,3072]{2,1,0:T(8,128)(2,1)S(1)}, bf16[4,256,3072]{2,1,0:T(8,128)(2,1)}, u32[]{:S(2)}) copy-start(bf16[4,256,3072]{2,1,0:T(8,128)(2,1)} %get-tuple-element.97) | copy-start | bytes 18874372
  442.8 3.5 copy-start.9
  446.3 1.5 copy-start.8
  447.4 1.7 copy-start.5

commit v4 on v3

--- a/solution.py
+++ b/solution.py
@@ -822,6 +822,12 @@
     )(numbers, query, key, value, grad, mixed, logs, start_row)
 
 
+ROOT = math.sqrt(2.0 / math.pi)
+CUBIC = 0.044715
+CONTRACT_FIRST = (((0,), (0,)), ((), ()))
+CONTRACT_LAST = (((1,), (1,)), ((), ()))
+
+
 def statistics(value):
     row_mean = jnp.mean(value, axis=1, keepdims=True)
     centred = value - row_mean
@@ -829,17 +835,28 @@
     return centred * inverse, inverse
 
 
-def route_rows(by_head, out_proj, tokens, dispatch, gain):
+def stacked(value):
+    return value.reshape(-1, value.shape[-1])
+
+
+def experts_exchange(by_head, out_proj, tokens, dispatch, gain, cotangent, grads, first_proj, second_proj):
     count = lax.axis_size("ctx")
-    early = count // 2
-    lanes = by_head.shape[2]
-    half_rows = by_head.shape[1]
+    half_rows, lanes = by_head.shape[1:]
     rows, width = tokens.shape
-    experts = EXPERTS // count
+    number, _, units = first_proj.shape
+    cap = CAP
+    total_rows = 4 * count * cap
+    quarter = width // 4
+    splits = 2
+    part_units = units // splits
 
     def kernel(
-        a_ref, w_ref, x_ref, d_ref, g_ref, mixed, middle, out, routed, slots, mirror,
-        ss, rs, ss1, rs1, ssm, rsm, ss2, rs2, sse, ssx, sss, rss, ssf, rsf,
+        a_ref, w0_ref, w1_ref, w2_ref, w3_ref, x_ref, d_ref, g_ref, c_ref, g0_ref, g1_ref, g2_ref, g3_ref, first_ref, second_ref,
+        mixed, middle, rows_out, active_out, hidden_out, own_out, far_out, heads, grad_middle, gain_out, shard,
+        routed, slots, rows_v, g_buf, first_buf, second_buf, active_v, hidden_v, back_v, back_near, back_far, back_got,
+        out_v, out_near, own_v, far_v, summed, home_got, back, shard_near, shard_far, shard_got,
+        ss_m, rs_m, ss_1, rs_1, ss_x, rs_x, ss_s, rs_s, ss_f, rs_f, ss_bn, rs_bn, ss_bf, rs_bf, ss_on, rs_on, ss_h, rs_h,
+        ss_t, rs_t, ss_n, rs_n, ss_w, rs_w, l_first, l_second, l_g, st_r, st_a, st_h, st_o, st_f,
     ):
         c, f, z, y, x, k = place()
         sib = (c, f + 1 - 2 * k)
@@ -847,16 +864,30 @@
         pair = 2 * z + k
         target = 2 * x + y
 
+        def load_first(e, u):
+            cols = pl.ds(u * part_units, part_units)
+            return pltpu.make_async_copy(first_ref.at[e, :, cols], first_buf.at[u], l_first.at[u])
+
+        def load_second(e, u):
+            part = pl.ds(u * part_units, part_units)
+            return pltpu.make_async_copy(second_ref.at[e, part], second_buf.at[u], l_second.at[u])
+
+        def load_grads(e, slot):
+            refs = (g0_ref, g1_ref, g2_ref, g3_ref)
+            return [pltpu.make_async_copy(ref.at[:, e], g_buf.at[slot, j], l_g.at[slot, j]) for j, ref in enumerate(refs)]
+
         def there(half):
             column = (2 * relative(z, target) + k) * lanes
             return mixed.at[half, :, pl.ds(pl.multiple_of(column, lanes), lanes)]
 
         def send(i, half):
             ct = (c + i) % count
-            return remote(a_ref.at[block_at(ct, half, count)], there(half), ss.at[i, half], rs.at[pair, half], (ct, target))
+            return remote(
+                a_ref.at[block_at(ct, half, count)], there(half), ss_m.at[i, half], rs_m.at[pair, half], (ct, target)
+            )
 
         def keep(half):
-            return pltpu.make_async_copy(a_ref.at[block_at(c, half, count)], there(half), rs.at[pair, half])
+            return pltpu.make_async_copy(a_ref.at[block_at(c, half, count)], there(half), rs_m.at[pair, half])
 
         for half in range(2):
             for i in range(1, count):
@@ -869,348 +900,374 @@
             @pl.when(k != y)
             def _(half=half):
                 send(0, half).start()
+
+        for u in range(splits):
+            load_first(0, u).start()
+            load_second(0, u).start()
+        for load in load_grads(0, 0):
+            load.start()
 
         for half in range(2):
             for other in range(count):
                 column = (2 * relative(other // 2, f) + other % 2) * lanes
                 cols = pl.ds(pl.multiple_of(column, lanes), lanes)
-                remote(a_ref.at[0], mixed.at[half, :, cols], ss.at[0, half], rs.at[other, half], sib).wait_recv()
+                remote(a_ref.at[0], mixed.at[half, :, cols], ss_m.at[0, half], rs_m.at[other, half], sib).wait_recv()
             here = pl.ds(half * half_rows, half_rows)
-            value = x_ref[here, :].astype(F32) + jnp.dot(mixed[half], w_ref[...], preferred_element_type=F32)
+            value = x_ref[here, :].astype(F32)
+            for j, w_ref in enumerate((w0_ref, w1_ref, w2_ref, w3_ref)):
+                cols = pl.ds(j * quarter, quarter)
+                value += jnp.dot(mixed[half, :, cols], w_ref[...], preferred_element_type=F32)
             middle[here, :] = value
             hat, _ = statistics(value)
             routed[here, :] = (hat * g_ref[...]).astype(BF)
         slots[...] = jnp.dot(d_ref[...], routed[...], preferred_element_type=F32).astype(BF).reshape(slots.shape)
 
-        def owner(i):
-            return (c + i) % count
-
-        def straight(i):
-            return remote(slots.at[owner(i)], out.at[0, c], ss1.at[i], rs1.at[c], (owner(i), f))
-
-        def over(i):
-            return remote(slots.at[owner(i)], mirror.at[i], ssm.at[i], rsm.at[i], xn)
-
-        def onward(i):
-            return remote(mirror.at[i], out.at[2, c], sse.at[i], rs2.at[c], (owner(i), f))
-
-        own = pltpu.make_async_copy(slots.at[c], out.at[0, c], rs1.at[c])
-        beside = remote(slots.at[c], out.at[2, c], ss2, rs2.at[c], xn)
-        beside.start()
-        for i in range(1, early):
-            over(i).start()
-        own.start()
-        for i in [*range(early, count), *range(1, early)]:
-            straight(i).start()
-
-        def hop(source, send_sem, recv_sem, first, dst, dev):
-            return remote(out.at[first, source], out.at[dst, source], send_sem.at[source], recv_sem.at[source], dev)
-
-        def across(source):
-            return hop(source, ssx, rs2, 0, 2, xn)
-
-        def share(source):
-            return hop(source, sss, rss, 0, 1, sib)
-
-        def share_other(source):
-            return hop(source, ssf, rsf, 2, 3, sib)
-
-        def arrived(rel, source, recv_sem):
-            remote(out.at[rel, source], out.at[rel, source], ss2, recv_sem.at[source], sib).wait_recv()
-
-        def source_of(i):
-            return (c + count - i) % count
-
-        arrived(0, c, rs1)
-        share(c).start()
-        for i in range(early, count):
-            arrived(0, source_of(i), rs1)
-            across(source_of(i)).start()
-            share(source_of(i)).start()
-            j = i - early + 1
-            if j < early:
-                over(j).wait_recv()
-                onward(j).start()
-        for i in range(1, early):
-            arrived(0, source_of(i), rs1)
-            share(source_of(i)).start()
-        for i in range(count):
-            arrived(2, source_of(i), rs2)
-            share_other(source_of(i)).start()
-        for i in range(count):
-            cs = source_of(i)
-            share(cs).wait_send()
-            share_other(cs).wait_send()
-            arrived(1, cs, rss)
-            arrived(3, cs, rsf)
-            if i:
-                straight(i).wait_send()
-            if 1 <= i < early:
-                over(i).wait_send()
-                onward(i).wait_send()
-            if i >= early:
-                across(cs).wait_send()
-        beside.wait_send()
+        def rows_first(e, i):
+            owner = (c + i) % count
+            return remote(slots.at[owner, e], rows_v.at[0, e, c], ss_1.at[e], rs_1.at[e], (owner, f))
+
+        def hop(e, rel, dst, send_sem, recv_sem, dev):
+            return remote(rows_v.at[rel, e], rows_v.at[dst, e], send_sem.at[e], recv_sem.at[e], dev)
+
+        def rows_across(e):
+            return hop(e, 0, 2, ss_x, rs_x, xn)
+
+        def rows_share(e):
+            return hop(e, 0, 1, ss_s, rs_s, sib)
+
+        def rows_share_far(e):
+            return hop(e, 2, 3, ss_f, rs_f, sib)
+
+        def start_rows(e, carry):
+            for i in range(1, count):
+                rows_first(e, i).start()
+            pltpu.make_async_copy(slots.at[c, e], rows_v.at[0, e, c], rs_1.at[e]).start()
+            return carry
+
+        lax.fori_loop(0, number, start_rows, 0)
+
+        def forward(e):
+            remote(rows_v.at[0, e], rows_v.at[0, e], ss_x.at[e], rs_1.at[e], sib).wait_recv()
+            rows_across(e).start()
+            rows_share(e).start()
+
+        def forward_far(e):
+            rows_across(e).wait_recv()
+            rows_share_far(e).start()
+
+        def near_send(e, j):
+            return remote(back_v.at[2 * j + 1, e], back_near.at[j, e], ss_bn.at[e, j], rs_bn.at[e, j], sib)
+
+        def near_out(e, j):
+            return remote(out_v.at[2 * j + 1, e], out_near.at[j, e], ss_on.at[e, j], rs_on.at[e, j], sib)
+
+        def far_send(e):
+            return remote(back_far.at[e], back_got.at[e], ss_bf.at[e], rs_bf.at[e], xn)
+
+        def store_own(e):
+            return pltpu.make_async_copy(own_v.at[e], own_out.at[:, e], st_o.at[e])
+
+        def store_far(e):
+            return pltpu.make_async_copy(far_v.at[e], far_out.at[:, e], st_f.at[e])
+
+        def store_rows(e):
+            return pltpu.make_async_copy(rows_v.at[:, e], rows_out.at[:, e], st_r.at[e])
+
+        def store_active(e, slot):
+            return pltpu.make_async_copy(active_v.at[slot], active_out.at[e], st_a.at[slot])
+
+        def store_hidden(e, slot):
+            return pltpu.make_async_copy(hidden_v.at[slot], hidden_out.at[e], st_h.at[slot])
+
+        def sum_far(e):
+            near_send(e, 1).wait_recv()
+            back_far[e] = (back_v[2, e].astype(F32) + back_near[1, e].astype(F32)).astype(BF)
+            far_send(e).start()
+
+        def sum_outputs(e):
+            for j in range(2):
+                near_out(e, j).wait_recv()
+            own_v[e] = (out_v[0, e].astype(F32) + out_near[0, e].astype(F32)).astype(BF)
+            far_v[e] = (out_v[2, e].astype(F32) + out_near[1, e].astype(F32)).astype(BF)
+            store_own(e).start()
+            store_far(e).start()
+
+        def home(e, i):
+            ct = (c + i) % count
+            return remote(summed.at[e, ct], home_got.at[c, e], ss_h.at[e], rs_h, (ct, f))
+
+        def go_home(e):
+            near_send(e, 0).wait_recv()
+            far_send(e).wait_recv()
+            summed[e] = (
+                back_v[0, e].astype(F32) + back_near[0, e].astype(F32) + back_got[e].astype(F32)
+            ).astype(BF)
+            for i in range(1, count):
+                home(e, i).start()
+            pltpu.make_async_copy(summed.at[e, c], home_got.at[c, e], rs_h).start()
+
+        def expert(e, carry):
+            slot = e % 2
+
+            @pl.when(e + 1 < number)
+            def _():
+                for load in load_grads(e + 1, 1 - slot):
+                    load.start()
+
+            @pl.when(e + 2 < number)
+            def _():
+                forward(e + 2)
+
+            @pl.when(e + 1 < number)
+            def _():
+                forward_far(e + 1)
+
+            rows_share(e).wait_recv()
+            rows_share_far(e).wait_recv()
+            store_rows(e).start()
+            for load in load_grads(e, slot):
+                load.wait()
+
+            @pl.when(e >= 2)
+            def _():
+                store_active(e, slot).wait()
+                store_hidden(e, slot).wait()
+
+            row = rows_v[:, e].reshape(total_rows, width)
+            grad = g_buf[slot].reshape(total_rows, width)
+            term = jnp.zeros((total_rows, width), F32)
+            firsts, seconds = [], []
+            for u in range(splits):
+                load_first(e, u).wait()
+                load_second(e, u).wait()
+                first = first_buf[u].astype(BF)
+                second = second_buf[u].astype(BF)
+                seconds.append(second)
+                hidden = jnp.dot(row, first, preferred_element_type=F32)
+                upstream = lax.dot_general(grad, second, CONTRACT_LAST, preferred_element_type=F32)
+                bent = jnp.tanh(ROOT * (hidden + CUBIC * hidden * hidden * hidden))
+                cols = pl.ds(u * part_units, part_units)
+                active_v[slot, :, cols] = (0.5 * hidden * (1.0 + bent)).astype(BF)
+                slope = 0.5 * (1.0 + bent) + 0.5 * hidden * (1.0 - bent * bent) * (
+                    ROOT * (1.0 + 3.0 * CUBIC * hidden * hidden)
+                )
+                grad_hidden = (upstream * slope).astype(BF)
+                hidden_v[slot, :, cols] = grad_hidden
+                term += lax.dot_general(grad_hidden, first, CONTRACT_LAST, preferred_element_type=F32)
+            back_v[:, e] = term.astype(BF).reshape(4, count, cap, width)
+            near_send(e, 1).start()
+            near_send(e, 0).start()
+            result = jnp.zeros((total_rows, width), F32)
+            for u in range(splits):
+                cols = pl.ds(u * part_units, part_units)
+                result += jnp.dot(active_v[slot, :, cols], seconds[u], preferred_element_type=F32)
+            out_v[:, e] = result.astype(BF).reshape(4, count, cap, width)
+            near_out(e, 1).start()
+            near_out(e, 0).start()
+
+            @pl.when(e + 1 < number)
+            def _():
+                for u in range(splits):
+                    load_first(e + 1, u).start()
+                    load_second(e + 1, u).start()
+
+            store_active(e, slot).start()
+            store_hidden(e, slot).start()
+
+            @pl.when(e >= 1)
+            def _():
+                sum_far(e - 1)
+                sum_outputs(e - 1)
+
+            @pl.when(e >= 3)
+            def _():
+                go_home(e - 3)
+
+            return carry
+
+        forward(0)
+        forward(1)
+        forward_far(0)
+        lax.fori_loop(0, number, expert, 0)
+        sum_far(number - 1)
+        sum_outputs(number - 1)
+        for e in range(number - 3, number):
+            go_home(e)
+        hat, inverse = statistics(middle[...])
+        remote(home_got, home_got, ss_h.at[0], rs_h, sib).wait_recv()
+
+        returned = lax.dot_general(d_ref[...], home_got[...].reshape(-1, width), CONTRACT_FIRST, preferred_element_type=F32)
+        scaled = returned * g_ref[...]
+        mean_grad = jnp.mean(scaled, axis=1, keepdims=True)
+        mean_proj = jnp.mean(scaled * hat, axis=1, keepdims=True)
+        gain_out[...] = jnp.sum(returned * hat, axis=0, keepdims=True)
+        gradient = c_ref[...].astype(F32) + inverse * (scaled - mean_grad - hat * mean_proj)
+        grad_middle[...] = gradient
+        low = gradient.astype(BF)
+        for j, w_ref in enumerate((w0_ref, w1_ref, w2_ref, w3_ref)):
+            back[:, :, j * quarter : (j + 1) * quarter] = (
+                lax.dot_general(low, w_ref[...], CONTRACT_LAST, preferred_element_type=F32)
+                .astype(BF)
+                .reshape(2, half_rows, quarter)
+            )
+
+        def part(half, number_of_pair):
+            column = (2 * relative(number_of_pair // 2, f) + number_of_pair % 2) * lanes
+            return back.at[half, :, pl.ds(pl.multiple_of(column, lanes), lanes)]
+
+        def send_heads(i, half):
+            other = (2 * z + k + i) % count
+            b = block_at(c, half, count)
+            dev = (2 * (other // 2) + k, 2 * x + other % 2)
+            return remote(part(half, other), heads.at[b], ss_t.at[i, half], rs_t.at[b], dev)
+
+        for i in range(1, count):
+            for half in range(2):
+                send_heads(i, half).start()
+
+        @pl.when(k == y)
+        def _():
+            for half in range(2):
+                b = block_at(c, half, count)
+                pltpu.make_async_copy(part(half, 2 * z + k), heads.at[b], rs_t.at[b]).start()
+
+        @pl.when(k != y)
+        def _():
+            for half in range(2):
+                send_heads(0, half).start()
+
+        for e in range(number):
+            for j in range(2):
+                near_send(e, j).wait_send()
+
+        def term_place(j):
+            return back_v.at[j, 0 : quarter // (count * cap)]
+
+        def shard_term(j):
+            half_quarter = quarter // 2
+            mixed_part = [mixed[half, :, j * quarter : (j + 1) * quarter] for half in range(2)]
+            value = sum(
+                lax.dot_general(
+                    mixed_part[half], low[half * half_rows : (half + 1) * half_rows], CONTRACT_FIRST, preferred_element_type=F32
+                )
+                for half in range(2)
+            )
+            return value.astype(BF).reshape(shard_far.shape)
+
+        def core_send(j):
+            return remote(term_place(2 * j + 1), shard_near.at[j], ss_n.at[j], rs_n.at[j], sib)
+
+        across = remote(shard_far, shard_got, ss_w, rs_w, xn)
+        for j in (1, 0):
+            back_v[2 * j + 1, 0 : quarter // (count * cap)] = shard_term(2 * j + 1)
+            core_send(j).start()
+        own_far = shard_term(2)
+        core_send(1).wait_recv()
+        shard_far[...] = (own_far.astype(F32) + shard_near[1].astype(F32)).astype(BF)
+        across.start()
+        own_near = shard_term(0)
+        core_send(0).wait_recv()
+        across.wait_recv()
+        shard[...] = (
+            (own_near.astype(F32) + shard_near[0].astype(F32) + shard_got[...].astype(F32)).astype(BF).reshape(shard.shape)
+        )
+
+        for b in range(2 * count):
+            remote(part(0, 0), heads.at[b], ss_t.at[0, 0], rs_t.at[b], sib).wait_recv()
+
+        def leave(e, carry):
+            sent = pl.ds(0, count - 1)
+            remote(slots.at[sent, e], rows_v.at[0, e, sent], ss_1.at[e], rs_1.at[e], sib).wait_send()
+            remote(summed.at[e, sent], home_got.at[sent, e], ss_h.at[e], rs_h, sib).wait_send()
+            rows_across(e).wait_send()
+            rows_share(e).wait_send()
+            rows_share_far(e).wait_send()
+            far_send(e).wait_send()
+            for j in range(2):
+                near_out(e, j).wait_send()
+            store_own(e).wait()
+            store_far(e).wait()
+            store_rows(e).wait()
+            return carry
+
+        lax.fori_loop(0, number, leave, 0)
+        for e in (number - 2, number - 1):
+            store_active(e, e % 2).wait()
+            store_hidden(e, e % 2).wait()
         for i in range(1, count):
             for half in range(2):
                 send(i, half).wait_send()
+                send_heads(i, half).wait_send()
 
         @pl.when(k != y)
         def _():
             for half in range(2):
                 send(0, half).wait_send()
+                send_heads(0, half).wait_send()
+
+        core_send(0).wait_send()
+        core_send(1).wait_send()
+        across.wait_send()
 
     vmem = pl.BlockSpec(memory_space=pltpu.VMEM)
-    block = (experts, CAP, width)
+    block = (count, cap, width)
+    low = lambda *shape: pltpu.VMEM(shape, BF)
+    fold = (quarter // (count * cap),) + block
     return pl.pallas_call(
         kernel,
-        name="route_rows",
-        cost_estimate=lasting(50),
+        name="experts_exchange",
+        cost_estimate=lasting(100),
         out_shape=(
             jax.ShapeDtypeStruct((2, half_rows, width), BF),
             jax.ShapeDtypeStruct((rows, width), F32),
-            jax.ShapeDtypeStruct((4, count) + block, BF),
-        ),
-        in_specs=[ANY] + [vmem] * 4,
-        out_specs=(vmem, vmem, ANY),
-        scratch_shapes=[
-            pltpu.VMEM((rows, width), BF),
-            pltpu.VMEM((count,) + block, BF),
-            pltpu.VMEM((early,) + block, BF),
-            DMA((count, 2)), DMA((count, 2)),
-            DMA((count,)), DMA((count,)), DMA((early,)), DMA((early,)), DMA, DMA((count,)), DMA((early,)),
-            DMA((count,)), DMA((count,)), DMA((count,)), DMA((count,)), DMA((count,)),
-        ],
-        compiler_params=params(),
-    )(by_head, out_proj, tokens, dispatch, gain)
-
-
-def return_grads(own, near, far, ready, dispatch, cotangent, middle, mixed, out_proj, gain):
-    count = lax.axis_size("ctx")
-    lanes = width_of_pair = out_proj.shape[1] // count
-    rows, width = middle.shape
-    half_rows = rows // 2
-    quarter = width // 4
-
-    def kernel(
-        o_ref, n_ref, f_ref, z_ref, d_ref, c_ref, m_ref, a_ref, w_ref, g_ref, heads, grad_middle, gain_out, shard,
-        own_v, near_v, total, got, back, parts, got_near, far_v, got_far,
-        loc, ss, rs, ss_h, rs_h, ss_n, rs_n, ss_f, rs_f,
-    ):
-        c, f, z, y, x, k = place()
-        sib = (c, f + 1 - 2 * k)
-        xn = (c, (f + 2) % 4)
-        loads = [
-            pltpu.make_async_copy(o_ref.at[0], own_v, loc.at[0]),
-            pltpu.make_async_copy(n_ref.at[0], near_v, loc.at[1]),
-        ]
-        for load in loads:
-            load.start()
-        for load in loads:
-            load.wait()
-
-        def home(i):
-            ct = (c + i) % count
-            return remote(total.at[ct], got.at[c], ss.at[i], rs.at[c], (ct, f))
-
-        zero = z_ref[0:1, 0:1]
-        for i in [*range(1, count), 0]:
-            ct = (c + i) % count
-            value = own_v[ct].astype(F32) + near_v[ct].astype(F32) + f_ref[ct].astype(F32) + zero
-            if i:
-                total[ct] = value.astype(BF)
-                home(i).start()
-            else:
-                got[c] = value.astype(BF)
-        hat, inverse = statistics(m_ref[...])
-        for i in range(1, count):
-            cs = (c + i) % count
-            remote(total.at[cs], got.at[cs], ss.at[i], rs.at[cs], sib).wait_recv()
-        routed = lax.dot_general(
-            d_ref[...], got[...].reshape(-1, width), (((0,), (0,)), ((), ())), preferred_element_type=F32
-        )
-        scaled = routed * g_ref[...]
-        mean_grad = jnp.mean(scaled, axis=1, keepdims=True)
-        mean_proj = jnp.mean(scaled * hat, axis=1, keepdims=True)
-        gain_out[...] = jnp.sum(routed * hat, axis=0, keepdims=True)
-        grad = c_ref[...].astype(F32) + inverse * (scaled - mean_grad - hat * mean_proj)
-        grad_middle[...] = grad
-        low = grad.astype(BF)
-        back[...] = (
-            lax.dot_general(low, w_ref[...], (((1,), (1,)), ((), ())), preferred_element_type=F32)
-            .astype(BF)
-            .reshape(back.shape)
-        )
-
-        def part(half, pair):
-            column = (2 * relative(pair // 2, f) + pair % 2) * lanes
-            return back.at[half, :, pl.ds(pl.multiple_of(column, lanes), lanes)]
-
-        def send(i, half):
-            pair = (2 * z + k + i) % count
-            b = block_at(c, half, count)
-            dev = (2 * (pair // 2) + k, 2 * x + pair % 2)
-            return remote(part(half, pair), heads.at[b], ss_h.at[i, half], rs_h.at[b], dev)
-
-        for i in range(1, count):
-            for half in range(2):
-                send(i, half).start()
-
-        @pl.when(k == y)
-        def _():
-            for half in range(2):
-                b = block_at(c, half, count)
-                pltpu.make_async_copy(part(half, 2 * z + k), heads.at[b], rs_h.at[b]).start()
-
-        @pl.when(k != y)
-        def _():
-            for half in range(2):
-                send(0, half).start()
-
-        def term(j):
-            return lax.dot_general(
-                a_ref[:, j * quarter : (j + 1) * quarter], low, (((0,), (0,)), ((), ())), preferred_element_type=F32
-            ).astype(BF)
-
-        def core_send(j):
-            return remote(parts.at[2 * j + 1], got_near.at[j], ss_n.at[j], rs_n.at[j], sib)
-
-        across = remote(far_v, got_far, ss_f, rs_f, xn)
-        for j in (1, 0):
-            parts[2 * j + 1] = term(2 * j + 1)
-            core_send(j).start()
-        parts[2] = term(2)
-        core_send(1).wait_recv()
-        far_v[...] = (parts[2].astype(F32) + got_near[1].astype(F32)).astype(BF)
-        across.start()
-        parts[0] = term(0)
-        core_send(0).wait_recv()
-        across.wait_recv()
-        shard[...] = (parts[0].astype(F32) + got_near[0].astype(F32) + got_far[...].astype(F32)).astype(BF)
-
-        for b in range(2 * count):
-            remote(part(0, 0), heads.at[b], ss_h.at[0, 0], rs_h.at[b], sib).wait_recv()
-        for i in range(1, count):
-            home(i).wait_send()
-            for half in range(2):
-                send(i, half).wait_send()
-
-        @pl.when(k != y)
-        def _():
-            for half in range(2):
-                send(0, half).wait_send()
-
-        core_send(0).wait_send()
-        core_send(1).wait_send()
-        across.wait_send()
-
-    vmem = pl.BlockSpec(memory_space=pltpu.VMEM)
-    slots = pltpu.VMEM(far.shape, BF)
-    shard_shape = pltpu.VMEM((quarter, width), BF)
-    return pl.pallas_call(
-        kernel,
-        name="return_grads",
-        cost_estimate=lasting(35),
-        out_shape=(
-            jax.ShapeDtypeStruct((2 * count, half_rows, width_of_pair), BF),
+            jax.ShapeDtypeStruct((4, number) + block, BF),
+            jax.ShapeDtypeStruct((number, total_rows, units), BF),
+            jax.ShapeDtypeStruct((number, total_rows, units), BF),
+            jax.ShapeDtypeStruct((count, number, cap, width), BF),
+            jax.ShapeDtypeStruct((count, number, cap, width), BF),
+            jax.ShapeDtypeStruct((2 * count, half_rows, lanes), BF),
             jax.ShapeDtypeStruct((rows, width), F32),
             jax.ShapeDtypeStruct((1, width), F32),
             jax.ShapeDtypeStruct((quarter, width), BF),
         ),
-        in_specs=[ANY, ANY] + [vmem] * 8,
-        out_specs=(ANY, vmem, vmem, vmem),
+        in_specs=[ANY] + [vmem] * 8 + [ANY] * 6,
+        out_specs=(vmem, vmem, ANY, ANY, ANY, ANY, ANY, ANY, vmem, vmem, vmem),
         scratch_shapes=[
-            slots, slots, slots, slots,
-            pltpu.VMEM((2, half_rows, width), BF),
-            pltpu.VMEM((4, quarter, width), BF),
-            pltpu.VMEM((2, quarter, width), BF),
-            shard_shape, shard_shape,
-            DMA((2,)), DMA((count,)), DMA((count,)), DMA((count, 2)), DMA((2 * count,)), DMA((2,)), DMA((2,)), DMA, DMA,
+            low(rows, width), low(count, number, cap, width), low(4, number, *block), low(2, 4, *block),
+            pltpu.VMEM((splits, width, part_units), F32), pltpu.VMEM((splits, part_units, width), F32),
+            low(2, total_rows, units), low(2, total_rows, units),
+            low(4, number, *block), low(2, number, *block), low(number, *block), low(number, *block),
+            low(4, number, *block), low(2, number, *block), low(number, *block), low(number, *block),
+            low(number, *block), low(count, number, cap, width), low(2, half_rows, width),
+            low(2, *fold), low(*fold), low(*fold),
+            DMA((count, 2)), DMA((count, 2)), DMA((number,)), DMA((number,)), DMA((number,)), DMA((number,)),
+            DMA((number,)), DMA((number,)), DMA((number,)), DMA((number,)), DMA((number, 2)), DMA((number, 2)),
+            DMA((number,)), DMA((number,)), DMA((number, 2)), DMA((number, 2)), DMA((number,)), DMA,
+            DMA((count, 2)), DMA((2 * count,)), DMA((2,)), DMA((2,)), DMA, DMA,
+            DMA((splits,)), DMA((splits,)), DMA((2, 4)), DMA((number,)), DMA((2,)), DMA((2,)), DMA((number,)), DMA((number,)),
         ],
-        compiler_params=params(),
-    )(own, near, far, ready, dispatch, cotangent, middle, mixed, out_proj, gain)
-
-
-ROOT = math.sqrt(2.0 / math.pi)
-CUBIC = 0.044715
-
-
-def stacked(ref):
-    return ref[...].reshape(-1, ref.shape[-1])
-
-
-def experts_rows(rows, near, far, beside, first_proj, second_proj):
-    _, count, number, cap, width = rows.shape
-    units = first_proj.shape[2]
-    total = 4 * count * cap
-
-    def kernel(r_ref, n_ref, f_ref, b_ref, w1, w2, back, back_odd, out, out_odd, active_out, hidden_out, grad_out):
-        row = stacked(r_ref)
-        grad = jnp.concatenate(
-            [stacked(n_ref), b_ref[0].reshape(-1, width), stacked(f_ref), b_ref[1].reshape(-1, width)], axis=0
-        )
-        grad_out[0] = grad
-        first = w1[0].astype(BF)
-        second = w2[0].astype(BF)
-        hidden = jnp.dot(row, first, preferred_element_type=F32)
-        upstream = lax.dot_general(grad, second, (((1,), (1,)), ((), ())), preferred_element_type=F32)
-        bent = jnp.tanh(ROOT * (hidden + CUBIC * hidden * hidden * hidden))
-        active = (0.5 * hidden * (1.0 + bent)).astype(BF)
-        slope = 0.5 * (1.0 + bent) + 0.5 * hidden * (1.0 - bent * bent) * (ROOT * (1.0 + 3.0 * CUBIC * hidden * hidden))
-        grad_hidden = (upstream * slope).astype(BF)
-        active_out[0] = active
-        hidden_out[0] = grad_hidden
-        term = lax.dot_general(grad_hidden, first, (((1,), (1,)), ((), ())), preferred_element_type=F32)
-        result = jnp.dot(active, second, preferred_element_type=F32)
-        for j in range(4):
-            here = slice(j * total // 4, (j + 1) * total // 4)
-            (back_odd if j % 2 else back)[j // 2] = term[here].astype(BF).reshape(back.shape[1:])
-            (out_odd if j % 2 else out)[j // 2] = result[here].astype(BF).reshape(out.shape[1:])
-
-    parts = pl.BlockSpec((4, count, 1, cap, width), lambda e: (0, 0, e, 0, 0))
+        compiler_params=pltpu.CompilerParams(has_side_effects=True, vmem_limit_bytes=60 << 20),
+    )(by_head, *out_proj, tokens, dispatch, gain, cotangent, *grads, first_proj, second_proj)
+
+
+def experts_weights(rows, grads, active, grad_hidden):
+    _, number, count, cap, width = rows.shape
+    total, units = active.shape[1:]
+
+    def kernel(r_ref, g0_ref, g1_ref, g2_ref, g3_ref, a_ref, h_ref, da, db, done):
+        done[...] = jnp.zeros_like(done)
+        grad = jnp.concatenate([stacked(ref[...]) for ref in (g0_ref, g1_ref, g2_ref, g3_ref)], axis=0)
+        da[0] = lax.dot_general(stacked(r_ref[...]), h_ref[0], CONTRACT_FIRST, preferred_element_type=F32)
+        db[0] = lax.dot_general(a_ref[0], grad, CONTRACT_FIRST, preferred_element_type=F32)
+
+    parts = pl.BlockSpec((4, 1, count, cap, width), lambda e: (0, e, 0, 0, 0))
     quarter = pl.BlockSpec((count, 1, cap, width), lambda e: (0, e, 0, 0))
-    pair = pl.BlockSpec((2, count, 1, cap, width), lambda e: (0, 0, e, 0, 0))
-    left = pl.BlockSpec((1, width, units), lambda e: (e, 0, 0))
-    right = pl.BlockSpec((1, units, width), lambda e: (e, 0, 0))
     wide = pl.BlockSpec((1, total, units), lambda e: (e, 0, 0))
-    flat = pl.BlockSpec((1, total, width), lambda e: (e, 0, 0))
-    return pl.pallas_call(
-        kernel,
-        name="experts_rows",
-        grid=(number,),
-        in_specs=[parts, quarter, quarter, pair, left, right],
-        out_specs=[pair] * 4 + [wide, wide, flat],
-        out_shape=(
-            *[jax.ShapeDtypeStruct((2,) + rows.shape[1:], BF)] * 4,
-            jax.ShapeDtypeStruct((number, total, units), BF),
-            jax.ShapeDtypeStruct((number, total, units), BF),
-            jax.ShapeDtypeStruct((number, total, width), BF),
-        ),
-        cost_estimate=pl.CostEstimate(
-            flops=8 * number * total * units * width, bytes_accessed=8 * number * units * width, transcendentals=0
-        ),
-        compiler_params=params(False),
-    )(rows, near, far, beside, first_proj, second_proj)
-
-
-def experts_weights(rows, grads, active, grad_hidden):
-    _, count, number, cap, width = rows.shape
-    total, units = active.shape[1:]
-
-    def kernel(r_ref, g_ref, a_ref, h_ref, da, db, done):
-        done[...] = jnp.zeros_like(done)
-        turn = (((0,), (0,)), ((), ()))
-        da[0] = lax.dot_general(stacked(r_ref), h_ref[0], turn, preferred_element_type=F32)
-        db[0] = lax.dot_general(a_ref[0], g_ref[0], turn, preferred_element_type=F32)
-
-    parts = pl.BlockSpec((4, count, 1, cap, width), lambda e: (0, 0, e, 0, 0))
-    wide = pl.BlockSpec((1, total, units), lambda e: (e, 0, 0))
-    flat = pl.BlockSpec((1, total, width), lambda e: (e, 0, 0))
     return pl.pallas_call(
         kernel,
         name="experts_weights",
         grid=(number,),
-        in_specs=[parts, flat, wide, wide],
+        in_specs=[parts, quarter, quarter, quarter, quarter, wide, wide],
         out_specs=[
             pl.BlockSpec((1, width, units), lambda e: (e, 0, 0)),
             pl.BlockSpec((1, units, width), lambda e: (e, 0, 0)),
@@ -1225,7 +1282,7 @@
             flops=4 * number * total * units * width, bytes_accessed=12 * number * units * width, transcendentals=0
         ),
         compiler_params=params(False),
-    )(rows, grads, active, grad_hidden)
+    )(rows, *grads, active, grad_hidden)
 
 
 def after(value, *others):
@@ -1291,12 +1348,16 @@
             (2 * z + 1 - y, (f + 2) % 4, 2 * (1 - x) + 1 - y),
         ]
 
-        def scatter(d):
+        def third(ref, j):
+            return ref.at[:, pl.ds(j * lanes, lanes)]
+
+        def scatter(d, j):
             cp, fp, shard = peers[d]
-            return remote(p_ref.at[shard], got.at[d], ss_r.at[d], rs_r.at[d], (cp, fp))
-
-        for d in (2, 1, 0):
-            scatter(d).start()
+            return remote(third(p_ref.at[shard], j), third(got.at[d], j), ss_r.at[d, j], rs_r.at[d, j], (cp, fp))
+
+        for j in range(3):
+            for d in (2, 1, 0):
+                scatter(d, j).start()
 
         def there(half, a):
             return tok_out.at[half, :, pl.ds(pl.multiple_of(a * width + pair * lanes, lanes), lanes)]
@@ -1311,9 +1372,12 @@
             return pltpu.make_async_copy(ins[a].at[block_at(c, half, count)], there(half, a), rs.at[pair, half, a])
 
         pieces = [(half, a) for a in range(number) for half in range(2)]
-        for i in range(1, count):
-            for half, a in pieces:
-                send(i, half, a).start()
+        def send_all(numbers):
+            for i in numbers:
+                for half, a in pieces:
+                    send(i, half, a).start()
+
+        send_all(range(2, count, 2))
 
         @pl.when(k == y)
         def _():
@@ -1334,53 +1398,52 @@
         sum_g[1] = sum_g[0] + got_g[0]
         gain_send(1).start()
 
-        total = p_ref[2 * x + y].astype(F32)
-        for d in range(3):
-            scatter(d).wait_recv()
-            total += got[d].astype(F32)
-        held[z] = total.astype(BF)
-
-        def chain(zb, sem, dev):
-            return remote(held.at[zb], held.at[zb], sem, rs_z.at[zb], dev)
-
-        def piece(zb, j):
-            return held.at[zb, :, pl.ds(j * lanes, lanes)]
+        def chain(zb, j, sem, dev):
+            return remote(third(held.at[zb], j), third(held.at[zb], j), sem.at[j], rs_z.at[zb, j], dev)
 
         def goal(zb, j):
             return w_out.at[:, pl.ds(pl.multiple_of(j * width + (2 * zb + k) * lanes, lanes), lanes)]
 
         def own_column(zb, j):
-            return remote(piece(zb, j), goal(zb, j), ss_a.at[zb, j], rs_o.at[2 * zb + k, j], (c, target))
+            return remote(third(held.at[zb], j), goal(zb, j), ss_a.at[zb, j], rs_o.at[2 * zb + k, j], (c, target))
 
         def own_local(zb, j):
-            return pltpu.make_async_copy(piece(zb, j), goal(zb, j), rs_o.at[2 * zb + k, j])
+            return pltpu.make_async_copy(third(held.at[zb], j), goal(zb, j), rs_o.at[2 * zb + k, j])
 
         def next_column(zb, j):
-            return remote(piece(zb, j), goal(zb, j), ss_b.at[zb, j], rs_o.at[2 * zb + k, j], (2 * z + 1 - y, target))
-
-        def spread(zb):
-            for j in range(3):
-                next_column(zb, j).start()
+            return remote(
+                third(held.at[zb], j), goal(zb, j), ss_b.at[zb, j], rs_o.at[2 * zb + k, j], (2 * z + 1 - y, target)
+            )
+
+        def spread(zb, j):
+            next_column(zb, j).start()
 
             @pl.when(k == y)
             def _():
-                for j in range(3):
-                    own_local(zb, j).start()
+                own_local(zb, j).start()
 
             @pl.when(k != y)
             def _():
-                for j in range(3):
-                    own_column(zb, j).start()
-
-        @pl.when(z < depth - 1)
-        def _():
-            chain(z, ss_up.at[0], up).start()
-
-        @pl.when(z > 0)
-        def _():
-            chain(z, ss_dn.at[0], down).start()
-
-        spread(z)
+                own_column(zb, j).start()
+
+        for j in range(3):
+            at = pl.ds(j * lanes, lanes)
+            total = p_ref[2 * x + y, :, at].astype(F32)
+            for d in range(3):
+                scatter(d, j).wait_recv()
+                total += got[d, :, at].astype(F32)
+            held[z, :, at] = total.astype(BF)
+
+            @pl.when(z < depth - 1)
+            def _(j=j):
+                chain(z, j, ss_up.at[0], up).start()
+
+            @pl.when(z > 0)
+            def _(j=j):
+                chain(z, j, ss_dn.at[0], down).start()
+
+            spread(z, j)
+        send_all(range(1, count, 2))
 
         gain_send(1).wait_recv()
         sum_g[2] = sum_g[1] + got_g[1]
@@ -1397,29 +1460,30 @@
             remote(weight_part(shard, i), weight_part(shard, i), ss_wf.at[i], rs_wx.at[i], sib).wait_recv()
             weight_on(i, shard).start()
 
-        for j in range(1, depth):
-
-            @pl.when(z - j >= 0)
-            def _(j=j):
-                chain(z - j, ss_up.at[j], sib).wait_recv()
-
-                @pl.when(z < depth - 1)
-                def _():
-                    chain(z - j, ss_up.at[j], up).start()
-
-                spread(z - j)
-
-            @pl.when(z + j <= depth - 1)
-            def _(j=j):
-                chain(z + j, ss_dn.at[j], sib).wait_recv()
-
-                @pl.when(z > 0)
-                def _():
-                    chain(z + j, ss_dn.at[j], down).start()
-
-                spread(z + j)
-
-            weight_pass(j - 1)
+        for hop in range(1, depth):
+            for j in range(3):
+
+                @pl.when(z - hop >= 0)
+                def _(hop=hop, j=j):
+                    chain(z - hop, j, ss_up.at[hop], sib).wait_recv()
+
+                    @pl.when(z < depth - 1)
+                    def _():
+                        chain(z - hop, j, ss_up.at[hop], up).start()
+
+                    spread(z - hop, j)
+
+                @pl.when(z + hop <= depth - 1)
+                def _(hop=hop, j=j):
+                    chain(z + hop, j, ss_dn.at[hop], sib).wait_recv()
+
+                    @pl.when(z > 0)
+                    def _():
+                        chain(z + hop, j, ss_dn.at[hop], down).start()
+
+                    spread(z + hop, j)
+
+            weight_pass(hop - 1)
         for i in range(depth - 1, pieces_w):
             weight_pass(i)
 
@@ -1439,7 +1503,8 @@
         weight_share.wait()
         weight_own.wait()
         for d in range(3):
-            scatter(d).wait_send()
+            for j in range(3):
+                scatter(d, j).wait_send()
         for half, a in pieces:
             for other in range(count):
                 cols = pl.ds(a * width + other * lanes, lanes)
@@ -1464,17 +1529,19 @@
         for other in range(count):
             for j in range(3):
                 remote(
-                    piece(0, j), w_out.at[:, pl.ds(j * width + other * lanes, lanes)], ss_a.at[0, j], rs_o.at[other, j], sib
+                    third(held.at[0], j), third(w_out, j * count + other), ss_a.at[0, j], rs_o.at[other, j], sib
                 ).wait_recv()
-        for j in range(depth):
-
-            @pl.when((z < depth - 1) & (z - j >= 0))
-            def _(j=j):
-                chain(z - j, ss_up.at[j], up).wait_send()
-
-            @pl.when((z > 0) & (z + j <= depth - 1))
-            def _(j=j):
-                chain(z + j, ss_dn.at[j], down).wait_send()
+        for hop in range(depth):
+
+            @pl.when((z < depth - 1) & (z - hop >= 0))
+            def _(hop=hop):
+                for j in range(3):
+                    chain(z - hop, j, ss_up.at[hop], up).wait_send()
+
+            @pl.when((z > 0) & (z + hop <= depth - 1))
+            def _(hop=hop):
+                for j in range(3):
+                    chain(z + hop, j, ss_dn.at[hop], down).wait_send()
 
         for zb in range(depth):
             for j in range(3):
@@ -1502,7 +1569,7 @@
             pltpu.VMEM((3,) + eighth, F32),
             pltpu.VMEM((count,) + eighth, F32),
             DMA((count, 2, number)), DMA((count, 2, number)),
-            DMA((3,)), DMA((3,)), DMA((depth,)), DMA((depth,)), DMA((depth,)),
+            DMA((3, 3)), DMA((3, 3)), DMA((depth, 3)), DMA((depth, 3)), DMA((depth, 3)),
             DMA((depth, 3)), DMA((depth, 3)), DMA((count, 3)),
             DMA((count,)), DMA((count,)), DMA((2,)), DMA((2,)), DMA((count,)), DMA((count,)),
             DMA((pieces_w,)), DMA((pieces_w,)), DMA, DMA, DMA((pieces_w,)), DMA((pieces_w,)), DMA,
@@ -1551,45 +1618,37 @@
     grads_near = after(grads_near, stream)
     out_own = output_weight_matrix.astype(BF)
     grads_far = swap(grads_near, "fsdp", 2)
-    out_far = swap(after(out_own, stream), "fsdp", 2)
+    out_far = swap(out_own, "fsdp", 2)
+    out_far = after(out_far, stream)
+    out_beside = [swap(after(out_own, stream), "fsdp", 1), swap(out_far, "fsdp", 1)]
     stream = stream.reshape(length, width)
     start_row = jnp.concatenate([starts[:, 0].reshape(-1), starts[::-1, 1].reshape(-1)])[None]
     numbers = jnp.min(start_row.reshape(-1, TILE), axis=1) // TILE
     query, key, value, mixed16, mixed32, logs = attend_forward(stream, columns, start_row, numbers, scale)
-    grads_far, out_far = after(grads_far, mixed16), after(out_far, mixed16)
-    grads_beside = swap(jnp.stack([grads_near, grads_far]), "fsdp", 1)
-    out_beside = swap(jnp.stack([out_own, out_far]), "fsdp", 1)
-    out_proj = jnp.concatenate([out_own, out_beside[0], out_far, out_beside[1]], axis=0)
+    grads_far = after(grads_far, mixed16)
+    grads_beside = [swap(grads_near, "fsdp", 1), swap(grads_far, "fsdp", 1)]
+    out_proj = [out_own, out_beside[0], out_far, out_beside[1]]
     gain_row = gain_two.reshape(1, width)
-    mixed, middle, all_rows = route_rows(
-        mixed16.reshape(2 * count, half_rows, lanes), out_proj, tokens.reshape(rows, width), dispatch, gain_row
-    )
-    mixed = mixed.reshape(rows, width)
-    back_terms, back_odd, out_terms, out_odd, active, grad_hidden, all_grads = experts_rows(
-        all_rows, grads_near, grads_far, after(grads_beside, all_rows), expert_in, expert_out
+    all_grads = [grads_near, grads_beside[0], grads_far, grads_beside[1]]
+    (
+        mixed, middle, all_rows, active, grad_hidden, out_own, out_send, grad_heads, grad_middle, grad_gain_two, out_shard,
+    ) = experts_exchange(
+        mixed16.reshape(2 * count, half_rows, lanes), out_proj, tokens.reshape(rows, width), dispatch, gain_row, cotangent,
+        all_grads, expert_in, expert_out,
     )
     slots = (EXPERTS * CAP, width)
-    back_near = swap(back_odd, "fsdp", 1)
-    back_send = (back_terms[1].astype(F32) + back_near[1].astype(F32)).astype(BF)
-    back_far = swap(back_send, "fsdp", 2)
-    grad_in, grad_outw, done = experts_weights(after(all_rows, back_send), all_grads, active, grad_hidden)
-    out_near = swap(after(out_odd, back_send), "fsdp", 1)
-    out_send = (out_terms[1].astype(F32) + out_near[1].astype(F32) + done[0, 0]).astype(BF)
-    out_far_rows = swap(out_send, "fsdp", 2)
-    grad_heads, grad_middle, grad_gain_two, out_shard = return_grads(
-        back_terms, back_near, back_far, after(done, out_send), dispatch, cotangent, middle, mixed, out_proj, gain_row
-    )
-    out_far_rows = after(out_far_rows, grad_heads)
-    out_sum = (out_terms[0].astype(F32) + out_near[0].astype(F32) + out_far_rows.astype(F32)).astype(BF)
-    out_slabs = lax.all_to_all(
-        out_shard.reshape(count, shard_rows // count, width), "ctx", split_axis=0, concat_axis=0, tiled=True
-    )
-    back_rows = lax.all_to_all(out_sum, "ctx", split_axis=0, concat_axis=0, tiled=True)
+    out_got = swap(out_send, "fsdp", 2)
+    grad_in, grad_outw, done = experts_weights(after(all_rows, out_send), all_grads, active, grad_hidden)
+    out_sum = (out_own.astype(F32) + out_got.astype(F32) + done[0, 0]).astype(BF)
+    slab_rows = shard_rows // count
+    both_send = jnp.concatenate([out_shard.reshape(count, slab_rows, width), out_sum.reshape(count, -1, width)], axis=1)
+    both = lax.all_to_all(both_send, "ctx", split_axis=0, concat_axis=0, tiled=True)
     grad_q, grad_k, grad_v = attend_backward(
-        query, key, value, after(grad_heads, out_sum).reshape(length, lanes), mixed32, logs, start_row, numbers, scale
-    )
-    out_slabs, back_rows = after(out_slabs, grad_q), after(back_rows, grad_q)
-    out_slab = jnp.sum(out_slabs.astype(F32), axis=0).astype(BF)
+        query, key, value, after(grad_heads, both_send).reshape(length, lanes), mixed32, logs, start_row, numbers, scale
+    )
+    both = after(both, grad_q)
+    out_slab = jnp.sum(both[:, :slab_rows].astype(F32), axis=0).astype(BF)
+    back_rows = both[:, slab_rows:]
     blocks = (2 * count, half_rows, lanes)
     own_grads = jnp.concatenate([grad_q, grad_k, grad_v], axis=1)
     parts = lax.dot_general(stream, own_grads, pick, preferred_element_type=F32).astype(BF)

time: 453 us -> 395 us (0.87)
  Pallas kernels: 354 us -> 316 us
  starting transfers between devices: 30.8 us -> 15.2 us
  other arithmetic: 32 us -> 17.3 us
  waiting for transfers between devices: 13.2 us -> 24.2 us
    pallas_call x3 -> x1, Pallas kernels: 143 us -> 115 us  [experts_exchange(): pl.pallas_call(kernel, name='experts_exchange', cost_estimate=lasting(100...]
    all_to_all x2 -> x1, starting transfers between devices: 19.3 us -> 3.8 us  [by_head_pairs(): lax.all_to_all(both_send, 'ctx', split_axis=0, concat_axis=0, tiled=True)]
    all_to_all x2 -> x1, waiting for transfers between devices: 0.01 us -> 14.3 us  [by_head_pairs(): lax.all_to_all(both_send, 'ctx', split_axis=0, concat_axis=0, tiled=True)]
    convert_element_type x3 -> x0, other arithmetic: 10.2 us -> none  [the longest x1 3.48 us: by_head_pairs(): (out_terms[0].astype(F32) + out_near[0].astype(F32) + out_far_rows.astype...]
    pallas_call x1, Pallas kernels: 88.4 us -> 78.8 us  [finish_exchange(): pl.pallas_call(kernel, name='finish_exchange', cost_estimate=lasting(70),...]
    ppermute x8 -> x7, waiting for transfers between devices: 13.2 us -> 9.98 us  [swap(): return lax.ppermute(value, axis, [(i, i ^ bit) for i in range(size)])]
  transfers between devices with their start and end apart: 11 -> 9, of which waited for: 3 -> 3; matrix products, arithmetic and copies ran while one was open for 9% -> 4% of each run, Pallas kernels for 71% -> 31%
where the time goes in v4:
time: 395 us; the launch traced here: 394 us
  Pallas kernels  316 us (80%)
  waiting for transfers between devices  24.2 us (6%)
  other arithmetic  17.3 us (4%)
  matrix products  15.2 us (4%)
  starting transfers between devices  15.2 us (4%)
  local copies, waits for them, and re-layouts  5.37 us (1%)
    pallas_call x1, Pallas kernels, experts_exchange(): pl.pallas_call(kernel, name='experts_exchange', cost_estimate=lasting(100...  115 us
    pallas_call x1, Pallas kernels, finish_exchange(): pl.pallas_call(kernel, name='finish_exchange', cost_estimate=lasting(70),...  78.8 us
    pallas_call x1, Pallas kernels, gather_stream(): pl.pallas_call(kernel, name='gather_stream', cost_estimate=lasting(50), o...  58 us
    pallas_call x1, Pallas kernels, experts_weights(): pl.pallas_call(kernel, name='experts_weights', grid=(number,), in_specs=[...  27.3 us
    pallas_call x1, Pallas kernels, attend_forward(): pl.pallas_call(kernel, name='attend_forward', cost_estimate=lasting(22),...  20.4 us
    pallas_call x1, Pallas kernels, attend_backward(): pl.pallas_call(kernel, name='attend_backward', cost_estimate=lasting(19),...  16 us
    all_to_all x1, waiting for transfers between devices, by_head_pairs(): lax.all_to_all(both_send, 'ctx', split_axis=0, concat_axis=0, tiled=True)  14.3 us
    ppermute x7, waiting for transfers between devices, swap(): return lax.ppermute(value, axis, [(i, i ^ bit) for i in range(size)])  9.98 us
  transfers between devices with their start and end apart: 9, of which 3 were waited for; matrix products, arithmetic and copies ran while one was open for 4% of the time, Pallas kernels for 31%

profile of v4, /device:TPU:1, one launch (start us, length us, event | category | flops | bytes accessed | tf_op | source)
XLA Modules:
  0.0 394.0 jit_solution(535146807092737310)
XLA Ops:
  0.6 1.0 fusion.9
  2.3 2.5 convolution_convert_fusion
  4.7 6.5 %all-to-all-start = ((bf16[8,8,8,1024]{3,2,1,0:T(8,128)(2,1)}), bf16[8,8,8,1024]{3,2,1,0:T(8,128)(2,1)S(1)}, u32[]{:S(2)}, u32[]{:S(2)}) async-start(bf16[8,8,8,1024]{3,2,1,0:T(8,128)(2,1)} %bitcast.11), calls=%async_computation | async-start | bytes 2097152 | tf_op jit(solution)/shard_map/all_to_all | solution.py:1617
  11.3 3.3 convert_element_type.71.w_ref.refs_6_
  15.0 1.1 fusion.13.n_ref
  16.1 58.0 %gather_stream.1 = (bf16[16,128,1024]{2,1,0:T(8,128)(2,1)}, s32[8,2,128]{2,1,0:T(2,128)}, bf16[3,1024,128]{2,1,0:T(8,128)(2,1)}) custom-call(bf16[2,128,1024]{2,1,0:T(8,128)(2,1)} %fusion.13.n_ref, s32[2,128]{1,0:T(2,128)} %bitcast.70, bf16[256,3072]{1,0:T(8,128)(2,1)} %convert_element_type.71.w_ref.refs_6_), custom_call_target="tpu_custom_call" | custom-call | bytes 165000000 | tf_op jit(solution)/shard_map/gather_stream/pallas_call | solution.py:625
  74.1 1.3 collective-permute-start.4
  75.4 1.3 convert_element_type.72.w0_ref
  77.1 0.8 fusion.26
  79.2 20.4 %attend_forward.1 = (bf16[2048,128]{1,0:T(8,128)(2,1)}, bf16[2048,128]{1,0:T(8,128)(2,1)}, bf16[2048,128]{1,0:T(8,128)(2,1)}, bf16[2048,128]{1,0:T(8,128)(2,1)}, f32[128,2048]{1,0:T(8,128)}, /*index=5*/f32[2,2048]{1,0:T(2,128)}) custom-call(s32[8]{0:T(128)} %and_select_fusion.first, bf16[2048,1024]{1,0:T(8,128)(2,1)} %bitcast.52, ...), custom_call_target="tpu_custom_call" | custom-call | bytes 72600000 | tf_op jit(solution)/shard_map/attend_forward/pallas_call | solution.py:704
  100.8 9.2 %collective-permute-done.1.w2_ref = bf16[256,1024]{1,0:T(8,128)(2,1)S(1)} collective-permute-done((bf16[256,1024]{1,0:T(8,128)(2,1)S(1)}, bf16[256,1024]{1,0:T(8,128)(2,1)S(1)}, u32[]{:S(2)}, u32[]{:S(2)}) %collective-permute-start.1) | collective-permute-done | bytes 524320 | tf_op jit(solution)/shard_map/ppermute | solution.py:475
  110.0 1.0 collective-permute-start.2
  111.0 0.8 fusion.18.d_ref
  112.5 1.0 copy-done.8
  113.6 1.0 copy-done.9
  114.6 115.2 %experts_exchange.1 = (bf16[2,128,1024]{2,1,0:T(8,128)(2,1)}, f32[256,1024]{1,0:T(8,128)}, bf16[4,8,8,8,1024]{4,3,2,1,0:T(8,128)(2,1)}, bf16[8,256,1024]{2,1,0:T...) custom-call(bf16[16,128,128]{2,1,0:T(8,128)(2,1)} %bitcast.58, ...), custom_call_target="tpu_custom_call" | custom-call | bytes 330000000 | tf_op jit(solution)/shard_map/experts_exchange/pallas_call | solution.py:1216
  229.8 1.1 collective-permute-start.6
  230.9 27.3 %experts_weights.1 = (f32[8,1024,1024]{2,1,0:T(8,128)}, f32[8,1024,1024]{2,1,0:T(8,128)}, f32[8,128]{1,0:T(8,128)}) custom-call(bf16[4,8,8,8,1024]{4,3,2,1,0:T(8,128)(2,1)} %get-tuple-element.59.r_ref, bf16[8,8,8,1024]{3,2,1,0:T(8,128)(2,1)} %copy-done.4, bf16[8,8,8,1024]{3,2,1,0:T(8,128)(2,1)} %copy-done.8, bf16[8,8,8,1024]{3,2,1,0:T(8,128)(2,1)} %copy-done.7, ...), custom_call_target="tpu_custom_call" | custom-call | flops 8589934592 | bytes 100663296 | tf_op jit(solution)/shard_map/experts_weights/pallas_call | solution.py:1266
  258.2 1.2 slice.17
  259.4 1.1 fusion.16
  260.5 1.3 pad_maximum_fusion
  261.8 3.8 all-to-all-start.1
  265.6 16.0 %attend_backward.1 = (bf16[2048,128]{1,0:T(8,128)(2,1)}, bf16[2048,128]{1,0:T(8,128)(2,1)}, bf16[2048,128]{1,0:T(8,128)(2,1)}) custom-call(s32[8]{0:T(128)} %and_select_fusion.first, bf16[2048,128]{1,0:T(8,128)(2,1)} %get-tuple-element.63.q_ref, bf16[2048,128]{1,0:T(8,128)(2,1)} %get-tuple-element.64.k_ref, bf16[2048,128]{1,0:T(8,128)(2,1)} %get-tuple-element.65.v_ref, ...), custom_call_target="tpu_custom_call" | custom-call | bytes 62700000 | tf_op jit(solution)/shard_map/attend_backward/pallas_call | solution.py:797
  281.7 5.9 %fusion.6 = bf16[1024,384]{1,0:T(8,128)(2,1)} fusion(bf16[2048,1024]{1,0:T(8,128)(2,1)} %bitcast.53, bf16[2048,128]{1,0:T(8,128)(2,1)} %get-tuple-element.73, bf16[2048,128]{1,0:T(8,128)(2,1)} %get-tuple-element.72, bf16[2048,128]{1,0:T(8,128)(2,1)} %get-tuple-element.70), kind=kOutput, calls=%fused_computation.13 | convolution fusion | flops 1615724544 | bytes 6553600 | tf_op jit(solution)/shard_map/dot_general | solution.py:1654
  287.5 14.3 %all-to-all-done.1 = bf16[8,96,1024]{2,1,0:T(8,128)(2,1)S(1)} async-done(((bf16[8,96,1024]{2,1,0:T(8,128)(2,1)}), bf16[8,96,1024]{2,1,0:T(8,128)(2,1)S(1)}, u32[]{:S(2)}, u32[]{:S(2)}) %all-to-all-start.1) | async-done | bytes 1572896 | tf_op jit(solution)/shard_map/all_to_all | solution.py:1645
  301.8 0.8 slice_reduce_fusion.refs_4_
  302.6 78.8 %finish_exchange.1 = (bf16[2,128,3072]{2,1,0:T(8,128)(2,1)}, bf16[256,3072]{1,0:T(8,128)(2,1)}, bf16[8,32,1024]{2,1,0:T(8,128)(2,1)}, f32[1,1024]{1,0:T(1,128)}, bf16[4,256,3072]{2,1,0:T(8,128)(2,1)}) custom-call(bf16[16,128,128]{2,1,0:T(8,128)(2,1)} %bitcast.59, bf16[16,128,128]{2,1,0:T(8,128)(2,1)} %bitcast.60, bf16[16,128,128]{2,1,0:T(8,128)(2,1)} %bitcast.61, ...), custom_call_target="tpu_custom_call" | custom-call | bytes 231000000 | tf_op jit(solution)/shard_map/finish_exchange/pallas_call | solution.py:1552
  381.5 5.4 %fusion.25 = (f32[256]{0:T(256)S(1)}, f32[256]{0:T(256)S(1)}, f32[256,1024]{1,0:T(8,128)S(1)}) fusion(f32[256]{0:T(256)S(1)} %get-tuple-element.93, f32[256]{0:T(256)S(1)} %get-tuple-element.91, bf16[1,1,2,128,1024]{4,3,2,1,0:T(8,128)(2,1)S(1)} %copy-done.1, f32[1024]{0:T(1024)S(1)} %copy-done.18, bf16[256,3072]{1,0:T(8,128)(2,1)} %bitcast.75, ...), kind=kOutput, calls=%fused_computation.56 | convolution fusion | flops 1612447232 | bytes 9445376 | tf_op jit(solution)/shard_map/dot_general | solution.py:1669
  387.0 2.0 multiply_reduce_fusion
  389.4 1.1 bitcast_convert_fusion
  391.2 1.2 constant_dynamic-slice_fusion
  392.4 1.6 multiply_add_fusion
  (65 shorter events, 6.0 us)
Async XLA Ops:
  4.7 9.8 %copy-start = (bf16[1,1,2,128,1024]{4,3,2,1,0:T(8,128)(2,1)S(1)}, bf16[1,1,2,128,1024]{4,3,2,1,0:T(8,128)(2,1)}, u32[]{:S(2)}) copy-start(bf16[1,1,2,128,1024]{4,3,2,1,0:T(8,128)(2,1)} %param.10) | copy-start | bytes 1572868
  4.7 69.4 %all-to-all-start = ((bf16[8,8,8,1024]{3,2,1,0:T(8,128)(2,1)}), bf16[8,8,8,1024]{3,2,1,0:T(8,128)(2,1)S(1)}, u32[]{:S(2)}, u32[]{:S(2)}) async-start(bf16[8,8,8,1024]{3,2,1,0:T(8,128)(2,1)} %bitcast.11), calls=%async_computation | async-start | bytes 2097152 | tf_op jit(solution)/shard_map/all_to_all | solution.py:1617
  11.3 3.7 copy-start.18
  74.1 25.5 %copy-start.4 = (bf16[8,8,8,1024]{3,2,1,0:T(8,128)(2,1)}, bf16[8,8,8,1024]{3,2,1,0:T(8,128)(2,1)S(1)}, u32[]{:S(2)}) copy-start(bf16[8,8,8,1024]{3,2,1,0:T(8,128)(2,1)S(1)} %all-to-all-done.g0_ref) | copy-start | bytes 3145732
  74.1 26.2 %collective-permute-start.4 = (bf16[8,8,8,1024]{3,2,1,0:T(8,128)(2,1)S(1)}, bf16[8,8,8,1024]{3,2,1,0:T(8,128)(2,1)S(1)}, u32[]{:S(2)}, u32[]{:S(2)}) collective-permute-start(bf16[8,8,8,1024]{3,2,1,0:T(8,128)(2,1)S(1)} %all-to-all-done.g0_ref), channel_id=1, source_target_pairs={{0,2},{1,3},{2,0},{3,1},{4,6},{5,7},{6,4},{7,5},{8,10},{9,11},{10,... | collective-permute-start | bytes 3145736 | tf_op jit(solution)/shard_map/ppermute | solution.py:475
  76.7 37.9 %copy-start.5 = (bf16[256,1024]{1,0:T(8,128)(2,1)}, bf16[256,1024]{1,0:T(8,128)(2,1)S(1)}, u32[]{:S(2)}) copy-start(bf16[256,1024]{1,0:T(8,128)(2,1)S(1)} %convert_element_type.72.w0_ref) | copy-start | bytes 1572868
  76.7 33.3 %collective-permute-start.1 = (bf16[256,1024]{1,0:T(8,128)(2,1)S(1)}, bf16[256,1024]{1,0:T(8,128)(2,1)S(1)}, u32[]{:S(2)}, u32[]{:S(2)}) collective-permute-start(bf16[256,1024]{1,0:T(8,128)(2,1)S(1)} %convert_element_type.72.w0_ref), channel_id=1, source_target_pairs={{0,2},{1,3},{2,0},{3,1},{4,6},{5,7},{6,4},{7,5},{8,10},{9,11},{10,... | collective-permute-start | bytes 1572872 | tf_op jit(solution)/shard_map/ppermute | solution.py:475
  99.6 13.0 %collective-permute-start.3 = (bf16[8,8,8,1024]{3,2,1,0:T(8,128)(2,1)S(1)}, bf16[8,8,8,1024]{3,2,1,0:T(8,128)(2,1)S(1)}, u32[]{:S(2)}, u32[]{:S(2)}) collective-permute-start(bf16[8,8,8,1024]{3,2,1,0:T(8,128)(2,1)S(1)} %all-to-all-done.g0_ref), channel_id=1, source_target_pairs={{0,1},{1,0},{2,3},{3,2},{4,5},{5,4},{6,7},{7,6},{8,9},{9,8},{10,11... | collective-permute-start | bytes 3145736 | tf_op jit(solution)/shard_map/ppermute | solution.py:475
  100.3 14.2 %copy-start.7 = (bf16[8,8,8,1024]{3,2,1,0:T(8,128)(2,1)}, bf16[8,8,8,1024]{3,2,1,0:T(8,128)(2,1)S(1)}, u32[]{:S(2)}) copy-start(bf16[8,8,8,1024]{3,2,1,0:T(8,128)(2,1)S(1)} %collective-permute-done.4.g2_ref) | copy-start | bytes 3145732
  100.3 12.2 %collective-permute-start.5 = (bf16[8,8,8,1024]{3,2,1,0:T(8,128)(2,1)S(1)}, bf16[8,8,8,1024]{3,2,1,0:T(8,128)(2,1)S(1)}, u32[]{:S(2)}, u32[]{:S(2)}) collective-permute-start(bf16[8,8,8,1024]{3,2,1,0:T(8,128)(2,1)S(1)} %collective-permute-done.4.g2_ref), channel_id=1, source_target_pairs={{0,1},{1,0},{2,3},{3,2},{4,5},{5,4},{6,7},{7,6},{8,9},{9,8},{10,11... | collective-permute-start | bytes 3145736 | tf_op jit(solution)/shard_map/ppermute | solution.py:475
  100.4 11.4 %collective-permute-start = (bf16[256,1024]{1,0:T(8,128)(2,1)S(1)}, bf16[256,1024]{1,0:T(8,128)(2,1)S(1)}, u32[]{:S(2)}, u32[]{:S(2)}) collective-permute-start(bf16[256,1024]{1,0:T(8,128)(2,1)S(1)} %convert_element_type.72.w0_ref), channel_id=1, source_target_pairs={{0,1},{1,0},{2,3},{3,2},{4,5},{5,4},{6,7},{7,6},{8,9},{9,8},{10,11... | collective-permute-start | bytes 1572872 | tf_op jit(solution)/shard_map/ppermute | solution.py:475
  110.0 4.5 %copy-start.13 = (bf16[256,1024]{1,0:T(8,128)(2,1)}, bf16[256,1024]{1,0:T(8,128)(2,1)S(1)}, u32[]{:S(2)}) copy-start(bf16[256,1024]{1,0:T(8,128)(2,1)S(1)} %collective-permute-done.1.w2_ref) | copy-start | bytes 1572868
  110.0 2.5 collective-permute-start.2
  111.8 2.8 copy-start.14
  112.5 2.0 copy-start.15
  112.5 1.0 copy-start.8
  113.6 1.0 copy-start.9
  229.8 29.7 %collective-permute-start.6 = (bf16[8,8,8,1024]{3,2,1,0:T(8,128)(2,1)}, bf16[8,8,8,1024]{3,2,1,0:T(8,128)(2,1)S(1)}, u32[]{:S(2)}, u32[]{:S(2)}) collective-permute-start(bf16[8,8,8,1024]{3,2,1,0:T(8,128)(2,1)} %get-tuple-element.57), channel_id=1, source_target_pairs={{0,2},{1,3},{2,0},{3,1},{4,6},{5,7},{6,4},{7,5},{8,10},{9,11},{10,... | collective-permute-start | bytes 3145736 | tf_op jit(solution)/shard_map/ppermute | solution.py:475
  230.9 28.6 %copy-start.10 = (bf16[8,8,8,1024]{3,2,1,0:T(8,128)(2,1)S(1)}, bf16[8,8,8,1024]{3,2,1,0:T(8,128)(2,1)}, u32[]{:S(2)}) copy-start(bf16[8,8,8,1024]{3,2,1,0:T(8,128)(2,1)} %get-tuple-element.56) | copy-start | bytes 3145732
  258.2 2.3 copy-start.17
  261.8 40.0 %all-to-all-start.1 = ((bf16[8,96,1024]{2,1,0:T(8,128)(2,1)}), bf16[8,96,1024]{2,1,0:T(8,128)(2,1)S(1)}, u32[]{:S(2)}, u32[]{:S(2)}) async-start(bf16[8,96,1024]{2,1,0:T(8,128)(2,1)} %pad_maximum_fusion), calls=%async_computation.1 | async-start | bytes 3145728 | tf_op jit(solution)/shard_map/all_to_all | solution.py:1645
  301.8 79.7 %copy-start.3 = (bf16[8,96,1024]{2,1,0:T(8,128)(2,1)}, bf16[8,96,1024]{2,1,0:T(8,128)(2,1)S(1)}, u32[]{:S(2)}) copy-start(bf16[8,96,1024]{2,1,0:T(8,128)(2,1)S(1)} %all-to-all-done.1) | copy-start | bytes 4718596
  302.6 78.9 %copy-start.1 = (bf16[1,1,2,128,1024]{4,3,2,1,0:T(8,128)(2,1)S(1)}, bf16[1,1,2,128,1024]{4,3,2,1,0:T(8,128)(2,1)}, u32[]{:S(2)}) copy-start(bf16[1,1,2,128,1024]{4,3,2,1,0:T(8,128)(2,1)} %param.10) | copy-start | bytes 1572868
  381.5 5.5 %copy-start.2 = (f32[256,3072]{1,0:T(8,128)S(1)}, f32[256,3072]{1,0:T(8,128)}, u32[]{:S(2)}) copy-start(f32[256,3072]{1,0:T(8,128)} %param.13) | copy-start | bytes 9437188
  381.5 5.5 %copy-start.6 = (bf16[256,3072]{1,0:T(8,128)(2,1)S(1)}, bf16[256,3072]{1,0:T(8,128)(2,1)}, u32[]{:S(2)}) copy-start(bf16[256,3072]{1,0:T(8,128)(2,1)} %get-tuple-element.75) | copy-start | bytes 4718596
  387.0 2.0 slice-start
  387.0 2.5 copy-start.16
  388.9 3.5 copy-start.11
  388.9 3.5 copy-start.12

commit v5 on v4

--- a/solution.py
+++ b/solution.py
@@ -444,6 +444,8 @@
 
 BF = jnp.bfloat16
 F32 = jnp.float32
+CONTRACT_FIRST = (((0,), (0,)), ((), ()))
+CONTRACT_LAST = (((1,), (1,)), ((), ()))
 MESH_ID = pl.DeviceIdType.MESH
 ANY = pl.BlockSpec(memory_space=pl.ANY)
 DMA = pltpu.SemaphoreType.DMA
@@ -466,6 +468,17 @@
     return c if half == 0 else 2 * count - 1 - c
 
 
+def statistics(value):
+    row_mean = jnp.mean(value, axis=1, keepdims=True)
+    centred = value - row_mean
+    inverse = lax.rsqrt(jnp.mean(centred * centred, axis=1, keepdims=True) + EPS)
+    return centred * inverse, inverse
+
+
+def stacked(value):
+    return value.reshape(-1, value.shape[-1])
+
+
 def relative(a, b):
     return (a // 2 + b // 2) % 2 * 2 + (a + b) % 2
 
@@ -483,19 +496,29 @@
     return pltpu.CompilerParams(has_side_effects=side, vmem_limit_bytes=VMEM_CAP)
 
 
-def gather_stream(normed, starts, weight):
+def gather_stream(tokens, gain, routes, cotangent, starts, weight, matrix):
     count = lax.axis_size("ctx")
     depth = count // 2
     rows, wide = weight.shape
-    lanes = wide // 3 // count
-
-    def kernel(n_ref, s_ref, w_ref, tok, st, cols, rs_t, ss_p, ss_up, ss_dn, ss_sib, rs_s, ss_s, rs_w, ss_w):
+    part = wide // count
+    lanes = part // 3
+    half_rows, width = tokens.shape[1:]
+    own_rows = 2 * half_rows
+    own_experts = EXPERTS // count
+
+    def kernel(
+        x_ref, g_ref, e_ref, c_ref, s_ref, wf_ref, of_ref, tok, st, cols, beside, far, diagonal, got, w_ref, o_ref, hot,
+        n_ref, d_ref, rs_t, ss_p, ss_up, ss_dn, ss_sib, rs_s, ss_s, rs_w, ss_w, ss_o, rs_o, ss_d, rs_d,
+    ):
         c, f, z, y, x, k = place()
         sib = (c, f + 1 - 2 * k)
         partner = (c + 1 - 2 * y, f + 1 - 2 * k)
         up = (c + 2, f)
         down = (c - 2, f)
         holder = k == y
+        for h in range(2):
+            hat, _ = statistics(x_ref[h].astype(F32))
+            n_ref[h] = (hat * g_ref[...]).astype(BF)
 
         def send_in(h):
             b = block_at(c, h, count)
@@ -529,20 +552,33 @@
 
         goals = [(2 * z + k, (c, (f + 2) % 4)), (2 * z + 1 - k, (c, (sib[1] + 2) % 4)), (2 * z + 1 - k, sib)]
 
-        def columns(pair, j):
-            return w_ref.at[:, pl.ds(pl.multiple_of(j * count * lanes + pair * lanes, lanes), lanes)]
-
-        def weight_place(shard, j):
-            return cols.at[j, pl.ds(pl.multiple_of(shard * rows, rows), rows)]
-
-        def weight_send(t, j):
+        def columns(pair):
+            return w_ref.at[:, pl.ds(pl.multiple_of(pair * part, part), part)]
+
+        def weight_place(shard):
+            return cols.at[pl.ds(pl.multiple_of(shard * rows, rows), rows)]
+
+        def weight_send(t):
             pair, dev = goals[t]
-            return remote(columns(pair, j), weight_place(f, j), ss_w.at[t, j], rs_w.at[f, j], dev)
-
-        for j in range(3):
-            for t in range(3):
-                weight_send(t, j).start()
-            pltpu.make_async_copy(columns(2 * z + k, j), weight_place(f, j), rs_w.at[f, j]).start()
+            return remote(columns(pair), weight_place(f), ss_w.at[t], rs_w.at[f], dev)
+
+        for number in range(count):
+            for j in range(3):
+                at = number * part + j * lanes
+                w_ref[:, at : at + lanes] = wf_ref[:, j * count * lanes + number * lanes :][:, :lanes].astype(BF)
+        for t in range(3):
+            weight_send(t).start()
+        pltpu.make_async_copy(columns(2 * z + k), weight_place(f), rs_w.at[f]).start()
+        o_ref[...] = of_ref[...].astype(BF)
+        matrix_far = remote(o_ref, far, ss_o.at[0], rs_o.at[0], goals[0][1])
+        matrix_beside = remote(o_ref, beside, ss_o.at[1], rs_o.at[1], sib)
+        matrix_on = remote(far, diagonal, ss_o.at[2], rs_o.at[2], sib)
+        matrix_far.start()
+        matrix_beside.start()
+
+        def slots_send(i):
+            ct = (c + i) % count
+            return remote(d_ref.at[ct], got.at[c], ss_d.at[i], rs_d.at[c], (ct, f))
 
         def copy_block(zb, h, ss, dev):
             b = block_at(2 * zb + k, h, count)
@@ -562,6 +598,27 @@
                         copy_block(z, h, ss_dn.at[0, h], down).start()
 
                     copy_block(z, h, ss_sib.at[z, h], sib).start()
+                    if h == 1:
+                        expert = lax.broadcasted_iota(jnp.int32, (EXPERTS, own_rows), 0)
+                        chosen = expert == e_ref[...]
+                        earlier = lax.broadcasted_iota(jnp.int32, (own_rows, own_rows), 0) <= lax.broadcasted_iota(
+                            jnp.int32, (own_rows, own_rows), 1
+                        )
+                        running = jnp.dot(
+                            jnp.where(chosen, 1.0, 0.0).astype(BF),
+                            jnp.where(earlier, 1.0, 0.0).astype(BF),
+                            preferred_element_type=F32,
+                        )
+                        rank = jnp.sum(jnp.where(chosen, running, 0.0), axis=0, keepdims=True).astype(jnp.int32) - 1
+                        slot = e_ref[...] * CAP + rank
+                        index = lax.broadcasted_iota(jnp.int32, (EXPERTS * CAP, own_rows), 0)
+                        hot[...] = jnp.where(index == slot, 1.0, 0.0).astype(BF)
+                        d_ref[...] = (
+                            jnp.dot(hot[...], c_ref[...], preferred_element_type=F32).astype(BF).reshape(d_ref.shape)
+                        )
+                        for i in range(1, count):
+                            slots_send(i).start()
+                        pltpu.make_async_copy(d_ref.at[c], got.at[c], rs_d.at[c]).start()
                     continue
 
                 @pl.when(z - j >= 0)
@@ -584,6 +641,8 @@
 
                     copy_block(z + j, h, ss_sib.at[z + j, h], sib).start()
 
+        matrix_far.wait_recv()
+        matrix_on.start()
         for zt in range(depth):
             for h in range(2):
                 b = block_at(2 * zt + 1 - k, h, count)
@@ -591,11 +650,17 @@
                 copy_block(zt, h, ss_sib.at[zt, h], sib).wait_send()
         for ct in range(count):
             remote(s_ref, st.at[ct], ss_s.at[0], rs_s.at[ct], sib).wait_recv()
-        for j in range(3):
-            for shard in range(4):
-                remote(columns(0, j), weight_place(shard, j), ss_w.at[0, j], rs_w.at[shard, j], sib).wait_recv()
-            for t in range(3):
-                weight_send(t, j).wait_send()
+        for shard in range(4):
+            remote(columns(0), weight_place(shard), ss_w.at[0], rs_w.at[shard], sib).wait_recv()
+        for t in range(3):
+            weight_send(t).wait_send()
+        matrix_far.wait_send()
+        matrix_beside.wait()
+        matrix_on.wait()
+        for i in range(count):
+            if i:
+                slots_send(i).wait_send()
+            remote(d_ref.at[i], got.at[i], ss_d.at[i], rs_d.at[i], sib).wait_recv()
 
         @pl.when(jnp.logical_not(holder))
         def _():
@@ -627,18 +692,24 @@
         name="gather_stream",
         cost_estimate=lasting(50),
         out_shape=(
-            jax.ShapeDtypeStruct((2 * count,) + normed.shape[1:], normed.dtype),
+            jax.ShapeDtypeStruct((2 * count, half_rows, width), BF),
             jax.ShapeDtypeStruct((count,) + starts.shape, starts.dtype),
-            jax.ShapeDtypeStruct((3, 4 * rows, lanes), weight.dtype),
+            jax.ShapeDtypeStruct((4 * rows, part), BF),
+            *[jax.ShapeDtypeStruct(matrix.shape, BF)] * 3,
+            jax.ShapeDtypeStruct((count, own_experts, CAP, width), BF),
+            jax.ShapeDtypeStruct((rows, wide), BF),
+            jax.ShapeDtypeStruct(matrix.shape, BF),
+            jax.ShapeDtypeStruct((EXPERTS * CAP, own_rows), BF),
         ),
-        in_specs=[ANY] * 3,
-        out_specs=(ANY,) * 3,
+        in_specs=[pl.BlockSpec(memory_space=pltpu.VMEM)] * 7,
+        out_specs=(ANY,) * 7 + (pl.BlockSpec(memory_space=pltpu.VMEM),) * 3,
         scratch_shapes=[
+            pltpu.VMEM((2, half_rows, width), BF), pltpu.VMEM((count, own_experts, CAP, width), BF),
             DMA((2 * count,)), DMA((2,)), DMA((depth, 2)), DMA((depth, 2)), DMA((depth, 2)),
-            DMA((count,)), DMA((count,)), DMA((4, 3)), DMA((3, 3)),
+            DMA((count,)), DMA((count,)), DMA((4,)), DMA((3,)), DMA((3,)), DMA((3,)), DMA((count,)), DMA((count,)),
         ],
         compiler_params=params(),
-    )(normed, starts, weight)
+    )(tokens, gain, routes, cotangent, starts, weight, matrix)
 
 
 TILE = 256
@@ -657,14 +728,14 @@
     lanes = 128
     size = lanes // 2
 
-    def kernel(first, x_ref, w_ref, s_ref, q_out, k_out, v_out, m16, m32, lse, v_turned):
+    def kernel(first, x_ref, w_ref, s_ref, out, m16, m32, lse, k_rows, v_turned):
         i = pl.program_id(0)
         own = pl.ds(pl.multiple_of(i * TILE, TILE), TILE)
         rows = x_ref[...]
-        query, key, value = [jnp.dot(rows, w_ref[j], preferred_element_type=F32).astype(BF) for j in range(3)]
-        q_out[...] = query
-        k_out[own, :] = key
-        v_out[...] = value
+        projected = jnp.dot(rows, w_ref[...], preferred_element_type=F32).astype(BF)
+        out[...] = projected
+        query, key, value = [projected[:, j * lanes : (j + 1) * lanes] for j in range(3)]
+        k_rows[own, :] = key
         v_turned[:, own] = value.T
         queries = halves((query * scale).T, 0)
         start = s_ref[...]
@@ -673,7 +744,7 @@
 
         def step(j, carried):
             at = pl.multiple_of(j * TILE, TILE)
-            keys = k_out[pl.ds(at, TILE), :]
+            keys = k_rows[pl.ds(at, TILE), :]
             seen = (key_row + at <= query_column) & (key_row + at >= start)
             out = []
             for h in range(2):
@@ -710,23 +781,19 @@
             grid=(tiles,),
             in_specs=[
                 pl.BlockSpec((TILE, width), lambda i, n: (i, 0)),
-                pl.BlockSpec((3, width, lanes), lambda i, n: (0, 0, 0)),
+                pl.BlockSpec((width, 3 * lanes), lambda i, n: (0, 0)),
                 pl.BlockSpec((1, TILE), lambda i, n: (0, i)),
             ],
             out_specs=[
-                tile,
-                pl.BlockSpec((length, lanes), lambda i, n: (0, 0)),
-                tile,
+                pl.BlockSpec((TILE, 3 * lanes), lambda i, n: (i, 0)),
                 tile,
                 turned,
                 pl.BlockSpec((2, TILE), lambda i, n: (0, i)),
             ],
-            scratch_shapes=[pltpu.VMEM((lanes, length), BF)],
+            scratch_shapes=[pltpu.VMEM((length, lanes), BF), pltpu.VMEM((lanes, length), BF)],
         ),
         out_shape=(
-            jax.ShapeDtypeStruct((length, lanes), BF),
-            jax.ShapeDtypeStruct((length, lanes), BF),
-            jax.ShapeDtypeStruct((length, lanes), BF),
+            jax.ShapeDtypeStruct((length, 3 * lanes), BF),
             jax.ShapeDtypeStruct((length, lanes), BF),
             jax.ShapeDtypeStruct((lanes, length), F32),
             jax.ShapeDtypeStruct((2, length), F32),
@@ -735,13 +802,23 @@
     )(numbers, stream, columns, start_row)
 
 
-def attend_backward(query, key, value, grad, mixed, logs, start_row, numbers, scale):
-    length, lanes = query.shape
+def backward_local(qkv, grad, mixed, logs, start_row, numbers, scale, stream, rows, cotangents, active, grad_hidden):
+    length = qkv.shape[0]
+    lanes = 128
     tiles = length // TILE
     size = lanes // 2
-
-    def kernel(first, q_ref, k_ref, v_ref, g_ref, m_ref, l_ref, s_ref, dq, dk, dv, acc_k, acc_v, k_turned):
+    _, number, count, cap, width = rows.shape
+    total_rows, units = active.shape[1:]
+    assert tiles == number
+
+    def kernel(
+        first, q_ref, k_ref, v_ref, g_ref, m_ref, l_ref, s_ref, x_ref, r_ref, g0_ref, g1_ref, g2_ref, g3_ref, a_ref, h_ref,
+        out, weight, da, db, acc_k, acc_v, k_turned,
+    ):
         i = pl.program_id(0)
+        gradient = jnp.concatenate([stacked(ref[...]) for ref in (g0_ref, g1_ref, g2_ref, g3_ref)], axis=0)
+        da[0] = lax.dot_general(stacked(r_ref[...]), h_ref[0], CONTRACT_FIRST, preferred_element_type=F32)
+        db[0] = lax.dot_general(a_ref[0], gradient, CONTRACT_FIRST, preferred_element_type=F32)
 
         @pl.when(i == 0)
         def _():
@@ -785,58 +862,66 @@
 
         zero = jnp.zeros((size, TILE), F32)
         total = lax.fori_loop(first[i], i + 1, step, (zero, zero))
-        dq[...] = (jnp.concatenate(total, axis=0) * scale).T.astype(BF)
+        own = pl.ds(pl.multiple_of(i * TILE, TILE), TILE)
+        out[own, 0:lanes] = (jnp.concatenate(total, axis=0) * scale).T.astype(BF)
 
         @pl.when(i == tiles - 1)
         def _():
-            dk[...] = acc_k[...].astype(BF)
-            dv[...] = acc_v[...].astype(BF)
+            out[:, lanes : 2 * lanes] = acc_k[...].astype(BF)
+            out[:, 2 * lanes : 3 * lanes] = acc_v[...].astype(BF)
+            weight[...] = lax.dot_general(x_ref[...], out[...], CONTRACT_FIRST, preferred_element_type=F32).astype(BF)
 
     tile = pl.BlockSpec((TILE, lanes), lambda i, n: (i, 0))
-    full = pl.BlockSpec((length, lanes), lambda i, n: (0, 0))
+    quarter = pl.BlockSpec((count, 1, cap, width), lambda i, n: (0, i, 0, 0))
+    wide = pl.BlockSpec((1, total_rows, units), lambda i, n: (i, 0, 0))
     return pl.pallas_call(
         kernel,
-        name="attend_backward",
-        cost_estimate=lasting(19),
+        name="backward_local",
+        cost_estimate=lasting(30),
         grid_spec=pltpu.PrefetchScalarGridSpec(
             num_scalar_prefetch=1,
             grid=(tiles,),
             in_specs=[
                 tile,
-                full,
-                full,
+                pl.BlockSpec((length, lanes), lambda i, n: (0, 1)),
+                pl.BlockSpec((length, lanes), lambda i, n: (0, 2)),
                 tile,
                 pl.BlockSpec((lanes, TILE), lambda i, n: (0, i)),
                 pl.BlockSpec((2, TILE), lambda i, n: (0, i)),
                 pl.BlockSpec((1, TILE), lambda i, n: (0, i)),
+                pl.BlockSpec((length, width), lambda i, n: (0, 0), pipeline_mode=pl.Buffered(1)),
+                pl.BlockSpec((4, 1, count, cap, width), lambda i, n: (0, i, 0, 0, 0)),
+                quarter,
+                quarter,
+                quarter,
+                quarter,
+                wide,
+                wide,
             ],
-            out_specs=[tile, full, full],
+            out_specs=[
+                pl.BlockSpec((length, 3 * lanes), lambda i, n: (0, 0)),
+                pl.BlockSpec((width, 3 * lanes), lambda i, n: (0, 0)),
+                pl.BlockSpec((1, width, units), lambda i, n: (i, 0, 0)),
+                pl.BlockSpec((1, units, width), lambda i, n: (i, 0, 0)),
+            ],
             scratch_shapes=[
                 pltpu.VMEM((length, lanes), F32),
                 pltpu.VMEM((length, lanes), F32),
                 pltpu.VMEM((lanes, length), BF),
             ],
         ),
-        out_shape=(jax.ShapeDtypeStruct((length, lanes), BF),) * 3,
+        out_shape=(
+            jax.ShapeDtypeStruct((length, 3 * lanes), BF),
+            jax.ShapeDtypeStruct((width, 3 * lanes), BF),
+            jax.ShapeDtypeStruct((number, width, units), F32),
+            jax.ShapeDtypeStruct((number, units, width), F32),
+        ),
         compiler_params=params(False),
-    )(numbers, query, key, value, grad, mixed, logs, start_row)
+    )(numbers, qkv, qkv, qkv, grad, mixed, logs, start_row, stream, rows, *cotangents, active, grad_hidden)
 
 
 ROOT = math.sqrt(2.0 / math.pi)
 CUBIC = 0.044715
-CONTRACT_FIRST = (((0,), (0,)), ((), ()))
-CONTRACT_LAST = (((1,), (1,)), ((), ()))
-
-
-def statistics(value):
-    row_mean = jnp.mean(value, axis=1, keepdims=True)
-    centred = value - row_mean
-    inverse = lax.rsqrt(jnp.mean(centred * centred, axis=1, keepdims=True) + EPS)
-    return centred * inverse, inverse
-
-
-def stacked(value):
-    return value.reshape(-1, value.shape[-1])
 
 
 def experts_exchange(by_head, out_proj, tokens, dispatch, gain, cotangent, grads, first_proj, second_proj):
@@ -847,16 +932,17 @@
     cap = CAP
     total_rows = 4 * count * cap
     quarter = width // 4
+    slab = quarter // count
     splits = 2
     part_units = units // splits
 
     def kernel(
         a_ref, w0_ref, w1_ref, w2_ref, w3_ref, x_ref, d_ref, g_ref, c_ref, g0_ref, g1_ref, g2_ref, g3_ref, first_ref, second_ref,
-        mixed, middle, rows_out, active_out, hidden_out, own_out, far_out, heads, grad_middle, gain_out, shard,
+        mixed, middle, rows_out, active_out, hidden_out, heads, grad_middle, gain_out, later,
         routed, slots, rows_v, g_buf, first_buf, second_buf, active_v, hidden_v, back_v, back_near, back_far, back_got,
-        out_v, out_near, own_v, far_v, summed, home_got, back, shard_near, shard_far, shard_got,
+        out_v, out_near, own_v, far_v, out_got, summed, home_got, back, shard_near, shard_far, shard_got, shard_v,
         ss_m, rs_m, ss_1, rs_1, ss_x, rs_x, ss_s, rs_s, ss_f, rs_f, ss_bn, rs_bn, ss_bf, rs_bf, ss_on, rs_on, ss_h, rs_h,
-        ss_t, rs_t, ss_n, rs_n, ss_w, rs_w, l_first, l_second, l_g, st_r, st_a, st_h, st_o, st_f,
+        ss_t, rs_t, ss_n, rs_n, ss_w, rs_w, l_first, l_second, l_g, st_r, st_a, st_h, st_o, ss_of, rs_of, st_w,
     ):
         c, f, z, y, x, k = place()
         sib = (c, f + 1 - 2 * k)
@@ -965,10 +1051,10 @@
             return remote(back_far.at[e], back_got.at[e], ss_bf.at[e], rs_bf.at[e], xn)
 
         def store_own(e):
-            return pltpu.make_async_copy(own_v.at[e], own_out.at[:, e], st_o.at[e])
-
-        def store_far(e):
-            return pltpu.make_async_copy(far_v.at[e], far_out.at[:, e], st_f.at[e])
+            return pltpu.make_async_copy(own_v.at[e], later.at[:, pl.ds(pl.multiple_of(slab + e * cap, cap), cap)], st_o.at[e])
+
+        def far_out(e):
+            return remote(far_v.at[e], out_got.at[e], ss_of.at[e], rs_of.at[e], xn)
 
         def store_rows(e):
             return pltpu.make_async_copy(rows_v.at[:, e], rows_out.at[:, e], st_r.at[e])
@@ -989,8 +1075,6 @@
                 near_out(e, j).wait_recv()
             own_v[e] = (out_v[0, e].astype(F32) + out_near[0, e].astype(F32)).astype(BF)
             far_v[e] = (out_v[2, e].astype(F32) + out_near[1, e].astype(F32)).astype(BF)
-            store_own(e).start()
-            store_far(e).start()
 
         def home(e, i):
             ct = (c + i) % count
@@ -1091,6 +1175,8 @@
         lax.fori_loop(0, number, expert, 0)
         sum_far(number - 1)
         sum_outputs(number - 1)
+        for e in range(number):
+            far_out(e).start()
         for e in range(number - 3, number):
             go_home(e)
         hat, inverse = statistics(middle[...])
@@ -1167,10 +1253,20 @@
         across.start()
         own_near = shard_term(0)
         core_send(0).wait_recv()
+
+        def finish_output(e, carry):
+            far_out(e).wait_recv()
+            own_v[e] = (own_v[e].astype(F32) + out_got[e].astype(F32)).astype(BF)
+            store_own(e).start()
+            return carry
+
+        lax.fori_loop(0, number, finish_output, 0)
         across.wait_recv()
-        shard[...] = (
-            (own_near.astype(F32) + shard_near[0].astype(F32) + shard_got[...].astype(F32)).astype(BF).reshape(shard.shape)
+        shard_v[...] = (
+            (own_near.astype(F32) + shard_near[0].astype(F32) + shard_got[...].astype(F32)).astype(BF).reshape(shard_v.shape)
         )
+        store_shard = pltpu.make_async_copy(shard_v, later.at[:, pl.ds(0, slab)], st_w)
+        store_shard.start()
 
         for b in range(2 * count):
             remote(part(0, 0), heads.at[b], ss_t.at[0, 0], rs_t.at[b], sib).wait_recv()
@@ -1186,11 +1282,12 @@
             for j in range(2):
                 near_out(e, j).wait_send()
             store_own(e).wait()
-            store_far(e).wait()
+            far_out(e).wait_send()
             store_rows(e).wait()
             return carry
 
         lax.fori_loop(0, number, leave, 0)
+        store_shard.wait()
         for e in (number - 2, number - 1):
             store_active(e, e % 2).wait()
             store_hidden(e, e % 2).wait()
@@ -1223,94 +1320,49 @@
             jax.ShapeDtypeStruct((4, number) + block, BF),
             jax.ShapeDtypeStruct((number, total_rows, units), BF),
             jax.ShapeDtypeStruct((number, total_rows, units), BF),
-            jax.ShapeDtypeStruct((count, number, cap, width), BF),
-            jax.ShapeDtypeStruct((count, number, cap, width), BF),
             jax.ShapeDtypeStruct((2 * count, half_rows, lanes), BF),
             jax.ShapeDtypeStruct((rows, width), F32),
             jax.ShapeDtypeStruct((1, width), F32),
-            jax.ShapeDtypeStruct((quarter, width), BF),
+            jax.ShapeDtypeStruct((count, slab + number * cap, width), BF),
         ),
         in_specs=[ANY] + [vmem] * 8 + [ANY] * 6,
-        out_specs=(vmem, vmem, ANY, ANY, ANY, ANY, ANY, ANY, vmem, vmem, vmem),
+        out_specs=(vmem, vmem, ANY, ANY, ANY, ANY, vmem, vmem, ANY),
         scratch_shapes=[
             low(rows, width), low(count, number, cap, width), low(4, number, *block), low(2, 4, *block),
             pltpu.VMEM((splits, width, part_units), F32), pltpu.VMEM((splits, part_units, width), F32),
             low(2, total_rows, units), low(2, total_rows, units),
             low(4, number, *block), low(2, number, *block), low(number, *block), low(number, *block),
-            low(4, number, *block), low(2, number, *block), low(number, *block), low(number, *block),
+            low(4, number, *block), low(2, number, *block), low(number, *block), low(number, *block), low(number, *block),
             low(number, *block), low(count, number, cap, width), low(2, half_rows, width),
-            low(2, *fold), low(*fold), low(*fold),
+            low(2, *fold), low(*fold), low(*fold), low(count, slab, width),
             DMA((count, 2)), DMA((count, 2)), DMA((number,)), DMA((number,)), DMA((number,)), DMA((number,)),
             DMA((number,)), DMA((number,)), DMA((number,)), DMA((number,)), DMA((number, 2)), DMA((number, 2)),
             DMA((number,)), DMA((number,)), DMA((number, 2)), DMA((number, 2)), DMA((number,)), DMA,
             DMA((count, 2)), DMA((2 * count,)), DMA((2,)), DMA((2,)), DMA, DMA,
-            DMA((splits,)), DMA((splits,)), DMA((2, 4)), DMA((number,)), DMA((2,)), DMA((2,)), DMA((number,)), DMA((number,)),
+            DMA((splits,)), DMA((splits,)), DMA((2, 4)), DMA((number,)), DMA((2,)), DMA((2,)), DMA((number,)), DMA((number,)), DMA((number,)), DMA,
         ],
         compiler_params=pltpu.CompilerParams(has_side_effects=True, vmem_limit_bytes=60 << 20),
     )(by_head, *out_proj, tokens, dispatch, gain, cotangent, *grads, first_proj, second_proj)
 
 
-def experts_weights(rows, grads, active, grad_hidden):
-    _, number, count, cap, width = rows.shape
-    total, units = active.shape[1:]
-
-    def kernel(r_ref, g0_ref, g1_ref, g2_ref, g3_ref, a_ref, h_ref, da, db, done):
-        done[...] = jnp.zeros_like(done)
-        grad = jnp.concatenate([stacked(ref[...]) for ref in (g0_ref, g1_ref, g2_ref, g3_ref)], axis=0)
-        da[0] = lax.dot_general(stacked(r_ref[...]), h_ref[0], CONTRACT_FIRST, preferred_element_type=F32)
-        db[0] = lax.dot_general(a_ref[0], grad, CONTRACT_FIRST, preferred_element_type=F32)
-
-    parts = pl.BlockSpec((4, 1, count, cap, width), lambda e: (0, e, 0, 0, 0))
-    quarter = pl.BlockSpec((count, 1, cap, width), lambda e: (0, e, 0, 0))
-    wide = pl.BlockSpec((1, total, units), lambda e: (e, 0, 0))
-    return pl.pallas_call(
-        kernel,
-        name="experts_weights",
-        grid=(number,),
-        in_specs=[parts, quarter, quarter, quarter, quarter, wide, wide],
-        out_specs=[
-            pl.BlockSpec((1, width, units), lambda e: (e, 0, 0)),
-            pl.BlockSpec((1, units, width), lambda e: (e, 0, 0)),
-            pl.BlockSpec((8, 128), lambda e: (0, 0)),
-        ],
-        out_shape=(
-            jax.ShapeDtypeStruct((number, width, units), F32),
-            jax.ShapeDtypeStruct((number, units, width), F32),
-            jax.ShapeDtypeStruct((8, 128), F32),
-        ),
-        cost_estimate=pl.CostEstimate(
-            flops=4 * number * total * units * width, bytes_accessed=12 * number * units * width, transcendentals=0
-        ),
-        compiler_params=params(False),
-    )(rows, *grads, active, grad_hidden)
-
-
 def after(value, *others):
     return lax.optimization_barrier((value,) + others)[0]
 
 
-def finish_exchange(arrays, parts, out_slab, gain_part, weight):
+def finish_exchange(grads, parts, out_slab, gain_part, weight):
     count = lax.axis_size("ctx")
     depth = count // 2
-    number = len(arrays)
-    lanes = arrays[0].shape[2]
-    width = count * lanes
-    _, rows, wide = parts.shape
-    slab = rows // count
-    pieces_w = 4
-    piece_w = rows // pieces_w
-
-    def kernel(*refs):
-        ins, (p_ref, o_ref, g_ref, w_ref), (tok_out, w_out, o_out, g_out, w_all) = (
-            refs[:number],
-            refs[number : number + 4],
-            refs[number + 4 : number + 9],
-        )
-        (
-            got, held, got_g, sum_g, got_gc,
-            ss, rs, ss_r, rs_r, ss_up, ss_dn, rs_z, ss_a, ss_b, rs_o,
-            ss_of, rs_of, ss_g, rs_g, ss_gc, rs_gc, ss_wx, rs_wx, ss_ws, rs_ws, ss_wf, rs_wf, loc,
-        ) = refs[number + 9 :]
+    part = grads.shape[2]
+    half_rows = grads.shape[1]
+    _, rows, _ = parts.shape
+    pieces = 4
+    piece = rows // pieces
+
+    def kernel(
+        a_ref, p_ref, o_ref, g_ref, w_ref, tok_out, w_out, o_out, g_out, w_all, got, held, got_g, sum_g, got_gc,
+        ss, rs, ss_r, rs_r, ss_up, ss_dn, rs_z, ss_a, ss_b, rs_o,
+        ss_of, rs_of, ss_g, rs_g, ss_gc, rs_gc, ss_wx, rs_wx, ss_ws, rs_ws, ss_wf, rs_wf, loc,
+    ):
         c, f, z, y, x, k = place()
         pair = 2 * z + k
         target = 2 * x + y
@@ -1319,28 +1371,8 @@
         up = (c + 2, f)
         down = (c - 2, f)
 
-        def gain_send(j):
-            return remote(sum_g.at[j], got_g.at[j], ss_g.at[j], rs_g.at[j], sib if j == 0 else xn)
-
-        sum_g[0] = g_ref[...]
-        gain_send(0).start()
-
-        def slab_spread(i):
-            return remote(o_ref, o_out.at[c], ss_of.at[i], rs_of.at[c], ((c + i) % count, f))
-
-        slab_own = pltpu.make_async_copy(o_ref, o_out.at[c], rs_of.at[c])
-
-        def weight_part(shard, i):
-            return w_all.at[shard, pl.ds(i * piece_w, piece_w)]
-
-        def weight_across(i):
-            return remote(w_ref.at[pl.ds(i * piece_w, piece_w)], weight_part(f, i), ss_wx.at[i], rs_wx.at[i], xn)
-
-        def weight_on(i, shard):
-            return remote(weight_part(shard, i), weight_part(shard, i), ss_wf.at[i], rs_wf.at[i], sib)
-
-        weight_share = remote(w_ref, w_all.at[f], ss_ws, rs_ws, sib)
-        weight_own = pltpu.make_async_copy(w_ref, w_all.at[f], loc)
+        def columns(ref, number):
+            return ref.at[:, pl.ds(pl.multiple_of(number * part, part), part)]
 
         peers = [
             (2 * z + 1 - y, f, 2 * x + 1 - y),
@@ -1348,145 +1380,149 @@
             (2 * z + 1 - y, (f + 2) % 4, 2 * (1 - x) + 1 - y),
         ]
 
-        def third(ref, j):
-            return ref.at[:, pl.ds(j * lanes, lanes)]
-
-        def scatter(d, j):
+        def scatter(d):
             cp, fp, shard = peers[d]
-            return remote(third(p_ref.at[shard], j), third(got.at[d], j), ss_r.at[d, j], rs_r.at[d, j], (cp, fp))
-
-        for j in range(3):
-            for d in (2, 1, 0):
-                scatter(d, j).start()
-
-        def there(half, a):
-            return tok_out.at[half, :, pl.ds(pl.multiple_of(a * width + pair * lanes, lanes), lanes)]
-
-        def send(i, half, a):
-            ct = (c + i) % count
-            return remote(
-                ins[a].at[block_at(ct, half, count)], there(half, a), ss.at[i, half, a], rs.at[pair, half, a], (ct, target)
-            )
-
-        def own(half, a):
-            return pltpu.make_async_copy(ins[a].at[block_at(c, half, count)], there(half, a), rs.at[pair, half, a])
-
-        pieces = [(half, a) for a in range(number) for half in range(2)]
-        def send_all(numbers):
-            for i in numbers:
-                for half, a in pieces:
-                    send(i, half, a).start()
-
-        send_all(range(2, count, 2))
-
-        @pl.when(k == y)
-        def _():
-            for half, a in pieces:
-                own(half, a).start()
-
-        @pl.when(k != y)
-        def _():
-            for half, a in pieces:
-                send(0, half, a).start()
-
-        for i in range(pieces_w):
-            weight_across(i).start()
-        weight_share.start()
-        weight_own.start()
-        slab_own.start()
-        gain_send(0).wait_recv()
-        sum_g[1] = sum_g[0] + got_g[0]
-        gain_send(1).start()
-
-        def chain(zb, j, sem, dev):
-            return remote(third(held.at[zb], j), third(held.at[zb], j), sem.at[j], rs_z.at[zb, j], dev)
-
-        def goal(zb, j):
-            return w_out.at[:, pl.ds(pl.multiple_of(j * width + (2 * zb + k) * lanes, lanes), lanes)]
-
-        def own_column(zb, j):
-            return remote(third(held.at[zb], j), goal(zb, j), ss_a.at[zb, j], rs_o.at[2 * zb + k, j], (c, target))
-
-        def own_local(zb, j):
-            return pltpu.make_async_copy(third(held.at[zb], j), goal(zb, j), rs_o.at[2 * zb + k, j])
-
-        def next_column(zb, j):
-            return remote(
-                third(held.at[zb], j), goal(zb, j), ss_b.at[zb, j], rs_o.at[2 * zb + k, j], (2 * z + 1 - y, target)
-            )
-
-        def spread(zb, j):
-            next_column(zb, j).start()
-
-            @pl.when(k == y)
-            def _():
-                own_local(zb, j).start()
-
-            @pl.when(k != y)
-            def _():
-                own_column(zb, j).start()
-
-        for j in range(3):
-            at = pl.ds(j * lanes, lanes)
-            total = p_ref[2 * x + y, :, at].astype(F32)
-            for d in range(3):
-                scatter(d, j).wait_recv()
-                total += got[d, :, at].astype(F32)
-            held[z, :, at] = total.astype(BF)
-
-            @pl.when(z < depth - 1)
-            def _(j=j):
-                chain(z, j, ss_up.at[0], up).start()
-
-            @pl.when(z > 0)
-            def _(j=j):
-                chain(z, j, ss_dn.at[0], down).start()
-
-            spread(z, j)
-        send_all(range(1, count, 2))
-
-        gain_send(1).wait_recv()
-        sum_g[2] = sum_g[1] + got_g[1]
-
-        def gain_spread(i):
-            return remote(sum_g.at[2], got_gc.at[c], ss_gc.at[i], rs_gc.at[c], ((c + i) % count, f))
-
-        for i in range(1, count):
-            gain_spread(i).start()
-            slab_spread(i).start()
+            return remote(p_ref.at[shard], got.at[d], ss_r.at[d], rs_r.at[d], (cp, fp))
+
+        for d in (2, 1, 0):
+            scatter(d).start()
+
+        def weight_part(shard, i):
+            return w_all.at[shard, pl.ds(i * piece, piece)]
+
+        def weight_across(i):
+            return remote(w_ref.at[pl.ds(i * piece, piece)], weight_part(f, i), ss_wx.at[i], rs_wx.at[i], xn)
+
+        def weight_on(i, shard):
+            return remote(weight_part(shard, i), weight_part(shard, i), ss_wf.at[i], rs_wf.at[i], sib)
 
         def weight_pass(i):
             shard = (f + 2) % 4
             remote(weight_part(shard, i), weight_part(shard, i), ss_wf.at[i], rs_wx.at[i], sib).wait_recv()
             weight_on(i, shard).start()
 
+        weight_share = remote(w_ref, w_all.at[f], ss_ws, rs_ws, sib)
+        weight_own = pltpu.make_async_copy(w_ref, w_all.at[f], loc)
+        for i in range(pieces):
+            weight_across(i).start()
+
+        def there(half):
+            return columns(tok_out.at[half], pair)
+
+        def send(i, half):
+            ct = (c + i) % count
+            return remote(a_ref.at[block_at(ct, half, count)], there(half), ss.at[i, half], rs.at[pair, half], (ct, target))
+
+        def send_all(numbers):
+            for i in numbers:
+                for half in range(2):
+                    send(i, half).start()
+
+        send_all(range(2, count, 2))
+
+        def gain_send(j):
+            return remote(sum_g.at[j], got_g.at[j], ss_g.at[j], rs_g.at[j], sib if j == 0 else xn)
+
+        sum_g[0] = g_ref[...]
+        gain_send(0).start()
+
+        def chain(zb, sem, dev):
+            return remote(held.at[zb], held.at[zb], sem, rs_z.at[zb], dev)
+
+        def own_column(zb):
+            return remote(held.at[zb], columns(w_out, 2 * zb + k), ss_a.at[zb], rs_o.at[2 * zb + k], (c, target))
+
+        def own_local(zb):
+            return pltpu.make_async_copy(held.at[zb], columns(w_out, 2 * zb + k), rs_o.at[2 * zb + k])
+
+        def next_column(zb):
+            return remote(
+                held.at[zb], columns(w_out, 2 * zb + k), ss_b.at[zb], rs_o.at[2 * zb + k], (2 * z + 1 - y, target)
+            )
+
+        def spread(zb):
+            next_column(zb).start()
+
+            @pl.when(k == y)
+            def _():
+                own_local(zb).start()
+
+            @pl.when(k != y)
+            def _():
+                own_column(zb).start()
+
+        total = p_ref[2 * x + y].astype(F32)
+        for d in range(3):
+            scatter(d).wait_recv()
+            total += got[d].astype(F32)
+        held[z] = total.astype(BF)
+
+        @pl.when(z < depth - 1)
+        def _():
+            chain(z, ss_up.at[0], up).start()
+
+        @pl.when(z > 0)
+        def _():
+            chain(z, ss_dn.at[0], down).start()
+
+        spread(z)
+        send_all(range(1, count, 2))
+
+        @pl.when(k == y)
+        def _():
+            for half in range(2):
+                pltpu.make_async_copy(a_ref.at[block_at(c, half, count)], there(half), rs.at[pair, half]).start()
+
+        @pl.when(k != y)
+        def _():
+            for half in range(2):
+                send(0, half).start()
+
+        weight_share.start()
+        weight_own.start()
+        gain_send(0).wait_recv()
+        sum_g[1] = sum_g[0] + got_g[0]
+        gain_send(1).start()
+
+        def slab_spread(i):
+            return remote(o_ref, o_out.at[c], ss_of.at[i], rs_of.at[c], ((c + i) % count, f))
+
+        def gain_spread(i):
+            return remote(sum_g.at[2], got_gc.at[c], ss_gc.at[i], rs_gc.at[c], ((c + i) % count, f))
+
+        slab_own = pltpu.make_async_copy(o_ref, o_out.at[c], rs_of.at[c])
+        slab_own.start()
         for hop in range(1, depth):
-            for j in range(3):
-
-                @pl.when(z - hop >= 0)
-                def _(hop=hop, j=j):
-                    chain(z - hop, j, ss_up.at[hop], sib).wait_recv()
-
-                    @pl.when(z < depth - 1)
-                    def _():
-                        chain(z - hop, j, ss_up.at[hop], up).start()
-
-                    spread(z - hop, j)
-
-                @pl.when(z + hop <= depth - 1)
-                def _(hop=hop, j=j):
-                    chain(z + hop, j, ss_dn.at[hop], sib).wait_recv()
-
-                    @pl.when(z > 0)
-                    def _():
-                        chain(z + hop, j, ss_dn.at[hop], down).start()
-
-                    spread(z + hop, j)
+
+            @pl.when(z - hop >= 0)
+            def _(hop=hop):
+                chain(z - hop, ss_up.at[hop], sib).wait_recv()
+
+                @pl.when(z < depth - 1)
+                def _():
+                    chain(z - hop, ss_up.at[hop], up).start()
+
+                spread(z - hop)
+
+            @pl.when(z + hop <= depth - 1)
+            def _(hop=hop):
+                chain(z + hop, ss_dn.at[hop], sib).wait_recv()
+
+                @pl.when(z > 0)
+                def _():
+                    chain(z + hop, ss_dn.at[hop], down).start()
+
+                spread(z + hop)
 
             weight_pass(hop - 1)
-        for i in range(depth - 1, pieces_w):
+            if hop == 1:
+                gain_send(1).wait_recv()
+                sum_g[2] = sum_g[1] + got_g[1]
+                for i in range(1, count):
+                    gain_spread(i).start()
+                    slab_spread(i).start()
+        for i in range(depth - 1, pieces):
             weight_pass(i)
-
         total_g = sum_g[2]
         for i in range(1, count):
             cs = (c + i) % count
@@ -1496,22 +1532,21 @@
 
         gain_send(0).wait_send()
         gain_send(1).wait_send()
-        for i in range(pieces_w):
+        for i in range(pieces):
             weight_across(i).wait_send()
             weight_on(i, (f + 2) % 4).wait_send()
             remote(weight_part(0, i), weight_part(0, i), ss_wf.at[i], rs_wf.at[i], sib).wait_recv()
         weight_share.wait()
         weight_own.wait()
         for d in range(3):
-            for j in range(3):
-                scatter(d, j).wait_send()
-        for half, a in pieces:
-            for other in range(count):
-                cols = pl.ds(a * width + other * lanes, lanes)
-                remote(ins[a].at[0], tok_out.at[half, :, cols], ss.at[0, half, a], rs.at[other, half, a], sib).wait_recv()
+            scatter(d).wait_send()
+        for other in range(count):
+            for half in range(2):
+                remote(a_ref.at[0], columns(tok_out.at[half], other), ss.at[0, half], rs.at[other, half], sib).wait_recv()
+            remote(held.at[0], columns(w_out, other), ss_a.at[0], rs_o.at[other], sib).wait_recv()
         for i in range(1, count):
-            for half, a in pieces:
-                send(i, half, a).wait_send()
+            for half in range(2):
+                send(i, half).wait_send()
             gain_spread(i).wait_send()
             slab_spread(i).wait_send()
             cs = (c + i) % count
@@ -1520,72 +1555,114 @@
 
         @pl.when(k != y)
         def _():
-            for half, a in pieces:
-                send(0, half, a).wait_send()
+            for half in range(2):
+                send(0, half).wait_send()
             for zb in range(depth):
-                for j in range(3):
-                    own_column(zb, j).wait_send()
-
-        for other in range(count):
-            for j in range(3):
-                remote(
-                    third(held.at[0], j), third(w_out, j * count + other), ss_a.at[0, j], rs_o.at[other, j], sib
-                ).wait_recv()
+                own_column(zb).wait_send()
+
+        for zb in range(depth):
+            next_column(zb).wait_send()
         for hop in range(depth):
 
             @pl.when((z < depth - 1) & (z - hop >= 0))
             def _(hop=hop):
-                for j in range(3):
-                    chain(z - hop, j, ss_up.at[hop], up).wait_send()
+                chain(z - hop, ss_up.at[hop], up).wait_send()
 
             @pl.when((z > 0) & (z + hop <= depth - 1))
             def _(hop=hop):
-                for j in range(3):
-                    chain(z + hop, j, ss_dn.at[hop], down).wait_send()
-
-        for zb in range(depth):
-            for j in range(3):
-                next_column(zb, j).wait_send()
+                chain(z + hop, ss_dn.at[hop], down).wait_send()
 
     vmem = pl.BlockSpec(memory_space=pltpu.VMEM)
     eighth = gain_part.shape
     return pl.pallas_call(
         kernel,
         name="finish_exchange",
-        cost_estimate=lasting(70),
+        cost_estimate=lasting(60),
         out_shape=(
-            jax.ShapeDtypeStruct((2, arrays[0].shape[1], number * width), BF),
-            jax.ShapeDtypeStruct((rows, 3 * width), BF),
-            jax.ShapeDtypeStruct((count, slab, width), BF),
+            jax.ShapeDtypeStruct((2, half_rows, count * part), BF),
+            jax.ShapeDtypeStruct((rows, count * part), BF),
+            jax.ShapeDtypeStruct((count,) + out_slab.shape, BF),
             jax.ShapeDtypeStruct(eighth, F32),
             jax.ShapeDtypeStruct((4,) + weight.shape, BF),
         ),
-        in_specs=[ANY] * number + [vmem, ANY, vmem, ANY],
+        in_specs=[vmem] * 5,
         out_specs=(ANY, ANY, ANY, vmem, ANY),
         scratch_shapes=[
-            pltpu.VMEM((3, rows, wide), BF),
-            pltpu.VMEM((depth, rows, wide), BF),
+            pltpu.VMEM((3, rows, part), BF),
+            pltpu.VMEM((depth, rows, part), BF),
             pltpu.VMEM((2,) + eighth, F32),
             pltpu.VMEM((3,) + eighth, F32),
             pltpu.VMEM((count,) + eighth, F32),
-            DMA((count, 2, number)), DMA((count, 2, number)),
-            DMA((3, 3)), DMA((3, 3)), DMA((depth, 3)), DMA((depth, 3)), DMA((depth, 3)),
-            DMA((depth, 3)), DMA((depth, 3)), DMA((count, 3)),
+            DMA((count, 2)), DMA((count, 2)), DMA((3,)), DMA((3,)), DMA((depth,)), DMA((depth,)), DMA((depth,)),
+            DMA((depth,)), DMA((depth,)), DMA((count,)),
             DMA((count,)), DMA((count,)), DMA((2,)), DMA((2,)), DMA((count,)), DMA((count,)),
-            DMA((pieces_w,)), DMA((pieces_w,)), DMA, DMA, DMA((pieces_w,)), DMA((pieces_w,)), DMA,
+            DMA((pieces,)), DMA((pieces,)), DMA, DMA, DMA((pieces,)), DMA((pieces,)), DMA,
         ],
         compiler_params=params(),
-    )(*arrays, parts, out_slab, gain_part, weight)
-
-
-def slots_of(routes):
-    tokens = routes.shape[0]
-    chosen = routes[:, None] == jnp.arange(EXPERTS, dtype=jnp.int32)[None, :]
-    earlier = (jnp.arange(tokens)[:, None] >= jnp.arange(tokens)[None, :]).astype(BF)
-    running = jnp.dot(earlier, chosen.astype(BF), preferred_element_type=F32)
-    rank = jnp.sum(jnp.where(chosen, running, 0.0), axis=1).astype(jnp.int32) - 1
-    slot = routes * CAP + rank
-    return (jnp.arange(EXPERTS * CAP, dtype=jnp.int32)[:, None] == slot[None, :]).astype(BF)
+    )(grads, parts, out_slab, gain_part, weight)
+
+
+def finish_local(
+    grad_projected, projection, tokens, gain, grad_middle, middle, dispatch, expert_rows, weight_grad, weight, own_gain, out_slabs
+):
+    rows, width = tokens.shape
+    quarter, wide = weight.shape
+    lanes = 128
+    part = 3 * lanes
+    count = wide // part
+
+    def kernel(p_ref, w_ref, x_ref, g_ref, m_ref, mid_ref, d_ref, e_ref, wg_ref, wl_ref, og_ref, o_ref, block, token, wout, gout, oout, acc):
+        j = pl.program_id(0)
+        acc[j] = lax.dot_general(p_ref[...], w_ref[0], CONTRACT_LAST, preferred_element_type=F32)
+
+        @pl.when(j == 0)
+        def _():
+            summed = lax.dot_general(d_ref[...], e_ref[...], CONTRACT_FIRST, preferred_element_type=F32)
+            block[...] = (mid_ref[...] + summed).astype(BF)
+            oout[...] = o_ref[...].astype(F32)
+
+        @pl.when(j == 1)
+        def _():
+            total = jnp.zeros((quarter, 1), F32)
+            for number in range(count):
+                for kind in range(3):
+                    at = number * part + kind * lanes
+                    value = wg_ref[:, at : at + lanes].astype(F32)
+                    to = (kind * count + number) * lanes
+                    wout[:, to : to + lanes] = value
+                    total += jnp.sum(value * wl_ref[:, at : at + lanes].astype(F32), axis=1, keepdims=True)
+            gout[...] = total / og_ref[...]
+
+        @pl.when(j == 3)
+        def _():
+            hat, inverse = statistics(x_ref[...].astype(F32))
+            scaled = jnp.concatenate([acc[i] for i in range(4)], axis=1) * g_ref[...]
+            mean_grad = jnp.mean(scaled, axis=1, keepdims=True)
+            mean_proj = jnp.mean(scaled * hat, axis=1, keepdims=True)
+            token[...] = m_ref[...] + inverse * (scaled - mean_grad - hat * mean_proj)
+
+    def whole(value):
+        return pl.BlockSpec(value.shape, lambda j: (0,) * value.ndim)
+
+    shapes = (
+        jax.ShapeDtypeStruct((rows, width), BF),
+        jax.ShapeDtypeStruct((rows, width), F32),
+        jax.ShapeDtypeStruct((quarter, wide), F32),
+        jax.ShapeDtypeStruct((quarter, 1), F32),
+        jax.ShapeDtypeStruct((quarter, width), F32),
+    )
+    rest = (tokens, gain, grad_middle, middle, dispatch, expert_rows, weight_grad, weight, own_gain, out_slabs)
+    return pl.pallas_call(
+        kernel,
+        name="finish_local",
+        cost_estimate=lasting(9),
+        grid=(4,),
+        in_specs=[whole(grad_projected), pl.BlockSpec((1, quarter, wide), lambda j: (j, 0, 0))] + [whole(v) for v in rest],
+        out_specs=[whole(v) for v in shapes],
+        out_shape=shapes,
+        scratch_shapes=[pltpu.VMEM((4, rows, quarter), F32)],
+        compiler_params=params(False),
+    )(grad_projected, projection, *rest)
 
 
 def by_head_pairs(
@@ -1600,77 +1677,78 @@
     f = lax.axis_index("fsdp")
     lanes = 2 * (width // HEADS)
     shard_rows = width // 4
-    pick = (((0,), (0,)), ((), ()))
-    turn = (((1,), (1,)), ((), ()))
-    start_x = tokens.reshape(rows, width).astype(F32)
+    own_tokens = tokens.reshape(rows, width)
     cotangent = grad_output.reshape(rows, width)
-    qkv_low = query_key_value_weight.astype(BF)
-    first_normed, hat_one, inverse_one = norm_forward(start_x, gain_one)
-    normed = first_normed.astype(BF)
-    stream, starts, columns = gather_stream(
-        normed.reshape(2, half_rows, width), doc_starts.reshape(2, half_rows), qkv_low
-    )
-    dispatch = slots_of(expert_ids.reshape(rows))
-    own_experts = EXPERTS // count
-    shape = (count, own_experts, CAP, width)
-    send_grads = jnp.dot(dispatch, cotangent, preferred_element_type=F32).astype(BF).reshape(shape)
-    grads_near = lax.all_to_all(send_grads, "ctx", split_axis=0, concat_axis=0, tiled=True)
-    grads_near = after(grads_near, stream)
-    out_own = output_weight_matrix.astype(BF)
+    gain_row = gain_one.reshape(1, width)
+    stream, starts, columns, out_beside, out_far, out_diagonal, grads_near, qkv_low, out_own, dispatch = gather_stream(
+        own_tokens.reshape(2, half_rows, width),
+        gain_row,
+        expert_ids.reshape(1, rows),
+        cotangent,
+        doc_starts.reshape(2, half_rows),
+        query_key_value_weight,
+        output_weight_matrix,
+    )
     grads_far = swap(grads_near, "fsdp", 2)
-    out_far = swap(out_own, "fsdp", 2)
-    out_far = after(out_far, stream)
-    out_beside = [swap(after(out_own, stream), "fsdp", 1), swap(out_far, "fsdp", 1)]
     stream = stream.reshape(length, width)
     start_row = jnp.concatenate([starts[:, 0].reshape(-1), starts[::-1, 1].reshape(-1)])[None]
     numbers = jnp.min(start_row.reshape(-1, TILE), axis=1) // TILE
-    query, key, value, mixed16, mixed32, logs = attend_forward(stream, columns, start_row, numbers, scale)
+    qkv, mixed16, mixed32, logs = attend_forward(stream, columns, start_row, numbers, scale)
     grads_far = after(grads_far, mixed16)
-    grads_beside = [swap(grads_near, "fsdp", 1), swap(grads_far, "fsdp", 1)]
-    out_proj = [out_own, out_beside[0], out_far, out_beside[1]]
-    gain_row = gain_two.reshape(1, width)
-    all_grads = [grads_near, grads_beside[0], grads_far, grads_beside[1]]
-    (
-        mixed, middle, all_rows, active, grad_hidden, out_own, out_send, grad_heads, grad_middle, grad_gain_two, out_shard,
-    ) = experts_exchange(
-        mixed16.reshape(2 * count, half_rows, lanes), out_proj, tokens.reshape(rows, width), dispatch, gain_row, cotangent,
-        all_grads, expert_in, expert_out,
-    )
-    slots = (EXPERTS * CAP, width)
-    out_got = swap(out_send, "fsdp", 2)
-    grad_in, grad_outw, done = experts_weights(after(all_rows, out_send), all_grads, active, grad_hidden)
-    out_sum = (out_own.astype(F32) + out_got.astype(F32) + done[0, 0]).astype(BF)
+    all_grads = [grads_near, swap(grads_near, "fsdp", 1), grads_far, swap(grads_far, "fsdp", 1)]
+    mixed, middle, all_rows, active, grad_hidden, grad_heads, grad_middle, grad_gain_two, later = experts_exchange(
+        mixed16.reshape(2 * count, half_rows, lanes),
+        [out_own, out_beside, out_far, out_diagonal],
+        own_tokens,
+        dispatch,
+        gain_two.reshape(1, width),
+        cotangent,
+        all_grads,
+        expert_in,
+        expert_out,
+    )
+    home = lax.all_to_all(later, "ctx", split_axis=0, concat_axis=0, tiled=True)
+    own_grads, parts, grad_in, grad_outw = backward_local(
+        qkv,
+        after(grad_heads, later).reshape(length, lanes),
+        mixed32,
+        logs,
+        start_row,
+        numbers,
+        scale,
+        stream,
+        all_rows,
+        all_grads,
+        active,
+        grad_hidden,
+    )
+    home = after(home, own_grads)
     slab_rows = shard_rows // count
-    both_send = jnp.concatenate([out_shard.reshape(count, slab_rows, width), out_sum.reshape(count, -1, width)], axis=1)
-    both = lax.all_to_all(both_send, "ctx", split_axis=0, concat_axis=0, tiled=True)
-    grad_q, grad_k, grad_v = attend_backward(
-        query, key, value, after(grad_heads, both_send).reshape(length, lanes), mixed32, logs, start_row, numbers, scale
-    )
-    both = after(both, grad_q)
-    out_slab = jnp.sum(both[:, :slab_rows].astype(F32), axis=0).astype(BF)
-    back_rows = both[:, slab_rows:]
-    blocks = (2 * count, half_rows, lanes)
-    own_grads = jnp.concatenate([grad_q, grad_k, grad_v], axis=1)
-    parts = lax.dot_general(stream, own_grads, pick, preferred_element_type=F32).astype(BF)
+    out_slab = jnp.sum(home[:, :slab_rows].astype(F32), axis=0).astype(BF)
+    back_rows = home[:, slab_rows:]
     grad_projected, weight_grad, shard_out, gain_sum, projection = finish_exchange(
-        [grad_q.reshape(blocks), grad_k.reshape(blocks), grad_v.reshape(blocks)],
+        own_grads.reshape(2 * count, half_rows, 3 * lanes),
         parts.reshape(4, shard_rows, 3 * lanes),
         out_slab,
         grad_gain_two,
         qkv_low,
     )
-    grad_projected = grad_projected.reshape(rows, 3 * width)
-    projection = projection.reshape(width, 3 * width)
-    back_rows = after(back_rows, weight_grad)
-    expert_sum = lax.dot_general(dispatch, back_rows.reshape(slots), pick, preferred_element_type=F32)
-    block_out = (middle + expert_sum).astype(BF)
-    weight_grad = weight_grad.astype(F32)
-    shard_out = shard_out.reshape(shard_rows, width).astype(F32)
-    grad_normed = lax.dot_general(grad_projected, projection, turn, preferred_element_type=F32)
-    grad_in_norm, _ = norm_backward(grad_normed[None], hat_one[None], inverse_one[None], gain_one)
-    grad_start = grad_middle + grad_in_norm[0]
-    own_gain = lax.dynamic_slice(gain_one, (f * shard_rows,), (shard_rows,))
-    shard_gain_one = jnp.sum(weight_grad * qkv_low.astype(F32), axis=1) / own_gain
+    own_gain = lax.dynamic_slice(gain_one, (f * shard_rows,), (shard_rows,)).reshape(shard_rows, 1)
+    block_out, grad_start, weight_grad, shard_gain_one, shard_out = finish_local(
+        grad_projected.reshape(rows, 3 * width),
+        projection,
+        own_tokens,
+        gain_row,
+        grad_middle,
+        middle,
+        dispatch,
+        back_rows.reshape(EXPERTS * CAP, width),
+        weight_grad,
+        qkv_low,
+        own_gain,
+        shard_out.reshape(shard_rows, width),
+    )
+    shard_gain_one = shard_gain_one.reshape(shard_rows)
     shard_gain_two = lax.dynamic_slice(gain_sum.reshape(width), (f * shard_rows,), (shard_rows,))
     return (
         block_out.reshape(tokens.shape),

time: 395 us -> 366 us (0.927)
  Pallas kernels: 316 us -> 340 us
  waiting for transfers between devices: 24.2 us -> 3.76 us
  matrix products: 15.2 us -> 0 us
  other arithmetic: 17.3 us -> 3.53 us
    dot_general x5 -> x0, matrix products: 15.2 us -> none  [the longest x1 5.86 us: by_head_pairs(): lax.dot_general(stream, own_grads, pick, preferred_element_type=F32)]
    all_to_all x2 -> x1, waiting for transfers between devices: 14.3 us -> 0.01 us  [by_head_pairs(): home = lax.all_to_all(later, 'ctx', split_axis=0, concat_axis=0, tiled=True)]
    pallas_call x1, Pallas kernels: 58 us -> 69 us  [gather_stream(): pl.pallas_call(kernel, name='gather_stream', cost_estimate=lasting(50), o...]
    pallas_call x1, Pallas kernels: 115 us -> 125 us  [experts_exchange(): pl.pallas_call(kernel, name='experts_exchange', cost_estimate=lasting(100...]
    convert_element_type x5 -> x0, other arithmetic: 7.54 us -> none  [the longest x1 3.26 us: by_head_pairs(): qkv_low = query_key_value_weight.astype(BF)]
    ppermute x7 -> x3, waiting for transfers between devices: 9.98 us -> 3.75 us  [swap(): return lax.ppermute(value, axis, [(i, i ^ bit) for i in range(size)])]
    pallas_call x3, Pallas kernels: 122 us -> 127 us  [the longest x1 77.9 us: finish_exchange(): pl.pallas_call(kernel, name='finish_exchange', cost_estimate=lasting(60),...]
    all_to_all x2 -> x1, starting transfers between devices: 10.3 us -> 8.26 us  [by_head_pairs(): home = lax.all_to_all(later, 'ctx', split_axis=0, concat_axis=0, tiled=True)]
  transfers between devices with their start and end apart: 9 -> 4, of which waited for: 3 -> 2; matrix products, arithmetic and copies ran while one was open for 4% -> 1% of each run, Pallas kernels for 31% -> 15%
where the time goes in v5:
time: 366 us; the launch traced here: 365 us
  Pallas kernels  340 us (93%)
  starting transfers between devices  11.4 us (3%)
  local copies, waits for them, and re-layouts  5.83 us (2%)
  waiting for transfers between devices  3.76 us (1%)
    pallas_call x1, Pallas kernels, experts_exchange(): pl.pallas_call(kernel, name='experts_exchange', cost_estimate=lasting(100...  125 us
    pallas_call x1, Pallas kernels, finish_exchange(): pl.pallas_call(kernel, name='finish_exchange', cost_estimate=lasting(60),...  77.9 us
    pallas_call x1, Pallas kernels, gather_stream(): pl.pallas_call(kernel, name='gather_stream', cost_estimate=lasting(50), o...  69 us
    pallas_call x1, Pallas kernels, backward_local(): pl.pallas_call(kernel, name='backward_local', cost_estimate=lasting(30),...  37.4 us
    pallas_call x1, Pallas kernels, attend_forward(): pl.pallas_call(kernel, name='attend_forward', cost_estimate=lasting(22),...  19.2 us
    pallas_call x1, Pallas kernels, finish_local(): pl.pallas_call(kernel, name='finish_local', cost_estimate=lasting(9), gri...  12.1 us
    all_to_all x1, starting transfers between devices, by_head_pairs(): home = lax.all_to_all(later, 'ctx', split_axis=0, concat_axis=0, tiled=True)  8.26 us
  transfers between devices with their start and end apart: 4, of which 2 were waited for; matrix products, arithmetic and copies ran while one was open for 1% of the time, Pallas kernels for 15%

profile of v5, /device:TPU:1, one launch (start us, length us, event | category | flops | bytes accessed | tf_op | source)
XLA Modules:
  0.0 365.4 jit_solution(12756234266253676558)
XLA Ops:
  0.6 69.0 %gather_stream.1 = (bf16[16,128,1024]{2,1,0:T(8,128)(2,1)}, s32[8,2,128]{2,1,0:T(2,128)}, bf16[1024,384]{1,0:T(8,128)(2,1)}, bf16[256,1024]{1,0:T(8,128)(2,1)}, ...) custom-call(bf16[2,128,1024]{2,1,0:T(8,128)(2,1)} %bitcast.24, ...), custom_call_target="tpu_custom_call" | custom-call | bytes 165000000 | tf_op jit(solution)/shard_map/gather_stream/pallas_call | solution.py:690
  69.7 1.3 collective-permute-start.1
  70.9 0.6 collective-permute-start
  71.6 0.8 fusion
  72.4 0.1 add_reduce_fusion
  72.5 0.6 pad_add_fusion
  73.1 0.5 and_select_fusion.first
  73.7 19.2 %attend_forward.1 = (bf16[2048,384]{1,0:T(8,128)(2,1)}, bf16[2048,128]{1,0:T(8,128)(2,1)}, f32[128,2048]{1,0:T(8,128)}, f32[2,2048]{1,0:T(2,128)}) custom-call(s32[8]{0:T(128)} %and_select_fusion.first, bf16[2048,1024]{1,0:T(8,128)(2,1)} %bitcast.22, bf16[1024,384]{1,0:T(8,128)(2,1)} %get-tuple-element.49.w_ref, s32[1,2048]{1,0:T(1,128)} %bitcast.36), custom_call_target="tpu_custom_call" | custom-call | bytes 72600000 | tf_op jit(solution)/shard_map/attend_forward/pallas_call | solution.py:775
  92.8 1.5 collective-permute-done.1.g2_ref
  94.3 0.0 copy-start
  94.3 1.2 collective-permute-start.2
  95.5 0.0 collective-permute-done.g1_ref
  95.5 0.0 copy-start.1
  95.5 2.3 collective-permute-done.2.g3_ref
  97.8 0.0 copy-start.2
  97.8 1.0 copy-done.2
  98.8 0.0 copy-done
  98.8 0.0 copy-done.1
  98.8 124.6 %experts_exchange.1 = (bf16[2,128,1024]{2,1,0:T(8,128)(2,1)}, f32[256,1024]{1,0:T(8,128)}, bf16[4,8,8,8,1024]{4,3,2,1,0:T(8,128)(2,1)}, bf16[8,256,1024]{2,1,0:T...) custom-call(bf16[16,128,128]{2,1,0:T(8,128)(2,1)} %bitcast.33, ...), custom_call_target="tpu_custom_call" | custom-call | bytes 330000000 | tf_op jit(solution)/shard_map/experts_exchange/pallas_call | solution.py:1313
  223.5 8.3 %all-to-all-start = ((bf16[8,96,1024]{2,1,0:T(8,128)(2,1)}), bf16[8,96,1024]{2,1,0:T(8,128)(2,1)S(1)}, u32[]{:S(2)}, u32[]{:S(2)}) async-start(bf16[8,96,1024]{2,1,0:T(8,128)(2,1)} %get-tuple-element.60), calls=%async_computation | async-start | bytes 3145728 | tf_op jit(solution)/shard_map/all_to_all | solution.py:1710
  231.7 0.8 dynamic_slice.8
  232.5 0.8 copy.18.og_ref
  233.3 37.4 %backward_local.1 = (bf16[2048,384]{1,0:T(8,128)(2,1)}, bf16[1024,384]{1,0:T(8,128)(2,1)}, f32[8,1024,1024]{2,1,0:T(8,128)}, f32[8,1024,1024]{2,1,0:T(8,128)}) custom-call(s32[8]{0:T(128)} %and_select_fusion.first, bf16[2048,384]{1,0:T(8,128)(2,1)} %get-tuple-element.50.q_ref.k_ref.v_ref, bf16[2048,384]{1,0:T(8,128)(2,1)} %get-tuple-element.50.q_ref.k_ref.v_ref, ...), custom_call_target="tpu_custom_call" | custom-call | bytes 99000000 | tf_op jit(solution)/shard_map/backward_local/pallas_call | solution.py:877
  270.7 0.0 all-to-all-done
  270.7 0.7 slice_reduce_fusion.o_ref
  271.4 1.2 slice.15
  272.6 77.9 %finish_exchange.1 = (bf16[2,128,3072]{2,1,0:T(8,128)(2,1)}, bf16[256,3072]{1,0:T(8,128)(2,1)}, bf16[8,32,1024]{2,1,0:T(8,128)(2,1)}, f32[1,1024]{1,0:T(1,128)}, bf16[4,256,3072]{2,1,0:T(8,128)(2,1)}) custom-call(bf16[16,128,384]{2,1,0:T(8,128)(2,1)} %bitcast.31, bf16[4,256,384]{2,1,0:T(8,128)(2,1)} %bitcast.32, bf16[32,1024]{1,0:T(8,128)(2,1)} %slice_reduce_fusion.o_ref, ...), custom_call_target="tpu_custom_call" | custom-call | bytes 198000000 | tf_op jit(solution)/shard_map/finish_exchange/pallas_call | solution.py:1577
  350.5 1.2 constant_dynamic-slice_fusion
  351.8 12.1 %finish_local.1 = (bf16[256,1024]{1,0:T(8,128)(2,1)}, f32[256,1024]{1,0:T(8,128)}, f32[256,3072]{1,0:T(8,128)}, f32[256,1]{1,0:T(8,128)}, f32[256,1024]{1,0:T(8,128)}) custom-call(bf16[256,3072]{1,0:T(8,128)(2,1)} %bitcast.30, bf16[4,256,3072]{2,1,0:T(8,128)(2,1)} %get-tuple-element.73.w_ref, bf16[256,1024]{1,0:T(8,128)(2,1)} %bitcast.26, ...), custom_call_target="tpu_custom_call" | custom-call | bytes 29700000 | tf_op jit(solution)/shard_map/finish_local/pallas_call | solution.py:1655
  363.8 1.6 reduce.3
  (4 shorter events, 0.0 us)
Async XLA Ops:
  69.7 24.6 %collective-permute-start.1 = (bf16[8,8,8,1024]{3,2,1,0:T(8,128)(2,1)}, bf16[8,8,8,1024]{3,2,1,0:T(8,128)(2,1)S(1)}, u32[]{:S(2)}, u32[]{:S(2)}) collective-permute-start(bf16[8,8,8,1024]{3,2,1,0:T(8,128)(2,1)} %get-tuple-element.57.g0_ref), channel_id=1, source_target_pairs={{0,2},{1,3},{2,0},{3,1},{4,6},{5,7},{6,4},{7,5},{8,10},{9,11},{10,... | collective-permute-start | bytes 3145736 | tf_op jit(solution)/shard_map/ppermute | solution.py:488
  70.9 24.6 %collective-permute-start = (bf16[8,8,8,1024]{3,2,1,0:T(8,128)(2,1)}, bf16[8,8,8,1024]{3,2,1,0:T(8,128)(2,1)S(1)}, u32[]{:S(2)}, u32[]{:S(2)}) collective-permute-start(bf16[8,8,8,1024]{3,2,1,0:T(8,128)(2,1)} %get-tuple-element.57.g0_ref), channel_id=1, source_target_pairs={{0,1},{1,0},{2,3},{3,2},{4,5},{5,4},{6,7},{7,6},{8,9},{9,8},{10,11... | collective-permute-start | bytes 3145736 | tf_op jit(solution)/shard_map/ppermute | solution.py:488
  94.3 4.5 %copy-start = (bf16[8,8,8,1024]{3,2,1,0:T(8,128)(2,1)}, bf16[8,8,8,1024]{3,2,1,0:T(8,128)(2,1)S(1)}, u32[]{:S(2)}) copy-start(bf16[8,8,8,1024]{3,2,1,0:T(8,128)(2,1)S(1)} %collective-permute-done.1.g2_ref) | copy-start | bytes 3145732
  94.3 3.5 collective-permute-start.2
  95.5 3.3 copy-start.1
  97.8 1.0 copy-start.2
  223.5 47.3 %all-to-all-start = ((bf16[8,96,1024]{2,1,0:T(8,128)(2,1)}), bf16[8,96,1024]{2,1,0:T(8,128)(2,1)S(1)}, u32[]{:S(2)}, u32[]{:S(2)}) async-start(bf16[8,96,1024]{2,1,0:T(8,128)(2,1)} %get-tuple-element.60), calls=%async_computation | async-start | bytes 3145728 | tf_op jit(solution)/shard_map/all_to_all | solution.py:1710

commit v6 on v5

--- a/solution.py
+++ b/solution.py
@@ -507,8 +507,8 @@
     own_experts = EXPERTS // count
 
     def kernel(
-        x_ref, g_ref, e_ref, c_ref, s_ref, wf_ref, of_ref, tok, st, cols, beside, far, diagonal, got, w_ref, o_ref, hot,
-        n_ref, d_ref, rs_t, ss_p, ss_up, ss_dn, ss_sib, rs_s, ss_s, rs_w, ss_w, ss_o, rs_o, ss_d, rs_d,
+        x_ref, g_ref, e_ref, c_ref, s_ref, wf_ref, of_ref, tok, st, cols, beside, far, diagonal, d_ref, w_ref, o_ref, hot,
+        n_ref, rs_t, ss_p, ss_up, ss_dn, ss_sib, rs_s, ss_s, rs_w, ss_w, ss_o, rs_o,
     ):
         c, f, z, y, x, k = place()
         sib = (c, f + 1 - 2 * k)
@@ -575,10 +575,6 @@
         matrix_on = remote(far, diagonal, ss_o.at[2], rs_o.at[2], sib)
         matrix_far.start()
         matrix_beside.start()
-
-        def slots_send(i):
-            ct = (c + i) % count
-            return remote(d_ref.at[ct], got.at[c], ss_d.at[i], rs_d.at[c], (ct, f))
 
         def copy_block(zb, h, ss, dev):
             b = block_at(2 * zb + k, h, count)
@@ -616,9 +612,6 @@
                         d_ref[...] = (
                             jnp.dot(hot[...], c_ref[...], preferred_element_type=F32).astype(BF).reshape(d_ref.shape)
                         )
-                        for i in range(1, count):
-                            slots_send(i).start()
-                        pltpu.make_async_copy(d_ref.at[c], got.at[c], rs_d.at[c]).start()
                     continue
 
                 @pl.when(z - j >= 0)
@@ -657,10 +650,6 @@
         matrix_far.wait_send()
         matrix_beside.wait()
         matrix_on.wait()
-        for i in range(count):
-            if i:
-                slots_send(i).wait_send()
-            remote(d_ref.at[i], got.at[i], ss_d.at[i], rs_d.at[i], sib).wait_recv()
 
         @pl.when(jnp.logical_not(holder))
         def _():
@@ -702,11 +691,11 @@
             jax.ShapeDtypeStruct((EXPERTS * CAP, own_rows), BF),
         ),
         in_specs=[pl.BlockSpec(memory_space=pltpu.VMEM)] * 7,
-        out_specs=(ANY,) * 7 + (pl.BlockSpec(memory_space=pltpu.VMEM),) * 3,
+        out_specs=(ANY,) * 6 + (pl.BlockSpec(memory_space=pltpu.VMEM),) * 4,
         scratch_shapes=[
-            pltpu.VMEM((2, half_rows, width), BF), pltpu.VMEM((count, own_experts, CAP, width), BF),
+            pltpu.VMEM((2, half_rows, width), BF),
             DMA((2 * count,)), DMA((2,)), DMA((depth, 2)), DMA((depth, 2)), DMA((depth, 2)),
-            DMA((count,)), DMA((count,)), DMA((4,)), DMA((3,)), DMA((3,)), DMA((3,)), DMA((count,)), DMA((count,)),
+            DMA((count,)), DMA((count,)), DMA((4,)), DMA((3,)), DMA((3,)), DMA((3,)),
         ],
         compiler_params=params(),
     )(tokens, gain, routes, cotangent, starts, weight, matrix)
@@ -924,7 +913,7 @@
 CUBIC = 0.044715
 
 
-def experts_exchange(by_head, out_proj, tokens, dispatch, gain, cotangent, grads, first_proj, second_proj):
+def experts_exchange(by_head, out_proj, tokens, dispatch, gain, cotangent, near, first_proj, second_proj):
     count = lax.axis_size("ctx")
     half_rows, lanes = by_head.shape[1:]
     rows, width = tokens.shape
@@ -937,12 +926,12 @@
     part_units = units // splits
 
     def kernel(
-        a_ref, w0_ref, w1_ref, w2_ref, w3_ref, x_ref, d_ref, g_ref, c_ref, g0_ref, g1_ref, g2_ref, g3_ref, first_ref, second_ref,
-        mixed, middle, rows_out, active_out, hidden_out, heads, grad_middle, gain_out, later,
+        a_ref, w0_ref, w1_ref, w2_ref, w3_ref, x_ref, d_ref, g_ref, c_ref, g0_ref, first_ref, second_ref,
+        mixed, middle, rows_out, g1_ref, g2_ref, g3_ref, active_out, hidden_out, heads, grad_middle, gain_out, later,
         routed, slots, rows_v, g_buf, first_buf, second_buf, active_v, hidden_v, back_v, back_near, back_far, back_got,
         out_v, out_near, own_v, far_v, out_got, summed, home_got, back, shard_near, shard_far, shard_got, shard_v,
         ss_m, rs_m, ss_1, rs_1, ss_x, rs_x, ss_s, rs_s, ss_f, rs_f, ss_bn, rs_bn, ss_bf, rs_bf, ss_on, rs_on, ss_h, rs_h,
-        ss_t, rs_t, ss_n, rs_n, ss_w, rs_w, l_first, l_second, l_g, st_r, st_a, st_h, st_o, ss_of, rs_of, st_w,
+        ss_t, rs_t, ss_n, rs_n, ss_w, rs_w, ss_g, rs_g, l_first, l_second, l_g, st_r, st_a, st_h, st_o, ss_of, rs_of, st_w,
     ):
         c, f, z, y, x, k = place()
         sib = (c, f + 1 - 2 * k)
@@ -962,6 +951,25 @@
             refs = (g0_ref, g1_ref, g2_ref, g3_ref)
             return [pltpu.make_async_copy(ref.at[:, e], g_buf.at[slot, j], l_g.at[slot, j]) for j, ref in enumerate(refs)]
 
+        def grads_across(e):
+            return remote(g0_ref.at[:, e], g2_ref.at[:, e], ss_g.at[0, e], rs_g.at[0, e], xn)
+
+        def grads_share(e):
+            return remote(g0_ref.at[:, e], g1_ref.at[:, e], ss_g.at[1, e], rs_g.at[1, e], sib)
+
+        def grads_share_far(e):
+            return remote(g2_ref.at[:, e], g3_ref.at[:, e], ss_g.at[2, e], rs_g.at[2, e], sib)
+
+        def forward_grads(e):
+            grads_across(e).wait_recv()
+            grads_share_far(e).start()
+
+        def start_load_grads(e, slot):
+            grads_share(e).wait_recv()
+            grads_share_far(e).wait_recv()
+            for load in load_grads(e, slot):
+                load.start()
+
         def there(half):
             column = (2 * relative(z, target) + k) * lanes
             return mixed.at[half, :, pl.ds(pl.multiple_of(column, lanes), lanes)]
@@ -990,9 +998,13 @@
         for u in range(splits):
             load_first(0, u).start()
             load_second(0, u).start()
-        for load in load_grads(0, 0):
-            load.start()
-
+
+        def start_grads(e, carry):
+            grads_across(e).start()
+            grads_share(e).start()
+            return carry
+
+        lax.fori_loop(0, number, start_grads, 0)
         for half in range(2):
             for other in range(count):
                 column = (2 * relative(other // 2, f) + other % 2) * lanes
@@ -1093,18 +1105,15 @@
         def expert(e, carry):
             slot = e % 2
 
-            @pl.when(e + 1 < number)
-            def _():
-                for load in load_grads(e + 1, 1 - slot):
-                    load.start()
-
             @pl.when(e + 2 < number)
             def _():
                 forward(e + 2)
+                forward_grads(e + 2)
 
             @pl.when(e + 1 < number)
             def _():
                 forward_far(e + 1)
+                start_load_grads(e + 1, 1 - slot)
 
             rows_share(e).wait_recv()
             rows_share_far(e).wait_recv()
@@ -1169,16 +1178,19 @@
 
             return carry
 
+        forward_grads(0)
+        forward_grads(1)
         forward(0)
         forward(1)
+        start_load_grads(0, 0)
         forward_far(0)
         lax.fori_loop(0, number, expert, 0)
         sum_far(number - 1)
         sum_outputs(number - 1)
+        for e in range(number - 3, number):
+            go_home(e)
         for e in range(number):
             far_out(e).start()
-        for e in range(number - 3, number):
-            go_home(e)
         hat, inverse = statistics(middle[...])
         remote(home_got, home_got, ss_h.at[0], rs_h, sib).wait_recv()
 
@@ -1278,6 +1290,9 @@
             rows_across(e).wait_send()
             rows_share(e).wait_send()
             rows_share_far(e).wait_send()
+            grads_across(e).wait_send()
+            grads_share(e).wait_send()
+            grads_share_far(e).wait_send()
             far_send(e).wait_send()
             for j in range(2):
                 near_out(e, j).wait_send()
@@ -1318,6 +1333,7 @@
             jax.ShapeDtypeStruct((2, half_rows, width), BF),
             jax.ShapeDtypeStruct((rows, width), F32),
             jax.ShapeDtypeStruct((4, number) + block, BF),
+            *[jax.ShapeDtypeStruct(near.shape, BF)] * 3,
             jax.ShapeDtypeStruct((number, total_rows, units), BF),
             jax.ShapeDtypeStruct((number, total_rows, units), BF),
             jax.ShapeDtypeStruct((2 * count, half_rows, lanes), BF),
@@ -1325,8 +1341,8 @@
             jax.ShapeDtypeStruct((1, width), F32),
             jax.ShapeDtypeStruct((count, slab + number * cap, width), BF),
         ),
-        in_specs=[ANY] + [vmem] * 8 + [ANY] * 6,
-        out_specs=(vmem, vmem, ANY, ANY, ANY, ANY, vmem, vmem, ANY),
+        in_specs=[ANY] + [vmem] * 8 + [ANY] * 3,
+        out_specs=(vmem, vmem) + (ANY,) * 7 + (vmem, vmem, ANY),
         scratch_shapes=[
             low(rows, width), low(count, number, cap, width), low(4, number, *block), low(2, 4, *block),
             pltpu.VMEM((splits, width, part_units), F32), pltpu.VMEM((splits, part_units, width), F32),
@@ -1338,18 +1354,18 @@
             DMA((count, 2)), DMA((count, 2)), DMA((number,)), DMA((number,)), DMA((number,)), DMA((number,)),
             DMA((number,)), DMA((number,)), DMA((number,)), DMA((number,)), DMA((number, 2)), DMA((number, 2)),
             DMA((number,)), DMA((number,)), DMA((number, 2)), DMA((number, 2)), DMA((number,)), DMA,
-            DMA((count, 2)), DMA((2 * count,)), DMA((2,)), DMA((2,)), DMA, DMA,
+            DMA((count, 2)), DMA((2 * count,)), DMA((2,)), DMA((2,)), DMA, DMA, DMA((3, number)), DMA((3, number)),
             DMA((splits,)), DMA((splits,)), DMA((2, 4)), DMA((number,)), DMA((2,)), DMA((2,)), DMA((number,)), DMA((number,)), DMA((number,)), DMA,
         ],
         compiler_params=pltpu.CompilerParams(has_side_effects=True, vmem_limit_bytes=60 << 20),
-    )(by_head, *out_proj, tokens, dispatch, gain, cotangent, *grads, first_proj, second_proj)
+    )(by_head, *out_proj, tokens, dispatch, gain, cotangent, near, first_proj, second_proj)
 
 
 def after(value, *others):
     return lax.optimization_barrier((value,) + others)[0]
 
 
-def finish_exchange(grads, parts, out_slab, gain_part, weight):
+def finish_exchange(grads, parts, slabs, gain_part, weight):
     count = lax.axis_size("ctx")
     depth = count // 2
     part = grads.shape[2]
@@ -1357,9 +1373,10 @@
     _, rows, _ = parts.shape
     pieces = 4
     piece = rows // pieces
+    slab = rows // count
 
     def kernel(
-        a_ref, p_ref, o_ref, g_ref, w_ref, tok_out, w_out, o_out, g_out, w_all, got, held, got_g, sum_g, got_gc,
+        a_ref, p_ref, h_ref, g_ref, w_ref, tok_out, w_out, o_out, g_out, w_all, o_ref, got, held, got_g, sum_g, got_gc,
         ss, rs, ss_r, rs_r, ss_up, ss_dn, rs_z, ss_a, ss_b, rs_o,
         ss_of, rs_of, ss_g, rs_g, ss_gc, rs_gc, ss_wx, rs_wx, ss_ws, rs_ws, ss_wf, rs_wf, loc,
     ):
@@ -1484,14 +1501,29 @@
         sum_g[1] = sum_g[0] + got_g[0]
         gain_send(1).start()
 
-        def slab_spread(i):
-            return remote(o_ref, o_out.at[c], ss_of.at[i], rs_of.at[c], ((c + i) % count, f))
+        across_y = (c + 1 - 2 * y, f)
+
+        def slab_send(i):
+            zt = (z + i) % depth
+            return remote(o_ref, o_out.at[c], ss_of.at[i], rs_of.at[c], (2 * zt + y, f))
+
+        def slab_on(i):
+            cs = 2 * ((z + i) % depth) + y
+            src = o_out.at[cs] if i else o_ref
+            return remote(src, o_out.at[cs], ss_of.at[depth + i], rs_of.at[cs], across_y)
 
         def gain_spread(i):
             return remote(sum_g.at[2], got_gc.at[c], ss_gc.at[i], rs_gc.at[c], ((c + i) % count, f))
 
+        slab_sum = h_ref[0, 0:slab].astype(F32)
+        for i in range(1, count):
+            slab_sum += h_ref[i, 0:slab].astype(F32)
+        o_ref[...] = slab_sum.astype(BF)
         slab_own = pltpu.make_async_copy(o_ref, o_out.at[c], rs_of.at[c])
         slab_own.start()
+        slab_on(0).start()
+        for i in range(1, depth):
+            slab_send(i).start()
         for hop in range(1, depth):
 
             @pl.when(z - hop >= 0)
@@ -1515,12 +1547,16 @@
                 spread(z + hop)
 
             weight_pass(hop - 1)
+            if hop == 2:
+                for i in range(1, depth):
+                    cs = 2 * ((z + i) % depth) + y
+                    remote(o_ref, o_out.at[cs], ss_of.at[i], rs_of.at[cs], sib).wait_recv()
+                    slab_on(i).start()
             if hop == 1:
                 gain_send(1).wait_recv()
                 sum_g[2] = sum_g[1] + got_g[1]
                 for i in range(1, count):
                     gain_spread(i).start()
-                    slab_spread(i).start()
         for i in range(depth - 1, pieces):
             weight_pass(i)
         total_g = sum_g[2]
@@ -1548,8 +1584,11 @@
             for half in range(2):
                 send(i, half).wait_send()
             gain_spread(i).wait_send()
-            slab_spread(i).wait_send()
-            cs = (c + i) % count
+        for i in range(depth):
+            if i:
+                slab_send(i).wait_send()
+            slab_on(i).wait_send()
+            cs = 2 * ((z + i) % depth) + 1 - y
             remote(o_ref, o_out.at[cs], ss_of.at[i], rs_of.at[cs], sib).wait_recv()
         slab_own.wait()
 
@@ -1581,13 +1620,14 @@
         out_shape=(
             jax.ShapeDtypeStruct((2, half_rows, count * part), BF),
             jax.ShapeDtypeStruct((rows, count * part), BF),
-            jax.ShapeDtypeStruct((count,) + out_slab.shape, BF),
+            jax.ShapeDtypeStruct((count, slab, slabs.shape[2]), BF),
             jax.ShapeDtypeStruct(eighth, F32),
             jax.ShapeDtypeStruct((4,) + weight.shape, BF),
         ),
         in_specs=[vmem] * 5,
         out_specs=(ANY, ANY, ANY, vmem, ANY),
         scratch_shapes=[
+            pltpu.VMEM((slab, slabs.shape[2]), BF),
             pltpu.VMEM((3, rows, part), BF),
             pltpu.VMEM((depth, rows, part), BF),
             pltpu.VMEM((2,) + eighth, F32),
@@ -1599,25 +1639,28 @@
             DMA((pieces,)), DMA((pieces,)), DMA, DMA, DMA((pieces,)), DMA((pieces,)), DMA,
         ],
         compiler_params=params(),
-    )(grads, parts, out_slab, gain_part, weight)
+    )(grads, parts, slabs, gain_part, weight)
 
 
 def finish_local(
-    grad_projected, projection, tokens, gain, grad_middle, middle, dispatch, expert_rows, weight_grad, weight, own_gain, out_slabs
+    grad_projected, projection, tokens, gain, grad_middle, middle, dispatch, home, weight_grad, weight, out_slabs, gain_sum
 ):
     rows, width = tokens.shape
     quarter, wide = weight.shape
     lanes = 128
     part = 3 * lanes
     count = wide // part
-
-    def kernel(p_ref, w_ref, x_ref, g_ref, m_ref, mid_ref, d_ref, e_ref, wg_ref, wl_ref, og_ref, o_ref, block, token, wout, gout, oout, acc):
+    slot_rows = EXPERTS // count * CAP
+
+    def kernel(p_ref, w_ref, x_ref, g_ref, m_ref, mid_ref, d_ref, e_ref, wg_ref, wl_ref, o_ref, gs_ref, block, token, wout, oout, gout, gout_two, acc):
         j = pl.program_id(0)
+        own = pl.ds(pl.multiple_of(lax.axis_index("fsdp") * quarter, quarter), quarter)
         acc[j] = lax.dot_general(p_ref[...], w_ref[0], CONTRACT_LAST, preferred_element_type=F32)
 
         @pl.when(j == 0)
         def _():
-            summed = lax.dot_general(d_ref[...], e_ref[...], CONTRACT_FIRST, preferred_element_type=F32)
+            slots = e_ref[:, home.shape[1] - slot_rows :].reshape(-1, width)
+            summed = lax.dot_general(d_ref[...], slots, CONTRACT_FIRST, preferred_element_type=F32)
             block[...] = (mid_ref[...] + summed).astype(BF)
             oout[...] = o_ref[...].astype(F32)
 
@@ -1631,7 +1674,8 @@
                     to = (kind * count + number) * lanes
                     wout[:, to : to + lanes] = value
                     total += jnp.sum(value * wl_ref[:, at : at + lanes].astype(F32), axis=1, keepdims=True)
-            gout[...] = total / og_ref[...]
+            gout[...] = jnp.broadcast_to(total, (quarter, lanes)).T[0:1] / g_ref[:, own]
+            gout_two[...] = gs_ref[:, own]
 
         @pl.when(j == 3)
         def _():
@@ -1648,10 +1692,11 @@
         jax.ShapeDtypeStruct((rows, width), BF),
         jax.ShapeDtypeStruct((rows, width), F32),
         jax.ShapeDtypeStruct((quarter, wide), F32),
-        jax.ShapeDtypeStruct((quarter, 1), F32),
         jax.ShapeDtypeStruct((quarter, width), F32),
-    )
-    rest = (tokens, gain, grad_middle, middle, dispatch, expert_rows, weight_grad, weight, own_gain, out_slabs)
+        jax.ShapeDtypeStruct((1, quarter), F32),
+        jax.ShapeDtypeStruct((1, quarter), F32),
+    )
+    rest = (tokens, gain, grad_middle, middle, dispatch, home, weight_grad, weight, out_slabs, gain_sum)
     return pl.pallas_call(
         kernel,
         name="finish_local",
@@ -1674,13 +1719,12 @@
     rows = 2 * half_rows
     length = count * rows
     scale = (width // HEADS) ** (-0.5)
-    f = lax.axis_index("fsdp")
     lanes = 2 * (width // HEADS)
     shard_rows = width // 4
     own_tokens = tokens.reshape(rows, width)
     cotangent = grad_output.reshape(rows, width)
     gain_row = gain_one.reshape(1, width)
-    stream, starts, columns, out_beside, out_far, out_diagonal, grads_near, qkv_low, out_own, dispatch = gather_stream(
+    stream, starts, columns, out_beside, out_far, out_diagonal, send_grads, qkv_low, out_own, dispatch = gather_stream(
         own_tokens.reshape(2, half_rows, width),
         gain_row,
         expert_ids.reshape(1, rows),
@@ -1689,21 +1733,20 @@
         query_key_value_weight,
         output_weight_matrix,
     )
-    grads_far = swap(grads_near, "fsdp", 2)
+    grads_near = lax.all_to_all(send_grads, "ctx", split_axis=0, concat_axis=0, tiled=True)
     stream = stream.reshape(length, width)
     start_row = jnp.concatenate([starts[:, 0].reshape(-1), starts[::-1, 1].reshape(-1)])[None]
     numbers = jnp.min(start_row.reshape(-1, TILE), axis=1) // TILE
     qkv, mixed16, mixed32, logs = attend_forward(stream, columns, start_row, numbers, scale)
-    grads_far = after(grads_far, mixed16)
-    all_grads = [grads_near, swap(grads_near, "fsdp", 1), grads_far, swap(grads_far, "fsdp", 1)]
-    mixed, middle, all_rows, active, grad_hidden, grad_heads, grad_middle, grad_gain_two, later = experts_exchange(
+    grads_near = after(grads_near, mixed16)
+    mixed, middle, all_rows, *other_grads, active, grad_hidden, grad_heads, grad_middle, grad_gain_two, later = experts_exchange(
         mixed16.reshape(2 * count, half_rows, lanes),
         [out_own, out_beside, out_far, out_diagonal],
         own_tokens,
         dispatch,
         gain_two.reshape(1, width),
         cotangent,
-        all_grads,
+        grads_near,
         expert_in,
         expert_out,
     )
@@ -1718,23 +1761,19 @@
         scale,
         stream,
         all_rows,
-        all_grads,
+        [grads_near, *other_grads],
         active,
         grad_hidden,
     )
     home = after(home, own_grads)
-    slab_rows = shard_rows // count
-    out_slab = jnp.sum(home[:, :slab_rows].astype(F32), axis=0).astype(BF)
-    back_rows = home[:, slab_rows:]
     grad_projected, weight_grad, shard_out, gain_sum, projection = finish_exchange(
         own_grads.reshape(2 * count, half_rows, 3 * lanes),
         parts.reshape(4, shard_rows, 3 * lanes),
-        out_slab,
+        home,
         grad_gain_two,
         qkv_low,
     )
-    own_gain = lax.dynamic_slice(gain_one, (f * shard_rows,), (shard_rows,)).reshape(shard_rows, 1)
-    block_out, grad_start, weight_grad, shard_gain_one, shard_out = finish_local(
+    block_out, grad_start, weight_grad, shard_out, shard_gain_one, shard_gain_two = finish_local(
         grad_projected.reshape(rows, 3 * width),
         projection,
         own_tokens,
@@ -1742,14 +1781,14 @@
         grad_middle,
         middle,
         dispatch,
-        back_rows.reshape(EXPERTS * CAP, width),
+        home,
         weight_grad,
         qkv_low,
-        own_gain,
         shard_out.reshape(shard_rows, width),
+        gain_sum,
     )
     shard_gain_one = shard_gain_one.reshape(shard_rows)
-    shard_gain_two = lax.dynamic_slice(gain_sum.reshape(width), (f * shard_rows,), (shard_rows,))
+    shard_gain_two = shard_gain_two.reshape(shard_rows)
     return (
         block_out.reshape(tokens.shape),
         grad_start.reshape(tokens.shape),

time: 366 us -> 345 us (0.943)
  Pallas kernels: 340 us -> 328 us
    pallas_call x1, Pallas kernels: 69 us -> 52.2 us  [gather_stream(): pl.pallas_call(kernel, name='gather_stream', cost_estimate=lasting(50), o...]
    all_to_all x0 -> x1, starting transfers between devices: none -> 4.21 us  [by_head_pairs(): lax.all_to_all(send_grads, 'ctx', split_axis=0, concat_axis=0, tiled=True)]
    pallas_call x1, Pallas kernels: 77.9 us -> 73.7 us  [finish_exchange(): pl.pallas_call(kernel, name='finish_exchange', cost_estimate=lasting(60),...]
    ppermute x3 -> x0, waiting for transfers between devices: 3.75 us -> none  [swap(): return lax.ppermute(value, axis, [(i, i ^ bit) for i in range(size)])]
  transfers between devices with their start and end apart: 4 -> 2, of which waited for: 2 -> 1; matrix products, arithmetic and copies ran while one was open for 1% -> 1% of each run, Pallas kernels for 15% -> 18%
where the time goes in v6:
time: 345 us; the launch traced here: 344 us
  Pallas kernels  328 us (95%)
  starting transfers between devices  10 us (3%)
    pallas_call x1, Pallas kernels, experts_exchange(): pl.pallas_call(kernel, name='experts_exchange', cost_estimate=lasting(100...  128 us
    pallas_call x1, Pallas kernels, finish_exchange(): pl.pallas_call(kernel, name='finish_exchange', cost_estimate=lasting(60),...  73.7 us
    pallas_call x1, Pallas kernels, gather_stream(): pl.pallas_call(kernel, name='gather_stream', cost_estimate=lasting(50), o...  52.2 us
    pallas_call x1, Pallas kernels, backward_local(): pl.pallas_call(kernel, name='backward_local', cost_estimate=lasting(30),...  39.4 us
    pallas_call x1, Pallas kernels, attend_forward(): pl.pallas_call(kernel, name='attend_forward', cost_estimate=lasting(22),...  21.9 us
    pallas_call x1, Pallas kernels, finish_local(): pl.pallas_call(kernel, name='finish_local', cost_estimate=lasting(9), gri...  12.3 us
  transfers between devices with their start and end apart: 2, of which 1 were waited for; matrix products, arithmetic and copies ran while one was open for 1% of the time, Pallas kernels for 18%

profile of v6, /device:TPU:1, one launch (start us, length us, event | category | flops | bytes accessed | tf_op | source)
XLA Modules:
  0.0 344.1 jit_solution(5884597831083309051)
XLA Ops:
  0.6 52.2 %gather_stream.1 = (bf16[16,128,1024]{2,1,0:T(8,128)(2,1)}, s32[8,2,128]{2,1,0:T(2,128)}, bf16[1024,384]{1,0:T(8,128)(2,1)}, bf16[256,1024]{1,0:T(8,128)(2,1)}, ...) custom-call(bf16[2,128,1024]{2,1,0:T(8,128)(2,1)} %bitcast.23, ...), custom_call_target="tpu_custom_call" | custom-call | bytes 165000000 | tf_op jit(solution)/shard_map/gather_stream/pallas_call | solution.py:679
  52.9 4.2 %all-to-all-start = ((bf16[8,8,8,1024]{3,2,1,0:T(8,128)(2,1)}), bf16[8,8,8,1024]{3,2,1,0:T(8,128)(2,1)S(1)}, u32[]{:S(2)}, u32[]{:S(2)}) async-start(bf16[8,8,8,1024]{3,2,1,0:T(8,128)(2,1)} %get-tuple-element.61), calls=%async_computation | async-start | bytes 2097152 | tf_op jit(solution)/shard_map/all_to_all | solution.py:1736
  57.1 0.8 fusion
  57.9 0.1 add_reduce_fusion
  58.1 0.6 pad_add_fusion
  58.7 0.5 and_select_fusion.first
  59.2 21.9 %attend_forward.1 = (bf16[2048,384]{1,0:T(8,128)(2,1)}, bf16[2048,128]{1,0:T(8,128)(2,1)}, f32[128,2048]{1,0:T(8,128)}, f32[2,2048]{1,0:T(2,128)}) custom-call(s32[8]{0:T(128)} %and_select_fusion.first, bf16[2048,1024]{1,0:T(8,128)(2,1)} %bitcast.21, bf16[1024,384]{1,0:T(8,128)(2,1)} %get-tuple-element.53.w_ref, s32[1,2048]{1,0:T(1,128)} %bitcast.34), custom_call_target="tpu_custom_call" | custom-call | bytes 72600000 | tf_op jit(solution)/shard_map/attend_forward/pallas_call | solution.py:764
  81.1 1.5 all-to-all-done.g0_ref
  82.5 0.0 copy-start.1
  82.5 1.0 copy-done.1
  83.5 128.0 %experts_exchange.1 = (bf16[2,128,1024]{2,1,0:T(8,128)(2,1)}, f32[256,1024]{1,0:T(8,128)}, bf16[4,8,8,8,1024]{4,3,2,1,0:T(8,128)(2,1)}, bf16[8,8,8,1024]{3,2,1,0...) custom-call(bf16[16,128,128]{2,1,0:T(8,128)(2,1)} %bitcast.31, ...), custom_call_target="tpu_custom_call" | custom-call | bytes 330000000 | tf_op jit(solution)/shard_map/experts_exchange/pallas_call | solution.py:1328
  211.5 5.8 %all-to-all-start.1 = ((bf16[8,96,1024]{2,1,0:T(8,128)(2,1)}), bf16[8,96,1024]{2,1,0:T(8,128)(2,1)S(1)}, u32[]{:S(2)}, u32[]{:S(2)}) async-start(bf16[8,96,1024]{2,1,0:T(8,128)(2,1)} %get-tuple-element.64), calls=%async_computation.1 | async-start | bytes 3145728 | tf_op jit(solution)/shard_map/all_to_all | solution.py:1753
  217.4 39.4 %backward_local.1 = (bf16[2048,384]{1,0:T(8,128)(2,1)}, bf16[1024,384]{1,0:T(8,128)(2,1)}, f32[8,1024,1024]{2,1,0:T(8,128)}, f32[8,1024,1024]{2,1,0:T(8,128)}) custom-call(s32[8]{0:T(128)} %and_select_fusion.first, bf16[2048,384]{1,0:T(8,128)(2,1)} %get-tuple-element.54.q_ref.k_ref.v_ref, bf16[2048,384]{1,0:T(8,128)(2,1)} %get-tuple-element.54.q_ref.k_ref.v_ref, ...), custom_call_target="tpu_custom_call" | custom-call | bytes 99000000 | tf_op jit(solution)/shard_map/backward_local/pallas_call | solution.py:866
  256.8 0.0 all-to-all-done.1.h_ref.e_ref
  256.8 0.0 copy-start
  256.8 1.1 copy-done
  258.0 73.7 %finish_exchange.1 = (bf16[2,128,3072]{2,1,0:T(8,128)(2,1)}, bf16[256,3072]{1,0:T(8,128)(2,1)}, bf16[8,32,1024]{2,1,0:T(8,128)(2,1)}, f32[1,1024]{1,0:T(1,128)}, bf16[4,256,3072]{2,1,0:T(8,128)(2,1)}) custom-call(bf16[16,128,384]{2,1,0:T(8,128)(2,1)} %bitcast.29, bf16[4,256,384]{2,1,0:T(8,128)(2,1)} %bitcast.30, bf16[8,96,1024]{2,1,0:T(8,128)(2,1)} %copy-done, ...), custom_call_target="tpu_custom_call" | custom-call | bytes 198000000 | tf_op jit(solution)/shard_map/finish_exchange/pallas_call | solution.py:1616
  331.7 12.3 %finish_local.1 = (bf16[256,1024]{1,0:T(8,128)(2,1)}, f32[256,1024]{1,0:T(8,128)}, f32[256,3072]{1,0:T(8,128)}, f32[256,1024]{1,0:T(8,128)}, f32[1,256]{1,0:T(1,128)}, /*index=5*/f32[1,256]{1,0:T(1,128)}) custom-call(bf16[256,3072]{1,0:T(8,128)(2,1)} %bitcast.28, bf16[4,256,3072]{2,1,0:T(8,128)(2,1)} %get-tuple-element.80.w_ref, bf16[256,1024]{1,0:T(8,128)(2,1)} %bitcast.25, ...), custom_call_target="tpu_custom_call" | custom-call | bytes 29700000 | tf_op jit(solution)/shard_map/finish_local/pallas_call | solution.py:1700
  (4 shorter events, 0.0 us)
Async XLA Ops:
  52.9 29.6 %all-to-all-start = ((bf16[8,8,8,1024]{3,2,1,0:T(8,128)(2,1)}), bf16[8,8,8,1024]{3,2,1,0:T(8,128)(2,1)S(1)}, u32[]{:S(2)}, u32[]{:S(2)}) async-start(bf16[8,8,8,1024]{3,2,1,0:T(8,128)(2,1)} %get-tuple-element.61), calls=%async_computation | async-start | bytes 2097152 | tf_op jit(solution)/shard_map/all_to_all | solution.py:1736
  82.5 1.0 copy-start.1
  211.5 45.3 %all-to-all-start.1 = ((bf16[8,96,1024]{2,1,0:T(8,128)(2,1)}), bf16[8,96,1024]{2,1,0:T(8,128)(2,1)S(1)}, u32[]{:S(2)}, u32[]{:S(2)}) async-start(bf16[8,96,1024]{2,1,0:T(8,128)(2,1)} %get-tuple-element.64), calls=%async_computation.1 | async-start | bytes 3145728 | tf_op jit(solution)/shard_map/all_to_all | solution.py:1753
  256.8 1.2 copy-start

commit v7 on v6

--- a/solution.py
+++ b/solution.py
@@ -801,11 +801,11 @@
     assert tiles == number
 
     def kernel(
-        first, q_ref, k_ref, v_ref, g_ref, m_ref, l_ref, s_ref, x_ref, r_ref, g0_ref, g1_ref, g2_ref, g3_ref, a_ref, h_ref,
+        first, q_ref, k_ref, v_ref, g_ref, m_ref, l_ref, s_ref, x_ref, r_ref, g0_ref, g1_ref, a_ref, h_ref,
         out, weight, da, db, acc_k, acc_v, k_turned,
     ):
         i = pl.program_id(0)
-        gradient = jnp.concatenate([stacked(ref[...]) for ref in (g0_ref, g1_ref, g2_ref, g3_ref)], axis=0)
+        gradient = jnp.concatenate([stacked(g0_ref[...]), stacked(g1_ref[...])], axis=0)
         da[0] = lax.dot_general(stacked(r_ref[...]), h_ref[0], CONTRACT_FIRST, preferred_element_type=F32)
         db[0] = lax.dot_general(a_ref[0], gradient, CONTRACT_FIRST, preferred_element_type=F32)
 
@@ -881,9 +881,7 @@
                 pl.BlockSpec((length, width), lambda i, n: (0, 0), pipeline_mode=pl.Buffered(1)),
                 pl.BlockSpec((4, 1, count, cap, width), lambda i, n: (0, i, 0, 0, 0)),
                 quarter,
-                quarter,
-                quarter,
-                quarter,
+                pl.BlockSpec((3, count, 1, cap, width), lambda i, n: (0, 0, i, 0, 0)),
                 wide,
                 wide,
             ],
@@ -927,8 +925,8 @@
 
     def kernel(
         a_ref, w0_ref, w1_ref, w2_ref, w3_ref, x_ref, d_ref, g_ref, c_ref, g0_ref, first_ref, second_ref,
-        mixed, middle, rows_out, g1_ref, g2_ref, g3_ref, active_out, hidden_out, heads, grad_middle, gain_out, later,
-        routed, slots, rows_v, g_buf, first_buf, second_buf, active_v, hidden_v, back_v, back_near, back_far, back_got,
+        mixed, middle, rows_out, g_ref_rest, active_out, hidden_out, heads, grad_middle, gain_out, later,
+        routed, slots, rows_v, g_buf, first_buf, second_buf, first_low, second_low, active_v, hidden_v, back_v, back_near, back_far, back_got,
         out_v, out_near, own_v, far_v, out_got, summed, home_got, back, shard_near, shard_far, shard_got, shard_v,
         ss_m, rs_m, ss_1, rs_1, ss_x, rs_x, ss_s, rs_s, ss_f, rs_f, ss_bn, rs_bn, ss_bf, rs_bf, ss_on, rs_on, ss_h, rs_h,
         ss_t, rs_t, ss_n, rs_n, ss_w, rs_w, ss_g, rs_g, l_first, l_second, l_g, st_r, st_a, st_h, st_o, ss_of, rs_of, st_w,
@@ -948,25 +946,34 @@
             return pltpu.make_async_copy(second_ref.at[e, part], second_buf.at[u], l_second.at[u])
 
         def load_grads(e, slot):
-            refs = (g0_ref, g1_ref, g2_ref, g3_ref)
-            return [pltpu.make_async_copy(ref.at[:, e], g_buf.at[slot, j], l_g.at[slot, j]) for j, ref in enumerate(refs)]
+            return [
+                pltpu.make_async_copy(g0_ref.at[:, e], g_buf.at[slot, 0], l_g.at[slot, 0]),
+                pltpu.make_async_copy(g_ref_rest.at[:, :, e], g_buf.at[slot, pl.ds(1, 3)], l_g.at[slot, 1]),
+            ]
+
+        def two(e):
+            return pl.ds(pl.multiple_of(e // 2 * 2, 2), 2)
 
         def grads_across(e):
-            return remote(g0_ref.at[:, e], g2_ref.at[:, e], ss_g.at[0, e], rs_g.at[0, e], xn)
+            return remote(g0_ref.at[:, two(e)], g_ref_rest.at[1, :, two(e)], ss_g.at[0, e // 2], rs_g.at[0, e // 2], xn)
 
         def grads_share(e):
-            return remote(g0_ref.at[:, e], g1_ref.at[:, e], ss_g.at[1, e], rs_g.at[1, e], sib)
+            return remote(g0_ref.at[:, two(e)], g_ref_rest.at[0, :, two(e)], ss_g.at[1, e // 2], rs_g.at[1, e // 2], sib)
 
         def grads_share_far(e):
-            return remote(g2_ref.at[:, e], g3_ref.at[:, e], ss_g.at[2, e], rs_g.at[2, e], sib)
+            here, there_too = g_ref_rest.at[1, :, two(e)], g_ref_rest.at[2, :, two(e)]
+            return remote(here, there_too, ss_g.at[2, e // 2], rs_g.at[2, e // 2], sib)
 
         def forward_grads(e):
             grads_across(e).wait_recv()
             grads_share_far(e).start()
 
         def start_load_grads(e, slot):
-            grads_share(e).wait_recv()
-            grads_share_far(e).wait_recv()
+            @pl.when(e % 2 == 0)
+            def _():
+                grads_share(e).wait_recv()
+                grads_share_far(e).wait_recv()
+
             for load in load_grads(e, slot):
                 load.start()
 
@@ -999,12 +1006,12 @@
             load_first(0, u).start()
             load_second(0, u).start()
 
-        def start_grads(e, carry):
-            grads_across(e).start()
-            grads_share(e).start()
+        def start_grads(p, carry):
+            grads_across(2 * p).start()
+            grads_share(2 * p).start()
             return carry
 
-        lax.fori_loop(0, number, start_grads, 0)
+        lax.fori_loop(0, number // 2, start_grads, 0)
         for half in range(2):
             for other in range(count):
                 column = (2 * relative(other // 2, f) + other % 2) * lanes
@@ -1022,7 +1029,7 @@
 
         def rows_first(e, i):
             owner = (c + i) % count
-            return remote(slots.at[owner, e], rows_v.at[0, e, c], ss_1.at[e], rs_1.at[e], (owner, f))
+            return remote(slots.at[owner, two(e)], rows_v.at[0, two(e), c], ss_1.at[e // 2], rs_1.at[e // 2], (owner, f))
 
         def hop(e, rel, dst, send_sem, recv_sem, dev):
             return remote(rows_v.at[rel, e], rows_v.at[dst, e], send_sem.at[e], recv_sem.at[e], dev)
@@ -1036,16 +1043,19 @@
         def rows_share_far(e):
             return hop(e, 2, 3, ss_f, rs_f, sib)
 
-        def start_rows(e, carry):
+        def start_rows(p, carry):
             for i in range(1, count):
-                rows_first(e, i).start()
-            pltpu.make_async_copy(slots.at[c, e], rows_v.at[0, e, c], rs_1.at[e]).start()
+                rows_first(2 * p, i).start()
+            pltpu.make_async_copy(slots.at[c, two(2 * p)], rows_v.at[0, two(2 * p), c], rs_1.at[p]).start()
             return carry
 
-        lax.fori_loop(0, number, start_rows, 0)
+        lax.fori_loop(0, number // 2, start_rows, 0)
 
         def forward(e):
-            remote(rows_v.at[0, e], rows_v.at[0, e], ss_x.at[e], rs_1.at[e], sib).wait_recv()
+            @pl.when(e % 2 == 0)
+            def _():
+                remote(rows_v.at[0, two(e)], rows_v.at[0, two(e)], ss_x.at[e], rs_1.at[e // 2], sib).wait_recv()
+
             rows_across(e).start()
             rows_share(e).start()
 
@@ -1053,11 +1063,16 @@
             rows_across(e).wait_recv()
             rows_share_far(e).start()
 
-        def near_send(e, j):
-            return remote(back_v.at[2 * j + 1, e], back_near.at[j, e], ss_bn.at[e, j], rs_bn.at[e, j], sib)
-
-        def near_out(e, j):
-            return remote(out_v.at[2 * j + 1, e], out_near.at[j, e], ss_on.at[e, j], rs_on.at[e, j], sib)
+        def near_send(e):
+            return remote(back_v.at[pl.ds(2, 2), e], back_near.at[:, e], ss_bn.at[e], rs_bn.at[e], sib)
+
+        def near_out(e):
+            return remote(out_v.at[pl.ds(2, 2), e], out_near.at[:, e], ss_on.at[e], rs_on.at[e], sib)
+
+        def hold(ref, e, value):
+            parts = value.astype(BF).reshape(4, count, cap, width)
+            for at, rel in enumerate((0, 2, 1, 3)):
+                ref[at, e] = parts[rel]
 
         def far_send(e):
             return remote(back_far.at[e], back_got.at[e], ss_bf.at[e], rs_bf.at[e], xn)
@@ -1078,41 +1093,40 @@
             return pltpu.make_async_copy(hidden_v.at[slot], hidden_out.at[e], st_h.at[slot])
 
         def sum_far(e):
-            near_send(e, 1).wait_recv()
-            back_far[e] = (back_v[2, e].astype(F32) + back_near[1, e].astype(F32)).astype(BF)
+            near_send(e).wait_recv()
+            back_far[e] = (back_v[1, e].astype(F32) + back_near[1, e].astype(F32)).astype(BF)
             far_send(e).start()
 
         def sum_outputs(e):
-            for j in range(2):
-                near_out(e, j).wait_recv()
+            near_out(e).wait_recv()
             own_v[e] = (out_v[0, e].astype(F32) + out_near[0, e].astype(F32)).astype(BF)
-            far_v[e] = (out_v[2, e].astype(F32) + out_near[1, e].astype(F32)).astype(BF)
+            far_v[e] = (out_v[1, e].astype(F32) + out_near[1, e].astype(F32)).astype(BF)
 
         def home(e, i):
             ct = (c + i) % count
-            return remote(summed.at[e, ct], home_got.at[c, e], ss_h.at[e], rs_h, (ct, f))
+            return remote(summed.at[two(e), ct], home_got.at[c, two(e)], ss_h.at[e // 2], rs_h, (ct, f))
 
         def go_home(e):
-            near_send(e, 0).wait_recv()
             far_send(e).wait_recv()
             summed[e] = (
                 back_v[0, e].astype(F32) + back_near[0, e].astype(F32) + back_got[e].astype(F32)
             ).astype(BF)
-            for i in range(1, count):
-                home(e, i).start()
-            pltpu.make_async_copy(summed.at[e, c], home_got.at[c, e], rs_h).start()
+
+            @pl.when(e % 2 == 1)
+            def _():
+                for i in range(1, count):
+                    home(e, i).start()
+                pltpu.make_async_copy(summed.at[two(e), c], home_got.at[c, two(e)], rs_h).start()
 
         def expert(e, carry):
             slot = e % 2
 
-            @pl.when(e + 2 < number)
+            @pl.when(e >= 1)
             def _():
-                forward(e + 2)
-                forward_grads(e + 2)
+                sum_far(e - 1)
 
             @pl.when(e + 1 < number)
             def _():
-                forward_far(e + 1)
                 start_load_grads(e + 1, 1 - slot)
 
             rows_share(e).wait_recv()
@@ -1129,13 +1143,18 @@
             row = rows_v[:, e].reshape(total_rows, width)
             grad = g_buf[slot].reshape(total_rows, width)
             term = jnp.zeros((total_rows, width), F32)
-            firsts, seconds = [], []
             for u in range(splits):
                 load_first(e, u).wait()
                 load_second(e, u).wait()
-                first = first_buf[u].astype(BF)
-                second = second_buf[u].astype(BF)
-                seconds.append(second)
+                first_low[u] = first_buf[u].astype(BF)
+                second_low[u] = second_buf[u].astype(BF)
+
+                @pl.when(e + 1 < number)
+                def _(u=u):
+                    load_first(e + 1, u).start()
+                    load_second(e + 1, u).start()
+
+                first, second = first_low[u], second_low[u]
                 hidden = jnp.dot(row, first, preferred_element_type=F32)
                 upstream = lax.dot_general(grad, second, CONTRACT_LAST, preferred_element_type=F32)
                 bent = jnp.tanh(ROOT * (hidden + CUBIC * hidden * hidden * hidden))
@@ -1147,49 +1166,59 @@
                 grad_hidden = (upstream * slope).astype(BF)
                 hidden_v[slot, :, cols] = grad_hidden
                 term += lax.dot_general(grad_hidden, first, CONTRACT_LAST, preferred_element_type=F32)
-            back_v[:, e] = term.astype(BF).reshape(4, count, cap, width)
-            near_send(e, 1).start()
-            near_send(e, 0).start()
+            hold(back_v, e, term)
+            near_send(e).start()
             result = jnp.zeros((total_rows, width), F32)
             for u in range(splits):
                 cols = pl.ds(u * part_units, part_units)
-                result += jnp.dot(active_v[slot, :, cols], seconds[u], preferred_element_type=F32)
-            out_v[:, e] = result.astype(BF).reshape(4, count, cap, width)
-            near_out(e, 1).start()
-            near_out(e, 0).start()
-
-            @pl.when(e + 1 < number)
-            def _():
-                for u in range(splits):
-                    load_first(e + 1, u).start()
-                    load_second(e + 1, u).start()
+                result += jnp.dot(active_v[slot, :, cols], second_low[u], preferred_element_type=F32)
+            hold(out_v, e, result)
+            near_out(e).start()
 
             store_active(e, slot).start()
             store_hidden(e, slot).start()
 
+            @pl.when(e + 3 < number)
+            def _():
+                forward(e + 3)
+
+            @pl.when((e + 4 < number) & (e % 2 == 0))
+            def _():
+                forward_grads(e + 4)
+
+            @pl.when(e + 2 < number)
+            def _():
+                forward_far(e + 2)
+
             @pl.when(e >= 1)
             def _():
-                sum_far(e - 1)
                 sum_outputs(e - 1)
 
-            @pl.when(e >= 3)
+            @pl.when(e >= 2)
             def _():
-                go_home(e - 3)
+                go_home(e - 2)
+
+            @pl.when(e >= number - 3)
+            def _():
+                far_out(e - (number - 3)).start()
 
             return carry
 
         forward_grads(0)
-        forward_grads(1)
         forward(0)
         forward(1)
         start_load_grads(0, 0)
         forward_far(0)
+        forward_grads(2)
+        forward(2)
+        forward_far(1)
         lax.fori_loop(0, number, expert, 0)
         sum_far(number - 1)
         sum_outputs(number - 1)
-        for e in range(number - 3, number):
+        far_out(3).start()
+        for e in range(number - 2, number):
             go_home(e)
-        for e in range(number):
+        for e in range(4, number):
             far_out(e).start()
         hat, inverse = statistics(middle[...])
         remote(home_got, home_got, ss_h.at[0], rs_h, sib).wait_recv()
@@ -1235,11 +1264,7 @@
                 send_heads(0, half).start()
 
         for e in range(number):
-            for j in range(2):
-                near_send(e, j).wait_send()
-
-        def term_place(j):
-            return back_v.at[j, 0 : quarter // (count * cap)]
+            near_send(e).wait_send()
 
         def shard_term(j):
             half_quarter = quarter // 2
@@ -1252,19 +1277,17 @@
             )
             return value.astype(BF).reshape(shard_far.shape)
 
-        def core_send(j):
-            return remote(term_place(2 * j + 1), shard_near.at[j], ss_n.at[j], rs_n.at[j], sib)
-
+        sheet = pl.ds(0, quarter // (count * cap))
+        core_send = remote(back_v.at[pl.ds(2, 2), sheet], shard_near, ss_n, rs_n, sib)
         across = remote(shard_far, shard_got, ss_w, rs_w, xn)
-        for j in (1, 0):
-            back_v[2 * j + 1, 0 : quarter // (count * cap)] = shard_term(2 * j + 1)
-            core_send(j).start()
+        for j in range(2):
+            back_v[2 + j, sheet] = shard_term(2 * j + 1)
+        core_send.start()
         own_far = shard_term(2)
-        core_send(1).wait_recv()
+        core_send.wait_recv()
         shard_far[...] = (own_far.astype(F32) + shard_near[1].astype(F32)).astype(BF)
         across.start()
         own_near = shard_term(0)
-        core_send(0).wait_recv()
 
         def finish_output(e, carry):
             far_out(e).wait_recv()
@@ -1284,24 +1307,28 @@
             remote(part(0, 0), heads.at[b], ss_t.at[0, 0], rs_t.at[b], sib).wait_recv()
 
         def leave(e, carry):
-            sent = pl.ds(0, count - 1)
-            remote(slots.at[sent, e], rows_v.at[0, e, sent], ss_1.at[e], rs_1.at[e], sib).wait_send()
-            remote(summed.at[e, sent], home_got.at[sent, e], ss_h.at[e], rs_h, sib).wait_send()
             rows_across(e).wait_send()
             rows_share(e).wait_send()
             rows_share_far(e).wait_send()
-            grads_across(e).wait_send()
-            grads_share(e).wait_send()
-            grads_share_far(e).wait_send()
             far_send(e).wait_send()
-            for j in range(2):
-                near_out(e, j).wait_send()
+            near_out(e).wait_send()
             store_own(e).wait()
             far_out(e).wait_send()
             store_rows(e).wait()
             return carry
 
+        def leave_two(p, carry):
+            sent = pl.ds(0, count - 1)
+            first, last = slots.at[sent, two(2 * p)], summed.at[two(2 * p), sent]
+            remote(first, first, ss_1.at[p], rs_1.at[p], sib).wait_send()
+            remote(last, last, ss_h.at[p], rs_h, sib).wait_send()
+            grads_across(2 * p).wait_send()
+            grads_share(2 * p).wait_send()
+            grads_share_far(2 * p).wait_send()
+            return carry
+
         lax.fori_loop(0, number, leave, 0)
+        lax.fori_loop(0, number // 2, leave_two, 0)
         store_shard.wait()
         for e in (number - 2, number - 1):
             store_active(e, e % 2).wait()
@@ -1317,8 +1344,7 @@
                 send(0, half).wait_send()
                 send_heads(0, half).wait_send()
 
-        core_send(0).wait_send()
-        core_send(1).wait_send()
+        core_send.wait_send()
         across.wait_send()
 
     vmem = pl.BlockSpec(memory_space=pltpu.VMEM)
@@ -1333,7 +1359,7 @@
             jax.ShapeDtypeStruct((2, half_rows, width), BF),
             jax.ShapeDtypeStruct((rows, width), F32),
             jax.ShapeDtypeStruct((4, number) + block, BF),
-            *[jax.ShapeDtypeStruct(near.shape, BF)] * 3,
+            jax.ShapeDtypeStruct((3,) + near.shape, BF),
             jax.ShapeDtypeStruct((number, total_rows, units), BF),
             jax.ShapeDtypeStruct((number, total_rows, units), BF),
             jax.ShapeDtypeStruct((2 * count, half_rows, lanes), BF),
@@ -1342,20 +1368,21 @@
             jax.ShapeDtypeStruct((count, slab + number * cap, width), BF),
         ),
         in_specs=[ANY] + [vmem] * 8 + [ANY] * 3,
-        out_specs=(vmem, vmem) + (ANY,) * 7 + (vmem, vmem, ANY),
+        out_specs=(vmem, vmem) + (ANY,) * 5 + (vmem, vmem, ANY),
         scratch_shapes=[
             low(rows, width), low(count, number, cap, width), low(4, number, *block), low(2, 4, *block),
             pltpu.VMEM((splits, width, part_units), F32), pltpu.VMEM((splits, part_units, width), F32),
+            low(splits, width, part_units), low(splits, part_units, width),
             low(2, total_rows, units), low(2, total_rows, units),
             low(4, number, *block), low(2, number, *block), low(number, *block), low(number, *block),
             low(4, number, *block), low(2, number, *block), low(number, *block), low(number, *block), low(number, *block),
             low(number, *block), low(count, number, cap, width), low(2, half_rows, width),
             low(2, *fold), low(*fold), low(*fold), low(count, slab, width),
-            DMA((count, 2)), DMA((count, 2)), DMA((number,)), DMA((number,)), DMA((number,)), DMA((number,)),
-            DMA((number,)), DMA((number,)), DMA((number,)), DMA((number,)), DMA((number, 2)), DMA((number, 2)),
-            DMA((number,)), DMA((number,)), DMA((number, 2)), DMA((number, 2)), DMA((number,)), DMA,
-            DMA((count, 2)), DMA((2 * count,)), DMA((2,)), DMA((2,)), DMA, DMA, DMA((3, number)), DMA((3, number)),
-            DMA((splits,)), DMA((splits,)), DMA((2, 4)), DMA((number,)), DMA((2,)), DMA((2,)), DMA((number,)), DMA((number,)), DMA((number,)), DMA,
+            DMA((count, 2)), DMA((count, 2)), DMA((number // 2,)), DMA((number // 2,)), DMA((number,)), DMA((number,)),
+            DMA((number,)), DMA((number,)), DMA((number,)), DMA((number,)), DMA((number,)), DMA((number,)),
+            DMA((number,)), DMA((number,)), DMA((number,)), DMA((number,)), DMA((number // 2,)), DMA,
+            DMA((count, 2)), DMA((2 * count,)), DMA, DMA, DMA, DMA, DMA((3, number // 2)), DMA((3, number // 2)),
+            DMA((splits,)), DMA((splits,)), DMA((2, 2)), DMA((number,)), DMA((2,)), DMA((2,)), DMA((number,)), DMA((number,)), DMA((number,)), DMA,
         ],
         compiler_params=pltpu.CompilerParams(has_side_effects=True, vmem_limit_bytes=60 << 20),
     )(by_head, *out_proj, tokens, dispatch, gain, cotangent, near, first_proj, second_proj)
@@ -1739,7 +1766,7 @@
     numbers = jnp.min(start_row.reshape(-1, TILE), axis=1) // TILE
     qkv, mixed16, mixed32, logs = attend_forward(stream, columns, start_row, numbers, scale)
     grads_near = after(grads_near, mixed16)
-    mixed, middle, all_rows, *other_grads, active, grad_hidden, grad_heads, grad_middle, grad_gain_two, later = experts_exchange(
+    mixed, middle, all_rows, other_grads, active, grad_hidden, grad_heads, grad_middle, grad_gain_two, later = experts_exchange(
         mixed16.reshape(2 * count, half_rows, lanes),
         [out_own, out_beside, out_far, out_diagonal],
         own_tokens,
@@ -1761,7 +1788,7 @@
         scale,
         stream,
         all_rows,
-        [grads_near, *other_grads],
+        [grads_near, other_grads],
         active,
         grad_hidden,
     )

time: 345 us -> 335 us (0.971)
  Pallas kernels: 328 us -> 317 us
    pallas_call x1, Pallas kernels: 128 us -> 119 us  [experts_exchange(): pl.pallas_call(kernel, name='experts_exchange', cost_estimate=lasting(100...]
where the time goes in v7:
time: 335 us; the launch traced here: 334 us
  Pallas kernels  317 us (95%)
  starting transfers between devices  10.4 us (3%)
    pallas_call x1, Pallas kernels, experts_exchange(): pl.pallas_call(kernel, name='experts_exchange', cost_estimate=lasting(100...  119 us
    pallas_call x1, Pallas kernels, finish_exchange(): pl.pallas_call(kernel, name='finish_exchange', cost_estimate=lasting(60),...  72 us
    pallas_call x1, Pallas kernels, gather_stream(): pl.pallas_call(kernel, name='gather_stream', cost_estimate=lasting(50), o...  52.2 us
    pallas_call x1, Pallas kernels, backward_local(): pl.pallas_call(kernel, name='backward_local', cost_estimate=lasting(30),...  39.4 us
    pallas_call x1, Pallas kernels, attend_forward(): pl.pallas_call(kernel, name='attend_forward', cost_estimate=lasting(22),...  21.9 us
    pallas_call x1, Pallas kernels, finish_local(): pl.pallas_call(kernel, name='finish_local', cost_estimate=lasting(9), gri...  12.3 us
  transfers between devices with their start and end apart: 2, of which 1 were waited for; matrix products, arithmetic and copies ran while one was open for 1% of the time, Pallas kernels for 18%

profile of v7, /device:TPU:1, one launch (start us, length us, event | category | flops | bytes accessed | tf_op | source)
XLA Modules:
  0.0 333.6 jit_solution(18042403019445901649)
XLA Ops:
  0.6 52.2 %gather_stream.1 = (bf16[16,128,1024]{2,1,0:T(8,128)(2,1)}, s32[8,2,128]{2,1,0:T(2,128)}, bf16[1024,384]{1,0:T(8,128)(2,1)}, bf16[256,1024]{1,0:T(8,128)(2,1)}, ...) custom-call(bf16[2,128,1024]{2,1,0:T(8,128)(2,1)} %bitcast.23, ...), custom_call_target="tpu_custom_call" | custom-call | bytes 165000000 | tf_op jit(solution)/shard_map/gather_stream/pallas_call | solution.py:679
  52.9 4.2 %all-to-all-start = ((bf16[8,8,8,1024]{3,2,1,0:T(8,128)(2,1)}), bf16[8,8,8,1024]{3,2,1,0:T(8,128)(2,1)S(1)}, u32[]{:S(2)}, u32[]{:S(2)}) async-start(bf16[8,8,8,1024]{3,2,1,0:T(8,128)(2,1)} %get-tuple-element.59), calls=%async_computation | async-start | bytes 2097152 | tf_op jit(solution)/shard_map/all_to_all | solution.py:1763
  57.1 0.8 fusion
  57.9 0.1 add_reduce_fusion
  58.1 0.6 pad_add_fusion
  58.7 0.5 and_select_fusion.first
  59.2 21.9 %attend_forward.1 = (bf16[2048,384]{1,0:T(8,128)(2,1)}, bf16[2048,128]{1,0:T(8,128)(2,1)}, f32[128,2048]{1,0:T(8,128)}, f32[2,2048]{1,0:T(2,128)}) custom-call(s32[8]{0:T(128)} %and_select_fusion.first, bf16[2048,1024]{1,0:T(8,128)(2,1)} %bitcast.21, bf16[1024,384]{1,0:T(8,128)(2,1)} %get-tuple-element.51.w_ref, s32[1,2048]{1,0:T(1,128)} %bitcast.34), custom_call_target="tpu_custom_call" | custom-call | bytes 72600000 | tf_op jit(solution)/shard_map/attend_forward/pallas_call | solution.py:764
  81.1 1.5 all-to-all-done.g0_ref
  82.5 0.0 copy-start.1
  82.5 1.0 copy-done.1
  83.5 118.9 %experts_exchange.1 = (bf16[2,128,1024]{2,1,0:T(8,128)(2,1)}, f32[256,1024]{1,0:T(8,128)}, bf16[4,8,8,8,1024]{4,3,2,1,0:T(8,128)(2,1)}, bf16[3,8,8,8,1024]{4,3,2...) custom-call(bf16[16,128,128]{2,1,0:T(8,128)(2,1)} %bitcast.31, ...), custom_call_target="tpu_custom_call" | custom-call | bytes 330000000 | tf_op jit(solution)/shard_map/experts_exchange/pallas_call | solution.py:1354
  202.4 6.2 %all-to-all-start.1 = ((bf16[8,96,1024]{2,1,0:T(8,128)(2,1)}), bf16[8,96,1024]{2,1,0:T(8,128)(2,1)S(1)}, u32[]{:S(2)}, u32[]{:S(2)}) async-start(bf16[8,96,1024]{2,1,0:T(8,128)(2,1)} %get-tuple-element.62), calls=%async_computation.1 | async-start | bytes 3145728 | tf_op jit(solution)/shard_map/all_to_all | solution.py:1780
  208.5 39.4 %backward_local.1 = (bf16[2048,384]{1,0:T(8,128)(2,1)}, bf16[1024,384]{1,0:T(8,128)(2,1)}, f32[8,1024,1024]{2,1,0:T(8,128)}, f32[8,1024,1024]{2,1,0:T(8,128)}) custom-call(s32[8]{0:T(128)} %and_select_fusion.first, bf16[2048,384]{1,0:T(8,128)(2,1)} %get-tuple-element.52.q_ref.k_ref.v_ref, bf16[2048,384]{1,0:T(8,128)(2,1)} %get-tuple-element.52.q_ref.k_ref.v_ref, ...), custom_call_target="tpu_custom_call" | custom-call | bytes 99000000 | tf_op jit(solution)/shard_map/backward_local/pallas_call | solution.py:866
  247.9 0.0 all-to-all-done.1.h_ref.e_ref
  247.9 0.0 copy-start
  248.0 1.2 copy-done
  249.1 72.0 %finish_exchange.1 = (bf16[2,128,3072]{2,1,0:T(8,128)(2,1)}, bf16[256,3072]{1,0:T(8,128)(2,1)}, bf16[8,32,1024]{2,1,0:T(8,128)(2,1)}, f32[1,1024]{1,0:T(1,128)}, bf16[4,256,3072]{2,1,0:T(8,128)(2,1)}) custom-call(bf16[16,128,384]{2,1,0:T(8,128)(2,1)} %bitcast.29, bf16[4,256,384]{2,1,0:T(8,128)(2,1)} %bitcast.30, bf16[8,96,1024]{2,1,0:T(8,128)(2,1)} %copy-done, ...), custom_call_target="tpu_custom_call" | custom-call | bytes 198000000 | tf_op jit(solution)/shard_map/finish_exchange/pallas_call | solution.py:1643
  321.1 12.3 %finish_local.1 = (bf16[256,1024]{1,0:T(8,128)(2,1)}, f32[256,1024]{1,0:T(8,128)}, f32[256,3072]{1,0:T(8,128)}, f32[256,1024]{1,0:T(8,128)}, f32[1,256]{1,0:T(1,128)}, /*index=5*/f32[1,256]{1,0:T(1,128)}) custom-call(bf16[256,3072]{1,0:T(8,128)(2,1)} %bitcast.28, bf16[4,256,3072]{2,1,0:T(8,128)(2,1)} %get-tuple-element.76.w_ref, bf16[256,1024]{1,0:T(8,128)(2,1)} %bitcast.25, ...), custom_call_target="tpu_custom_call" | custom-call | bytes 29700000 | tf_op jit(solution)/shard_map/finish_local/pallas_call | solution.py:1727
  (4 shorter events, 0.0 us)
Async XLA Ops:
  52.9 29.6 %all-to-all-start = ((bf16[8,8,8,1024]{3,2,1,0:T(8,128)(2,1)}), bf16[8,8,8,1024]{3,2,1,0:T(8,128)(2,1)S(1)}, u32[]{:S(2)}, u32[]{:S(2)}) async-start(bf16[8,8,8,1024]{3,2,1,0:T(8,128)(2,1)} %get-tuple-element.59), calls=%async_computation | async-start | bytes 2097152 | tf_op jit(solution)/shard_map/all_to_all | solution.py:1763
  82.5 1.0 copy-start.1
  202.4 45.6 %all-to-all-start.1 = ((bf16[8,96,1024]{2,1,0:T(8,128)(2,1)}), bf16[8,96,1024]{2,1,0:T(8,128)(2,1)S(1)}, u32[]{:S(2)}, u32[]{:S(2)}) async-start(bf16[8,96,1024]{2,1,0:T(8,128)(2,1)} %get-tuple-element.62), calls=%async_computation.1 | async-start | bytes 3145728 | tf_op jit(solution)/shard_map/all_to_all | solution.py:1780
  247.9 1.2 copy-start

commit v8 on v7

--- a/solution.py
+++ b/solution.py
@@ -507,8 +507,8 @@
     own_experts = EXPERTS // count
 
     def kernel(
-        x_ref, g_ref, e_ref, c_ref, s_ref, wf_ref, of_ref, tok, st, cols, beside, far, diagonal, d_ref, w_ref, o_ref, hot,
-        n_ref, rs_t, ss_p, ss_up, ss_dn, ss_sib, rs_s, ss_s, rs_w, ss_w, ss_o, rs_o,
+        x_ref, g_ref, e_ref, c_ref, s_ref, wide_ref, matrix_ref, tok, st, cols, beside, far, diagonal, d_ref, w_ref, o_ref, hot,
+        n_ref, wf_ref, of_ref, loads, rs_t, ss_p, ss_up, ss_dn, ss_sib, rs_s, ss_s, rs_w, ss_w, ss_o, rs_o,
     ):
         c, f, z, y, x, k = place()
         sib = (c, f + 1 - 2 * k)
@@ -516,6 +516,10 @@
         up = (c + 2, f)
         down = (c - 2, f)
         holder = k == y
+        load_weight = pltpu.make_async_copy(wide_ref, wf_ref, loads.at[0])
+        load_matrix = pltpu.make_async_copy(matrix_ref, of_ref, loads.at[1])
+        load_weight.start()
+        load_matrix.start()
         for h in range(2):
             hat, _ = statistics(x_ref[h].astype(F32))
             n_ref[h] = (hat * g_ref[...]).astype(BF)
@@ -562,6 +566,7 @@
             pair, dev = goals[t]
             return remote(columns(pair), weight_place(f), ss_w.at[t], rs_w.at[f], dev)
 
+        load_weight.wait()
         for number in range(count):
             for j in range(3):
                 at = number * part + j * lanes
@@ -569,6 +574,7 @@
         for t in range(3):
             weight_send(t).start()
         pltpu.make_async_copy(columns(2 * z + k), weight_place(f), rs_w.at[f]).start()
+        load_matrix.wait()
         o_ref[...] = of_ref[...].astype(BF)
         matrix_far = remote(o_ref, far, ss_o.at[0], rs_o.at[0], goals[0][1])
         matrix_beside = remote(o_ref, beside, ss_o.at[1], rs_o.at[1], sib)
@@ -690,10 +696,10 @@
             jax.ShapeDtypeStruct(matrix.shape, BF),
             jax.ShapeDtypeStruct((EXPERTS * CAP, own_rows), BF),
         ),
-        in_specs=[pl.BlockSpec(memory_space=pltpu.VMEM)] * 7,
+        in_specs=[pl.BlockSpec(memory_space=pltpu.VMEM)] * 5 + [ANY] * 2,
         out_specs=(ANY,) * 6 + (pl.BlockSpec(memory_space=pltpu.VMEM),) * 4,
         scratch_shapes=[
-            pltpu.VMEM((2, half_rows, width), BF),
+            pltpu.VMEM((2, half_rows, width), BF), pltpu.VMEM((rows, wide), F32), pltpu.VMEM(matrix.shape, F32), DMA((2,)),
             DMA((2 * count,)), DMA((2,)), DMA((depth, 2)), DMA((depth, 2)), DMA((depth, 2)),
             DMA((count,)), DMA((count,)), DMA((4,)), DMA((3,)), DMA((3,)), DMA((3,)),
         ],
@@ -924,9 +930,9 @@
     part_units = units // splits
 
     def kernel(
-        a_ref, w0_ref, w1_ref, w2_ref, w3_ref, x_ref, d_ref, g_ref, c_ref, g0_ref, first_ref, second_ref,
+        a_ref, m0_ref, m1_ref, m2_ref, m3_ref, x_ref, d_ref, g_ref, c_ref, g0_ref, first_ref, second_ref,
         mixed, middle, rows_out, g_ref_rest, active_out, hidden_out, heads, grad_middle, gain_out, later,
-        routed, slots, rows_v, g_buf, first_buf, second_buf, first_low, second_low, active_v, hidden_v, back_v, back_near, back_far, back_got,
+        w_refs, l_w, routed, slots, rows_v, g_buf, first_buf, second_buf, first_low, second_low, active_v, hidden_v, back_v, back_near, back_far, back_got,
         out_v, out_near, own_v, far_v, out_got, summed, home_got, back, shard_near, shard_far, shard_got, shard_v,
         ss_m, rs_m, ss_1, rs_1, ss_x, rs_x, ss_s, rs_s, ss_f, rs_f, ss_bn, rs_bn, ss_bf, rs_bf, ss_on, rs_on, ss_h, rs_h,
         ss_t, rs_t, ss_n, rs_n, ss_w, rs_w, ss_g, rs_g, l_first, l_second, l_g, st_r, st_a, st_h, st_o, ss_of, rs_of, st_w,
@@ -977,6 +983,10 @@
             for load in load_grads(e, slot):
                 load.start()
 
+        matrix_loads = [
+            pltpu.make_async_copy(ref, w_refs.at[j], l_w.at[j]) for j, ref in enumerate((m0_ref, m1_ref, m2_ref, m3_ref))
+        ]
+
         def there(half):
             column = (2 * relative(z, target) + k) * lanes
             return mixed.at[half, :, pl.ds(pl.multiple_of(column, lanes), lanes)]
@@ -1002,6 +1012,8 @@
             def _(half=half):
                 send(0, half).start()
 
+        for load in matrix_loads:
+            load.start()
         for u in range(splits):
             load_first(0, u).start()
             load_second(0, u).start()
@@ -1012,6 +1024,8 @@
             return carry
 
         lax.fori_loop(0, number // 2, start_grads, 0)
+        for load in matrix_loads:
+            load.wait()
         for half in range(2):
             for other in range(count):
                 column = (2 * relative(other // 2, f) + other % 2) * lanes
@@ -1019,9 +1033,9 @@
                 remote(a_ref.at[0], mixed.at[half, :, cols], ss_m.at[0, half], rs_m.at[other, half], sib).wait_recv()
             here = pl.ds(half * half_rows, half_rows)
             value = x_ref[here, :].astype(F32)
-            for j, w_ref in enumerate((w0_ref, w1_ref, w2_ref, w3_ref)):
+            for j in range(4):
                 cols = pl.ds(j * quarter, quarter)
-                value += jnp.dot(mixed[half, :, cols], w_ref[...], preferred_element_type=F32)
+                value += jnp.dot(mixed[half, :, cols], w_refs[j], preferred_element_type=F32)
             middle[here, :] = value
             hat, _ = statistics(value)
             routed[here, :] = (hat * g_ref[...]).astype(BF)
@@ -1231,9 +1245,9 @@
         gradient = c_ref[...].astype(F32) + inverse * (scaled - mean_grad - hat * mean_proj)
         grad_middle[...] = gradient
         low = gradient.astype(BF)
-        for j, w_ref in enumerate((w0_ref, w1_ref, w2_ref, w3_ref)):
+        for j in range(4):
             back[:, :, j * quarter : (j + 1) * quarter] = (
-                lax.dot_general(low, w_ref[...], CONTRACT_LAST, preferred_element_type=F32)
+                lax.dot_general(low, w_refs[j], CONTRACT_LAST, preferred_element_type=F32)
                 .astype(BF)
                 .reshape(2, half_rows, quarter)
             )
@@ -1367,9 +1381,10 @@
             jax.ShapeDtypeStruct((1, width), F32),
             jax.ShapeDtypeStruct((count, slab + number * cap, width), BF),
         ),
-        in_specs=[ANY] + [vmem] * 8 + [ANY] * 3,
+        in_specs=[ANY] * 5 + [vmem] * 4 + [ANY] * 3,
         out_specs=(vmem, vmem) + (ANY,) * 5 + (vmem, vmem, ANY),
         scratch_shapes=[
+            low(4, quarter, width), DMA((4,)),
             low(rows, width), low(count, number, cap, width), low(4, number, *block), low(2, 4, *block),
             pltpu.VMEM((splits, width, part_units), F32), pltpu.VMEM((splits, part_units, width), F32),
             low(splits, width, part_units), low(splits, part_units, width),
@@ -1403,7 +1418,7 @@
     slab = rows // count
 
     def kernel(
-        a_ref, p_ref, h_ref, g_ref, w_ref, tok_out, w_out, o_out, g_out, w_all, o_ref, got, held, got_g, sum_g, got_gc,
+        a_ref, p_ref, home_ref, g_ref, w_ref, tok_out, w_out, o_out, g_out, w_all, h_ref, w_held, loads, o_ref, got, held, got_g, sum_g, got_gc,
         ss, rs, ss_r, rs_r, ss_up, ss_dn, rs_z, ss_a, ss_b, rs_o,
         ss_of, rs_of, ss_g, rs_g, ss_gc, rs_gc, ss_wx, rs_wx, ss_ws, rs_ws, ss_wf, rs_wf, loc,
     ):
@@ -1430,6 +1445,10 @@
 
         for d in (2, 1, 0):
             scatter(d).start()
+        load_slabs = pltpu.make_async_copy(home_ref.at[:, pl.ds(0, slab)], h_ref, loads.at[0])
+        load_weight = pltpu.make_async_copy(w_ref, w_held, loads.at[1])
+        load_slabs.start()
+        load_weight.start()
 
         def weight_part(shard, i):
             return w_all.at[shard, pl.ds(i * piece, piece)]
@@ -1446,7 +1465,7 @@
             weight_on(i, shard).start()
 
         weight_share = remote(w_ref, w_all.at[f], ss_ws, rs_ws, sib)
-        weight_own = pltpu.make_async_copy(w_ref, w_all.at[f], loc)
+        weight_own = pltpu.make_async_copy(w_held, w_all.at[f], loc)
         for i in range(pieces):
             weight_across(i).start()
 
@@ -1523,6 +1542,7 @@
                 send(0, half).start()
 
         weight_share.start()
+        load_weight.wait()
         weight_own.start()
         gain_send(0).wait_recv()
         sum_g[1] = sum_g[0] + got_g[0]
@@ -1542,9 +1562,10 @@
         def gain_spread(i):
             return remote(sum_g.at[2], got_gc.at[c], ss_gc.at[i], rs_gc.at[c], ((c + i) % count, f))
 
-        slab_sum = h_ref[0, 0:slab].astype(F32)
+        load_slabs.wait()
+        slab_sum = h_ref[0].astype(F32)
         for i in range(1, count):
-            slab_sum += h_ref[i, 0:slab].astype(F32)
+            slab_sum += h_ref[i].astype(F32)
         o_ref[...] = slab_sum.astype(BF)
         slab_own = pltpu.make_async_copy(o_ref, o_out.at[c], rs_of.at[c])
         slab_own.start()
@@ -1651,9 +1672,10 @@
             jax.ShapeDtypeStruct(eighth, F32),
             jax.ShapeDtypeStruct((4,) + weight.shape, BF),
         ),
-        in_specs=[vmem] * 5,
+        in_specs=[vmem, vmem, ANY, vmem, ANY],
         out_specs=(ANY, ANY, ANY, vmem, ANY),
         scratch_shapes=[
+            pltpu.VMEM((count, slab, slabs.shape[2]), BF), pltpu.VMEM(weight.shape, BF), DMA((2,)),
             pltpu.VMEM((slab, slabs.shape[2]), BF),
             pltpu.VMEM((3, rows, part), BF),
             pltpu.VMEM((depth, rows, part), BF),

time: 335 us -> 334 us (level)
  transfers between devices with their start and end apart: 2 -> 2, of which waited for: 1 -> 1; matrix products, arithmetic and copies ran while one was open for 1% -> 1% of each run, Pallas kernels for 18% -> 17%
where the time goes in v8:
time: 334 us
  Pallas kernels  315 us (94%)
  starting transfers between devices  10.4 us (3%)
  waiting for transfers between devices  3.51 us (1%)
    pallas_call x1, Pallas kernels, experts_exchange(): pl.pallas_call(kernel, name='experts_exchange', cost_estimate=lasting(100...  119 us
    pallas_call x1, Pallas kernels, finish_exchange(): pl.pallas_call(kernel, name='finish_exchange', cost_estimate=lasting(60),...  74 us
    pallas_call x1, Pallas kernels, gather_stream(): pl.pallas_call(kernel, name='gather_stream', cost_estimate=lasting(50), o...  52.4 us
    pallas_call x1, Pallas kernels, backward_local(): pl.pallas_call(kernel, name='backward_local', cost_estimate=lasting(30),...  37.4 us
    pallas_call x1, Pallas kernels, attend_forward(): pl.pallas_call(kernel, name='attend_forward', cost_estimate=lasting(22),...  19.8 us
    pallas_call x1, Pallas kernels, finish_local(): pl.pallas_call(kernel, name='finish_local', cost_estimate=lasting(9), gri...  12.3 us
  transfers between devices with their start and end apart: 2, of which 1 were waited for; matrix products, arithmetic and copies ran while one was open for 1% of the time, Pallas kernels for 17%

profile of v8, /device:TPU:1, one launch (start us, length us, event | category | flops | bytes accessed | tf_op | source)
XLA Modules:
  0.0 333.8 jit_solution(8312588507199591614)
XLA Ops:
  0.6 52.4 %gather_stream.1 = (bf16[16,128,1024]{2,1,0:T(8,128)(2,1)}, s32[8,2,128]{2,1,0:T(2,128)}, bf16[1024,384]{1,0:T(8,128)(2,1)}, bf16[256,1024]{1,0:T(8,128)(2,1)}, ...) custom-call(bf16[2,128,1024]{2,1,0:T(8,128)(2,1)} %bitcast.23, ...), custom_call_target="tpu_custom_call" | custom-call | bytes 165000000 | tf_op jit(solution)/shard_map/gather_stream/pallas_call | solution.py:685
  53.0 4.2 %all-to-all-start = ((bf16[8,8,8,1024]{3,2,1,0:T(8,128)(2,1)}), bf16[8,8,8,1024]{3,2,1,0:T(8,128)(2,1)S(1)}, u32[]{:S(2)}, u32[]{:S(2)}) async-start(bf16[8,8,8,1024]{3,2,1,0:T(8,128)(2,1)} %get-tuple-element.59), calls=%async_computation | async-start | bytes 2097152 | tf_op jit(solution)/shard_map/all_to_all | solution.py:1785
  57.2 0.8 fusion
  58.1 0.1 add_reduce_fusion
  58.2 0.6 pad_add_fusion
  58.8 0.5 and_select_fusion.first
  59.3 19.8 %attend_forward.1 = (bf16[2048,384]{1,0:T(8,128)(2,1)}, bf16[2048,128]{1,0:T(8,128)(2,1)}, f32[128,2048]{1,0:T(8,128)}, f32[2,2048]{1,0:T(2,128)}) custom-call(s32[8]{0:T(128)} %and_select_fusion.first, bf16[2048,1024]{1,0:T(8,128)(2,1)} %bitcast.21, bf16[1024,384]{1,0:T(8,128)(2,1)} %get-tuple-element.51.w_ref, s32[1,2048]{1,0:T(1,128)} %bitcast.34), custom_call_target="tpu_custom_call" | custom-call | bytes 72600000 | tf_op jit(solution)/shard_map/attend_forward/pallas_call | solution.py:770
  79.2 3.5 %all-to-all-done.g0_ref = bf16[8,8,8,1024]{3,2,1,0:T(8,128)(2,1)S(1)} async-done(((bf16[8,8,8,1024]{3,2,1,0:T(8,128)(2,1)}), bf16[8,8,8,1024]{3,2,1,0:T(8,128)(2,1)S(1)}, u32[]{:S(2)}, u32[]{:S(2)}) %all-to-all-start) | async-done | bytes 1048608 | tf_op jit(solution)/shard_map/all_to_all | solution.py:1785
  82.7 0.0 copy-start.1
  82.7 1.0 copy-done.1
  83.7 118.9 %experts_exchange.1 = (bf16[2,128,1024]{2,1,0:T(8,128)(2,1)}, f32[256,1024]{1,0:T(8,128)}, bf16[4,8,8,8,1024]{4,3,2,1,0:T(8,128)(2,1)}, bf16[3,8,8,8,1024]{4,3,2...) custom-call(bf16[16,128,128]{2,1,0:T(8,128)(2,1)} %bitcast.31, ...), custom_call_target="tpu_custom_call" | custom-call | bytes 330000000 | tf_op jit(solution)/shard_map/experts_exchange/pallas_call | solution.py:1368
  202.6 6.2 %all-to-all-start.1 = ((bf16[8,96,1024]{2,1,0:T(8,128)(2,1)}), bf16[8,96,1024]{2,1,0:T(8,128)(2,1)S(1)}, u32[]{:S(2)}, u32[]{:S(2)}) async-start(bf16[8,96,1024]{2,1,0:T(8,128)(2,1)} %get-tuple-element.62), calls=%async_computation.1 | async-start | bytes 3145728 | tf_op jit(solution)/shard_map/all_to_all | solution.py:1802
  208.8 37.4 %backward_local.1 = (bf16[2048,384]{1,0:T(8,128)(2,1)}, bf16[1024,384]{1,0:T(8,128)(2,1)}, f32[8,1024,1024]{2,1,0:T(8,128)}, f32[8,1024,1024]{2,1,0:T(8,128)}) custom-call(s32[8]{0:T(128)} %and_select_fusion.first, bf16[2048,384]{1,0:T(8,128)(2,1)} %get-tuple-element.52.q_ref.k_ref.v_ref, bf16[2048,384]{1,0:T(8,128)(2,1)} %get-tuple-element.52.q_ref.k_ref.v_ref, ...), custom_call_target="tpu_custom_call" | custom-call | bytes 99000000 | tf_op jit(solution)/shard_map/backward_local/pallas_call | solution.py:872
  246.2 0.0 all-to-all-done.1.home_ref.e_ref
  246.2 0.0 copy-start
  246.2 1.2 copy-done
  247.4 74.0 %finish_exchange.1 = (bf16[2,128,3072]{2,1,0:T(8,128)(2,1)}, bf16[256,3072]{1,0:T(8,128)(2,1)}, bf16[8,32,1024]{2,1,0:T(8,128)(2,1)}, f32[1,1024]{1,0:T(1,128)}, bf16[4,256,3072]{2,1,0:T(8,128)(2,1)}) custom-call(bf16[16,128,384]{2,1,0:T(8,128)(2,1)} %bitcast.29, bf16[4,256,384]{2,1,0:T(8,128)(2,1)} %bitcast.30, bf16[8,96,1024]{2,1,0:T(8,128)(2,1)} %copy-done, ...), custom_call_target="tpu_custom_call" | custom-call | bytes 198000000 | tf_op jit(solution)/shard_map/finish_exchange/pallas_call | solution.py:1664
  321.3 12.3 %finish_local.1 = (bf16[256,1024]{1,0:T(8,128)(2,1)}, f32[256,1024]{1,0:T(8,128)}, f32[256,3072]{1,0:T(8,128)}, f32[256,1024]{1,0:T(8,128)}, f32[1,256]{1,0:T(1,128)}, /*index=5*/f32[1,256]{1,0:T(1,128)}) custom-call(bf16[256,3072]{1,0:T(8,128)(2,1)} %bitcast.28, bf16[4,256,3072]{2,1,0:T(8,128)(2,1)} %get-tuple-element.76.w_ref, bf16[256,1024]{1,0:T(8,128)(2,1)} %bitcast.25, ...), custom_call_target="tpu_custom_call" | custom-call | bytes 29700000 | tf_op jit(solution)/shard_map/finish_local/pallas_call | solution.py:1749
  (4 shorter events, 0.0 us)
Async XLA Ops:
  53.0 29.7 %all-to-all-start = ((bf16[8,8,8,1024]{3,2,1,0:T(8,128)(2,1)}), bf16[8,8,8,1024]{3,2,1,0:T(8,128)(2,1)S(1)}, u32[]{:S(2)}, u32[]{:S(2)}) async-start(bf16[8,8,8,1024]{3,2,1,0:T(8,128)(2,1)} %get-tuple-element.59), calls=%async_computation | async-start | bytes 2097152 | tf_op jit(solution)/shard_map/all_to_all | solution.py:1785
  82.7 1.0 copy-start.1
  202.6 43.6 %all-to-all-start.1 = ((bf16[8,96,1024]{2,1,0:T(8,128)(2,1)}), bf16[8,96,1024]{2,1,0:T(8,128)(2,1)S(1)}, u32[]{:S(2)}, u32[]{:S(2)}) async-start(bf16[8,96,1024]{2,1,0:T(8,128)(2,1)} %get-tuple-element.62), calls=%async_computation.1 | async-start | bytes 3145728 | tf_op jit(solution)/shard_map/all_to_all | solution.py:1802
  246.2 1.2 copy-start
